TPU v7x, 256 devices: a whole 4x4x8 slice. The times are simulated.
256 devices in a mesh: grp: 4 (over y), col: 64 (over x, z, core).
Axes of the slice: x: 4, y: 4, z: 8, core: 2. Of those that a mesh axis runs over, the one named last changes fastest.
Arguments:
- right_side: float32 [2048, 2048], P('grp', 'col'), may hold values from -6 to 6
- solved_factor: float32 [2048, 49152], P('grp', 'col'), may hold values from -0.02734375 to 0.02734375
- solved_users: float32 [49152, 2048], P('col'), may hold values from -16 to 16
- diag_inverse: float32 [2048, 512], P('grp'), may hold values from -0.25 to 0.25
- coupling: float32 [2048, 1536], P('grp'), may hold values from -0.25 to 0.25
Outputs:
- solution: float32 [2048, 2048], P('grp', 'col')
All inputs are finite; a program needn't handle non-finite values.
Results may differ from a plain program's by a relative error of at most 0.0001.
Values sent between devices are 32-bit elements; how exact they have to be, the bound alone decides.
No kernel may reach another device: no remote copies, remote signals or barrier semaphores. Data moves between devices by JAX's collectives and lax.ppermute only.
A program may use at most 64 MiB of HBM per device.

v0:
```python
import jax
import jax.numpy as jnp
from jax import lax
from jax.sharding import Mesh
from jax.sharding import PartitionSpec as P

COL = ("col_0", "col_1", "col_2")


highest = lax.Precision.HIGHEST


def shifted(value, axis, by):
    peers = lax.axis_size(axis)
    pairs = [(i, i + by) for i in range(peers) if 0 <= i + by < peers]
    return lax.ppermute(value, axis, pairs)


def split_up(value, dim, peers):
    before, after = (value.shape[:dim], value.shape[dim + 1 :])
    return jnp.moveaxis(value.reshape(*before, peers, -1, *after), dim, 0)


def sum_at_owner(value, axis, dim):
    peers = lax.axis_size(axis)
    tiles = lax.all_to_all(split_up(value, dim, peers), axis, 0, 0, tiled=True)
    return jnp.sum(tiles, axis=0)


def summed_rows(value, axes, dim):
    far, near = axes
    own = sum_at_owner(split_up(value, dim, lax.axis_size(far)), near, dim + 1)
    return jnp.sum(lax.all_to_all(own, far, 0, 0, tiled=True), axis=0)


def apply_plain(matrix, vector):
    return jnp.dot(matrix, vector, precision=highest, preferred_element_type=jnp.float32)


def run_chain(residue, diag_inverse, coupling, apply_left):
    groups = lax.axis_size("grp")
    position = lax.axis_index("grp")
    block_rows = diag_inverse.shape[0]
    result = jnp.zeros_like(residue)
    carried = jnp.zeros((groups,) + residue.shape, jnp.float32)
    for section_index in range(groups):
        current = residue
        for earlier in range(section_index):
            coupling_block = coupling[:, earlier * block_rows : (earlier + 1) * block_rows]
            current = current - apply_left(coupling_block, carried[earlier])
        candidate = apply_left(diag_inverse, current)
        result = jnp.where(position == section_index, candidate, result)
        if section_index + 1 < groups:
            carried = carried.at[section_index].set(candidate)
            carried = shifted(carried, "grp", 1)
    return result


def on_device(right_side, solved_factor, solved_users, diag_inverse, coupling):
    partials = jnp.dot(
        solved_factor, solved_users, precision=highest, preferred_element_type=jnp.float32
    )
    shares = summed_rows(partials, (("col_0", "col_1"), "col_2"), 1)
    residue = right_side - shares
    return run_chain(residue, diag_inverse, coupling, apply_plain)


def solution(mesh):
    torus = Mesh(
        mesh.devices.reshape(mesh.shape["grp"], 4, 8, 2), ("grp", "col_0", "col_1", "col_2")
    )
    placed = (P("grp", COL), P("grp", COL), P(COL, None), P("grp", None), P("grp", None))
    return jax.shard_map(
        on_device, mesh=torus, in_specs=placed, out_specs=P("grp", COL), check_vma=False
    )
```

profile of v0, /device:TPU:32, one launch (start us, length us, event | category | flops | bytes accessed | tf_op | source)
XLA Modules:
  0.0 131.8 jit_solution(1979597726839969564)
XLA Ops:
  0.0 0.0 copy-start
  0.0 1.4 %copy-done = f32[512,768]{1,0:T(8,128)S(1)} copy-done((f32[512,768]{1,0:T(8,128)S(1)}, f32[512,768]{1,0:T(8,128)}, u32[]{:S(2)}) %copy-start) | copy-done | bytes 1572888
  1.4 12.1 %fusion.13 = f32[512,2048]{0,1:T(8,128)S(1)} fusion(f32[512,768]{1,0:T(8,128)S(1)} %copy-done, f32[768,2048]{1,0:T(8,128)} %param.13), kind=kOutput, calls=%fused_computation.31 | convolution fusion | flops 9663676416 | bytes 12058624 | tf_op jit(solution)/shard_map/dot_general | solution.py:60
  13.6 0.8 copy.8
  14.4 8.2 %all_to_all.10 = f32[2,32,512,32]{2,3,1,0:T(8,128)} all-to-all(f32[2,32,512,32]{2,3,1,0:T(8,128)S(1)} %copy.8), channel_id=1, replica_groups=mesh['grp'=4,'col_0'=4,'col_1'=8,'col_2'=2] {'col_2'}, dimensions={0} | all-to-all | bytes 8388608 | tf_op jit(solution)/shard_map/all_to_all | solution.py:26
  22.5 4.2 %reduce_sum.18 = f32[32,512,32]{1,2,0:T(8,128)} reduce(f32[2,32,512,32]{2,3,1,0:T(8,128)} %all_to_all.10, f32[]{:T(128)} %constant.93.clone.1), dimensions={0}, to_apply=%region_0.0 | reduce | flops 524288 | bytes 6291460 | tf_op jit(solution)/shard_map/reduce_sum | solution.py:27
  26.7 0.0 copy-start.3
  26.7 0.0 copy-start.1
  26.7 62.7 %all_to_all.11 = f32[32,512,32]{1,2,0:T(8,128)} all-to-all(f32[32,512,32]{1,2,0:T(8,128)} %reduce_sum.18), channel_id=1, replica_groups=mesh['grp'=4,'col_0'=4,'col_1'=8,'col_2'=2] {'col_0','col_1'}, dimensions={0} | all-to-all | bytes 4194304 | tf_op jit(solution)/shard_map/all_to_all | solution.py:33
  89.4 1.7 %reduce_sum.19 = f32[512,32]{0,1:T(8,128)S(1)} reduce(f32[32,512,32]{1,2,0:T(8,128)} %all_to_all.11, f32[]{:T(128)} %constant.93.clone.1), dimensions={0}, to_apply=%region_1.0 | reduce | flops 507904 | bytes 2162692 | tf_op jit(solution)/shard_map/reduce_sum | solution.py:33
  91.1 0.0 copy-done.3
  91.1 0.0 copy-start.2
  91.2 0.0 copy-done.1
  91.2 1.0 fusion.14
  92.3 3.5 %collective-permute-start = (f32[4,512,32]{1,2,0:T(8,128)S(1)}, f32[4,512,32]{1,2,0:T(8,128)S(1)}, u32[]{:S(2)}, u32[]{:S(2)}) collective-permute-start(f32[4,512,32]{1,2,0:T(8,128)S(1)} %scatter.10), channel_id=1, source_target_pairs={{0,64},{64,128},{128,192},{1,65},{65,129},{129,193},{2,66},{66,130... | collective-permute-start | bytes 786440 | tf_op jit(solution)/shard_map/ppermute | solution.py:16
  95.8 4.5 %collective-permute-done = f32[4,512,32]{1,2,0:T(8,128)S(1)} collective-permute-done((f32[4,512,32]{1,2,0:T(8,128)S(1)}, f32[4,512,32]{1,2,0:T(8,128)S(1)}, u32[]{:S(2)}, u32[]{:S(2)}) %collective-permute-start) | collective-permute-done | bytes 262176 | tf_op jit(solution)/shard_map/ppermute | solution.py:16
  100.3 2.3 %fusion.6 = f32[512,32]{0,1:T(8,128)S(1)} fusion(f32[512,32]{0,1:T(8,128)S(1)} %sub.21, f32[512,1536]{1,0:T(8,128)} %param.15, f32[4,512,32]{1,2,0:T(8,128)S(1)} %collective-permute-done), kind=kOutput, calls=%fused_computation.13 | convolution fusion | flops 100679680 | bytes 1245184 | tf_op jit(solution)/shard_map/dot_general | solution.py:37
  102.5 1.0 bitcast_dynamic-update-slice_fusion.1
  103.6 4.6 %collective-permute-start.1 = (f32[4,512,32]{1,2,0:T(8,128)S(1)}, f32[4,512,32]{1,2,0:T(8,128)S(1)}, u32[]{:S(2)}, u32[]{:S(2)}) collective-permute-start(f32[4,512,32]{1,2,0:T(8,128)S(1)} %get-tuple-element.41), channel_id=1, source_target_pairs={{0,64},{64,128},{128,192},{1,65},{65,129},{129,193},{2,66},{66,130... | collective-permute-start | bytes 786440 | tf_op jit(solution)/shard_map/ppermute | solution.py:16
  108.2 3.7 %collective-permute-done.1 = f32[4,512,32]{1,2,0:T(8,128)S(1)} collective-permute-done((f32[4,512,32]{1,2,0:T(8,128)S(1)}, f32[4,512,32]{1,2,0:T(8,128)S(1)}, u32[]{:S(2)}, u32[]{:S(2)}) %collective-permute-start.1) | collective-permute-done | bytes 262176 | tf_op jit(solution)/shard_map/ppermute | solution.py:16
  111.8 0.0 copy-done.2
  111.8 1.0 convolution_bitcast_fusion.4
  112.9 1.1 fusion.5
  114.0 1.0 bitcast_dynamic-update-slice_fusion
  115.0 4.4 %collective-permute-start.2 = (f32[4,512,32]{1,2,0:T(8,128)S(1)}, f32[4,512,32]{1,2,0:T(8,128)S(1)}, u32[]{:S(2)}, u32[]{:S(2)}) collective-permute-start(f32[4,512,32]{1,2,0:T(8,128)S(1)} %get-tuple-element.43), channel_id=1, source_target_pairs={{0,64},{64,128},{128,192},{1,65},{65,129},{129,193},{2,66},{66,130... | collective-permute-start | bytes 786440 | tf_op jit(solution)/shard_map/ppermute | solution.py:16
  119.4 3.8 %collective-permute-done.2 = f32[4,512,32]{1,2,0:T(8,128)S(1)} collective-permute-done((f32[4,512,32]{1,2,0:T(8,128)S(1)}, f32[4,512,32]{1,2,0:T(8,128)S(1)}, u32[]{:S(2)}, u32[]{:S(2)}) %collective-permute-start.2) | collective-permute-done | bytes 262176 | tf_op jit(solution)/shard_map/ppermute | solution.py:16
  123.3 2.3 %convolution_bitcast_fusion.1 = f32[512,32]{0,1:T(8,128)S(1)} fusion(f32[512,1536]{1,0:T(8,128)} %param.15, f32[4,512,32]{1,2,0:T(8,128)S(1)} %collective-permute-done.2), kind=kOutput, calls=%fused_computation.2 | convolution fusion | flops 100663296 | bytes 1179648 | tf_op jit(solution)/shard_map/dot_general | solution.py:37
  125.5 2.3 %convolution_bitcast_fusion.2 = f32[512,32]{0,1:T(8,128)S(1)} fusion(f32[512,1536]{1,0:T(8,128)} %param.15, f32[4,512,32]{1,2,0:T(8,128)S(1)} %collective-permute-done.2), kind=kOutput, calls=%fused_computation.3 | convolution fusion | flops 100663296 | bytes 1179648 | tf_op jit(solution)/shard_map/dot_general | solution.py:37
  127.8 2.3 %fusion.3 = f32[512,32]{0,1:T(8,128)S(1)} fusion(f32[512,32]{0,1:T(8,128)S(1)} %convolution_bitcast_fusion.1, f32[512,32]{0,1:T(8,128)S(1)} %convolution_bitcast_fusion.2, f32[512,32]{0,1:T(8,128)S(1)} %sub.21, f32[512,1536]{1,0:T(8,128)} %param.15, f32[4,512,32]{1,2,0:T(8,128)S(1)} %collective-permute-done.2), kind=kOutput, calls=%fused_computation.7 | convolution fusion | flops 100712448 | bytes 1376256 | tf_op jit(solution)/shard_map/dot_general | solution.py:37
  130.1 1.7 %fusion = f32[512,32]{0,1:T(8,128)} fusion(f32[512,32]{0,1:T(8,128)S(1)} %fusion.3, f32[512,512]{1,0:T(8,128)S(1)} %copy-done.1, f32[32,512]{1,0:T(8,128)S(1)} %get-tuple-element.44, f32[32,512]{1,0:T(8,128)S(1)} %get-tuple-element.42, f32[32,512]{1,0:T(8,128)S(1)} %fusion.14, pred[]{:T(512)S(6)} %eq.15, pred[]{:T(512)S(6)} %eq.14, pred[]{:T(512)S(6)} %eq.13, ...), kind=kOutput, calls=%fused_computation.1 | convolution fusion | flops 100728832 | bytes 1376260 | tf_op jit(solution)/shard_map/dot_general | solution.py:37
  (2 shorter events, 0.0 us)
Async XLA Ops:
  0.0 1.4 %copy-start = (f32[512,768]{1,0:T(8,128)S(1)}, f32[512,768]{1,0:T(8,128)}, u32[]{:S(2)}) copy-start(f32[512,768]{1,0:T(8,128)} %param.12) | copy-start | bytes 4718596
  26.7 64.4 %copy-start.3 = (f32[512,32]{0,1:T(8,128)S(1)}, f32[512,32]{0,1:T(8,128)}, u32[]{:S(2)}) copy-start(f32[512,32]{0,1:T(8,128)} %param.11) | copy-start | bytes 196612
  26.7 64.5 %copy-start.1 = (f32[512,512]{1,0:T(8,128)S(1)}, f32[512,512]{1,0:T(8,128)}, u32[]{:S(2)}) copy-start(f32[512,512]{1,0:T(8,128)} %param.14) | copy-start | bytes 3145732
  91.1 20.7 %copy-start.2 = (f32[512,1536]{1,0:T(8,128)S(1)}, f32[512,1536]{1,0:T(8,128)}, u32[]{:S(2)}) copy-start(f32[512,1536]{1,0:T(8,128)} %param.15) | copy-start | bytes 9437188
  92.3 8.0 %collective-permute-start = (f32[4,512,32]{1,2,0:T(8,128)S(1)}, f32[4,512,32]{1,2,0:T(8,128)S(1)}, u32[]{:S(2)}, u32[]{:S(2)}) collective-permute-start(f32[4,512,32]{1,2,0:T(8,128)S(1)} %scatter.10), channel_id=1, source_target_pairs={{0,64},{64,128},{128,192},{1,65},{65,129},{129,193},{2,66},{66,130... | collective-permute-start | bytes 786440 | tf_op jit(solution)/shard_map/ppermute | solution.py:16
  103.6 8.3 %collective-permute-start.1 = (f32[4,512,32]{1,2,0:T(8,128)S(1)}, f32[4,512,32]{1,2,0:T(8,128)S(1)}, u32[]{:S(2)}, u32[]{:S(2)}) collective-permute-start(f32[4,512,32]{1,2,0:T(8,128)S(1)} %get-tuple-element.41), channel_id=1, source_target_pairs={{0,64},{64,128},{128,192},{1,65},{65,129},{129,193},{2,66},{66,130... | collective-permute-start | bytes 786440 | tf_op jit(solution)/shard_map/ppermute | solution.py:16
  115.0 8.3 %collective-permute-start.2 = (f32[4,512,32]{1,2,0:T(8,128)S(1)}, f32[4,512,32]{1,2,0:T(8,128)S(1)}, u32[]{:S(2)}, u32[]{:S(2)}) collective-permute-start(f32[4,512,32]{1,2,0:T(8,128)S(1)} %get-tuple-element.43), channel_id=1, source_target_pairs={{0,64},{64,128},{128,192},{1,65},{65,129},{129,193},{2,66},{66,130... | collective-permute-start | bytes 786440 | tf_op jit(solution)/shard_map/ppermute | solution.py:16
where the time goes:
time: 133 us; the launch traced here: 132 us
  blocking collectives  70.8 us (53%)
  matrix products  28.1 us (21%)
  starting transfers between devices  12.5 us (9%)
  waiting for transfers between devices  12 us (9%)
  other arithmetic  5.94 us (4%)
  local copies, waits for them, and re-layouts  2.24 us (2%)
    all_to_all x1, blocking collectives, summed_rows(): return jnp.sum(lax.all_to_all(own, far, 0, 0, tiled=True), axis=0)  62.7 us
    dot_general x10, matrix products, apply_plain(): jnp.dot(matrix, vector, precision=highest, preferred_element_type=jnp.flo...  16 us
    ppermute x3, starting transfers between devices, shifted(): return lax.ppermute(value, axis, pairs)  12.5 us
    dot_general x1, matrix products, on_device(): jnp.dot(solved_factor, solved_users, precision=highest, preferred_element...  12.1 us
    ppermute x3, waiting for transfers between devices, shifted(): return lax.ppermute(value, axis, pairs)  12 us
    all_to_all x1, blocking collectives, sum_at_owner(): tiles = lax.all_to_all(split_up(value, dim, peers), axis, 0, 0, tiled=True)  8.15 us
    reduce_sum x1, other arithmetic, sum_at_owner(): return jnp.sum(tiles, axis=0)  4.19 us
  transfers between devices with their start and end apart: 3, of which 3 were waited for; matrix products, arithmetic and copies ran while one was open for 0% of the time, Pallas kernels for 0%

commit v1 on v0

v1 whole, which is shorter than its diff:
```python
import functools

import jax
import jax.numpy as jnp
from jax import lax
from jax.experimental import pallas as pl
from jax.experimental.pallas import tpu as pltpu
from jax.sharding import Mesh
from jax.sharding import PartitionSpec as P

COL = ("x", "z", "core")


def shifted(value, axis, by):
    peers = lax.axis_size(axis)
    return lax.ppermute(value, axis, [(i, (i + by) % peers) for i in range(peers)])


def halves(value):
    high = value.astype(jnp.bfloat16)
    return high, (value - high.astype(jnp.float32)).astype(jnp.bfloat16)


def contract(left, right, left_dim, right_dim):
    dims = (((left_dim,), (right_dim,)), ((), ()))
    return lax.dot_general(left, right, dims, preferred_element_type=jnp.float32)


def three_pass(left, right, left_dim, right_dim):
    left_high, left_low = halves(left)
    right_high, right_low = halves(right)
    return contract(left_high, right_high, left_dim, right_dim) + (
        contract(left_high, right_low, left_dim, right_dim)
        + contract(left_low, right_high, left_dim, right_dim)
    )


def product_body(n_z, n_core, place, users, factor, own_a, own_b, sent_a, sent_b):
    z, core = place[1], place[2]
    items, rows = users.shape[1], factor.shape[0]
    share = items // (n_z * n_core)
    total = three_pass(users[...], factor[...], 0, 1).reshape(n_z, n_core, share, rows)

    def keep(mine):
        for k in range(n_z):
            ahead = lax.rem(k - z + n_z, n_z)
            own, sent = total[k, mine], total[k, 1 - mine]
            own_a[0, ahead] = own[:, : rows // 2]
            own_b[ahead, 0] = own[:, rows // 2 :]
            sent_a[0, ahead] = sent[:, : rows // 2]
            sent_b[ahead, 0] = sent[:, rows // 2 :]

    pl.when(core == 0)(lambda: keep(0))
    pl.when(core == 1)(lambda: keep(1))


def product(place, users, factor, n_x, n_z, n_core):
    depth, items = users.shape
    rows = factor.shape[0]
    chunk, share = items // n_x, items // (n_x * n_z * n_core)
    by_x = pl.BlockSpec((1, n_z, share, rows // 2), lambda i, s: (i, 0, 0, 0))
    by_z = pl.BlockSpec((n_z, 1, share, rows // 2), lambda i, s: (0, i, 0, 0))
    shape_a = jax.ShapeDtypeStruct((n_x, n_z, share, rows // 2), jnp.float32)
    shape_b = jax.ShapeDtypeStruct((n_z, n_x, share, rows // 2), jnp.float32)
    return pl.pallas_call(
        functools.partial(product_body, n_z, n_core),
        grid_spec=pltpu.PrefetchScalarGridSpec(
            num_scalar_prefetch=1,
            grid=(n_x,),
            in_specs=[
                pl.BlockSpec((depth, chunk), lambda i, s: (0, lax.rem(s[0] + i, n_x))),
                pl.BlockSpec((rows, depth), lambda i, s: (0, 0)),
            ],
            out_specs=[by_x, by_z, by_x, by_z],
        ),
        out_shape=[shape_a, shape_b, shape_a, shape_b],
        compiler_params=pltpu.CompilerParams(vmem_limit_bytes=40 << 20),
    )(place, users, factor)


def ring_reduced(blocks, axis):
    blocks = list(blocks)
    peers = len(blocks)
    far = peers // 2
    cut = blocks[far].shape[0] // 2
    up = shifted(blocks[far][:cut], axis, 1)
    down = shifted(blocks[far][cut:], axis, -1)
    ahead, behind = far - 1, far + 1
    first, second = blocks[ahead], blocks[behind]
    blocks[ahead] = jnp.concatenate([first[:cut] + up, first[cut:]])
    blocks[behind] = jnp.concatenate([second[:cut], second[cut:] + down])
    for step in range(far - 1, 0, -1):
        up = shifted(blocks[step], axis, 1)
        down = shifted(blocks[peers - step], axis, -1)
        if step > 1:
            blocks[step - 1] = blocks[step - 1] + up
            blocks[peers - step + 1] = blocks[peers - step + 1] + down
    return blocks[0] + up + down


def direct_reduced(blocks, axis):
    peers = len(blocks)
    order = sorted(range(1, peers), key=lambda o: -min(o, peers - o))
    parts = [shifted(blocks[o], axis, o) for o in order]
    return functools.reduce(lambda a, b: a + b, parts, blocks[0])


def apply_rows(vectors, matrix):
    return jnp.dot(vectors, matrix.T, precision="highest", preferred_element_type=jnp.float32)


def chain(residue, diag_inverse, coupled):
    position = lax.axis_index("grp")
    groups = lax.axis_size("grp")

    def only(where, value):
        return jnp.where(where, value, jnp.zeros_like(value))

    result = apply_rows(residue, diag_inverse)
    later = []
    for step in range(groups - 1):
        near = shifted(result, "grp", 1)
        far = [(by, shifted(result, "grp", by)) for by in range(2, groups - step)]
        change = apply_rows(only(position == step + 1, near), coupled[step])
        for other, value in later:
            change = change + apply_rows(value, coupled[other])
        result = result - change
        later = [
            (step, functools.reduce(lambda a, b: a + b, [only(position == step + by, v) for by, v in far]))
        ] if far else []
    return result


def on_device(right_side, solved_factor, solved_users, diag_inverse, coupling):
    n_x, n_z, n_core = (lax.axis_size(a) for a in COL)
    place = jnp.stack([lax.axis_index(a) for a in COL]).astype(jnp.int32)
    own_a, own_b, sent_a, sent_b = product(place, solved_users, solved_factor, n_x, n_z, n_core)
    block = diag_inverse.shape[0]
    coupled = [
        jnp.dot(
            diag_inverse,
            coupling[:, h * block : (h + 1) * block],
            precision="highest",
            preferred_element_type=jnp.float32,
        )
        for h in range(coupling.shape[1] // block)
    ]
    sum_b = own_b + shifted(sent_b, "core", 1)
    sum_a = [None] * n_x
    for o in sorted(range(n_x), key=lambda o: -min(o, n_x - o)):
        sum_a[o] = own_a[o] + shifted(sent_a[o], "core", 1)
    part_b = ring_reduced([sum_b[o] for o in range(n_z)], "z")
    part_a = ring_reduced(sum_a, "x")
    share_a = direct_reduced([part_a[o] for o in range(n_z)], "z")
    share_b = direct_reduced([part_b[o] for o in range(n_x)], "x")
    residue = right_side.T - jnp.concatenate([share_a, share_b], axis=1)
    return chain(residue, diag_inverse, coupled).T


def solution(mesh):
    torus = Mesh(mesh.devices.reshape(mesh.shape["grp"], 4, 8, 2), ("grp",) + COL)
    placed = (P("grp", COL), P("grp", COL), P(COL, None), P("grp", None), P("grp", None))
    return jax.shard_map(
        on_device, mesh=torus, in_specs=placed, out_specs=P("grp", COL), check_vma=False
    )
```

time: 133 us -> 100 us (0.75)
  blocking collectives: 70.8 us -> 0 us
  starting transfers between devices: 12.5 us -> 50.7 us
  matrix products: 28.1 us -> 13.5 us
  waiting for transfers between devices: 12 us -> 22.6 us
  Pallas kernels: 0 us -> 7.49 us
  other arithmetic: 5.94 us -> 0.71 us
  local copies, waits for them, and re-layouts: 2.24 us -> 4.45 us
    all_to_all x2 -> x0, blocking collectives: 70.8 us -> none  [the longest x1 62.7 us: summed_rows(): return jnp.sum(lax.all_to_all(own, far, 0, 0, tiled=True), axis=0)]
    ppermute x3 -> x33, starting transfers between devices: 12.5 us -> 50.7 us  [shifted(): lax.ppermute(value, axis, [(i, (i + by) % peers) for i in range(peers)])]
    dot_general x11 -> x9, matrix products: 28.1 us -> 13.5 us  [the longest x6 6.97 us: apply_rows(): jnp.dot(vectors, matrix.T, precision='highest', preferred_element_type=jn...]
    ppermute x3 -> x33, waiting for transfers between devices: 12 us -> 22.6 us  [shifted(): lax.ppermute(value, axis, [(i, (i + by) % peers) for i in range(peers)])]
    pallas_call x0 -> x1, Pallas kernels: none -> 7.49 us  [product(): pl.pallas_call(functools.partial(product_body, n_z, n_core), grid_spec=pl...]
    reduce_sum x2 -> x0, other arithmetic: 5.93 us -> none  [the longest x1 4.19 us: sum_at_owner(): return jnp.sum(tiles, axis=0)]
    unnamed x8 -> x12, local copies, waits for them, and re-layouts: 1.42 us -> 4.29 us
  transfers between devices with their start and end apart: 3 -> 33, of which waited for: 3 -> 13; matrix products, arithmetic and copies ran while one was open for 0% -> 11% of each run, Pallas kernels for 0% -> 0%
where the time goes in v1:
time: 100 us; the launch traced here: 99.8 us
  starting transfers between devices  50.7 us (51%)
  waiting for transfers between devices  22.6 us (23%)
  matrix products  13.5 us (14%)
  Pallas kernels  7.49 us (7%)
  local copies, waits for them, and re-layouts  4.45 us (4%)
    ppermute x33, starting transfers between devices, shifted(): lax.ppermute(value, axis, [(i, (i + by) % peers) for i in range(peers)])  50.7 us
    ppermute x33, waiting for transfers between devices, shifted(): lax.ppermute(value, axis, [(i, (i + by) % peers) for i in range(peers)])  22.6 us
    pallas_call x1, Pallas kernels, product(): pl.pallas_call(functools.partial(product_body, n_z, n_core), grid_spec=pl...  7.49 us
    dot_general x6, matrix products, apply_rows(): jnp.dot(vectors, matrix.T, precision='highest', preferred_element_type=jn...  6.97 us
    dot_general x3, matrix products, on_device(): jnp.dot(diag_inverse, coupling[:, h * block:(h + 1) * block], precision='...  6.54 us
    unnamed x12, local copies, waits for them, and re-layouts  4.29 us
  transfers between devices with their start and end apart: 33, of which 13 were waited for; matrix products, arithmetic and copies ran while one was open for 11% of the time, Pallas kernels for 0%

profile of v1, /device:TPU:32, one launch (start us, length us, event | category | flops | bytes accessed | tf_op | source)
XLA Modules:
  0.0 99.8 jit_solution(8689027551261961238)
XLA Ops:
  0.0 0.1 pad_add_fusion.place
  0.1 2.9 %copy-done.1 = f32[768,2048]{1,0:T(8,128)S(1)} copy-done((f32[768,2048]{1,0:T(8,128)S(1)}, f32[768,2048]{1,0:T(8,128)}, u32[]{:S(2)}) %copy-start.1) | copy-done | bytes 6291480
  2.9 1.4 %copy-done.2 = f32[512,768]{1,0:T(8,128)S(1)} copy-done((f32[512,768]{1,0:T(8,128)S(1)}, f32[512,768]{1,0:T(8,128)}, u32[]{:S(2)}) %copy-start.2) | copy-done | bytes 1572888
  4.3 7.5 %shard_map.55 = (f32[4,8,32,256]{3,2,1,0:T(8,128)S(1)}, f32[8,4,32,256]{3,2,1,0:T(8,128)S(1)}, f32[4,8,32,256]{3,2,1,0:T(8,128)S(1)}, f32[8,4,32,256]{3,2,1,0:T(8,128)S(1)}) custom-call(s32[3]{0:T(128)S(1)} %pad_add_fusion.place, f32[768,2048]{1,0:T(8,128)S(1)} %copy-done.1, f32[512,768]{1,0:T(8,128)S(1)} %copy-done.2), custom_call_target="tpu_custom_call" | custom-call | tf_op jit(solution)/shard_map/pallas_call | solution.py:65
  11.9 0.0 copy-start.4
  11.9 0.1 slice_bitcast_fusion.3
  12.0 0.1 collective-permute-start.1
  12.1 0.5 collective-permute-start.2
  12.6 0.1 collective-permute-start.5
  12.7 0.4 collective-permute-start
  13.1 0.1 collective-permute-start.15
  13.2 0.4 collective-permute-done.1
  13.6 0.4 collective-permute-done.2
  14.0 0.4 collective-permute-done.5
  14.3 0.1 bitcast_add_fusion.2
  14.5 1.6 %collective-permute-start.3 = (f32[4,32,256]{2,1,0:T(8,128)S(1)}, f32[4,32,256]{2,1,0:T(8,128)S(1)}, u32[]{:S(2)}, u32[]{:S(2)}) collective-permute-start(f32[4,32,256]{2,1,0:T(8,128)S(1)} %get-tuple-element.37), channel_id=1, source_target_pairs={{0,16},{16,32},{32,48},{48,0},{1,17},{17,33},{33,49},{49,1},{2,18}... | collective-permute-start | bytes 393224 | tf_op jit(solution)/shard_map/ppermute | solution.py:16
  16.1 1.9 %fusion.6 = f32[512,512]{1,0:T(8,128)S(1)} fusion(f32[512,512]{1,0:T(8,128)S(1)} %copy-done, f32[512,1536]{1,0:T(8,128)S(1)} %copy-done.4), kind=kOutput, calls=%fused_computation.9 | convolution fusion | flops 1610612736 | bytes 3145728 | tf_op jit(solution)/shard_map/dot_general | solution.py:140
  17.9 1.8 %collective-permute-start.6 = (f32[4,32,256]{2,1,0:T(8,128)S(1)}, f32[4,32,256]{2,1,0:T(8,128)S(1)}, u32[]{:S(2)}, u32[]{:S(2)}) collective-permute-start(f32[4,32,256]{2,1,0:T(8,128)S(1)} %get-tuple-element.38), channel_id=1, source_target_pairs={{0,48},{16,0},{32,16},{48,32},{1,49},{17,1},{33,17},{49,33},{2,50}... | collective-permute-start | bytes 393224 | tf_op jit(solution)/shard_map/ppermute | solution.py:16
  19.8 1.6 %collective-permute-done.3 = f32[4,32,256]{2,1,0:T(8,128)S(1)} collective-permute-done((f32[4,32,256]{2,1,0:T(8,128)S(1)}, f32[4,32,256]{2,1,0:T(8,128)S(1)}, u32[]{:S(2)}, u32[]{:S(2)}) %collective-permute-start.3) | collective-permute-done | bytes 131104 | tf_op jit(solution)/shard_map/ppermute | solution.py:16
  21.4 0.4 collective-permute-start.4
  21.8 0.2 add.108
  22.0 2.0 %collective-permute-start.16 = (f32[2,32,256]{2,1,0:T(8,128)S(1)}, f32[2,32,256]{2,1,0:T(8,128)S(1)}, u32[]{:S(2)}, u32[]{:S(2)}) collective-permute-start(f32[2,32,256]{2,1,0:T(8,128)S(1)} %get-tuple-element.24), channel_id=1, source_target_pairs={{0,2},{2,4},{4,6},{6,8},{8,10},{10,12},{12,14},{14,0},{1,3},{3,5},... | collective-permute-start | bytes 196616 | tf_op jit(solution)/shard_map/ppermute | solution.py:16
  24.0 0.1 collective-permute-start.20
  24.1 2.2 %collective-permute-done.16 = f32[2,32,256]{2,1,0:T(8,128)S(1)} collective-permute-done((f32[2,32,256]{2,1,0:T(8,128)S(1)}, f32[2,32,256]{2,1,0:T(8,128)S(1)}, u32[]{:S(2)}, u32[]{:S(2)}) %collective-permute-start.16) | collective-permute-done | bytes 65568 | tf_op jit(solution)/shard_map/ppermute | solution.py:16
  26.3 1.9 %collective-permute-done.20 = f32[2,32,256]{2,1,0:T(8,128)S(1)} collective-permute-done((f32[2,32,256]{2,1,0:T(8,128)S(1)}, f32[2,32,256]{2,1,0:T(8,128)S(1)}, u32[]{:S(2)}, u32[]{:S(2)}) %collective-permute-start.20) | collective-permute-done | bytes 65568 | tf_op jit(solution)/shard_map/ppermute | solution.py:16
  28.3 3.1 %collective-permute-start.17 = (f32[4,32,256]{2,1,0:T(8,128)S(1)}, f32[4,32,256]{2,1,0:T(8,128)S(1)}, u32[]{:S(2)}, u32[]{:S(2)}) collective-permute-start(f32[4,32,256]{2,1,0:T(8,128)S(1)} %pad_maximum_fusion.2), channel_id=1, source_target_pairs={{0,2},{2,4},{4,6},{6,8},{8,10},{10,12},{12,14},{14,0},{1,3},{3,5},... | collective-permute-start | bytes 393224 | tf_op jit(solution)/shard_map/ppermute | solution.py:16
  31.4 3.0 %collective-permute-start.7 = (f32[8,32,256]{2,1,0:T(8,128)S(1)}, f32[8,32,256]{2,1,0:T(8,128)S(1)}, u32[]{:S(2)}, u32[]{:S(2)}) collective-permute-start(f32[8,32,256]{2,1,0:T(8,128)S(1)} %pad_maximum_fusion.1), channel_id=1, source_target_pairs={{0,48},{16,0},{32,16},{48,32},{1,49},{17,1},{33,17},{49,33},{2,50}... | collective-permute-start | bytes 786440 | tf_op jit(solution)/shard_map/ppermute | solution.py:16
  34.4 0.3 collective-permute-start.21
  34.8 0.0 copy-start.5
  34.8 3.3 %collective-permute-start.18 = (f32[4,32,256]{2,1,0:T(8,128)S(1)}, f32[4,32,256]{2,1,0:T(8,128)S(1)}, u32[]{:S(2)}, u32[]{:S(2)}) collective-permute-start(f32[4,32,256]{2,1,0:T(8,128)S(1)} %fusion.12), channel_id=1, source_target_pairs={{0,2},{2,4},{4,6},{6,8},{8,10},{10,12},{12,14},{14,0},{1,3},{3,5},... | collective-permute-start | bytes 393224 | tf_op jit(solution)/shard_map/ppermute | solution.py:16
  38.1 1.8 %fusion.4 = f32[512,512]{1,0:T(8,128)S(1)} fusion(f32[512,512]{1,0:T(8,128)S(1)} %copy-done, f32[512,1536]{1,0:T(8,128)S(1)} %copy-done.4), kind=kOutput, calls=%fused_computation.7 | convolution fusion | flops 1610612736 | bytes 3145728 | tf_op jit(solution)/shard_map/dot_general | solution.py:140
  39.9 1.7 %collective-permute-done.21 = f32[4,32,256]{2,1,0:T(8,128)S(1)} collective-permute-done((f32[4,32,256]{2,1,0:T(8,128)S(1)}, f32[4,32,256]{2,1,0:T(8,128)S(1)}, u32[]{:S(2)}, u32[]{:S(2)}) %collective-permute-start.21) | collective-permute-done | bytes 131104 | tf_op jit(solution)/shard_map/ppermute | solution.py:16
  41.6 1.8 %collective-permute-start.22 = (f32[4,32,256]{2,1,0:T(8,128)S(1)}, f32[4,32,256]{2,1,0:T(8,128)S(1)}, u32[]{:S(2)}, u32[]{:S(2)}) collective-permute-start(f32[4,32,256]{2,1,0:T(8,128)S(1)} %get-tuple-element.21), channel_id=1, source_target_pairs={{0,14},{2,0},{4,2},{6,4},{8,6},{10,8},{12,10},{14,12},{1,15},{3,1}... | collective-permute-start | bytes 393224 | tf_op jit(solution)/shard_map/ppermute | solution.py:16
  43.5 0.1 fusion.9
  43.5 0.6 collective-permute-start.19
  44.1 4.1 %collective-permute-done.22 = f32[4,32,256]{2,1,0:T(8,128)S(1)} collective-permute-done((f32[4,32,256]{2,1,0:T(8,128)S(1)}, f32[4,32,256]{2,1,0:T(8,128)S(1)}, u32[]{:S(2)}, u32[]{:S(2)}) %collective-permute-start.22) | collective-permute-done | bytes 131104 | tf_op jit(solution)/shard_map/ppermute | solution.py:16
  48.2 1.3 %collective-permute-start.23 = (f32[4,32,256]{2,1,0:T(8,128)S(1)}, f32[4,32,256]{2,1,0:T(8,128)S(1)}, u32[]{:S(2)}, u32[]{:S(2)}) collective-permute-start(f32[4,32,256]{2,1,0:T(8,128)S(1)} %fusion.11), channel_id=1, source_target_pairs={{0,14},{2,0},{4,2},{6,4},{8,6},{10,8},{12,10},{14,12},{1,15},{3,1}... | collective-permute-start | bytes 393224 | tf_op jit(solution)/shard_map/ppermute | solution.py:16
  49.6 2.9 %collective-permute-start.10 = (f32[32,256]{1,0:T(8,128)S(1)}, f32[32,256]{1,0:T(8,128)S(1)}, u32[]{:S(2)}, u32[]{:S(2)}) collective-permute-start(f32[32,256]{1,0:T(8,128)S(1)} %get-tuple-element.33), channel_id=1, source_target_pairs={{0,10},{2,12},{4,14},{6,0},{8,2},{10,4},{12,6},{14,8},{1,11},{3,13... | collective-permute-start | bytes 98312 | tf_op jit(solution)/shard_map/ppermute | solution.py:16
  52.4 3.1 %collective-permute-start.11 = (f32[32,256]{1,0:T(8,128)S(1)}, f32[32,256]{1,0:T(8,128)S(1)}, u32[]{:S(2)}, u32[]{:S(2)}) collective-permute-start(f32[32,256]{1,0:T(8,128)S(1)} %get-tuple-element.32), channel_id=1, source_target_pairs={{0,4},{2,6},{4,8},{6,10},{8,12},{10,14},{12,0},{14,2},{1,5},{3,7},... | collective-permute-start | bytes 98312 | tf_op jit(solution)/shard_map/ppermute | solution.py:16
  55.6 2.2 %collective-permute-start.12 = (f32[32,256]{1,0:T(8,128)S(1)}, f32[32,256]{1,0:T(8,128)S(1)}, u32[]{:S(2)}, u32[]{:S(2)}) collective-permute-start(f32[32,256]{1,0:T(8,128)S(1)} %get-tuple-element.31), channel_id=1, source_target_pairs={{0,12},{2,14},{4,0},{6,2},{8,4},{10,6},{12,8},{14,10},{1,13},{3,15... | collective-permute-start | bytes 98312 | tf_op jit(solution)/shard_map/ppermute | solution.py:16
  57.8 2.0 %collective-permute-start.14 = (f32[32,256]{1,0:T(8,128)S(1)}, f32[32,256]{1,0:T(8,128)S(1)}, u32[]{:S(2)}, u32[]{:S(2)}) collective-permute-start(f32[32,256]{1,0:T(8,128)S(1)} %get-tuple-element.29), channel_id=1, source_target_pairs={{0,14},{2,0},{4,2},{6,4},{8,6},{10,8},{12,10},{14,12},{1,15},{3,1}... | collective-permute-start | bytes 98312 | tf_op jit(solution)/shard_map/ppermute | solution.py:16
  59.9 0.8 collective-permute-done.10
  60.7 1.7 %collective-permute-start.8 = (f32[32,256]{1,0:T(8,128)S(1)}, f32[32,256]{1,0:T(8,128)S(1)}, u32[]{:S(2)}, u32[]{:S(2)}) collective-permute-start(f32[32,256]{1,0:T(8,128)S(1)} %get-tuple-element.28), channel_id=1, source_target_pairs={{0,8},{2,10},{4,12},{6,14},{8,0},{10,2},{12,4},{14,6},{1,9},{3,11}... | collective-permute-start | bytes 98312 | tf_op jit(solution)/shard_map/ppermute | solution.py:16
  62.4 4.5 %collective-permute-start.9 = (f32[32,256]{1,0:T(8,128)S(1)}, f32[32,256]{1,0:T(8,128)S(1)}, u32[]{:S(2)}, u32[]{:S(2)}) collective-permute-start(f32[32,256]{1,0:T(8,128)S(1)} %get-tuple-element.34), channel_id=1, source_target_pairs={{0,6},{2,8},{4,10},{6,12},{8,14},{10,0},{12,2},{14,4},{1,7},{3,9},... | collective-permute-start | bytes 98312 | tf_op jit(solution)/shard_map/ppermute | solution.py:16
  66.9 3.0 %collective-permute-start.24 = (f32[32,256]{1,0:T(8,128)S(1)}, f32[32,256]{1,0:T(8,128)S(1)}, u32[]{:S(2)}, u32[]{:S(2)}) collective-permute-start(f32[32,256]{1,0:T(8,128)S(1)} %get-tuple-element.41), channel_id=1, source_target_pairs={{0,32},{16,48},{32,0},{48,16},{1,33},{17,49},{33,1},{49,17},{2,34}... | collective-permute-start | bytes 98312 | tf_op jit(solution)/shard_map/ppermute | solution.py:16
  69.9 1.1 %collective-permute-start.25 = (f32[32,256]{1,0:T(8,128)S(1)}, f32[32,256]{1,0:T(8,128)S(1)}, u32[]{:S(2)}, u32[]{:S(2)}) collective-permute-start(f32[32,256]{1,0:T(8,128)S(1)} %get-tuple-element.43), channel_id=1, source_target_pairs={{0,16},{16,32},{32,48},{48,0},{1,17},{17,33},{33,49},{49,1},{2,18}... | collective-permute-start | bytes 98312 | tf_op jit(solution)/shard_map/ppermute | solution.py:16
  71.0 2.1 %collective-permute-start.26 = (f32[32,256]{1,0:T(8,128)S(1)}, f32[32,256]{1,0:T(8,128)S(1)}, u32[]{:S(2)}, u32[]{:S(2)}) collective-permute-start(f32[32,256]{1,0:T(8,128)S(1)} %get-tuple-element.42), channel_id=1, source_target_pairs={{0,48},{16,0},{32,16},{48,32},{1,49},{17,1},{33,17},{49,33},{2,50}... | collective-permute-start | bytes 98312 | tf_op jit(solution)/shard_map/ppermute | solution.py:16
  73.2 1.8 %collective-permute-done.25 = f32[32,256]{1,0:T(8,128)S(1)} collective-permute-done((f32[32,256]{1,0:T(8,128)S(1)}, f32[32,256]{1,0:T(8,128)S(1)}, u32[]{:S(2)}, u32[]{:S(2)}) %collective-permute-start.25) | collective-permute-done | bytes 32800 | tf_op jit(solution)/shard_map/ppermute | solution.py:16
  75.1 1.0 %fusion.18 = f32[32,512]{1,0:T(8,128)S(1)} fusion(f32[512,512]{1,0:T(8,128)S(1)} %copy-done, f32[32,256]{1,0:T(8,128)S(1)} %fusion.33, f32[32,256]{1,0:T(8,128)S(1)} %fusion.40, f32[512,32]{0,1:T(8,128)S(1)} %copy-done.5), kind=kOutput, calls=%fused_computation.47 | convolution fusion | flops 100696064 | bytes 1245184 | tf_op jit(solution)/shard_map/dot_general | solution.py:109
  76.1 1.7 %collective-permute-start.27 = (f32[32,512]{1,0:T(8,128)S(1)}, f32[32,512]{1,0:T(8,128)S(1)}, u32[]{:S(2)}, u32[]{:S(2)}) collective-permute-start(f32[32,512]{1,0:T(8,128)S(1)} %fusion.18), channel_id=1, source_target_pairs={{0,64},{64,128},{128,192},{192,0},{1,65},{65,129},{129,193},{193,1... | collective-permute-start | bytes 196616 | tf_op jit(solution)/shard_map/ppermute | solution.py:16
  77.8 2.8 %fusion.2 = f32[512,512]{1,0:T(8,128)} fusion(f32[512,512]{1,0:T(8,128)S(1)} %copy-done, f32[512,1536]{1,0:T(8,128)S(1)} %copy-done.4), kind=kOutput, calls=%fused_computation.5 | convolution fusion | flops 1610612736 | bytes 3145728 | tf_op jit(solution)/shard_map/dot_general | solution.py:140
  80.6 2.9 %collective-permute-start.29 = (f32[32,512]{1,0:T(8,128)S(1)}, f32[32,512]{1,0:T(8,128)S(1)}, u32[]{:S(2)}, u32[]{:S(2)}) collective-permute-start(f32[32,512]{1,0:T(8,128)S(1)} %fusion.18), channel_id=1, source_target_pairs={{0,128},{64,192},{128,0},{192,64},{1,129},{65,193},{129,1},{193,65... | collective-permute-start | bytes 196616 | tf_op jit(solution)/shard_map/ppermute | solution.py:16
  83.5 1.3 %collective-permute-start.30 = (f32[32,512]{1,0:T(8,128)S(1)}, f32[32,512]{1,0:T(8,128)S(1)}, u32[]{:S(2)}, u32[]{:S(2)}) collective-permute-start(f32[32,512]{1,0:T(8,128)S(1)} %fusion.18), channel_id=1, source_target_pairs={{0,192},{64,0},{128,64},{192,128},{1,193},{65,1},{129,65},{193,129... | collective-permute-start | bytes 196616 | tf_op jit(solution)/shard_map/ppermute | solution.py:16
  84.9 1.0 %convolution_subtract_fusion = f32[32,512]{1,0:T(8,128)S(1)} fusion(f32[32,512]{1,0:T(8,128)S(1)} %fusion.18, f32[512,512]{1,0:T(8,128)S(1)} %fusion.6, f32[32,512]{1,0:T(8,128)S(1)} %collective-permute-done.27, pred[]{:T(512)S(6)} %eq.12), kind=kOutput, calls=%fused_computation.4 | convolution fusion | flops 100696064 | bytes 1245185 | tf_op jit(solution)/shard_map/dot_general | solution.py:109
  85.9 0.8 collective-permute-start.28
  86.7 0.8 collective-permute-start.32
  87.5 0.3 collective-permute-done.30
  87.8 1.0 %fusion.25 = f32[32,512]{1,0:T(8,128)S(1)} fusion(f32[512,512]{1,0:T(8,128)S(1)} %fusion.6, f32[32,512]{1,0:T(8,128)S(1)} %collective-permute-done.30, f32[32,512]{1,0:T(8,128)S(1)} %collective-permute-done.29, pred[]{:T(512)S(6)} %eq.14, pred[]{:T(512)S(6)} %eq.13), kind=kOutput, calls=%fused_computation.54 | convolution fusion | flops 100712448 | bytes 1245186 | tf_op jit(solution)/shard_map/dot_general | solution.py:109
  88.9 2.6 %collective-permute-done.28 = f32[32,512]{1,0:T(8,128)S(1)} collective-permute-done((f32[32,512]{1,0:T(8,128)S(1)}, f32[32,512]{1,0:T(8,128)S(1)}, u32[]{:S(2)}, u32[]{:S(2)}) %collective-permute-start.28) | collective-permute-done | bytes 65568 | tf_op jit(solution)/shard_map/ppermute | solution.py:16
  91.5 1.1 %fusion.1 = f32[32,512]{1,0:T(8,128)S(1)} fusion(f32[32,512]{1,0:T(8,128)S(1)} %convolution_subtract_fusion, f32[32,512]{1,0:T(8,128)S(1)} %fusion.25, f32[512,512]{1,0:T(8,128)S(1)} %fusion.4, f32[32,512]{1,0:T(8,128)S(1)} %collective-permute-done.28, pred[]{:T(512)S(6)} %eq.13), kind=kOutput, calls=%fused_computation.3 | convolution fusion | flops 100712448 | bytes 1310721 | tf_op jit(solution)/shard_map/dot_general | solution.py:109
  92.6 0.1 collective-permute-start.31
  92.7 1.1 %fusion.22 = f32[512,32]{0,1:T(8,128)S(1)} fusion(f32[512,512]{1,0:T(8,128)S(1)} %fusion.4, f32[32,512]{1,0:T(8,128)S(1)} %collective-permute-done.32, pred[]{:T(512)S(6)} %eq.14), kind=kOutput, calls=%fused_computation.51 | convolution fusion | flops 100679680 | bytes 1179649 | tf_op jit(solution)/shard_map/dot_general | solution.py:109
  93.7 4.4 %collective-permute-done.31 = f32[32,512]{1,0:T(8,128)S(1)} collective-permute-done((f32[32,512]{1,0:T(8,128)S(1)}, f32[32,512]{1,0:T(8,128)S(1)}, u32[]{:S(2)}, u32[]{:S(2)}) %collective-permute-start.31) | collective-permute-done | bytes 65568 | tf_op jit(solution)/shard_map/ppermute | solution.py:16
  98.1 1.7 %fusion = f32[512,32]{0,1:T(8,128)} fusion(f32[512,32]{0,1:T(8,128)S(1)} %fusion.22, f32[512,512]{1,0:T(8,128)S(1)} %copy-done.3, f32[32,512]{1,0:T(8,128)S(1)} %fusion.1, f32[32,512]{1,0:T(8,128)S(1)} %collective-permute-done.31, pred[]{:T(512)S(6)} %eq.14), kind=kOutput, calls=%fused_computation.1 | convolution fusion | flops 100712448 | bytes 1310721 | tf_op jit(solution)/shard_map/dot_general | solution.py:109
  (46 shorter events, 0.4 us)
Async XLA Ops:
  0.0 16.1 %copy-start = (f32[512,512]{1,0:T(8,128)S(1)}, f32[512,512]{1,0:T(8,128)}, u32[]{:S(2)}) copy-start(f32[512,512]{1,0:T(8,128)} %param.8) | copy-start | bytes 3145732
  0.1 2.9 %copy-start.1 = (f32[768,2048]{1,0:T(8,128)S(1)}, f32[768,2048]{1,0:T(8,128)}, u32[]{:S(2)}) copy-start(f32[768,2048]{1,0:T(8,128)} %users.1) | copy-start | bytes 18874372
  2.9 1.4 %copy-start.2 = (f32[512,768]{1,0:T(8,128)S(1)}, f32[512,768]{1,0:T(8,128)}, u32[]{:S(2)}) copy-start(f32[512,768]{1,0:T(8,128)} %factor.1) | copy-start | bytes 4718596
  11.9 4.2 %copy-start.4 = (f32[512,1536]{1,0:T(8,128)S(1)}, f32[512,1536]{1,0:T(8,128)}, u32[]{:S(2)}) copy-start(f32[512,1536]{1,0:T(8,128)} %param.9) | copy-start | bytes 9437188
  12.0 1.6 %collective-permute-start.1 = (f32[8,32,256]{2,1,0:T(8,128)S(1)}, f32[8,32,256]{2,1,0:T(8,128)S(1)}, u32[]{:S(2)}, u32[]{:S(2)}) collective-permute-start(f32[8,32,256]{2,1,0:T(8,128)S(1)} %get-tuple-element.16), channel_id=1, source_target_pairs={{0,1},{1,0},{2,3},{3,2},{4,5},{5,4},{6,7},{7,6},{8,9},{9,8},{10,11... | collective-permute-start | bytes 786440 | tf_op jit(solution)/shard_map/ppermute | solution.py:16
  12.1 1.9 %collective-permute-start.2 = (f32[8,32,256]{2,1,0:T(8,128)S(1)}, f32[8,32,256]{2,1,0:T(8,128)S(1)}, u32[]{:S(2)}, u32[]{:S(2)}) collective-permute-start(f32[8,32,256]{2,1,0:T(8,128)S(1)} %get-tuple-element.15), channel_id=1, source_target_pairs={{0,1},{1,0},{2,3},{3,2},{4,5},{5,4},{6,7},{7,6},{8,9},{9,8},{10,11... | collective-permute-start | bytes 786440 | tf_op jit(solution)/shard_map/ppermute | solution.py:16
  12.6 1.8 %collective-permute-start.5 = (f32[8,32,256]{2,1,0:T(8,128)S(1)}, f32[8,32,256]{2,1,0:T(8,128)S(1)}, u32[]{:S(2)}, u32[]{:S(2)}) collective-permute-start(f32[8,32,256]{2,1,0:T(8,128)S(1)} %get-tuple-element.14), channel_id=1, source_target_pairs={{0,1},{1,0},{2,3},{3,2},{4,5},{5,4},{6,7},{7,6},{8,9},{9,8},{10,11... | collective-permute-start | bytes 786440 | tf_op jit(solution)/shard_map/ppermute | solution.py:16
  12.7 30.8 %collective-permute-start = (f32[8,32,256]{2,1,0:T(8,128)S(1)}, f32[8,32,256]{2,1,0:T(8,128)S(1)}, u32[]{:S(2)}, u32[]{:S(2)}) collective-permute-start(f32[8,32,256]{2,1,0:T(8,128)S(1)} %get-tuple-element.13), channel_id=1, source_target_pairs={{0,1},{1,0},{2,3},{3,2},{4,5},{5,4},{6,7},{7,6},{8,9},{9,8},{10,11... | collective-permute-start | bytes 786440 | tf_op jit(solution)/shard_map/ppermute | solution.py:16
  13.1 8.7 %collective-permute-start.15 = (f32[8,4,32,256]{3,2,1,0:T(8,128)S(1)}, f32[8,4,32,256]{3,2,1,0:T(8,128)S(1)}, u32[]{:S(2)}, u32[]{:S(2)}) collective-permute-start(f32[8,4,32,256]{3,2,1,0:T(8,128)S(1)} %get-tuple-element.12), channel_id=1, source_target_pairs={{0,1},{1,0},{2,3},{3,2},{4,5},{5,4},{6,7},{7,6},{8,9},{9,8},{10,11... | collective-permute-start | bytes 3145736 | tf_op jit(solution)/shard_map/ppermute | solution.py:16
  14.5 6.8 %collective-permute-start.3 = (f32[4,32,256]{2,1,0:T(8,128)S(1)}, f32[4,32,256]{2,1,0:T(8,128)S(1)}, u32[]{:S(2)}, u32[]{:S(2)}) collective-permute-start(f32[4,32,256]{2,1,0:T(8,128)S(1)} %get-tuple-element.37), channel_id=1, source_target_pairs={{0,16},{16,32},{32,48},{48,0},{1,17},{17,33},{33,49},{49,1},{2,18}... | collective-permute-start | bytes 393224 | tf_op jit(solution)/shard_map/ppermute | solution.py:16
  17.9 6.1 %collective-permute-start.6 = (f32[4,32,256]{2,1,0:T(8,128)S(1)}, f32[4,32,256]{2,1,0:T(8,128)S(1)}, u32[]{:S(2)}, u32[]{:S(2)}) collective-permute-start(f32[4,32,256]{2,1,0:T(8,128)S(1)} %get-tuple-element.38), channel_id=1, source_target_pairs={{0,48},{16,0},{32,16},{48,32},{1,49},{17,1},{33,17},{49,33},{2,50}... | collective-permute-start | bytes 393224 | tf_op jit(solution)/shard_map/ppermute | solution.py:16
  21.4 22.1 %collective-permute-start.4 = (f32[8,32,256]{2,1,0:T(8,128)S(1)}, f32[8,32,256]{2,1,0:T(8,128)S(1)}, u32[]{:S(2)}, u32[]{:S(2)}) collective-permute-start(f32[8,32,256]{2,1,0:T(8,128)S(1)} %pad_maximum_fusion), channel_id=1, source_target_pairs={{0,16},{16,32},{32,48},{48,0},{1,17},{17,33},{33,49},{49,1},{2,18}... | collective-permute-start | bytes 786440 | tf_op jit(solution)/shard_map/ppermute | solution.py:16
  22.0 4.3 %collective-permute-start.16 = (f32[2,32,256]{2,1,0:T(8,128)S(1)}, f32[2,32,256]{2,1,0:T(8,128)S(1)}, u32[]{:S(2)}, u32[]{:S(2)}) collective-permute-start(f32[2,32,256]{2,1,0:T(8,128)S(1)} %get-tuple-element.24), channel_id=1, source_target_pairs={{0,2},{2,4},{4,6},{6,8},{8,10},{10,12},{12,14},{14,0},{1,3},{3,5},... | collective-permute-start | bytes 196616 | tf_op jit(solution)/shard_map/ppermute | solution.py:16
  24.0 4.3 %collective-permute-start.20 = (f32[2,32,256]{2,1,0:T(8,128)S(1)}, f32[2,32,256]{2,1,0:T(8,128)S(1)}, u32[]{:S(2)}, u32[]{:S(2)}) collective-permute-start(f32[2,32,256]{2,1,0:T(8,128)S(1)} %get-tuple-element.25), channel_id=1, source_target_pairs={{0,14},{2,0},{4,2},{6,4},{8,6},{10,8},{12,10},{14,12},{1,15},{3,1}... | collective-permute-start | bytes 196616 | tf_op jit(solution)/shard_map/ppermute | solution.py:16
  28.3 6.4 %collective-permute-start.17 = (f32[4,32,256]{2,1,0:T(8,128)S(1)}, f32[4,32,256]{2,1,0:T(8,128)S(1)}, u32[]{:S(2)}, u32[]{:S(2)}) collective-permute-start(f32[4,32,256]{2,1,0:T(8,128)S(1)} %pad_maximum_fusion.2), channel_id=1, source_target_pairs={{0,2},{2,4},{4,6},{6,8},{8,10},{10,12},{12,14},{14,0},{1,3},{3,5},... | collective-permute-start | bytes 393224 | tf_op jit(solution)/shard_map/ppermute | solution.py:16
  31.4 12.1 %collective-permute-start.7 = (f32[8,32,256]{2,1,0:T(8,128)S(1)}, f32[8,32,256]{2,1,0:T(8,128)S(1)}, u32[]{:S(2)}, u32[]{:S(2)}) collective-permute-start(f32[8,32,256]{2,1,0:T(8,128)S(1)} %pad_maximum_fusion.1), channel_id=1, source_target_pairs={{0,48},{16,0},{32,16},{48,32},{1,49},{17,1},{33,17},{49,33},{2,50}... | collective-permute-start | bytes 786440 | tf_op jit(solution)/shard_map/ppermute | solution.py:16
  34.4 7.2 %collective-permute-start.21 = (f32[4,32,256]{2,1,0:T(8,128)S(1)}, f32[4,32,256]{2,1,0:T(8,128)S(1)}, u32[]{:S(2)}, u32[]{:S(2)}) collective-permute-start(f32[4,32,256]{2,1,0:T(8,128)S(1)} %pad_maximum_fusion.3), channel_id=1, source_target_pairs={{0,14},{2,0},{4,2},{6,4},{8,6},{10,8},{12,10},{14,12},{1,15},{3,1}... | collective-permute-start | bytes 393224 | tf_op jit(solution)/shard_map/ppermute | solution.py:16
  34.8 40.3 %copy-start.5 = (f32[512,32]{0,1:T(8,128)S(1)}, f32[512,32]{0,1:T(8,128)}, u32[]{:S(2)}) copy-start(f32[512,32]{0,1:T(8,128)} %param.5) | copy-start | bytes 196612
  34.8 6.8 %collective-permute-start.18 = (f32[4,32,256]{2,1,0:T(8,128)S(1)}, f32[4,32,256]{2,1,0:T(8,128)S(1)}, u32[]{:S(2)}, u32[]{:S(2)}) collective-permute-start(f32[4,32,256]{2,1,0:T(8,128)S(1)} %fusion.12), channel_id=1, source_target_pairs={{0,2},{2,4},{4,6},{6,8},{8,10},{10,12},{12,14},{14,0},{1,3},{3,5},... | collective-permute-start | bytes 393224 | tf_op jit(solution)/shard_map/ppermute | solution.py:16
  41.6 6.5 %collective-permute-start.22 = (f32[4,32,256]{2,1,0:T(8,128)S(1)}, f32[4,32,256]{2,1,0:T(8,128)S(1)}, u32[]{:S(2)}, u32[]{:S(2)}) collective-permute-start(f32[4,32,256]{2,1,0:T(8,128)S(1)} %get-tuple-element.21), channel_id=1, source_target_pairs={{0,14},{2,0},{4,2},{6,4},{8,6},{10,8},{12,10},{14,12},{1,15},{3,1}... | collective-permute-start | bytes 393224 | tf_op jit(solution)/shard_map/ppermute | solution.py:16
  43.5 14.3 %collective-permute-start.19 = (f32[4,32,256]{2,1,0:T(8,128)S(1)}, f32[4,32,256]{2,1,0:T(8,128)S(1)}, u32[]{:S(2)}, u32[]{:S(2)}) collective-permute-start(f32[4,32,256]{2,1,0:T(8,128)S(1)} %get-tuple-element.20), channel_id=1, source_target_pairs={{0,2},{2,4},{4,6},{6,8},{8,10},{10,12},{12,14},{14,0},{1,3},{3,5},... | collective-permute-start | bytes 393224 | tf_op jit(solution)/shard_map/ppermute | solution.py:16
  48.2 9.6 %collective-permute-start.23 = (f32[4,32,256]{2,1,0:T(8,128)S(1)}, f32[4,32,256]{2,1,0:T(8,128)S(1)}, u32[]{:S(2)}, u32[]{:S(2)}) collective-permute-start(f32[4,32,256]{2,1,0:T(8,128)S(1)} %fusion.11), channel_id=1, source_target_pairs={{0,14},{2,0},{4,2},{6,4},{8,6},{10,8},{12,10},{14,12},{1,15},{3,1}... | collective-permute-start | bytes 393224 | tf_op jit(solution)/shard_map/ppermute | solution.py:16
  49.6 11.1 %collective-permute-start.10 = (f32[32,256]{1,0:T(8,128)S(1)}, f32[32,256]{1,0:T(8,128)S(1)}, u32[]{:S(2)}, u32[]{:S(2)}) collective-permute-start(f32[32,256]{1,0:T(8,128)S(1)} %get-tuple-element.33), channel_id=1, source_target_pairs={{0,10},{2,12},{4,14},{6,0},{8,2},{10,4},{12,6},{14,8},{1,11},{3,13... | collective-permute-start | bytes 98312 | tf_op jit(solution)/shard_map/ppermute | solution.py:16
  52.4 10.0 %collective-permute-start.11 = (f32[32,256]{1,0:T(8,128)S(1)}, f32[32,256]{1,0:T(8,128)S(1)}, u32[]{:S(2)}, u32[]{:S(2)}) collective-permute-start(f32[32,256]{1,0:T(8,128)S(1)} %get-tuple-element.32), channel_id=1, source_target_pairs={{0,4},{2,6},{4,8},{6,10},{8,12},{10,14},{12,0},{14,2},{1,5},{3,7},... | collective-permute-start | bytes 98312 | tf_op jit(solution)/shard_map/ppermute | solution.py:16
  55.6 11.3 %collective-permute-start.12 = (f32[32,256]{1,0:T(8,128)S(1)}, f32[32,256]{1,0:T(8,128)S(1)}, u32[]{:S(2)}, u32[]{:S(2)}) collective-permute-start(f32[32,256]{1,0:T(8,128)S(1)} %get-tuple-element.31), channel_id=1, source_target_pairs={{0,12},{2,14},{4,0},{6,2},{8,4},{10,6},{12,8},{14,10},{1,13},{3,15... | collective-permute-start | bytes 98312 | tf_op jit(solution)/shard_map/ppermute | solution.py:16
  57.8 12.1 %collective-permute-start.13 = (f32[32,256]{1,0:T(8,128)S(1)}, f32[32,256]{1,0:T(8,128)S(1)}, u32[]{:S(2)}, u32[]{:S(2)}) collective-permute-start(f32[32,256]{1,0:T(8,128)S(1)} %get-tuple-element.30), channel_id=1, source_target_pairs={{0,2},{2,4},{4,6},{6,8},{8,10},{10,12},{12,14},{14,0},{1,3},{3,5},... | collective-permute-start | bytes 98312 | tf_op jit(solution)/shard_map/ppermute | solution.py:16
  57.8 13.2 %collective-permute-start.14 = (f32[32,256]{1,0:T(8,128)S(1)}, f32[32,256]{1,0:T(8,128)S(1)}, u32[]{:S(2)}, u32[]{:S(2)}) collective-permute-start(f32[32,256]{1,0:T(8,128)S(1)} %get-tuple-element.29), channel_id=1, source_target_pairs={{0,14},{2,0},{4,2},{6,4},{8,6},{10,8},{12,10},{14,12},{1,15},{3,1}... | collective-permute-start | bytes 98312 | tf_op jit(solution)/shard_map/ppermute | solution.py:16
  60.7 12.5 %collective-permute-start.8 = (f32[32,256]{1,0:T(8,128)S(1)}, f32[32,256]{1,0:T(8,128)S(1)}, u32[]{:S(2)}, u32[]{:S(2)}) collective-permute-start(f32[32,256]{1,0:T(8,128)S(1)} %get-tuple-element.28), channel_id=1, source_target_pairs={{0,8},{2,10},{4,12},{6,14},{8,0},{10,2},{12,4},{14,6},{1,9},{3,11}... | collective-permute-start | bytes 98312 | tf_op jit(solution)/shard_map/ppermute | solution.py:16
  62.4 10.8 %collective-permute-start.9 = (f32[32,256]{1,0:T(8,128)S(1)}, f32[32,256]{1,0:T(8,128)S(1)}, u32[]{:S(2)}, u32[]{:S(2)}) collective-permute-start(f32[32,256]{1,0:T(8,128)S(1)} %get-tuple-element.34), channel_id=1, source_target_pairs={{0,6},{2,8},{4,10},{6,12},{8,14},{10,0},{12,2},{14,4},{1,7},{3,9},... | collective-permute-start | bytes 98312 | tf_op jit(solution)/shard_map/ppermute | solution.py:16
  66.9 6.3 %collective-permute-start.24 = (f32[32,256]{1,0:T(8,128)S(1)}, f32[32,256]{1,0:T(8,128)S(1)}, u32[]{:S(2)}, u32[]{:S(2)}) collective-permute-start(f32[32,256]{1,0:T(8,128)S(1)} %get-tuple-element.41), channel_id=1, source_target_pairs={{0,32},{16,48},{32,0},{48,16},{1,33},{17,49},{33,1},{49,17},{2,34}... | collective-permute-start | bytes 98312 | tf_op jit(solution)/shard_map/ppermute | solution.py:16
  69.9 5.1 %collective-permute-start.25 = (f32[32,256]{1,0:T(8,128)S(1)}, f32[32,256]{1,0:T(8,128)S(1)}, u32[]{:S(2)}, u32[]{:S(2)}) collective-permute-start(f32[32,256]{1,0:T(8,128)S(1)} %get-tuple-element.43), channel_id=1, source_target_pairs={{0,16},{16,32},{32,48},{48,0},{1,17},{17,33},{33,49},{49,1},{2,18}... | collective-permute-start | bytes 98312 | tf_op jit(solution)/shard_map/ppermute | solution.py:16
  71.0 4.0 %collective-permute-start.26 = (f32[32,256]{1,0:T(8,128)S(1)}, f32[32,256]{1,0:T(8,128)S(1)}, u32[]{:S(2)}, u32[]{:S(2)}) collective-permute-start(f32[32,256]{1,0:T(8,128)S(1)} %get-tuple-element.42), channel_id=1, source_target_pairs={{0,48},{16,0},{32,16},{48,32},{1,49},{17,1},{33,17},{49,33},{2,50}... | collective-permute-start | bytes 98312 | tf_op jit(solution)/shard_map/ppermute | solution.py:16
  76.1 8.8 %collective-permute-start.27 = (f32[32,512]{1,0:T(8,128)S(1)}, f32[32,512]{1,0:T(8,128)S(1)}, u32[]{:S(2)}, u32[]{:S(2)}) collective-permute-start(f32[32,512]{1,0:T(8,128)S(1)} %fusion.18), channel_id=1, source_target_pairs={{0,64},{64,128},{128,192},{192,0},{1,65},{65,129},{129,193},{193,1... | collective-permute-start | bytes 196616 | tf_op jit(solution)/shard_map/ppermute | solution.py:16
  80.6 17.5 %copy-start.3 = (f32[512,512]{1,0:T(8,128)S(1)}, f32[512,512]{1,0:T(8,128)}, u32[]{:S(2)}) copy-start(f32[512,512]{1,0:T(8,128)} %fusion.2) | copy-start | bytes 3145732
  80.6 6.9 %collective-permute-start.29 = (f32[32,512]{1,0:T(8,128)S(1)}, f32[32,512]{1,0:T(8,128)S(1)}, u32[]{:S(2)}, u32[]{:S(2)}) collective-permute-start(f32[32,512]{1,0:T(8,128)S(1)} %fusion.18), channel_id=1, source_target_pairs={{0,128},{64,192},{128,0},{192,64},{1,129},{65,193},{129,1},{193,65... | collective-permute-start | bytes 196616 | tf_op jit(solution)/shard_map/ppermute | solution.py:16
  83.5 4.3 %collective-permute-start.30 = (f32[32,512]{1,0:T(8,128)S(1)}, f32[32,512]{1,0:T(8,128)S(1)}, u32[]{:S(2)}, u32[]{:S(2)}) collective-permute-start(f32[32,512]{1,0:T(8,128)S(1)} %fusion.18), channel_id=1, source_target_pairs={{0,192},{64,0},{128,64},{192,128},{1,193},{65,1},{129,65},{193,129... | collective-permute-start | bytes 196616 | tf_op jit(solution)/shard_map/ppermute | solution.py:16
  85.9 5.6 %collective-permute-start.28 = (f32[32,512]{1,0:T(8,128)S(1)}, f32[32,512]{1,0:T(8,128)S(1)}, u32[]{:S(2)}, u32[]{:S(2)}) collective-permute-start(f32[32,512]{1,0:T(8,128)S(1)} %convolution_subtract_fusion), channel_id=1, source_target_pairs={{0,64},{64,128},{128,192},{192,0},{1,65},{65,129},{129,193},{193,1... | collective-permute-start | bytes 196616 | tf_op jit(solution)/shard_map/ppermute | solution.py:16
  86.7 6.0 %collective-permute-start.32 = (f32[32,512]{1,0:T(8,128)S(1)}, f32[32,512]{1,0:T(8,128)S(1)}, u32[]{:S(2)}, u32[]{:S(2)}) collective-permute-start(f32[32,512]{1,0:T(8,128)S(1)} %convolution_subtract_fusion), channel_id=1, source_target_pairs={{0,128},{64,192},{128,0},{192,64},{1,129},{65,193},{129,1},{193,65... | collective-permute-start | bytes 196616 | tf_op jit(solution)/shard_map/ppermute | solution.py:16
  92.6 5.6 %collective-permute-start.31 = (f32[32,512]{1,0:T(8,128)S(1)}, f32[32,512]{1,0:T(8,128)S(1)}, u32[]{:S(2)}, u32[]{:S(2)}) collective-permute-start(f32[32,512]{1,0:T(8,128)S(1)} %fusion.1), channel_id=1, source_target_pairs={{0,64},{64,128},{128,192},{192,0},{1,65},{65,129},{129,193},{193,1... | collective-permute-start | bytes 196616 | tf_op jit(solution)/shard_map/ppermute | solution.py:16

commit v2 on v1

v2 whole, which is shorter than its diff:
```python
import functools

import jax
import jax.numpy as jnp
from jax import lax
from jax.experimental import pallas as pl
from jax.experimental.pallas import tpu as pltpu
from jax.sharding import Mesh
from jax.sharding import PartitionSpec as P

COL = ("x", "z", "core")


def shifted(value, axis, by):
    peers = lax.axis_size(axis)
    return lax.ppermute(value, axis, [(i, (i + by) % peers) for i in range(peers)])


def summed_at_owner(blocks, axis):
    return jnp.sum(lax.all_to_all(blocks, axis, 0, 0, tiled=True), axis=0)


def halves(value):
    high = value.astype(jnp.bfloat16)
    return high, (value - high.astype(jnp.float32)).astype(jnp.bfloat16)


def contract(left, right, left_dim, right_dim):
    dims = (((left_dim,), (right_dim,)), ((), ()))
    return lax.dot_general(left, right, dims, preferred_element_type=jnp.float32)


def three_pass(left, right, left_dim, right_dim):
    left_high, left_low = halves(left)
    right_high, right_low = halves(right)
    return contract(left_high, right_high, left_dim, right_dim) + (
        contract(left_high, right_low, left_dim, right_dim)
        + contract(left_low, right_high, left_dim, right_dim)
    )


def ring_order(peers):
    return sorted(range(peers), key=lambda o: (-min(o, peers - o), o))


def product_body(n_z, n_core, split, place, users, factor, far_own, own_a, own_b, far_sent, sent_a, sent_b):
    core, step = place[0], pl.program_id(0)
    items, rows = users.shape[1], factor.shape[0]
    share = items // (n_z * n_core)
    total = three_pass(users[...], factor[...], 0, 1).reshape(n_z, n_core, share, rows)

    def keep(mine):
        own, sent = total[:, mine], total[:, 1 - mine]
        own_b[:, 0] = own[..., split:]
        sent_b[:, 0] = sent[..., split:]

        @pl.when(step == 0)
        def _():
            far_own[...] = own[..., :split]
            far_sent[...] = sent[..., :split]

        @pl.when(step > 0)
        def _():
            own_a[0] = own[..., :split]
            sent_a[0] = sent[..., :split]

    pl.when(core == 0)(lambda: keep(0))
    pl.when(core == 1)(lambda: keep(1))


def product(place, users, factor, n_x, n_z, n_core, split):
    depth, items = users.shape
    rows = factor.shape[0]
    chunk, share = items // n_x, items // (n_x * n_z * n_core)
    specs = [
        pl.BlockSpec((n_z, share, split), lambda i, s: (0, 0, 0)),
        pl.BlockSpec((1, n_z, share, split), lambda i, s: (lax.max(i - 1, 0), 0, 0, 0)),
        pl.BlockSpec((n_z, 1, share, rows - split), lambda i, s: (0, s[1 + i], 0, 0)),
    ]
    shapes = [
        jax.ShapeDtypeStruct((n_z, share, split), jnp.float32),
        jax.ShapeDtypeStruct((n_x - 1, n_z, share, split), jnp.float32),
        jax.ShapeDtypeStruct((n_z, n_x, share, rows - split), jnp.float32),
    ]
    return pl.pallas_call(
        functools.partial(product_body, n_z, n_core, split),
        grid_spec=pltpu.PrefetchScalarGridSpec(
            num_scalar_prefetch=1,
            grid=(n_x,),
            in_specs=[
                pl.BlockSpec((depth, chunk), lambda i, s: (0, s[1 + i])),
                pl.BlockSpec((rows, depth), lambda i, s: (0, 0)),
            ],
            out_specs=specs * 2,
        ),
        out_shape=shapes * 2,
        compiler_params=pltpu.CompilerParams(vmem_limit_bytes=56 << 20),
    )(place, users, factor)


def weights_body(diag, coupling, high, low):
    step = pl.program_id(0)

    def keep(value):
        high[0], low[0] = halves(value)

    pl.when(step == 0)(lambda: keep(diag[...].T))
    pl.when(step > 0)(lambda: keep(-three_pass(coupling[...], diag[...], 0, 1)))


def hop_weights(diag, coupling):
    block = diag.shape[0]
    count = 1 + coupling.shape[1] // block
    shape = jax.ShapeDtypeStruct((count, block, block), jnp.bfloat16)
    return pl.pallas_call(
        weights_body,
        grid=(count,),
        in_specs=[
            pl.BlockSpec((block, block), lambda i: (0, 0)),
            pl.BlockSpec((block, block), lambda i: (0, lax.max(i - 1, 0))),
        ],
        out_specs=[pl.BlockSpec((1, block, block), lambda i: (i, 0, 0))] * 2,
        out_shape=[shape] * 2,
        compiler_params=pltpu.CompilerParams(vmem_limit_bytes=24 << 20),
    )(diag, coupling)


def apply_body(wanted, place, *refs):
    *values, base, high, low, out = refs
    total = jnp.zeros_like(base)
    for group, value in zip(wanted, values):
        total = total + (value[...] if group is None else jnp.where(place[0] == group, value[...], 0.0))
    value_high, value_low = halves(total)
    count = value_high.shape[0]
    both = contract(jnp.concatenate([value_high, value_low]), high[0], 1, 0)
    out[...] = base[...] + (both[:count] + both[count:] + contract(value_high, low[0], 1, 0))


def applied(position, base, values, weights, index):
    whole = pl.BlockSpec(base.shape, lambda i, s: (0, 0))
    block = weights[0].shape[1]
    weight = pl.BlockSpec((1, block, block), lambda i, s: (index, 0, 0))
    return pl.pallas_call(
        functools.partial(apply_body, [group for group, _ in values]),
        grid_spec=pltpu.PrefetchScalarGridSpec(
            num_scalar_prefetch=1,
            grid=(1,),
            in_specs=[whole] * (len(values) + 1) + [weight] * 2,
            out_specs=whole,
        ),
        out_shape=jax.ShapeDtypeStruct(base.shape, jnp.float32),
        compiler_params=pltpu.CompilerParams(vmem_limit_bytes=8 << 20),
    )(position, *[value for _, value in values], base, *weights)


def chain(position, residue, weights):
    groups = lax.axis_size("grp")
    result = applied(position, jnp.zeros_like(residue), [(None, residue)], weights, 0)
    later = []
    for step in range(groups - 1):
        near = shifted(result, "grp", 1)
        far = [(step + by, shifted(result, "grp", by)) for by in range(2, groups - step)]
        if later:
            result = applied(position, result, later, weights, step)
        result = applied(position, result, [(step + 1, near)], weights, step + 1)
        later = far
    return result


def ring_reduced(far, near, axis):
    cut = far.shape[0] // 2
    up = shifted(far[:cut], axis, 1)
    down = shifted(far[cut:], axis, -1)
    up = shifted(jnp.concatenate([near[0, :cut] + up, near[0, cut:]]), axis, 1)
    down = shifted(jnp.concatenate([near[1, :cut], near[1, cut:] + down]), axis, -1)
    return near[2] + up + down


def on_device(right_side, solved_factor, solved_users, diag_inverse, coupling):
    n_x, n_z, n_core = (lax.axis_size(a) for a in COL)
    x, core = lax.axis_index("x"), lax.axis_index("core")
    place = jnp.stack([core] + [(x + o) % n_x for o in ring_order(n_x)]).astype(jnp.int32)
    position = lax.axis_index("grp").reshape(1).astype(jnp.int32)
    rows = solved_factor.shape[0]
    far_own, own_a, own_b, far_sent, sent_a, sent_b = product(
        place, solved_users, solved_factor, n_x, n_z, n_core, rows * 3 // 4
    )
    weights = hop_weights(diag_inverse, coupling)
    sum_b = own_b + shifted(sent_b, "core", 1)
    far_a = far_own + shifted(far_sent, "core", 1)
    near_a = own_a + shifted(sent_a, "core", 1)
    part_b = summed_at_owner(sum_b, "z")
    part_a = ring_reduced(far_a, near_a, "x")
    share_b = summed_at_owner(part_b, "x")
    share_a = summed_at_owner(part_a, "z")
    residue = right_side.T - jnp.concatenate([share_a, share_b], axis=1)
    return chain(position, residue, weights).T


def solution(mesh):
    torus = Mesh(mesh.devices.reshape(mesh.shape["grp"], 4, 8, 2), ("grp",) + COL)
    placed = (P("grp", COL), P("grp", COL), P(COL, None), P("grp", None), P("grp", None))
    return jax.shard_map(
        on_device, mesh=torus, in_specs=placed, out_specs=P("grp", COL), check_vma=False
    )
```

time: 100 us -> 93.7 us (0.937)
  starting transfers between devices: 50.7 us -> 30.4 us
  matrix products: 13.5 us -> 0 us
  Pallas kernels: 7.49 us -> 16.3 us
  waiting for transfers between devices: 22.6 us -> 31.1 us
  other arithmetic: 0.71 us -> 7.86 us
  local copies, waits for them, and re-layouts: 4.45 us -> 7.14 us
    ppermute x33 -> x13, starting transfers between devices: 50.7 us -> 13.7 us  [shifted(): lax.ppermute(value, axis, [(i, (i + by) % peers) for i in range(peers)])]
    all_to_all x0 -> x3, waiting for transfers between devices: none -> 18.2 us  [summed_at_owner(): return jnp.sum(lax.all_to_all(blocks, axis, 0, 0, tiled=True), axis=0)]
    all_to_all x0 -> x3, starting transfers between devices: none -> 16.7 us  [summed_at_owner(): return jnp.sum(lax.all_to_all(blocks, axis, 0, 0, tiled=True), axis=0)]
    dot_general x9 -> x0, matrix products: 13.5 us -> none  [the longest x6 6.97 us: apply_rows(): jnp.dot(vectors, matrix.T, precision='highest', preferred_element_type=jn...]
    ppermute x33 -> x13, waiting for transfers between devices: 22.6 us -> 12.9 us  [shifted(): lax.ppermute(value, axis, [(i, (i + by) % peers) for i in range(peers)])]
    pallas_call x1 -> x8, Pallas kernels: 7.49 us -> 16.3 us  [the longest x1 10.3 us: product(): pl.pallas_call(functools.partial(product_body, n_z, n_core, split), grid_...]
    add x10 -> x4, other arithmetic: 0.37 us -> 4.53 us  [the longest x1 2.01 us: ring_reduced(): return near[2] + up + down]
    reduce_sum x0 -> x3, other arithmetic: none -> 1.54 us  [summed_at_owner(): return jnp.sum(lax.all_to_all(blocks, axis, 0, 0, tiled=True), axis=0)]
  transfers between devices with their start and end apart: 33 -> 16, of which waited for: 13 -> 7; matrix products, arithmetic and copies ran while one was open for 11% -> 8% of each run, Pallas kernels for 0% -> 5%
where the time goes in v2:
time: 93.7 us; the launch traced here: 93 us
  waiting for transfers between devices  31.1 us (33%)
  starting transfers between devices  30.4 us (32%)
  Pallas kernels  16.3 us (17%)
  other arithmetic  7.86 us (8%)
  local copies, waits for them, and re-layouts  7.14 us (8%)
    all_to_all x3, waiting for transfers between devices, summed_at_owner(): return jnp.sum(lax.all_to_all(blocks, axis, 0, 0, tiled=True), axis=0)  18.2 us
    all_to_all x3, starting transfers between devices, summed_at_owner(): return jnp.sum(lax.all_to_all(blocks, axis, 0, 0, tiled=True), axis=0)  16.7 us
    ppermute x13, starting transfers between devices, shifted(): lax.ppermute(value, axis, [(i, (i + by) % peers) for i in range(peers)])  13.7 us
    ppermute x13, waiting for transfers between devices, shifted(): lax.ppermute(value, axis, [(i, (i + by) % peers) for i in range(peers)])  12.9 us
    pallas_call x1, Pallas kernels, product(): pl.pallas_call(functools.partial(product_body, n_z, n_core, split), grid_...  10.3 us
    unnamed x16, local copies, waits for them, and re-layouts  5.82 us
    pallas_call x1, Pallas kernels, hop_weights(): pl.pallas_call(weights_body, grid=(count,), in_specs=[pl.BlockSpec((block...  3.81 us
    pallas_call x6, Pallas kernels, applied(): pl.pallas_call(functools.partial(apply_body, [group for group, _ in value...  2.29 us
  transfers between devices with their start and end apart: 16, of which 7 were waited for; matrix products, arithmetic and copies ran while one was open for 8% of the time, Pallas kernels for 5%

profile of v2, /device:TPU:32, one launch (start us, length us, event | category | flops | bytes accessed | tf_op | source)
XLA Modules:
  0.0 93.0 jit_solution(16792866203845663547)
XLA Ops:
  0.0 0.6 stack.23.place
  0.6 10.3 %shard_map.55 = (f32[8,32,384]{2,1,0:T(8,128)}, f32[3,8,32,384]{3,2,1,0:T(8,128)}, f32[8,4,32,128]{3,2,1,0:T(8,128)}, f32[8,32,384]{2,1,0:T(8,128)}, f32[3,8,32,...) custom-call(s32[5]{0:T(128)} %stack.23.place, f32[768,2048]{1,0:T(8,128)} %users.1, f32[512,768]{1,0:T(8,128)} %factor.1), custom_call_target="tpu_custom_call" | custom-call | tf_op jit(solution)/shard_map/pallas_call | solution.py:85
  10.8 0.0 copy-start.6
  10.9 0.1 collective-permute-start
  10.9 0.5 collective-permute-start.1
  11.4 0.1 collective-permute-start.6
  11.5 3.0 %collective-permute-done.1 = f32[8,32,384]{2,1,0:T(8,128)S(1)} collective-permute-done((f32[8,32,384]{2,1,0:T(8,128)}, f32[8,32,384]{2,1,0:T(8,128)S(1)}, u32[]{:S(2)}, u32[]{:S(2)}) %collective-permute-start.1) | collective-permute-done | bytes 393248 | tf_op jit(solution)/shard_map/ppermute | solution.py:16
  14.5 1.0 %add.51 = f32[8,32,384]{2,1,0:T(8,128)S(1)} add(f32[8,32,384]{2,1,0:T(8,128)} %get-tuple-element.15, f32[8,32,384]{2,1,0:T(8,128)S(1)} %collective-permute-done.1) | non-fusion elementwise | flops 98304 | bytes 1179648 | tf_op jit(solution)/shard_map/add | solution.py:190
  15.6 0.7 fusion.4
  16.3 1.5 %collective-permute-start.2 = (f32[4,32,384]{2,1,0:T(8,128)}, f32[4,32,384]{2,1,0:T(8,128)S(1)}, u32[]{:S(2)}, u32[]{:S(2)}) collective-permute-start(f32[4,32,384]{2,1,0:T(8,128)} %get-tuple-element.25), channel_id=1, source_target_pairs={{0,16},{16,32},{32,48},{48,0},{1,17},{17,33},{33,49},{49,1},{2,18}... | collective-permute-start | bytes 589832 | tf_op jit(solution)/shard_map/ppermute | solution.py:16
  17.8 1.8 %collective-permute-start.4 = (f32[4,32,384]{2,1,0:T(8,128)S(1)}, f32[4,32,384]{2,1,0:T(8,128)S(1)}, u32[]{:S(2)}, u32[]{:S(2)}) collective-permute-start(f32[4,32,384]{2,1,0:T(8,128)S(1)} %get-tuple-element.26), channel_id=1, source_target_pairs={{0,48},{16,0},{32,16},{48,32},{1,49},{17,1},{33,17},{49,33},{2,50}... | collective-permute-start | bytes 589832 | tf_op jit(solution)/shard_map/ppermute | solution.py:16
  19.5 0.0 collective-permute-done.6
  19.5 0.0 copy-done.6
  19.5 0.0 copy-start.4
  19.5 0.9 add.56
  20.4 8.6 %all-to-all-start.1 = ((f32[8,4,32,128]{3,2,1,0:T(8,128)}), f32[8,4,32,128]{3,2,1,0:T(8,128)S(1)}, u32[]{:S(2)}, u32[]{:S(2)}) async-start(f32[8,4,32,128]{3,2,1,0:T(8,128)} %add.56), calls=%async_computation.1 | async-start | bytes 1048576 | tf_op jit(solution)/shard_map/all_to_all | solution.py:20
  29.0 0.0 collective-permute-done
  29.0 0.0 copy-start.5
  29.0 1.0 %copy-done.5 = f32[3,8,32,384]{3,2,1,0:T(8,128)} copy-done((f32[3,8,32,384]{3,2,1,0:T(8,128)}, f32[3,8,32,384]{3,2,1,0:T(8,128)S(1)}, u32[]{:S(2)}) %copy-start.5) | copy-done | bytes 1179672
  30.0 0.0 copy-done.4
  30.0 1.4 %add.50 = f32[3,8,32,384]{3,2,1,0:T(8,128)S(1)} add(f32[3,8,32,384]{3,2,1,0:T(8,128)S(1)} %copy-done.4, f32[3,8,32,384]{3,2,1,0:T(8,128)} %copy-done.5) | non-fusion elementwise | flops 294912 | bytes 3538944 | tf_op jit(solution)/shard_map/add | solution.py:191
  31.5 0.0 collective-permute-done.2
  31.5 0.0 collective-permute-done.4
  31.6 1.6 %collective-permute-start.5 = (f32[8,32,384]{2,1,0:T(8,128)S(1)}, f32[8,32,384]{2,1,0:T(8,128)}, u32[]{:S(2)}, u32[]{:S(2)}) collective-permute-start(f32[8,32,384]{2,1,0:T(8,128)S(1)} %pad_maximum_fusion.1), channel_id=1, source_target_pairs={{0,48},{16,0},{32,16},{48,32},{1,49},{17,1},{33,17},{49,33},{2,50}... | collective-permute-start | bytes 1179656 | tf_op jit(solution)/shard_map/ppermute | solution.py:16
  33.2 0.6 collective-permute-start.3
  33.8 11.0 %all-to-all-done.1 = f32[8,4,32,128]{3,2,1,0:T(8,128)S(1)} async-done(((f32[8,4,32,128]{3,2,1,0:T(8,128)}), f32[8,4,32,128]{3,2,1,0:T(8,128)S(1)}, u32[]{:S(2)}, u32[]{:S(2)}) %all-to-all-start.1) | async-done | bytes 524320 | tf_op jit(solution)/shard_map/all_to_all | solution.py:20
  44.8 0.7 reduce_sum.28
  45.4 3.3 %all-to-all-start.2 = ((f32[4,32,128]{2,1,0:T(8,128)}), f32[4,32,128]{2,1,0:T(8,128)S(1)}, u32[]{:S(2)}, u32[]{:S(2)}) async-start(f32[4,32,128]{2,1,0:T(8,128)} %reduce_sum.28), calls=%async_computation.2 | async-start | bytes 131072 | tf_op jit(solution)/shard_map/all_to_all | solution.py:20
  48.7 0.0 copy-start.3
  48.7 0.0 collective-permute-done.5
  48.7 0.0 collective-permute-done.3
  48.8 2.0 %fusion.1 = f32[8,32,384]{2,1,0:T(8,128)} fusion(f32[8,32,384]{2,1,0:T(8,128)} %collective-permute-done.5, f32[8,32,384]{2,1,0:T(8,128)} %collective-permute-done.3, f32[3,8,32,384]{3,2,1,0:T(8,128)S(1)} %add.50), kind=kLoop, calls=%fused_computation.2 | loop fusion | flops 196608 | bytes 1572864 | tf_op jit(solution)/shard_map/add | solution.py:176
  50.8 3.6 %all-to-all-done.2 = f32[4,32,128]{2,1,0:T(8,128)S(1)} async-done(((f32[4,32,128]{2,1,0:T(8,128)}), f32[4,32,128]{2,1,0:T(8,128)S(1)}, u32[]{:S(2)}, u32[]{:S(2)}) %all-to-all-start.2) | async-done | bytes 65568 | tf_op jit(solution)/shard_map/all_to_all | solution.py:20
  54.3 4.8 %all-to-all-start = ((f32[8,32,384]{2,1,0:T(8,128)}), f32[8,32,384]{2,1,0:T(8,128)S(1)}, u32[]{:S(2)}, u32[]{:S(2)}) async-start(f32[8,32,384]{2,1,0:T(8,128)} %fusion.1), calls=%async_computation | async-start | bytes 786432 | tf_op jit(solution)/shard_map/all_to_all | solution.py:20
  59.1 0.0 copy-done.7
  59.1 0.0 copy-done.3
  59.1 0.0 copy-start.2
  59.2 1.9 %copy-done.2 = f32[512,1536]{1,0:T(8,128)S(1)} copy-done((f32[512,1536]{1,0:T(8,128)S(1)}, f32[512,1536]{1,0:T(8,128)}, u32[]{:S(2)}) %copy-start.2) | copy-done | bytes 3145752
  61.0 3.8 %shard_map.56 = (bf16[4,512,512]{2,1,0:T(8,128)(2,1)S(1)}, bf16[4,512,512]{2,1,0:T(8,128)(2,1)S(1)}) custom-call(f32[512,512]{1,0:T(8,128)S(1)} %copy-done.3, f32[512,1536]{1,0:T(8,128)S(1)} %copy-done.2), custom_call_target="tpu_custom_call" | custom-call | tf_op jit(solution)/shard_map/pallas_call | solution.py:115
  64.9 0.0 copy-start
  64.9 1.3 %copy-done = bf16[4,512,512]{2,1,0:T(8,128)(2,1)} copy-done((bf16[4,512,512]{2,1,0:T(8,128)(2,1)}, bf16[4,512,512]{2,1,0:T(8,128)(2,1)S(1)}, u32[]{:S(2)}) %copy-start) | copy-done | bytes 2097176
  66.2 0.8 reduce_sum.29
  67.0 3.7 %all-to-all-done = f32[8,32,384]{2,1,0:T(8,128)S(1)} async-done(((f32[8,32,384]{2,1,0:T(8,128)}), f32[8,32,384]{2,1,0:T(8,128)S(1)}, u32[]{:S(2)}, u32[]{:S(2)}) %all-to-all-start) | async-done | bytes 393248 | tf_op jit(solution)/shard_map/all_to_all | solution.py:20
  70.7 0.9 maximum_subtract_fusion.refs_0_
  71.6 0.0 copy-start.1
  71.6 1.6 %copy-done.1 = bf16[4,512,512]{2,1,0:T(8,128)(2,1)S(1)} copy-done((bf16[4,512,512]{2,1,0:T(8,128)(2,1)S(1)}, bf16[4,512,512]{2,1,0:T(8,128)(2,1)}, u32[]{:S(2)}) %copy-start.1) | copy-done | bytes 2097176
  73.2 0.3 shard_map.57.refs_1_
  73.5 1.6 %collective-permute-start.7 = (f32[32,512]{1,0:T(8,128)S(1)}, f32[32,512]{1,0:T(8,128)S(1)}, u32[]{:S(2)}, u32[]{:S(2)}) collective-permute-start(f32[32,512]{1,0:T(8,128)S(1)} %shard_map.57.refs_1_), channel_id=1, source_target_pairs={{0,64},{64,128},{128,192},{192,0},{1,65},{65,129},{129,193},{193,1... | collective-permute-start | bytes 196616 | tf_op jit(solution)/shard_map/ppermute | solution.py:16
  75.1 1.7 %collective-permute-start.10 = (f32[32,512]{1,0:T(8,128)S(1)}, f32[32,512]{1,0:T(8,128)S(1)}, u32[]{:S(2)}, u32[]{:S(2)}) collective-permute-start(f32[32,512]{1,0:T(8,128)S(1)} %shard_map.57.refs_1_), channel_id=1, source_target_pairs={{0,192},{64,0},{128,64},{192,128},{1,193},{65,1},{129,65},{193,129... | collective-permute-start | bytes 196616 | tf_op jit(solution)/shard_map/ppermute | solution.py:16
  76.7 2.0 %collective-permute-start.9 = (f32[32,512]{1,0:T(8,128)S(1)}, f32[32,512]{1,0:T(8,128)S(1)}, u32[]{:S(2)}, u32[]{:S(2)}) collective-permute-start(f32[32,512]{1,0:T(8,128)S(1)} %shard_map.57.refs_1_), channel_id=1, source_target_pairs={{0,128},{64,192},{128,0},{192,64},{1,129},{65,193},{129,1},{193,65... | collective-permute-start | bytes 196616 | tf_op jit(solution)/shard_map/ppermute | solution.py:16
  78.7 1.2 %collective-permute-done.7.refs_0_ = f32[32,512]{1,0:T(8,128)S(1)} collective-permute-done((f32[32,512]{1,0:T(8,128)S(1)}, f32[32,512]{1,0:T(8,128)S(1)}, u32[]{:S(2)}, u32[]{:S(2)}) %collective-permute-start.7) | collective-permute-done | bytes 65568 | tf_op jit(solution)/shard_map/ppermute | solution.py:16
  79.9 0.3 shard_map.58.refs_2_
  80.1 0.0 collective-permute-start.8
  80.2 2.4 %collective-permute-start.12 = (f32[32,512]{1,0:T(8,128)S(1)}, f32[32,512]{1,0:T(8,128)S(1)}, u32[]{:S(2)}, u32[]{:S(2)}) collective-permute-start(f32[32,512]{1,0:T(8,128)S(1)} %shard_map.58.refs_2_), channel_id=1, source_target_pairs={{0,128},{64,192},{128,0},{192,64},{1,129},{65,193},{129,1},{193,65... | collective-permute-start | bytes 196616 | tf_op jit(solution)/shard_map/ppermute | solution.py:16
  82.5 0.0 collective-permute-done.10.refs_1_
  82.5 0.0 collective-permute-done.9.refs_0_
  82.5 0.3 shard_map.59.refs_1_
  82.8 3.5 %collective-permute-done.8.refs_0_ = f32[32,512]{1,0:T(8,128)S(1)} collective-permute-done((f32[32,512]{1,0:T(8,128)S(1)}, f32[32,512]{1,0:T(8,128)S(1)}, u32[]{:S(2)}, u32[]{:S(2)}) %collective-permute-start.8) | collective-permute-done | bytes 65568 | tf_op jit(solution)/shard_map/ppermute | solution.py:16
  86.3 0.3 shard_map.60.refs_1_
  86.6 0.0 collective-permute-start.11
  86.6 0.0 collective-permute-done.12.refs_0_
  86.6 0.3 shard_map.61.refs_1_
  86.9 5.2 %collective-permute-done.11.refs_0_ = f32[32,512]{1,0:T(8,128)S(1)} collective-permute-done((f32[32,512]{1,0:T(8,128)S(1)}, f32[32,512]{1,0:T(8,128)S(1)}, u32[]{:S(2)}, u32[]{:S(2)}) %collective-permute-start.11) | collective-permute-done | bytes 65568 | tf_op jit(solution)/shard_map/ppermute | solution.py:16
  92.1 0.9 shard_map.62
  (7 shorter events, 0.2 us)
Async XLA Ops:
  10.8 8.7 %copy-start.6 = (f32[8,4,32,128]{3,2,1,0:T(8,128)S(1)}, f32[8,4,32,128]{3,2,1,0:T(8,128)}, u32[]{:S(2)}) copy-start(f32[8,4,32,128]{3,2,1,0:T(8,128)} %get-tuple-element.17) | copy-start | bytes 1572868
  10.9 18.1 %collective-permute-start = (f32[3,8,32,384]{3,2,1,0:T(8,128)}, f32[3,8,32,384]{3,2,1,0:T(8,128)S(1)}, u32[]{:S(2)}, u32[]{:S(2)}) collective-permute-start(f32[3,8,32,384]{3,2,1,0:T(8,128)} %get-tuple-element.14), channel_id=1, source_target_pairs={{0,1},{1,0},{2,3},{3,2},{4,5},{5,4},{6,7},{7,6},{8,9},{9,8},{10,11... | collective-permute-start | bytes 3538952 | tf_op jit(solution)/shard_map/ppermute | solution.py:16
  10.9 3.6 %collective-permute-start.1 = (f32[8,32,384]{2,1,0:T(8,128)}, f32[8,32,384]{2,1,0:T(8,128)S(1)}, u32[]{:S(2)}, u32[]{:S(2)}) collective-permute-start(f32[8,32,384]{2,1,0:T(8,128)} %get-tuple-element.16), channel_id=1, source_target_pairs={{0,1},{1,0},{2,3},{3,2},{4,5},{5,4},{6,7},{7,6},{8,9},{9,8},{10,11... | collective-permute-start | bytes 1179656 | tf_op jit(solution)/shard_map/ppermute | solution.py:16
  11.4 8.1 %collective-permute-start.6 = (f32[8,4,32,128]{3,2,1,0:T(8,128)}, f32[8,4,32,128]{3,2,1,0:T(8,128)S(1)}, u32[]{:S(2)}, u32[]{:S(2)}) collective-permute-start(f32[8,4,32,128]{3,2,1,0:T(8,128)} %get-tuple-element.18), channel_id=1, source_target_pairs={{0,1},{1,0},{2,3},{3,2},{4,5},{5,4},{6,7},{7,6},{8,9},{9,8},{10,11... | collective-permute-start | bytes 1572872 | tf_op jit(solution)/shard_map/ppermute | solution.py:16
  16.3 15.2 %collective-permute-start.2 = (f32[4,32,384]{2,1,0:T(8,128)}, f32[4,32,384]{2,1,0:T(8,128)S(1)}, u32[]{:S(2)}, u32[]{:S(2)}) collective-permute-start(f32[4,32,384]{2,1,0:T(8,128)} %get-tuple-element.25), channel_id=1, source_target_pairs={{0,16},{16,32},{32,48},{48,0},{1,17},{17,33},{33,49},{49,1},{2,18}... | collective-permute-start | bytes 589832 | tf_op jit(solution)/shard_map/ppermute | solution.py:16
  17.8 13.7 %collective-permute-start.4 = (f32[4,32,384]{2,1,0:T(8,128)S(1)}, f32[4,32,384]{2,1,0:T(8,128)S(1)}, u32[]{:S(2)}, u32[]{:S(2)}) collective-permute-start(f32[4,32,384]{2,1,0:T(8,128)S(1)} %get-tuple-element.26), channel_id=1, source_target_pairs={{0,48},{16,0},{32,16},{48,32},{1,49},{17,1},{33,17},{49,33},{2,50}... | collective-permute-start | bytes 589832 | tf_op jit(solution)/shard_map/ppermute | solution.py:16
  19.5 10.5 %copy-start.4 = (f32[3,8,32,384]{3,2,1,0:T(8,128)S(1)}, f32[3,8,32,384]{3,2,1,0:T(8,128)}, u32[]{:S(2)}) copy-start(f32[3,8,32,384]{3,2,1,0:T(8,128)} %get-tuple-element.13) | copy-start | bytes 3538948
  20.4 24.3 %all-to-all-start.1 = ((f32[8,4,32,128]{3,2,1,0:T(8,128)}), f32[8,4,32,128]{3,2,1,0:T(8,128)S(1)}, u32[]{:S(2)}, u32[]{:S(2)}) async-start(f32[8,4,32,128]{3,2,1,0:T(8,128)} %add.56), calls=%async_computation.1 | async-start | bytes 1048576 | tf_op jit(solution)/shard_map/all_to_all | solution.py:20
  29.0 1.0 %copy-start.5 = (f32[3,8,32,384]{3,2,1,0:T(8,128)}, f32[3,8,32,384]{3,2,1,0:T(8,128)S(1)}, u32[]{:S(2)}) copy-start(f32[3,8,32,384]{3,2,1,0:T(8,128)S(1)} %collective-permute-done) | copy-start | bytes 3538948
  31.6 17.1 %collective-permute-start.5 = (f32[8,32,384]{2,1,0:T(8,128)S(1)}, f32[8,32,384]{2,1,0:T(8,128)}, u32[]{:S(2)}, u32[]{:S(2)}) collective-permute-start(f32[8,32,384]{2,1,0:T(8,128)S(1)} %pad_maximum_fusion.1), channel_id=1, source_target_pairs={{0,48},{16,0},{32,16},{48,32},{1,49},{17,1},{33,17},{49,33},{2,50}... | collective-permute-start | bytes 1179656 | tf_op jit(solution)/shard_map/ppermute | solution.py:16
  33.2 15.5 %collective-permute-start.3 = (f32[8,32,384]{2,1,0:T(8,128)S(1)}, f32[8,32,384]{2,1,0:T(8,128)}, u32[]{:S(2)}, u32[]{:S(2)}) collective-permute-start(f32[8,32,384]{2,1,0:T(8,128)S(1)} %pad_maximum_fusion), channel_id=1, source_target_pairs={{0,16},{16,32},{32,48},{48,0},{1,17},{17,33},{33,49},{49,1},{2,18}... | collective-permute-start | bytes 1179656 | tf_op jit(solution)/shard_map/ppermute | solution.py:16
  45.4 8.9 %all-to-all-start.2 = ((f32[4,32,128]{2,1,0:T(8,128)}), f32[4,32,128]{2,1,0:T(8,128)S(1)}, u32[]{:S(2)}, u32[]{:S(2)}) async-start(f32[4,32,128]{2,1,0:T(8,128)} %reduce_sum.28), calls=%async_computation.2 | async-start | bytes 131072 | tf_op jit(solution)/shard_map/all_to_all | solution.py:20
  48.7 10.4 %copy-start.3 = (f32[512,512]{1,0:T(8,128)S(1)}, f32[512,512]{1,0:T(8,128)}, u32[]{:S(2)}) copy-start(f32[512,512]{1,0:T(8,128)} %diag.1) | copy-start | bytes 3145732
  54.3 4.8 %copy-start.7 = (f32[4,32,128]{2,1,0:T(8,128)}, f32[4,32,128]{2,1,0:T(8,128)S(1)}, u32[]{:S(2)}) copy-start(f32[4,32,128]{2,1,0:T(8,128)S(1)} %all-to-all-done.2) | copy-start | bytes 196612
  54.3 16.4 %all-to-all-start = ((f32[8,32,384]{2,1,0:T(8,128)}), f32[8,32,384]{2,1,0:T(8,128)S(1)}, u32[]{:S(2)}, u32[]{:S(2)}) async-start(f32[8,32,384]{2,1,0:T(8,128)} %fusion.1), calls=%async_computation | async-start | bytes 786432 | tf_op jit(solution)/shard_map/all_to_all | solution.py:20
  59.1 1.9 %copy-start.2 = (f32[512,1536]{1,0:T(8,128)S(1)}, f32[512,1536]{1,0:T(8,128)}, u32[]{:S(2)}) copy-start(f32[512,1536]{1,0:T(8,128)} %coupling.1) | copy-start | bytes 9437188
  64.9 1.3 %copy-start = (bf16[4,512,512]{2,1,0:T(8,128)(2,1)}, bf16[4,512,512]{2,1,0:T(8,128)(2,1)S(1)}, u32[]{:S(2)}) copy-start(bf16[4,512,512]{2,1,0:T(8,128)(2,1)S(1)} %get-tuple-element.20.refs_3_.refs_4_) | copy-start | bytes 6291460
  71.6 1.6 %copy-start.1 = (bf16[4,512,512]{2,1,0:T(8,128)(2,1)S(1)}, bf16[4,512,512]{2,1,0:T(8,128)(2,1)}, u32[]{:S(2)}) copy-start(bf16[4,512,512]{2,1,0:T(8,128)(2,1)} %copy-done) | copy-start | bytes 6291460
  73.5 6.4 %collective-permute-start.7 = (f32[32,512]{1,0:T(8,128)S(1)}, f32[32,512]{1,0:T(8,128)S(1)}, u32[]{:S(2)}, u32[]{:S(2)}) collective-permute-start(f32[32,512]{1,0:T(8,128)S(1)} %shard_map.57.refs_1_), channel_id=1, source_target_pairs={{0,64},{64,128},{128,192},{192,0},{1,65},{65,129},{129,193},{193,1... | collective-permute-start | bytes 196616 | tf_op jit(solution)/shard_map/ppermute | solution.py:16
  75.1 7.5 %collective-permute-start.10 = (f32[32,512]{1,0:T(8,128)S(1)}, f32[32,512]{1,0:T(8,128)S(1)}, u32[]{:S(2)}, u32[]{:S(2)}) collective-permute-start(f32[32,512]{1,0:T(8,128)S(1)} %shard_map.57.refs_1_), channel_id=1, source_target_pairs={{0,192},{64,0},{128,64},{192,128},{1,193},{65,1},{129,65},{193,129... | collective-permute-start | bytes 196616 | tf_op jit(solution)/shard_map/ppermute | solution.py:16
  76.7 5.8 %collective-permute-start.9 = (f32[32,512]{1,0:T(8,128)S(1)}, f32[32,512]{1,0:T(8,128)S(1)}, u32[]{:S(2)}, u32[]{:S(2)}) collective-permute-start(f32[32,512]{1,0:T(8,128)S(1)} %shard_map.57.refs_1_), channel_id=1, source_target_pairs={{0,128},{64,192},{128,0},{192,64},{1,129},{65,193},{129,1},{193,65... | collective-permute-start | bytes 196616 | tf_op jit(solution)/shard_map/ppermute | solution.py:16
  80.1 6.2 %collective-permute-start.8 = (f32[32,512]{1,0:T(8,128)S(1)}, f32[32,512]{1,0:T(8,128)S(1)}, u32[]{:S(2)}, u32[]{:S(2)}) collective-permute-start(f32[32,512]{1,0:T(8,128)S(1)} %shard_map.58.refs_2_), channel_id=1, source_target_pairs={{0,64},{64,128},{128,192},{192,0},{1,65},{65,129},{129,193},{193,1... | collective-permute-start | bytes 196616 | tf_op jit(solution)/shard_map/ppermute | solution.py:16
  80.2 6.5 %collective-permute-start.12 = (f32[32,512]{1,0:T(8,128)S(1)}, f32[32,512]{1,0:T(8,128)S(1)}, u32[]{:S(2)}, u32[]{:S(2)}) collective-permute-start(f32[32,512]{1,0:T(8,128)S(1)} %shard_map.58.refs_2_), channel_id=1, source_target_pairs={{0,128},{64,192},{128,0},{192,64},{1,129},{65,193},{129,1},{193,65... | collective-permute-start | bytes 196616 | tf_op jit(solution)/shard_map/ppermute | solution.py:16
  86.6 5.5 %collective-permute-start.11 = (f32[32,512]{1,0:T(8,128)S(1)}, f32[32,512]{1,0:T(8,128)S(1)}, u32[]{:S(2)}, u32[]{:S(2)}) collective-permute-start(f32[32,512]{1,0:T(8,128)S(1)} %shard_map.60.refs_1_), channel_id=1, source_target_pairs={{0,64},{64,128},{128,192},{192,0},{1,65},{65,129},{129,193},{193,1... | collective-permute-start | bytes 196616 | tf_op jit(solution)/shard_map/ppermute | solution.py:16

commit v3 on v2

--- a/solution.py
+++ b/solution.py
@@ -18,6 +18,10 @@
 
 def summed_at_owner(blocks, axis):
     return jnp.sum(lax.all_to_all(blocks, axis, 0, 0, tiled=True), axis=0)
+
+
+def in_hbm(value):
+    return pltpu.with_memory_space_constraint(value, pltpu.HBM)
 
 
 def halves(value):
@@ -43,58 +47,37 @@
     return sorted(range(peers), key=lambda o: (-min(o, peers - o), o))
 
 
-def product_body(n_z, n_core, split, place, users, factor, far_own, own_a, own_b, far_sent, sent_a, sent_b):
-    core, step = place[0], pl.program_id(0)
+def product_body(n_z, n_core, place, users, factor, own_out, sent_out):
     items, rows = users.shape[1], factor.shape[0]
     share = items // (n_z * n_core)
     total = three_pass(users[...], factor[...], 0, 1).reshape(n_z, n_core, share, rows)
 
     def keep(mine):
-        own, sent = total[:, mine], total[:, 1 - mine]
-        own_b[:, 0] = own[..., split:]
-        sent_b[:, 0] = sent[..., split:]
+        own_out[0] = total[:, mine]
+        sent_out[0] = total[:, 1 - mine]
 
-        @pl.when(step == 0)
-        def _():
-            far_own[...] = own[..., :split]
-            far_sent[...] = sent[..., :split]
-
-        @pl.when(step > 0)
-        def _():
-            own_a[0] = own[..., :split]
-            sent_a[0] = sent[..., :split]
-
-    pl.when(core == 0)(lambda: keep(0))
-    pl.when(core == 1)(lambda: keep(1))
+    pl.when(place[0] == 0)(lambda: keep(0))
+    pl.when(place[0] == 1)(lambda: keep(1))
 
 
-def product(place, users, factor, n_x, n_z, n_core, split):
+def product(place, first, count, users, factor, sizes):
+    n_x, n_z, n_core = sizes
     depth, items = users.shape
     rows = factor.shape[0]
     chunk, share = items // n_x, items // (n_x * n_z * n_core)
-    specs = [
-        pl.BlockSpec((n_z, share, split), lambda i, s: (0, 0, 0)),
-        pl.BlockSpec((1, n_z, share, split), lambda i, s: (lax.max(i - 1, 0), 0, 0, 0)),
-        pl.BlockSpec((n_z, 1, share, rows - split), lambda i, s: (0, s[1 + i], 0, 0)),
-    ]
-    shapes = [
-        jax.ShapeDtypeStruct((n_z, share, split), jnp.float32),
-        jax.ShapeDtypeStruct((n_x - 1, n_z, share, split), jnp.float32),
-        jax.ShapeDtypeStruct((n_z, n_x, share, rows - split), jnp.float32),
-    ]
     return pl.pallas_call(
-        functools.partial(product_body, n_z, n_core, split),
+        functools.partial(product_body, n_z, n_core),
         grid_spec=pltpu.PrefetchScalarGridSpec(
             num_scalar_prefetch=1,
-            grid=(n_x,),
+            grid=(count,),
             in_specs=[
-                pl.BlockSpec((depth, chunk), lambda i, s: (0, s[1 + i])),
+                pl.BlockSpec((depth, chunk), lambda i, s: (0, s[1 + first + i])),
                 pl.BlockSpec((rows, depth), lambda i, s: (0, 0)),
             ],
-            out_specs=specs * 2,
+            out_specs=[pl.BlockSpec((1, n_z, share, rows), lambda i, s: (i, 0, 0, 0))] * 2,
         ),
-        out_shape=shapes * 2,
-        compiler_params=pltpu.CompilerParams(vmem_limit_bytes=56 << 20),
+        out_shape=[jax.ShapeDtypeStruct((count, n_z, share, rows), jnp.float32)] * 2,
+        compiler_params=pltpu.CompilerParams(vmem_limit_bytes=24 << 20),
     )(place, users, factor)
 
 
@@ -167,33 +150,32 @@
     return result
 
 
-def ring_reduced(far, near, axis):
+def on_device(right_side, solved_factor, solved_users, diag_inverse, coupling):
+    sizes = tuple(lax.axis_size(a) for a in COL)
+    x, core = lax.axis_index("x"), lax.axis_index("core")
+    place = jnp.stack([core] + [(x + o) % sizes[0] for o in ring_order(sizes[0])]).astype(jnp.int32)
+    position = lax.axis_index("grp").reshape(1).astype(jnp.int32)
+    users, factor = in_hbm(solved_users), in_hbm(solved_factor)
+
+    def part(first, count, place):
+        own, sent = product(place, first, count, users, factor, sizes)
+        place, sent = lax.optimization_barrier((place, sent))
+        return own, shifted(sent, "core", 1), place
+
+    far_own, far_other, place = part(0, 1, place)
+    near_own, near_other, place = part(1, 2, place)
+    far = (far_own + far_other)[0]
+    place, far = lax.optimization_barrier((place, far))
     cut = far.shape[0] // 2
-    up = shifted(far[:cut], axis, 1)
-    down = shifted(far[cut:], axis, -1)
-    up = shifted(jnp.concatenate([near[0, :cut] + up, near[0, cut:]]), axis, 1)
-    down = shifted(jnp.concatenate([near[1, :cut], near[1, cut:] + down]), axis, -1)
-    return near[2] + up + down
-
-
-def on_device(right_side, solved_factor, solved_users, diag_inverse, coupling):
-    n_x, n_z, n_core = (lax.axis_size(a) for a in COL)
-    x, core = lax.axis_index("x"), lax.axis_index("core")
-    place = jnp.stack([core] + [(x + o) % n_x for o in ring_order(n_x)]).astype(jnp.int32)
-    position = lax.axis_index("grp").reshape(1).astype(jnp.int32)
-    rows = solved_factor.shape[0]
-    far_own, own_a, own_b, far_sent, sent_a, sent_b = product(
-        place, solved_users, solved_factor, n_x, n_z, n_core, rows * 3 // 4
-    )
-    weights = hop_weights(diag_inverse, coupling)
-    sum_b = own_b + shifted(sent_b, "core", 1)
-    far_a = far_own + shifted(far_sent, "core", 1)
-    near_a = own_a + shifted(sent_a, "core", 1)
-    part_b = summed_at_owner(sum_b, "z")
-    part_a = ring_reduced(far_a, near_a, "x")
-    share_b = summed_at_owner(part_b, "x")
-    share_a = summed_at_owner(part_a, "z")
-    residue = right_side.T - jnp.concatenate([share_a, share_b], axis=1)
+    up = shifted(far[:cut], "x", 1)
+    down = shifted(far[cut:], "x", -1)
+    home_own, home_other, _ = part(3, 1, place)
+    weights = [in_hbm(half) for half in hop_weights(diag_inverse, coupling)]
+    ahead, behind = near_own[0] + near_other[0], near_own[1] + near_other[1]
+    up = shifted(jnp.concatenate([ahead[:cut] + up, ahead[cut:]]), "x", 1)
+    down = shifted(jnp.concatenate([behind[:cut], behind[cut:] + down]), "x", -1)
+    along_z = home_own[0] + home_other[0] + up + down
+    residue = right_side.T - summed_at_owner(along_z, "z")
     return chain(position, residue, weights).T
 
 

time: 93.7 us -> 93.9 us (level); the launches traced: 93 us -> 92 us
  Pallas kernels: 16.3 us -> 26.6 us
  starting transfers between devices: 30.4 us -> 24.3 us
  other arithmetic: 7.86 us -> 2.55 us
  waiting for transfers between devices: 31.1 us -> 34.4 us
  local copies, waits for them, and re-layouts: 7.14 us -> 4.01 us
    ppermute x13, waiting for transfers between devices: 12.9 us -> 27 us  [shifted(): lax.ppermute(value, axis, [(i, (i + by) % peers) for i in range(peers)])]
    all_to_all x3 -> x1, waiting for transfers between devices: 18.2 us -> 7.38 us  [summed_at_owner(): return jnp.sum(lax.all_to_all(blocks, axis, 0, 0, tiled=True), axis=0)]
    all_to_all x3 -> x1, starting transfers between devices: 16.7 us -> 8.58 us  [summed_at_owner(): return jnp.sum(lax.all_to_all(blocks, axis, 0, 0, tiled=True), axis=0)]
    pallas_call x6, Pallas kernels: 2.29 us -> 9.5 us  [applied(): pl.pallas_call(functools.partial(apply_body, [group for group, _ in value...]
    add x5 -> x4, other arithmetic: 5.42 us -> 1.3 us  [the longest x1 1 us: on_device(): along_z = home_own[0] + home_other[0] + up + down]
    pallas_call x1 -> x3, Pallas kernels: 10.3 us -> 13.3 us  [product(): pl.pallas_call(functools.partial(product_body, n_z, n_core), grid_spec=pl...]
    ppermute x13, starting transfers between devices: 13.7 us -> 15.7 us  [shifted(): lax.ppermute(value, axis, [(i, (i + by) % peers) for i in range(peers)])]
    unnamed x16 -> x10, local copies, waits for them, and re-layouts: 5.82 us -> 3.85 us
  transfers between devices with their start and end apart: 16 -> 14, of which waited for: 7 -> 9; matrix products, arithmetic and copies ran while one was open for 8% -> 1% of each run, Pallas kernels for 5% -> 15%
where the time goes in v3:
time: 93.9 us; the launch traced here: 92 us
  waiting for transfers between devices  34.4 us (37%)
  Pallas kernels  26.6 us (28%)
  starting transfers between devices  24.3 us (26%)
  local copies, waits for them, and re-layouts  4.01 us (4%)
  other arithmetic  2.55 us (3%)
    ppermute x13, waiting for transfers between devices, shifted(): lax.ppermute(value, axis, [(i, (i + by) % peers) for i in range(peers)])  27 us
    ppermute x13, starting transfers between devices, shifted(): lax.ppermute(value, axis, [(i, (i + by) % peers) for i in range(peers)])  15.7 us
    pallas_call x3, Pallas kernels, product(): pl.pallas_call(functools.partial(product_body, n_z, n_core), grid_spec=pl...  13.3 us
    pallas_call x6, Pallas kernels, applied(): pl.pallas_call(functools.partial(apply_body, [group for group, _ in value...  9.5 us
    all_to_all x1, starting transfers between devices, summed_at_owner(): return jnp.sum(lax.all_to_all(blocks, axis, 0, 0, tiled=True), axis=0)  8.58 us
    all_to_all x1, waiting for transfers between devices, summed_at_owner(): return jnp.sum(lax.all_to_all(blocks, axis, 0, 0, tiled=True), axis=0)  7.38 us
    unnamed x10, local copies, waits for them, and re-layouts  3.85 us
    pallas_call x1, Pallas kernels, hop_weights(): pl.pallas_call(weights_body, grid=(count,), in_specs=[pl.BlockSpec((block...  3.81 us
  transfers between devices with their start and end apart: 14, of which 9 were waited for; matrix products, arithmetic and copies ran while one was open for 1% of the time, Pallas kernels for 15%

profile of v3, /device:TPU:32, one launch (start us, length us, event | category | flops | bytes accessed | tf_op | source)
XLA Modules:
  0.0 92.0 jit_solution(10668017217700903718)
XLA Ops:
  0.0 0.1 stack.23.place
  0.1 3.9 %shard_map.55 = (f32[1,8,32,512]{3,2,1,0:T(8,128)S(1)}, f32[1,8,32,512]{3,2,1,0:T(8,128)S(1)}) custom-call(s32[5]{0:T(128)S(1)} %stack.23.place, f32[768,2048]{1,0:T(8,128)} %users.5, f32[512,768]{1,0:T(8,128)} %factor.5), custom_call_target="tpu_custom_call" | custom-call | tf_op jit(solution)/shard_map/pallas_call | solution.py:68
  4.0 5.4 %shard_map.56 = (f32[2,8,32,512]{3,2,1,0:T(8,128)S(1)}, f32[2,8,32,512]{3,2,1,0:T(8,128)S(1)}) custom-call(s32[5]{0:T(128)S(1)} %stack.23.place, f32[768,2048]{1,0:T(8,128)} %users.5, f32[512,768]{1,0:T(8,128)} %factor.5), custom_call_target="tpu_custom_call" | custom-call | tf_op jit(solution)/shard_map/pallas_call | solution.py:68
  9.5 0.1 collective-permute-start.2
  9.6 0.5 collective-permute-start
  10.0 2.9 %collective-permute-done = f32[1,8,32,512]{3,2,1,0:T(8,128)S(1)} collective-permute-done((f32[1,8,32,512]{3,2,1,0:T(8,128)S(1)}, f32[1,8,32,512]{3,2,1,0:T(8,128)S(1)}, u32[]{:S(2)}, u32[]{:S(2)}) %collective-permute-start) | collective-permute-done | bytes 524320 | tf_op jit(solution)/shard_map/ppermute | solution.py:16
  12.9 0.1 add_bitcast_fusion
  13.1 1.6 %collective-permute-start.3 = (f32[4,32,512]{2,1,0:T(8,128)S(1)}, f32[4,32,512]{2,1,0:T(8,128)S(1)}, u32[]{:S(2)}, u32[]{:S(2)}) collective-permute-start(f32[4,32,512]{2,1,0:T(8,128)S(1)} %get-tuple-element.37), channel_id=1, source_target_pairs={{0,16},{16,32},{32,48},{48,0},{1,17},{17,33},{33,49},{49,1},{2,18}... | collective-permute-start | bytes 786440 | tf_op jit(solution)/shard_map/ppermute | solution.py:16
  14.7 3.9 %shard_map.57 = (f32[1,8,32,512]{3,2,1,0:T(8,128)S(1)}, f32[1,8,32,512]{3,2,1,0:T(8,128)S(1)}) custom-call(s32[5]{0:T(128)S(1)} %stack.23.place, f32[768,2048]{1,0:T(8,128)} %users.5, f32[512,768]{1,0:T(8,128)} %factor.5), custom_call_target="tpu_custom_call" | custom-call | tf_op jit(solution)/shard_map/pallas_call | solution.py:68
  18.6 0.1 collective-permute-start.1
  18.7 1.8 %collective-permute-start.5 = (f32[4,32,512]{2,1,0:T(8,128)S(1)}, f32[4,32,512]{2,1,0:T(8,128)S(1)}, u32[]{:S(2)}, u32[]{:S(2)}) collective-permute-start(f32[4,32,512]{2,1,0:T(8,128)S(1)} %get-tuple-element.38), channel_id=1, source_target_pairs={{0,48},{16,0},{32,16},{48,32},{1,49},{17,1},{33,17},{49,33},{2,50}... | collective-permute-start | bytes 786440 | tf_op jit(solution)/shard_map/ppermute | solution.py:16
  20.5 0.0 collective-permute-done.2
  20.5 0.2 slice_add_fusion.1
  20.8 2.0 %collective-permute-done.3 = f32[4,32,512]{2,1,0:T(8,128)S(1)} collective-permute-done((f32[4,32,512]{2,1,0:T(8,128)S(1)}, f32[4,32,512]{2,1,0:T(8,128)S(1)}, u32[]{:S(2)}, u32[]{:S(2)}) %collective-permute-start.3) | collective-permute-done | bytes 262176 | tf_op jit(solution)/shard_map/ppermute | solution.py:16
  22.8 0.4 collective-permute-start.4
  23.2 4.2 %collective-permute-done.5 = f32[4,32,512]{2,1,0:T(8,128)S(1)} collective-permute-done((f32[4,32,512]{2,1,0:T(8,128)S(1)}, f32[4,32,512]{2,1,0:T(8,128)S(1)}, u32[]{:S(2)}, u32[]{:S(2)}) %collective-permute-start.5) | collective-permute-done | bytes 262176 | tf_op jit(solution)/shard_map/ppermute | solution.py:16
  27.5 0.0 copy-start.2
  27.5 3.0 %collective-permute-start.6 = (f32[8,32,512]{2,1,0:T(8,128)S(1)}, f32[8,32,512]{2,1,0:T(8,128)S(1)}, u32[]{:S(2)}, u32[]{:S(2)}) collective-permute-start(f32[8,32,512]{2,1,0:T(8,128)S(1)} %pad_maximum_fusion.1), channel_id=1, source_target_pairs={{0,48},{16,0},{32,16},{48,32},{1,49},{17,1},{33,17},{49,33},{2,50}... | collective-permute-start | bytes 1572872 | tf_op jit(solution)/shard_map/ppermute | solution.py:16
  30.5 0.0 collective-permute-done.1
  30.5 6.7 %collective-permute-done.4 = f32[8,32,512]{2,1,0:T(8,128)S(1)} collective-permute-done((f32[8,32,512]{2,1,0:T(8,128)S(1)}, f32[8,32,512]{2,1,0:T(8,128)S(1)}, u32[]{:S(2)}, u32[]{:S(2)}) %collective-permute-start.4) | collective-permute-done | bytes 524320 | tf_op jit(solution)/shard_map/ppermute | solution.py:16
  37.2 4.3 %collective-permute-done.6 = f32[8,32,512]{2,1,0:T(8,128)S(1)} collective-permute-done((f32[8,32,512]{2,1,0:T(8,128)S(1)}, f32[8,32,512]{2,1,0:T(8,128)S(1)}, u32[]{:S(2)}, u32[]{:S(2)}) %collective-permute-start.6) | collective-permute-done | bytes 524320 | tf_op jit(solution)/shard_map/ppermute | solution.py:16
  41.5 1.0 %fusion = f32[8,32,512]{2,1,0:T(8,128)} fusion(f32[8,32,512]{2,1,0:T(8,128)S(1)} %collective-permute-done.6, f32[8,32,512]{2,1,0:T(8,128)S(1)} %collective-permute-done.4, f32[1,8,32,512]{3,2,1,0:T(8,128)S(1)} %get-tuple-element.27, f32[1,8,32,512]{3,2,1,0:T(8,128)S(1)} %collective-permute-done.1), kind=kLoop, calls=%fused_computation.5 | loop fusion | flops 393216 | bytes 2621440 | tf_op jit(solution)/shard_map/add | solution.py:177
  42.5 8.6 %all-to-all-start = ((f32[8,32,512]{2,1,0:T(8,128)}), f32[8,32,512]{2,1,0:T(8,128)}, u32[]{:S(2)}, u32[]{:S(2)}) async-start(f32[8,32,512]{2,1,0:T(8,128)} %fusion), calls=%async_computation | async-start | bytes 1048576 | tf_op jit(solution)/shard_map/all_to_all | solution.py:20
  51.1 0.0 copy-done.2
  51.1 0.0 copy-start.3
  51.1 1.2 %copy-done.3 = f32[512,512]{1,0:T(8,128)S(1)} copy-done((f32[512,512]{1,0:T(8,128)S(1)}, f32[512,512]{1,0:T(8,128)}, u32[]{:S(2)}) %copy-start.3) | copy-done | bytes 1048600
  52.3 0.0 copy-start.4
  52.3 3.8 %shard_map.58 = (bf16[4,512,512]{2,1,0:T(8,128)(2,1)S(1)}, bf16[4,512,512]{2,1,0:T(8,128)(2,1)S(1)}) custom-call(f32[512,512]{1,0:T(8,128)S(1)} %copy-done.3, f32[512,1536]{1,0:T(8,128)S(1)} %copy-done.2), custom_call_target="tpu_custom_call" | custom-call | tf_op jit(solution)/shard_map/pallas_call | solution.py:98
  56.1 0.0 copy-start
  56.1 1.3 %copy-done = bf16[4,512,512]{2,1,0:T(8,128)(2,1)} copy-done((bf16[4,512,512]{2,1,0:T(8,128)(2,1)}, bf16[4,512,512]{2,1,0:T(8,128)(2,1)S(1)}, u32[]{:S(2)}) %copy-start) | copy-done | bytes 2097176
  57.5 0.0 copy-start.1
  57.5 1.3 %copy-done.1 = bf16[4,512,512]{2,1,0:T(8,128)(2,1)} copy-done((bf16[4,512,512]{2,1,0:T(8,128)(2,1)}, bf16[4,512,512]{2,1,0:T(8,128)(2,1)S(1)}, u32[]{:S(2)}) %copy-start.1) | copy-done | bytes 2097176
  58.8 7.4 %all-to-all-done = f32[8,32,512]{2,1,0:T(8,128)} async-done(((f32[8,32,512]{2,1,0:T(8,128)}), f32[8,32,512]{2,1,0:T(8,128)}, u32[]{:S(2)}, u32[]{:S(2)}) %all-to-all-start) | async-done | bytes 524320 | tf_op jit(solution)/shard_map/all_to_all | solution.py:20
  66.1 1.1 %reduce_sum.9 = f32[32,512]{1,0:T(8,128)S(1)} reduce(f32[8,32,512]{2,1,0:T(8,128)} %all-to-all-done, f32[]{:T(128)} %constant.46.clone.1), dimensions={0}, to_apply=%region_0.1 | reduce | flops 114688 | bytes 589828 | tf_op jit(solution)/shard_map/reduce_sum | solution.py:20
  67.2 0.0 copy-done.4
  67.3 1.5 %shard_map.59.refs_1_ = f32[32,512]{1,0:T(8,128)S(1)} custom-call(s32[1]{0:T(128)} %bitcast.place, f32[32,512]{1,0:T(8,128)S(1)} %bitcast_subtract_fusion.refs_0_, f32[32,512]{1,0:T(8,128)S(1)} %broadcast_in_dim.3.refs_1_, bf16[4,512,512]{2,1,0:T(8,128)(2,1)} %copy-done, bf16[4,512,512]{2,1,0:T(8,128)(2,1)} %copy-done.1), custom_call_target="tpu_custom_call" | custom-call | tf_op jit(solution)/shard_map/pallas_call | solution.py:126
  68.7 1.6 %collective-permute-start.7 = (f32[32,512]{1,0:T(8,128)S(1)}, f32[32,512]{1,0:T(8,128)S(1)}, u32[]{:S(2)}, u32[]{:S(2)}) collective-permute-start(f32[32,512]{1,0:T(8,128)S(1)} %shard_map.59.refs_1_), channel_id=1, source_target_pairs={{0,64},{64,128},{128,192},{192,0},{1,65},{65,129},{129,193},{193,1... | collective-permute-start | bytes 196616 | tf_op jit(solution)/shard_map/ppermute | solution.py:16
  70.4 1.7 %collective-permute-start.10 = (f32[32,512]{1,0:T(8,128)S(1)}, f32[32,512]{1,0:T(8,128)S(1)}, u32[]{:S(2)}, u32[]{:S(2)}) collective-permute-start(f32[32,512]{1,0:T(8,128)S(1)} %shard_map.59.refs_1_), channel_id=1, source_target_pairs={{0,192},{64,0},{128,64},{192,128},{1,193},{65,1},{129,65},{193,129... | collective-permute-start | bytes 196616 | tf_op jit(solution)/shard_map/ppermute | solution.py:16
  72.1 1.9 %collective-permute-start.9 = (f32[32,512]{1,0:T(8,128)S(1)}, f32[32,512]{1,0:T(8,128)S(1)}, u32[]{:S(2)}, u32[]{:S(2)}) collective-permute-start(f32[32,512]{1,0:T(8,128)S(1)} %shard_map.59.refs_1_), channel_id=1, source_target_pairs={{0,128},{64,192},{128,0},{192,64},{1,129},{65,193},{129,1},{193,65... | collective-permute-start | bytes 196616 | tf_op jit(solution)/shard_map/ppermute | solution.py:16
  74.0 1.0 %collective-permute-done.7.refs_0_ = f32[32,512]{1,0:T(8,128)S(1)} collective-permute-done((f32[32,512]{1,0:T(8,128)S(1)}, f32[32,512]{1,0:T(8,128)S(1)}, u32[]{:S(2)}, u32[]{:S(2)}) %collective-permute-start.7) | collective-permute-done | bytes 65568 | tf_op jit(solution)/shard_map/ppermute | solution.py:16
  75.0 1.5 %shard_map.60.refs_2_ = f32[32,512]{1,0:T(8,128)S(1)} custom-call(s32[1]{0:T(128)} %bitcast.place, f32[32,512]{1,0:T(8,128)S(1)} %collective-permute-done.7.refs_0_, f32[32,512]{1,0:T(8,128)S(1)} %shard_map.59.refs_1_, bf16[4,512,512]{2,1,0:T(8,128)(2,1)} %copy-done, bf16[4,512,512]{2,1,0:T(8,128)(2,1)} %copy-done.1), custom_call_target="tpu_custom_call" | custom-call | tf_op jit(solution)/shard_map/pallas_call | solution.py:126
  76.5 0.0 collective-permute-start.8
  76.6 2.9 %collective-permute-start.12 = (f32[32,512]{1,0:T(8,128)S(1)}, f32[32,512]{1,0:T(8,128)S(1)}, u32[]{:S(2)}, u32[]{:S(2)}) collective-permute-start(f32[32,512]{1,0:T(8,128)S(1)} %shard_map.60.refs_2_), channel_id=1, source_target_pairs={{0,128},{64,192},{128,0},{192,64},{1,129},{65,193},{129,1},{193,65... | collective-permute-start | bytes 196616 | tf_op jit(solution)/shard_map/ppermute | solution.py:16
  79.5 0.0 collective-permute-done.10.refs_1_
  79.5 0.0 collective-permute-done.9.refs_0_
  79.5 1.5 %shard_map.61.refs_1_ = f32[32,512]{1,0:T(8,128)S(1)} custom-call(s32[1]{0:T(128)} %bitcast.place, f32[32,512]{1,0:T(8,128)S(1)} %collective-permute-done.9.refs_0_, f32[32,512]{1,0:T(8,128)S(1)} %collective-permute-done.10.refs_1_, f32[32,512]{1,0:T(8,128)S(1)} %shard_map.60.refs_2_, bf16[4,512,512]{2,1,0:T(8,128)(2,1)} %copy-done, ...), custom_call_target="tpu_custom_call" | custom-call | tf_op jit(solution)/shard_map/pallas_call | solution.py:126
  81.0 1.9 %collective-permute-done.8.refs_0_ = f32[32,512]{1,0:T(8,128)S(1)} collective-permute-done((f32[32,512]{1,0:T(8,128)S(1)}, f32[32,512]{1,0:T(8,128)S(1)}, u32[]{:S(2)}, u32[]{:S(2)}) %collective-permute-start.8) | collective-permute-done | bytes 65568 | tf_op jit(solution)/shard_map/ppermute | solution.py:16
  82.9 1.5 %shard_map.62.refs_1_ = f32[32,512]{1,0:T(8,128)S(1)} custom-call(s32[1]{0:T(128)} %bitcast.place, f32[32,512]{1,0:T(8,128)S(1)} %collective-permute-done.8.refs_0_, f32[32,512]{1,0:T(8,128)S(1)} %shard_map.61.refs_1_, bf16[4,512,512]{2,1,0:T(8,128)(2,1)} %copy-done, bf16[4,512,512]{2,1,0:T(8,128)(2,1)} %copy-done.1), custom_call_target="tpu_custom_call" | custom-call | tf_op jit(solution)/shard_map/pallas_call | solution.py:126
  84.4 0.0 collective-permute-start.11
  84.4 0.0 collective-permute-done.12.refs_0_
  84.4 1.5 %shard_map.63.refs_1_ = f32[32,512]{1,0:T(8,128)S(1)} custom-call(s32[1]{0:T(128)} %bitcast.place, f32[32,512]{1,0:T(8,128)S(1)} %collective-permute-done.12.refs_0_, f32[32,512]{1,0:T(8,128)S(1)} %shard_map.62.refs_1_, bf16[4,512,512]{2,1,0:T(8,128)(2,1)} %copy-done, bf16[4,512,512]{2,1,0:T(8,128)(2,1)} %copy-done.1), custom_call_target="tpu_custom_call" | custom-call | tf_op jit(solution)/shard_map/pallas_call | solution.py:126
  85.9 4.0 %collective-permute-done.11.refs_0_ = f32[32,512]{1,0:T(8,128)S(1)} collective-permute-done((f32[32,512]{1,0:T(8,128)S(1)}, f32[32,512]{1,0:T(8,128)S(1)}, u32[]{:S(2)}, u32[]{:S(2)}) %collective-permute-start.11) | collective-permute-done | bytes 65568 | tf_op jit(solution)/shard_map/ppermute | solution.py:16
  89.9 2.1 %shard_map.64 = f32[32,512]{1,0:T(8,128)} custom-call(s32[1]{0:T(128)} %bitcast.place, f32[32,512]{1,0:T(8,128)S(1)} %collective-permute-done.11.refs_0_, f32[32,512]{1,0:T(8,128)S(1)} %shard_map.63.refs_1_, bf16[4,512,512]{2,1,0:T(8,128)(2,1)} %copy-done, bf16[4,512,512]{2,1,0:T(8,128)(2,1)} %copy-done.1), custom_call_target="tpu_custom_call" | custom-call | tf_op jit(solution)/shard_map/pallas_call | solution.py:126
  (9 shorter events, 0.2 us)
Async XLA Ops:
  9.5 11.0 %collective-permute-start.2 = (f32[2,8,32,512]{3,2,1,0:T(8,128)S(1)}, f32[2,8,32,512]{3,2,1,0:T(8,128)S(1)}, u32[]{:S(2)}, u32[]{:S(2)}) collective-permute-start(f32[2,8,32,512]{3,2,1,0:T(8,128)S(1)} %get-tuple-element.31), channel_id=1, source_target_pairs={{0,1},{1,0},{2,3},{3,2},{4,5},{5,4},{6,7},{7,6},{8,9},{9,8},{10,11... | collective-permute-start | bytes 3145736 | tf_op jit(solution)/shard_map/ppermute | solution.py:16
  9.6 3.4 %collective-permute-start = (f32[1,8,32,512]{3,2,1,0:T(8,128)S(1)}, f32[1,8,32,512]{3,2,1,0:T(8,128)S(1)}, u32[]{:S(2)}, u32[]{:S(2)}) collective-permute-start(f32[1,8,32,512]{3,2,1,0:T(8,128)S(1)} %get-tuple-element.25), channel_id=1, source_target_pairs={{0,1},{1,0},{2,3},{3,2},{4,5},{5,4},{6,7},{7,6},{8,9},{9,8},{10,11... | collective-permute-start | bytes 1572872 | tf_op jit(solution)/shard_map/ppermute | solution.py:16
  13.1 9.6 %collective-permute-start.3 = (f32[4,32,512]{2,1,0:T(8,128)S(1)}, f32[4,32,512]{2,1,0:T(8,128)S(1)}, u32[]{:S(2)}, u32[]{:S(2)}) collective-permute-start(f32[4,32,512]{2,1,0:T(8,128)S(1)} %get-tuple-element.37), channel_id=1, source_target_pairs={{0,16},{16,32},{32,48},{48,0},{1,17},{17,33},{33,49},{49,1},{2,18}... | collective-permute-start | bytes 786440 | tf_op jit(solution)/shard_map/ppermute | solution.py:16
  18.6 11.9 %collective-permute-start.1 = (f32[1,8,32,512]{3,2,1,0:T(8,128)S(1)}, f32[1,8,32,512]{3,2,1,0:T(8,128)S(1)}, u32[]{:S(2)}, u32[]{:S(2)}) collective-permute-start(f32[1,8,32,512]{3,2,1,0:T(8,128)S(1)} %get-tuple-element.29), channel_id=1, source_target_pairs={{0,1},{1,0},{2,3},{3,2},{4,5},{5,4},{6,7},{7,6},{8,9},{9,8},{10,11... | collective-permute-start | bytes 1572872 | tf_op jit(solution)/shard_map/ppermute | solution.py:16
  18.7 8.7 %collective-permute-start.5 = (f32[4,32,512]{2,1,0:T(8,128)S(1)}, f32[4,32,512]{2,1,0:T(8,128)S(1)}, u32[]{:S(2)}, u32[]{:S(2)}) collective-permute-start(f32[4,32,512]{2,1,0:T(8,128)S(1)} %get-tuple-element.38), channel_id=1, source_target_pairs={{0,48},{16,0},{32,16},{48,32},{1,49},{17,1},{33,17},{49,33},{2,50}... | collective-permute-start | bytes 786440 | tf_op jit(solution)/shard_map/ppermute | solution.py:16
  22.8 14.4 %collective-permute-start.4 = (f32[8,32,512]{2,1,0:T(8,128)S(1)}, f32[8,32,512]{2,1,0:T(8,128)S(1)}, u32[]{:S(2)}, u32[]{:S(2)}) collective-permute-start(f32[8,32,512]{2,1,0:T(8,128)S(1)} %pad_maximum_fusion), channel_id=1, source_target_pairs={{0,16},{16,32},{32,48},{48,0},{1,17},{17,33},{33,49},{49,1},{2,18}... | collective-permute-start | bytes 1572872 | tf_op jit(solution)/shard_map/ppermute | solution.py:16
  27.5 23.6 %copy-start.2 = (f32[512,1536]{1,0:T(8,128)S(1)}, f32[512,1536]{1,0:T(8,128)}, u32[]{:S(2)}) copy-start(f32[512,1536]{1,0:T(8,128)} %coupling.1) | copy-start | bytes 9437188
  27.5 14.0 %collective-permute-start.6 = (f32[8,32,512]{2,1,0:T(8,128)S(1)}, f32[8,32,512]{2,1,0:T(8,128)S(1)}, u32[]{:S(2)}, u32[]{:S(2)}) collective-permute-start(f32[8,32,512]{2,1,0:T(8,128)S(1)} %pad_maximum_fusion.1), channel_id=1, source_target_pairs={{0,48},{16,0},{32,16},{48,32},{1,49},{17,1},{33,17},{49,33},{2,50}... | collective-permute-start | bytes 1572872 | tf_op jit(solution)/shard_map/ppermute | solution.py:16
  42.5 23.6 %all-to-all-start = ((f32[8,32,512]{2,1,0:T(8,128)}), f32[8,32,512]{2,1,0:T(8,128)}, u32[]{:S(2)}, u32[]{:S(2)}) async-start(f32[8,32,512]{2,1,0:T(8,128)} %fusion), calls=%async_computation | async-start | bytes 1048576 | tf_op jit(solution)/shard_map/all_to_all | solution.py:20
  51.1 1.2 %copy-start.3 = (f32[512,512]{1,0:T(8,128)S(1)}, f32[512,512]{1,0:T(8,128)}, u32[]{:S(2)}) copy-start(f32[512,512]{1,0:T(8,128)} %diag.1) | copy-start | bytes 3145732
  52.3 14.9 %copy-start.4 = (f32[512,32]{0,1:T(8,128)S(1)}, f32[512,32]{0,1:T(8,128)}, u32[]{:S(2)}) copy-start(f32[512,32]{0,1:T(8,128)} %param.5) | copy-start | bytes 196612
  56.1 1.3 %copy-start = (bf16[4,512,512]{2,1,0:T(8,128)(2,1)}, bf16[4,512,512]{2,1,0:T(8,128)(2,1)S(1)}, u32[]{:S(2)}) copy-start(bf16[4,512,512]{2,1,0:T(8,128)(2,1)S(1)} %get-tuple-element.33.refs_2_.refs_3_) | copy-start | bytes 6291460
  57.5 1.3 %copy-start.1 = (bf16[4,512,512]{2,1,0:T(8,128)(2,1)}, bf16[4,512,512]{2,1,0:T(8,128)(2,1)S(1)}, u32[]{:S(2)}) copy-start(bf16[4,512,512]{2,1,0:T(8,128)(2,1)S(1)} %get-tuple-element.34.refs_3_.refs_4_) | copy-start | bytes 6291460
  68.7 6.3 %collective-permute-start.7 = (f32[32,512]{1,0:T(8,128)S(1)}, f32[32,512]{1,0:T(8,128)S(1)}, u32[]{:S(2)}, u32[]{:S(2)}) collective-permute-start(f32[32,512]{1,0:T(8,128)S(1)} %shard_map.59.refs_1_), channel_id=1, source_target_pairs={{0,64},{64,128},{128,192},{192,0},{1,65},{65,129},{129,193},{193,1... | collective-permute-start | bytes 196616 | tf_op jit(solution)/shard_map/ppermute | solution.py:16
  70.4 9.1 %collective-permute-start.10 = (f32[32,512]{1,0:T(8,128)S(1)}, f32[32,512]{1,0:T(8,128)S(1)}, u32[]{:S(2)}, u32[]{:S(2)}) collective-permute-start(f32[32,512]{1,0:T(8,128)S(1)} %shard_map.59.refs_1_), channel_id=1, source_target_pairs={{0,192},{64,0},{128,64},{192,128},{1,193},{65,1},{129,65},{193,129... | collective-permute-start | bytes 196616 | tf_op jit(solution)/shard_map/ppermute | solution.py:16
  72.1 7.4 %collective-permute-start.9 = (f32[32,512]{1,0:T(8,128)S(1)}, f32[32,512]{1,0:T(8,128)S(1)}, u32[]{:S(2)}, u32[]{:S(2)}) collective-permute-start(f32[32,512]{1,0:T(8,128)S(1)} %shard_map.59.refs_1_), channel_id=1, source_target_pairs={{0,128},{64,192},{128,0},{192,64},{1,129},{65,193},{129,1},{193,65... | collective-permute-start | bytes 196616 | tf_op jit(solution)/shard_map/ppermute | solution.py:16
  76.5 6.4 %collective-permute-start.8 = (f32[32,512]{1,0:T(8,128)S(1)}, f32[32,512]{1,0:T(8,128)S(1)}, u32[]{:S(2)}, u32[]{:S(2)}) collective-permute-start(f32[32,512]{1,0:T(8,128)S(1)} %shard_map.60.refs_2_), channel_id=1, source_target_pairs={{0,64},{64,128},{128,192},{192,0},{1,65},{65,129},{129,193},{193,1... | collective-permute-start | bytes 196616 | tf_op jit(solution)/shard_map/ppermute | solution.py:16
  76.6 7.8 %collective-permute-start.12 = (f32[32,512]{1,0:T(8,128)S(1)}, f32[32,512]{1,0:T(8,128)S(1)}, u32[]{:S(2)}, u32[]{:S(2)}) collective-permute-start(f32[32,512]{1,0:T(8,128)S(1)} %shard_map.60.refs_2_), channel_id=1, source_target_pairs={{0,128},{64,192},{128,0},{192,64},{1,129},{65,193},{129,1},{193,65... | collective-permute-start | bytes 196616 | tf_op jit(solution)/shard_map/ppermute | solution.py:16
  84.4 5.5 %collective-permute-start.11 = (f32[32,512]{1,0:T(8,128)S(1)}, f32[32,512]{1,0:T(8,128)S(1)}, u32[]{:S(2)}, u32[]{:S(2)}) collective-permute-start(f32[32,512]{1,0:T(8,128)S(1)} %shard_map.62.refs_1_), channel_id=1, source_target_pairs={{0,64},{64,128},{128,192},{192,0},{1,65},{65,129},{129,193},{193,1... | collective-permute-start | bytes 196616 | tf_op jit(solution)/shard_map/ppermute | solution.py:16

commit v4 on v3

--- a/solution.py
+++ b/solution.py
@@ -16,10 +16,6 @@
     return lax.ppermute(value, axis, [(i, (i + by) % peers) for i in range(peers)])
 
 
-def summed_at_owner(blocks, axis):
-    return jnp.sum(lax.all_to_all(blocks, axis, 0, 0, tiled=True), axis=0)
-
-
 def in_hbm(value):
     return pltpu.with_memory_space_constraint(value, pltpu.HBM)
 
@@ -47,36 +43,54 @@
     return sorted(range(peers), key=lambda o: (-min(o, peers - o), o))
 
 
-def product_body(n_z, n_core, place, users, factor, own_out, sent_out):
+def product_body(n_z, n_core, place, users, factor, far_own, own, far_sent, sent):
     items, rows = users.shape[1], factor.shape[0]
     share = items // (n_z * n_core)
     total = three_pass(users[...], factor[...], 0, 1).reshape(n_z, n_core, share, rows)
 
-    def keep(mine):
-        own_out[0] = total[:, mine]
-        sent_out[0] = total[:, 1 - mine]
-
-    pl.when(place[0] == 0)(lambda: keep(0))
-    pl.when(place[0] == 1)(lambda: keep(1))
-
-
-def product(place, first, count, users, factor, sizes):
+    def keep(mine, kept, given):
+        for k in range(n_z):
+            ahead = lax.rem(k - place[1] + n_z, n_z)
+            kept[ahead] = total[k, mine]
+            given[ahead] = total[k, 1 - mine]
+
+    for mine in range(2):
+        for first in (True, False):
+            kept, given = (far_own, far_sent) if first else (own.at[0], sent.at[0])
+            chosen = (place[0] == mine) & ((pl.program_id(0) == 0) == first)
+            pl.when(chosen)(functools.partial(keep, mine, kept, given))
+
+
+def product(place, users, factor, sizes):
     n_x, n_z, n_core = sizes
     depth, items = users.shape
     rows = factor.shape[0]
     chunk, share = items // n_x, items // (n_x * n_z * n_core)
+    specs = [
+        pl.BlockSpec((n_z, share, rows), lambda i, s: (0, 0, 0)),
+        pl.BlockSpec((1, n_z, share, rows), lambda i, s: (lax.max(i - 1, 0), 0, 0, 0)),
+    ]
+    shapes = [
+        jax.ShapeDtypeStruct((n_z, share, rows), jnp.float32),
+        jax.ShapeDtypeStruct((n_x - 1, n_z, share, rows), jnp.float32),
+    ]
     return pl.pallas_call(
         functools.partial(product_body, n_z, n_core),
         grid_spec=pltpu.PrefetchScalarGridSpec(
             num_scalar_prefetch=1,
-            grid=(count,),
+            grid=(n_x,),
             in_specs=[
-                pl.BlockSpec((depth, chunk), lambda i, s: (0, s[1 + first + i])),
+                pl.BlockSpec((depth, chunk), lambda i, s: (0, s[2 + i])),
                 pl.BlockSpec((rows, depth), lambda i, s: (0, 0)),
             ],
-            out_specs=[pl.BlockSpec((1, n_z, share, rows), lambda i, s: (i, 0, 0, 0))] * 2,
-        ),
-        out_shape=[jax.ShapeDtypeStruct((count, n_z, share, rows), jnp.float32)] * 2,
+            out_specs=specs * 2,
+        ),
+        out_shape=shapes * 2,
+        cost_estimate=pl.CostEstimate(
+            flops=6 * items * rows * depth,
+            transcendentals=0,
+            bytes_accessed=4 * (items + rows) * depth + 4 * items * rows,
+        ),
         compiler_params=pltpu.CompilerParams(vmem_limit_bytes=24 << 20),
     )(place, users, factor)
 
@@ -104,6 +118,9 @@
         ],
         out_specs=[pl.BlockSpec((1, block, block), lambda i: (i, 0, 0))] * 2,
         out_shape=[shape] * 2,
+        cost_estimate=pl.CostEstimate(
+            flops=6 * (count - 1) * block**3, transcendentals=0, bytes_accessed=8 * count * block**2
+        ),
         compiler_params=pltpu.CompilerParams(vmem_limit_bytes=24 << 20),
     )(diag, coupling)
 
@@ -150,32 +167,46 @@
     return result
 
 
+def reduced_over_z(blocks):
+    share = blocks.shape[1]
+    half = share // 2
+    rows = blocks.reshape(-1, blocks.shape[2])
+    middle = 4 * share + half
+    up = shifted(rows[3 * share : middle], "z", 2)
+    down = shifted(rows[middle : 6 * share], "z", -2)
+    far_up = jnp.concatenate([blocks[2, :half] + up[share:], blocks[2, half:]])
+    far_down = jnp.concatenate([blocks[6, :half], blocks[6, half:] + down[:half]])
+    arrived = [
+        shifted(far_up, "z", 2),
+        shifted(far_down, "z", -2),
+        shifted(blocks[1] + up[:share], "z", 1),
+        shifted(blocks[7] + down[half:], "z", -1),
+    ]
+    return functools.reduce(lambda a, b: a + b, arrived, blocks[0])
+
+
 def on_device(right_side, solved_factor, solved_users, diag_inverse, coupling):
     sizes = tuple(lax.axis_size(a) for a in COL)
-    x, core = lax.axis_index("x"), lax.axis_index("core")
-    place = jnp.stack([core] + [(x + o) % sizes[0] for o in ring_order(sizes[0])]).astype(jnp.int32)
+    x, z, core = (lax.axis_index(a) for a in COL)
+    place = [core, z] + [(x + o) % sizes[0] for o in ring_order(sizes[0])]
+    place = jnp.stack(place).astype(jnp.int32)
     position = lax.axis_index("grp").reshape(1).astype(jnp.int32)
     users, factor = in_hbm(solved_users), in_hbm(solved_factor)
 
-    def part(first, count, place):
-        own, sent = product(place, first, count, users, factor, sizes)
-        place, sent = lax.optimization_barrier((place, sent))
-        return own, shifted(sent, "core", 1), place
-
-    far_own, far_other, place = part(0, 1, place)
-    near_own, near_other, place = part(1, 2, place)
-    far = (far_own + far_other)[0]
-    place, far = lax.optimization_barrier((place, far))
+    far_own, own, far_sent, sent = product(place, users, factor, sizes)
+    far_other = shifted(far_sent, "core", 1)
+    sent, far_other = lax.optimization_barrier((sent, far_other))
+    far = far_own + far_other
+    near = own + shifted(sent, "core", 1)
     cut = far.shape[0] // 2
     up = shifted(far[:cut], "x", 1)
     down = shifted(far[cut:], "x", -1)
-    home_own, home_other, _ = part(3, 1, place)
-    weights = [in_hbm(half) for half in hop_weights(diag_inverse, coupling)]
-    ahead, behind = near_own[0] + near_other[0], near_own[1] + near_other[1]
-    up = shifted(jnp.concatenate([ahead[:cut] + up, ahead[cut:]]), "x", 1)
-    down = shifted(jnp.concatenate([behind[:cut], behind[cut:] + down]), "x", -1)
-    along_z = home_own[0] + home_other[0] + up + down
-    residue = right_side.T - summed_at_owner(along_z, "z")
+    up = shifted(jnp.concatenate([near[0, :cut] + up, near[0, cut:]]), "x", 1)
+    down = shifted(jnp.concatenate([near[1, :cut], near[1, cut:] + down]), "x", -1)
+    weights = hop_weights(diag_inverse, coupling)
+    home, weights = lax.optimization_barrier((near[2], weights))
+    along_z = home + up + down
+    residue = right_side.T - reduced_over_z(along_z)
     return chain(position, residue, weights).T
 
 

time: 93.9 us -> 79.8 us (0.85); the launches traced: 92 us -> 79.3 us
  Pallas kernels: 26.6 us -> 14.7 us
  starting transfers between devices: 24.3 us -> 27.7 us
  local copies, waits for them, and re-layouts: 4.01 us -> 1.83 us
  other arithmetic: 2.55 us -> 0.82 us
    ppermute x13 -> x18, starting transfers between devices: 15.7 us -> 27.7 us  [shifted(): lax.ppermute(value, axis, [(i, (i + by) % peers) for i in range(peers)])]
    all_to_all x1 -> x0, starting transfers between devices: 8.58 us -> none  [summed_at_owner(): return jnp.sum(lax.all_to_all(blocks, axis, 0, 0, tiled=True), axis=0)]
    all_to_all x1 -> x0, waiting for transfers between devices: 7.38 us -> none  [summed_at_owner(): return jnp.sum(lax.all_to_all(blocks, axis, 0, 0, tiled=True), axis=0)]
    pallas_call x6, Pallas kernels: 9.5 us -> 2.29 us  [applied(): pl.pallas_call(functools.partial(apply_body, [group for group, _ in value...]
    ppermute x13 -> x18, waiting for transfers between devices: 27 us -> 34.1 us  [shifted(): lax.ppermute(value, axis, [(i, (i + by) % peers) for i in range(peers)])]
    pallas_call x3 -> x1, Pallas kernels: 13.3 us -> 8.62 us  [product(): pl.pallas_call(functools.partial(product_body, n_z, n_core), grid_spec=pl...]
    unnamed x10, local copies, waits for them, and re-layouts: 3.85 us -> 1.61 us
    reduce_sum x1 -> x0, other arithmetic: 1.08 us -> none  [summed_at_owner(): return jnp.sum(lax.all_to_all(blocks, axis, 0, 0, tiled=True), axis=0)]
  transfers between devices with their start and end apart: 14 -> 18, of which waited for: 9 -> 10; matrix products, arithmetic and copies ran while one was open for 1% -> 1% of each run, Pallas kernels for 15% -> 6%
where the time goes in v4:
time: 79.8 us; the launch traced here: 79.3 us
  waiting for transfers between devices  34.1 us (43%)
  starting transfers between devices  27.7 us (35%)
  Pallas kernels  14.7 us (18%)
  local copies, waits for them, and re-layouts  1.83 us (2%)
  other arithmetic  0.82 us (1%)
    ppermute x18, waiting for transfers between devices, shifted(): lax.ppermute(value, axis, [(i, (i + by) % peers) for i in range(peers)])  34.1 us
    ppermute x18, starting transfers between devices, shifted(): lax.ppermute(value, axis, [(i, (i + by) % peers) for i in range(peers)])  27.7 us
    pallas_call x1, Pallas kernels, product(): pl.pallas_call(functools.partial(product_body, n_z, n_core), grid_spec=pl...  8.62 us
    pallas_call x1, Pallas kernels, hop_weights(): pl.pallas_call(weights_body, grid=(count,), in_specs=[pl.BlockSpec((block...  3.81 us
    pallas_call x6, Pallas kernels, applied(): pl.pallas_call(functools.partial(apply_body, [group for group, _ in value...  2.29 us
    unnamed x10, local copies, waits for them, and re-layouts  1.61 us
  transfers between devices with their start and end apart: 18, of which 10 were waited for; matrix products, arithmetic and copies ran while one was open for 1% of the time, Pallas kernels for 6%

profile of v4, /device:TPU:32, one launch (start us, length us, event | category | flops | bytes accessed | tf_op | source)
XLA Modules:
  0.0 79.3 jit_solution(17710553325858719343)
XLA Ops:
  0.0 0.1 stack.27.place
  0.1 8.6 %shard_map.55 = (f32[8,32,512]{2,1,0:T(8,128)S(1)}, f32[3,8,32,512]{3,2,1,0:T(8,128)S(1)}, f32[8,32,512]{2,1,0:T(8,128)S(1)}, f32[3,8,32,512]{3,2,1,0:T(8,128)S(1)}) custom-call(s32[6]{0:T(128)S(1)} %stack.27.place, f32[768,2048]{1,0:T(8,128)} %users.1, f32[512,768]{1,0:T(8,128)} %factor.1), custom_call_target="tpu_custom_call" | custom-call | flops 4831838208 | bytes 12058624 | tf_op jit(solution)/shard_map/pallas_call | solution.py:77
  8.7 0.1 collective-permute-start
  8.8 1.9 %collective-permute-done = f32[8,32,512]{2,1,0:T(8,128)S(1)} collective-permute-done((f32[8,32,512]{2,1,0:T(8,128)S(1)}, f32[8,32,512]{2,1,0:T(8,128)S(1)}, u32[]{:S(2)}, u32[]{:S(2)}) %collective-permute-start) | collective-permute-done | bytes 524320 | tf_op jit(solution)/shard_map/ppermute | solution.py:16
  10.7 0.1 collective-permute-start.1
  10.8 0.1 add.72
  11.0 1.6 %collective-permute-start.2 = (f32[4,32,512]{2,1,0:T(8,128)S(1)}, f32[4,32,512]{2,1,0:T(8,128)S(1)}, u32[]{:S(2)}, u32[]{:S(2)}) collective-permute-start(f32[4,32,512]{2,1,0:T(8,128)S(1)} %get-tuple-element.39), channel_id=1, source_target_pairs={{0,16},{16,32},{32,48},{48,0},{1,17},{17,33},{33,49},{49,1},{2,18}... | collective-permute-start | bytes 786440 | tf_op jit(solution)/shard_map/ppermute | solution.py:16
  12.6 1.7 %collective-permute-start.4 = (f32[4,32,512]{2,1,0:T(8,128)S(1)}, f32[4,32,512]{2,1,0:T(8,128)S(1)}, u32[]{:S(2)}, u32[]{:S(2)}) collective-permute-start(f32[4,32,512]{2,1,0:T(8,128)S(1)} %get-tuple-element.40), channel_id=1, source_target_pairs={{0,48},{16,0},{32,16},{48,32},{1,49},{17,1},{33,17},{49,33},{2,50}... | collective-permute-start | bytes 786440 | tf_op jit(solution)/shard_map/ppermute | solution.py:16
  14.3 0.0 collective-permute-done.1
  14.3 0.3 add.71
  14.7 0.0 copy-start.3
  14.7 0.0 copy-start.2
  14.7 6.1 %collective-permute-done.2 = f32[4,32,512]{2,1,0:T(8,128)S(1)} collective-permute-done((f32[4,32,512]{2,1,0:T(8,128)S(1)}, f32[4,32,512]{2,1,0:T(8,128)S(1)}, u32[]{:S(2)}, u32[]{:S(2)}) %collective-permute-start.2) | collective-permute-done | bytes 262176 | tf_op jit(solution)/shard_map/ppermute | solution.py:16
  20.8 0.0 collective-permute-done.4
  20.8 0.1 fusion.1
  21.0 1.6 %collective-permute-start.3 = (f32[8,32,512]{2,1,0:T(8,128)S(1)}, f32[8,32,512]{2,1,0:T(8,128)S(1)}, u32[]{:S(2)}, u32[]{:S(2)}) collective-permute-start(f32[8,32,512]{2,1,0:T(8,128)S(1)} %pad_maximum_fusion), channel_id=1, source_target_pairs={{0,16},{16,32},{32,48},{48,0},{1,17},{17,33},{33,49},{49,1},{2,18}... | collective-permute-start | bytes 1572872 | tf_op jit(solution)/shard_map/ppermute | solution.py:16
  22.6 1.8 %collective-permute-start.5 = (f32[8,32,512]{2,1,0:T(8,128)S(1)}, f32[8,32,512]{2,1,0:T(8,128)S(1)}, u32[]{:S(2)}, u32[]{:S(2)}) collective-permute-start(f32[8,32,512]{2,1,0:T(8,128)S(1)} %pad_maximum_fusion.1), channel_id=1, source_target_pairs={{0,48},{16,0},{32,16},{48,32},{1,49},{17,1},{33,17},{49,33},{2,50}... | collective-permute-start | bytes 1572872 | tf_op jit(solution)/shard_map/ppermute | solution.py:16
  24.4 0.0 copy-done.3
  24.4 0.0 copy-done.2
  24.4 3.8 %shard_map.56 = (bf16[4,512,512]{2,1,0:T(8,128)(2,1)S(1)}, bf16[4,512,512]{2,1,0:T(8,128)(2,1)S(1)}) custom-call(f32[512,512]{1,0:T(8,128)S(1)} %copy-done.3, f32[512,1536]{1,0:T(8,128)S(1)} %copy-done.2), custom_call_target="tpu_custom_call" | custom-call | flops 2415919104 | bytes 8388608 | tf_op jit(solution)/shard_map/pallas_call | solution.py:112
  28.2 0.0 copy-start
  28.3 0.0 copy-start.4
  28.3 7.4 %collective-permute-done.3 = f32[8,32,512]{2,1,0:T(8,128)S(1)} collective-permute-done((f32[8,32,512]{2,1,0:T(8,128)S(1)}, f32[8,32,512]{2,1,0:T(8,128)S(1)}, u32[]{:S(2)}, u32[]{:S(2)}) %collective-permute-start.3) | collective-permute-done | bytes 524320 | tf_op jit(solution)/shard_map/ppermute | solution.py:16
  35.7 0.0 collective-permute-done.5
  35.7 0.2 add_add_fusion
  35.8 0.0 copy-done
  35.9 3.3 %collective-permute-start.6 = (f32[48,512]{1,0:T(8,128)S(1)}, f32[48,512]{1,0:T(8,128)S(1)}, u32[]{:S(2)}, u32[]{:S(2)}) collective-permute-start(f32[48,512]{1,0:T(8,128)S(1)} %get-tuple-element.37), channel_id=1, source_target_pairs={{0,4},{2,6},{4,8},{6,10},{8,12},{10,14},{12,0},{14,2},{1,5},{3,7},... | collective-permute-start | bytes 294920 | tf_op jit(solution)/shard_map/ppermute | solution.py:16
  39.2 2.2 %collective-permute-start.8 = (f32[48,512]{1,0:T(8,128)S(1)}, f32[48,512]{1,0:T(8,128)S(1)}, u32[]{:S(2)}, u32[]{:S(2)}) collective-permute-start(f32[48,512]{1,0:T(8,128)S(1)} %get-tuple-element.38), channel_id=1, source_target_pairs={{0,12},{2,14},{4,0},{6,2},{8,4},{10,6},{12,8},{14,10},{1,13},{3,15... | collective-permute-start | bytes 294920 | tf_op jit(solution)/shard_map/ppermute | solution.py:16
  41.4 3.6 %collective-permute-done.6 = f32[48,512]{1,0:T(8,128)S(1)} collective-permute-done((f32[48,512]{1,0:T(8,128)S(1)}, f32[48,512]{1,0:T(8,128)S(1)}, u32[]{:S(2)}, u32[]{:S(2)}) %collective-permute-start.6) | collective-permute-done | bytes 98336 | tf_op jit(solution)/shard_map/ppermute | solution.py:16
  45.1 0.9 %collective-permute-done.8 = f32[48,512]{1,0:T(8,128)S(1)} collective-permute-done((f32[48,512]{1,0:T(8,128)S(1)}, f32[48,512]{1,0:T(8,128)S(1)}, u32[]{:S(2)}, u32[]{:S(2)}) %collective-permute-start.8) | collective-permute-done | bytes 98336 | tf_op jit(solution)/shard_map/ppermute | solution.py:16
  46.0 4.2 %collective-permute-start.7 = (f32[32,512]{1,0:T(8,128)S(1)}, f32[32,512]{1,0:T(8,128)S(1)}, u32[]{:S(2)}, u32[]{:S(2)}) collective-permute-start(f32[32,512]{1,0:T(8,128)S(1)} %pad_maximum_fusion.2), channel_id=1, source_target_pairs={{0,4},{2,6},{4,8},{6,10},{8,12},{10,14},{12,0},{14,2},{1,5},{3,7},... | collective-permute-start | bytes 196616 | tf_op jit(solution)/shard_map/ppermute | solution.py:16
  50.1 0.1 collective-permute-start.9
  50.2 3.1 %collective-permute-start.10 = (f32[32,512]{1,0:T(8,128)S(1)}, f32[32,512]{1,0:T(8,128)S(1)}, u32[]{:S(2)}, u32[]{:S(2)}) collective-permute-start(f32[32,512]{1,0:T(8,128)S(1)} %get-tuple-element.35), channel_id=1, source_target_pairs={{0,2},{2,4},{4,6},{6,8},{8,10},{10,12},{12,14},{14,0},{1,3},{3,5},... | collective-permute-start | bytes 196616 | tf_op jit(solution)/shard_map/ppermute | solution.py:16
  53.3 0.0 collective-permute-start.11
  53.3 0.0 collective-permute-done.7
  53.3 2.1 %collective-permute-done.9 = f32[32,512]{1,0:T(8,128)S(1)} collective-permute-done((f32[32,512]{1,0:T(8,128)S(1)}, f32[32,512]{1,0:T(8,128)S(1)}, u32[]{:S(2)}, u32[]{:S(2)}) %collective-permute-start.9) | collective-permute-done | bytes 65568 | tf_op jit(solution)/shard_map/ppermute | solution.py:16
  55.3 0.0 collective-permute-done.10
  55.4 2.2 %collective-permute-done.11 = f32[32,512]{1,0:T(8,128)S(1)} collective-permute-done((f32[32,512]{1,0:T(8,128)S(1)}, f32[32,512]{1,0:T(8,128)S(1)}, u32[]{:S(2)}, u32[]{:S(2)}) %collective-permute-start.11) | collective-permute-done | bytes 65568 | tf_op jit(solution)/shard_map/ppermute | solution.py:16
  57.5 0.0 copy-done.4
  57.6 0.0 copy-start.1
  57.6 1.6 %copy-done.1 = bf16[4,512,512]{2,1,0:T(8,128)(2,1)S(1)} copy-done((bf16[4,512,512]{2,1,0:T(8,128)(2,1)S(1)}, bf16[4,512,512]{2,1,0:T(8,128)(2,1)}, u32[]{:S(2)}) %copy-start.1) | copy-done | bytes 2097176
  59.2 0.3 shard_map.57.refs_1_
  59.4 1.6 %collective-permute-start.12 = (f32[32,512]{1,0:T(8,128)S(1)}, f32[32,512]{1,0:T(8,128)S(1)}, u32[]{:S(2)}, u32[]{:S(2)}) collective-permute-start(f32[32,512]{1,0:T(8,128)S(1)} %shard_map.57.refs_1_), channel_id=1, source_target_pairs={{0,64},{64,128},{128,192},{192,0},{1,65},{65,129},{129,193},{193,1... | collective-permute-start | bytes 196616 | tf_op jit(solution)/shard_map/ppermute | solution.py:16
  61.0 2.9 %collective-permute-start.14 = (f32[32,512]{1,0:T(8,128)S(1)}, f32[32,512]{1,0:T(8,128)S(1)}, u32[]{:S(2)}, u32[]{:S(2)}) collective-permute-start(f32[32,512]{1,0:T(8,128)S(1)} %shard_map.57.refs_1_), channel_id=1, source_target_pairs={{0,128},{64,192},{128,0},{192,64},{1,129},{65,193},{129,1},{193,65... | collective-permute-start | bytes 196616 | tf_op jit(solution)/shard_map/ppermute | solution.py:16
  63.9 1.3 %collective-permute-start.15 = (f32[32,512]{1,0:T(8,128)S(1)}, f32[32,512]{1,0:T(8,128)S(1)}, u32[]{:S(2)}, u32[]{:S(2)}) collective-permute-start(f32[32,512]{1,0:T(8,128)S(1)} %shard_map.57.refs_1_), channel_id=1, source_target_pairs={{0,192},{64,0},{128,64},{192,128},{1,193},{65,1},{129,65},{193,129... | collective-permute-start | bytes 196616 | tf_op jit(solution)/shard_map/ppermute | solution.py:16
  65.3 0.9 %collective-permute-done.12.refs_0_ = f32[32,512]{1,0:T(8,128)S(1)} collective-permute-done((f32[32,512]{1,0:T(8,128)S(1)}, f32[32,512]{1,0:T(8,128)S(1)}, u32[]{:S(2)}, u32[]{:S(2)}) %collective-permute-start.12) | collective-permute-done | bytes 65568 | tf_op jit(solution)/shard_map/ppermute | solution.py:16
  66.2 0.3 shard_map.58.refs_2_
  66.4 0.0 collective-permute-start.13
  66.5 2.0 %collective-permute-start.17 = (f32[32,512]{1,0:T(8,128)S(1)}, f32[32,512]{1,0:T(8,128)S(1)}, u32[]{:S(2)}, u32[]{:S(2)}) collective-permute-start(f32[32,512]{1,0:T(8,128)S(1)} %shard_map.58.refs_2_), channel_id=1, source_target_pairs={{0,128},{64,192},{128,0},{192,64},{1,129},{65,193},{129,1},{193,65... | collective-permute-start | bytes 196616 | tf_op jit(solution)/shard_map/ppermute | solution.py:16
  68.5 0.0 collective-permute-done.14.refs_0_
  68.5 0.0 collective-permute-done.15.refs_1_
  68.5 0.3 shard_map.59.refs_1_
  68.8 3.9 %collective-permute-done.13.refs_0_ = f32[32,512]{1,0:T(8,128)S(1)} collective-permute-done((f32[32,512]{1,0:T(8,128)S(1)}, f32[32,512]{1,0:T(8,128)S(1)}, u32[]{:S(2)}, u32[]{:S(2)}) %collective-permute-start.13) | collective-permute-done | bytes 65568 | tf_op jit(solution)/shard_map/ppermute | solution.py:16
  72.6 0.3 shard_map.60.refs_1_
  72.9 0.0 collective-permute-start.16
  72.9 0.0 collective-permute-done.17.refs_0_
  72.9 0.3 shard_map.61.refs_1_
  73.2 5.2 %collective-permute-done.16.refs_0_ = f32[32,512]{1,0:T(8,128)S(1)} collective-permute-done((f32[32,512]{1,0:T(8,128)S(1)}, f32[32,512]{1,0:T(8,128)S(1)}, u32[]{:S(2)}, u32[]{:S(2)}) %collective-permute-start.16) | collective-permute-done | bytes 65568 | tf_op jit(solution)/shard_map/ppermute | solution.py:16
  78.4 0.9 %shard_map.62 = f32[32,512]{1,0:T(8,128)} custom-call(s32[1]{0:T(128)} %bitcast.place, f32[32,512]{1,0:T(8,128)S(1)} %collective-permute-done.16.refs_0_, f32[32,512]{1,0:T(8,128)S(1)} %shard_map.61.refs_1_, bf16[4,512,512]{2,1,0:T(8,128)(2,1)S(1)} %get-tuple-element.25.refs_2_.refs_3_, bf16[4,512,512]{2,1,0:T(8,128)(2,1)S(1)} %copy-done.1), custom_call_target="tpu_custom_call" | custom-call | tf_op jit(solution)/shard_map/pallas_call | solution.py:143
  (13 shorter events, 0.3 us)
Async XLA Ops:
  8.7 2.0 %collective-permute-start = (f32[8,32,512]{2,1,0:T(8,128)S(1)}, f32[8,32,512]{2,1,0:T(8,128)S(1)}, u32[]{:S(2)}, u32[]{:S(2)}) collective-permute-start(f32[8,32,512]{2,1,0:T(8,128)S(1)} %get-tuple-element.18), channel_id=1, source_target_pairs={{0,1},{1,0},{2,3},{3,2},{4,5},{5,4},{6,7},{7,6},{8,9},{9,8},{10,11... | collective-permute-start | bytes 1572872 | tf_op jit(solution)/shard_map/ppermute | solution.py:16
  10.7 3.6 %collective-permute-start.1 = (f32[3,8,32,512]{3,2,1,0:T(8,128)S(1)}, f32[3,8,32,512]{3,2,1,0:T(8,128)S(1)}, u32[]{:S(2)}, u32[]{:S(2)}) collective-permute-start(f32[3,8,32,512]{3,2,1,0:T(8,128)S(1)} %get-tuple-element.19), channel_id=1, source_target_pairs={{0,1},{1,0},{2,3},{3,2},{4,5},{5,4},{6,7},{7,6},{8,9},{9,8},{10,11... | collective-permute-start | bytes 4718600 | tf_op jit(solution)/shard_map/ppermute | solution.py:16
  11.0 9.9 %collective-permute-start.2 = (f32[4,32,512]{2,1,0:T(8,128)S(1)}, f32[4,32,512]{2,1,0:T(8,128)S(1)}, u32[]{:S(2)}, u32[]{:S(2)}) collective-permute-start(f32[4,32,512]{2,1,0:T(8,128)S(1)} %get-tuple-element.39), channel_id=1, source_target_pairs={{0,16},{16,32},{32,48},{48,0},{1,17},{17,33},{33,49},{49,1},{2,18}... | collective-permute-start | bytes 786440 | tf_op jit(solution)/shard_map/ppermute | solution.py:16
  12.6 8.3 %collective-permute-start.4 = (f32[4,32,512]{2,1,0:T(8,128)S(1)}, f32[4,32,512]{2,1,0:T(8,128)S(1)}, u32[]{:S(2)}, u32[]{:S(2)}) collective-permute-start(f32[4,32,512]{2,1,0:T(8,128)S(1)} %get-tuple-element.40), channel_id=1, source_target_pairs={{0,48},{16,0},{32,16},{48,32},{1,49},{17,1},{33,17},{49,33},{2,50}... | collective-permute-start | bytes 786440 | tf_op jit(solution)/shard_map/ppermute | solution.py:16
  14.7 9.8 %copy-start.3 = (f32[512,512]{1,0:T(8,128)S(1)}, f32[512,512]{1,0:T(8,128)}, u32[]{:S(2)}) copy-start(f32[512,512]{1,0:T(8,128)} %diag.1) | copy-start | bytes 3145732
  14.7 9.7 %copy-start.2 = (f32[512,1536]{1,0:T(8,128)S(1)}, f32[512,1536]{1,0:T(8,128)}, u32[]{:S(2)}) copy-start(f32[512,1536]{1,0:T(8,128)} %coupling.1) | copy-start | bytes 9437188
  21.0 14.7 %collective-permute-start.3 = (f32[8,32,512]{2,1,0:T(8,128)S(1)}, f32[8,32,512]{2,1,0:T(8,128)S(1)}, u32[]{:S(2)}, u32[]{:S(2)}) collective-permute-start(f32[8,32,512]{2,1,0:T(8,128)S(1)} %pad_maximum_fusion), channel_id=1, source_target_pairs={{0,16},{16,32},{32,48},{48,0},{1,17},{17,33},{33,49},{49,1},{2,18}... | collective-permute-start | bytes 1572872 | tf_op jit(solution)/shard_map/ppermute | solution.py:16
  22.6 13.1 %collective-permute-start.5 = (f32[8,32,512]{2,1,0:T(8,128)S(1)}, f32[8,32,512]{2,1,0:T(8,128)S(1)}, u32[]{:S(2)}, u32[]{:S(2)}) collective-permute-start(f32[8,32,512]{2,1,0:T(8,128)S(1)} %pad_maximum_fusion.1), channel_id=1, source_target_pairs={{0,48},{16,0},{32,16},{48,32},{1,49},{17,1},{33,17},{49,33},{2,50}... | collective-permute-start | bytes 1572872 | tf_op jit(solution)/shard_map/ppermute | solution.py:16
  28.2 7.6 %copy-start = (bf16[4,512,512]{2,1,0:T(8,128)(2,1)}, bf16[4,512,512]{2,1,0:T(8,128)(2,1)S(1)}, u32[]{:S(2)}) copy-start(bf16[4,512,512]{2,1,0:T(8,128)(2,1)S(1)} %get-tuple-element.26.refs_3_.refs_4_) | copy-start | bytes 6291460
  28.3 29.2 %copy-start.4 = (f32[512,32]{0,1:T(8,128)S(1)}, f32[512,32]{0,1:T(8,128)}, u32[]{:S(2)}) copy-start(f32[512,32]{0,1:T(8,128)} %param.5) | copy-start | bytes 196612
  35.9 9.2 %collective-permute-start.6 = (f32[48,512]{1,0:T(8,128)S(1)}, f32[48,512]{1,0:T(8,128)S(1)}, u32[]{:S(2)}, u32[]{:S(2)}) collective-permute-start(f32[48,512]{1,0:T(8,128)S(1)} %get-tuple-element.37), channel_id=1, source_target_pairs={{0,4},{2,6},{4,8},{6,10},{8,12},{10,14},{12,0},{14,2},{1,5},{3,7},... | collective-permute-start | bytes 294920 | tf_op jit(solution)/shard_map/ppermute | solution.py:16
  39.2 6.7 %collective-permute-start.8 = (f32[48,512]{1,0:T(8,128)S(1)}, f32[48,512]{1,0:T(8,128)S(1)}, u32[]{:S(2)}, u32[]{:S(2)}) collective-permute-start(f32[48,512]{1,0:T(8,128)S(1)} %get-tuple-element.38), channel_id=1, source_target_pairs={{0,12},{2,14},{4,0},{6,2},{8,4},{10,6},{12,8},{14,10},{1,13},{3,15... | collective-permute-start | bytes 294920 | tf_op jit(solution)/shard_map/ppermute | solution.py:16
  46.0 7.3 %collective-permute-start.7 = (f32[32,512]{1,0:T(8,128)S(1)}, f32[32,512]{1,0:T(8,128)S(1)}, u32[]{:S(2)}, u32[]{:S(2)}) collective-permute-start(f32[32,512]{1,0:T(8,128)S(1)} %pad_maximum_fusion.2), channel_id=1, source_target_pairs={{0,4},{2,6},{4,8},{6,10},{8,12},{10,14},{12,0},{14,2},{1,5},{3,7},... | collective-permute-start | bytes 196616 | tf_op jit(solution)/shard_map/ppermute | solution.py:16
  50.1 5.2 %collective-permute-start.9 = (f32[32,512]{1,0:T(8,128)S(1)}, f32[32,512]{1,0:T(8,128)S(1)}, u32[]{:S(2)}, u32[]{:S(2)}) collective-permute-start(f32[32,512]{1,0:T(8,128)S(1)} %pad_maximum_fusion.3), channel_id=1, source_target_pairs={{0,12},{2,14},{4,0},{6,2},{8,4},{10,6},{12,8},{14,10},{1,13},{3,15... | collective-permute-start | bytes 196616 | tf_op jit(solution)/shard_map/ppermute | solution.py:16
  50.2 5.2 %collective-permute-start.10 = (f32[32,512]{1,0:T(8,128)S(1)}, f32[32,512]{1,0:T(8,128)S(1)}, u32[]{:S(2)}, u32[]{:S(2)}) collective-permute-start(f32[32,512]{1,0:T(8,128)S(1)} %get-tuple-element.35), channel_id=1, source_target_pairs={{0,2},{2,4},{4,6},{6,8},{8,10},{10,12},{12,14},{14,0},{1,3},{3,5},... | collective-permute-start | bytes 196616 | tf_op jit(solution)/shard_map/ppermute | solution.py:16
  53.3 4.3 %collective-permute-start.11 = (f32[32,512]{1,0:T(8,128)S(1)}, f32[32,512]{1,0:T(8,128)S(1)}, u32[]{:S(2)}, u32[]{:S(2)}) collective-permute-start(f32[32,512]{1,0:T(8,128)S(1)} %get-tuple-element.36), channel_id=1, source_target_pairs={{0,14},{2,0},{4,2},{6,4},{8,6},{10,8},{12,10},{14,12},{1,15},{3,1}... | collective-permute-start | bytes 196616 | tf_op jit(solution)/shard_map/ppermute | solution.py:16
  57.6 1.6 %copy-start.1 = (bf16[4,512,512]{2,1,0:T(8,128)(2,1)S(1)}, bf16[4,512,512]{2,1,0:T(8,128)(2,1)}, u32[]{:S(2)}) copy-start(bf16[4,512,512]{2,1,0:T(8,128)(2,1)} %copy-done) | copy-start | bytes 6291460
  59.4 6.7 %collective-permute-start.12 = (f32[32,512]{1,0:T(8,128)S(1)}, f32[32,512]{1,0:T(8,128)S(1)}, u32[]{:S(2)}, u32[]{:S(2)}) collective-permute-start(f32[32,512]{1,0:T(8,128)S(1)} %shard_map.57.refs_1_), channel_id=1, source_target_pairs={{0,64},{64,128},{128,192},{192,0},{1,65},{65,129},{129,193},{193,1... | collective-permute-start | bytes 196616 | tf_op jit(solution)/shard_map/ppermute | solution.py:16
  61.0 7.5 %collective-permute-start.14 = (f32[32,512]{1,0:T(8,128)S(1)}, f32[32,512]{1,0:T(8,128)S(1)}, u32[]{:S(2)}, u32[]{:S(2)}) collective-permute-start(f32[32,512]{1,0:T(8,128)S(1)} %shard_map.57.refs_1_), channel_id=1, source_target_pairs={{0,128},{64,192},{128,0},{192,64},{1,129},{65,193},{129,1},{193,65... | collective-permute-start | bytes 196616 | tf_op jit(solution)/shard_map/ppermute | solution.py:16
  63.9 4.6 %collective-permute-start.15 = (f32[32,512]{1,0:T(8,128)S(1)}, f32[32,512]{1,0:T(8,128)S(1)}, u32[]{:S(2)}, u32[]{:S(2)}) collective-permute-start(f32[32,512]{1,0:T(8,128)S(1)} %shard_map.57.refs_1_), channel_id=1, source_target_pairs={{0,192},{64,0},{128,64},{192,128},{1,193},{65,1},{129,65},{193,129... | collective-permute-start | bytes 196616 | tf_op jit(solution)/shard_map/ppermute | solution.py:16
  66.4 6.2 %collective-permute-start.13 = (f32[32,512]{1,0:T(8,128)S(1)}, f32[32,512]{1,0:T(8,128)S(1)}, u32[]{:S(2)}, u32[]{:S(2)}) collective-permute-start(f32[32,512]{1,0:T(8,128)S(1)} %shard_map.58.refs_2_), channel_id=1, source_target_pairs={{0,64},{64,128},{128,192},{192,0},{1,65},{65,129},{129,193},{193,1... | collective-permute-start | bytes 196616 | tf_op jit(solution)/shard_map/ppermute | solution.py:16
  66.5 6.5 %collective-permute-start.17 = (f32[32,512]{1,0:T(8,128)S(1)}, f32[32,512]{1,0:T(8,128)S(1)}, u32[]{:S(2)}, u32[]{:S(2)}) collective-permute-start(f32[32,512]{1,0:T(8,128)S(1)} %shard_map.58.refs_2_), channel_id=1, source_target_pairs={{0,128},{64,192},{128,0},{192,64},{1,129},{65,193},{129,1},{193,65... | collective-permute-start | bytes 196616 | tf_op jit(solution)/shard_map/ppermute | solution.py:16
  72.9 5.5 %collective-permute-start.16 = (f32[32,512]{1,0:T(8,128)S(1)}, f32[32,512]{1,0:T(8,128)S(1)}, u32[]{:S(2)}, u32[]{:S(2)}) collective-permute-start(f32[32,512]{1,0:T(8,128)S(1)} %shard_map.60.refs_1_), channel_id=1, source_target_pairs={{0,64},{64,128},{128,192},{192,0},{1,65},{65,129},{129,193},{193,1... | collective-permute-start | bytes 196616 | tf_op jit(solution)/shard_map/ppermute | solution.py:16

commit v5 on v4

v5 whole, which is shorter than its diff:
```python
import functools

import jax
import jax.numpy as jnp
from jax import lax
from jax.experimental import pallas as pl
from jax.experimental.pallas import tpu as pltpu
from jax.sharding import Mesh
from jax.sharding import PartitionSpec as P

COL = ("x", "z", "core")


def shifted(value, axis, by):
    peers = lax.axis_size(axis)
    return lax.ppermute(value, axis, [(i, (i + by) % peers) for i in range(peers)])


def in_hbm(value):
    return pltpu.with_memory_space_constraint(value, pltpu.HBM)


def halves(value):
    high = value.astype(jnp.bfloat16)
    return high, (value - high.astype(jnp.float32)).astype(jnp.bfloat16)


def contract(left, right, left_dim, right_dim):
    dims = (((left_dim,), (right_dim,)), ((), ()))
    return lax.dot_general(left, right, dims, preferred_element_type=jnp.float32)


def three_pass(left, right, left_dim, right_dim):
    left_high, left_low = halves(left)
    right_high, right_low = halves(right)
    return contract(left_high, right_high, left_dim, right_dim) + (
        contract(left_high, right_low, left_dim, right_dim)
        + contract(left_low, right_high, left_dim, right_dim)
    )


def ring_order(peers):
    return sorted(range(peers), key=lambda o: (-min(o, peers - o), o))


def product_body(n_z, n_core, place, users, factor, own, sent):
    items, rows = users.shape[1], factor.shape[0]
    share = items // (n_z * n_core)
    total = three_pass(users[...], factor[...], 0, 1).reshape(n_z, n_core, share, rows)

    def keep(mine):
        for k in range(n_z):
            ahead = lax.rem(k - place[1] + n_z, n_z)
            own[0, ahead] = total[k, mine]
            sent[0, ahead] = total[k, 1 - mine]

    pl.when(place[0] == 0)(lambda: keep(0))
    pl.when(place[0] == 1)(lambda: keep(1))


def product(place, first, count, users, factor, sizes):
    n_x, n_z, n_core = sizes
    depth, items = users.shape
    rows = factor.shape[0]
    chunk, share = items // n_x, items // (n_x * n_z * n_core)
    return pl.pallas_call(
        functools.partial(product_body, n_z, n_core),
        grid_spec=pltpu.PrefetchScalarGridSpec(
            num_scalar_prefetch=1,
            grid=(count,),
            in_specs=[
                pl.BlockSpec((depth, chunk), lambda i, s: (0, s[2 + first + i])),
                pl.BlockSpec((rows, depth), lambda i, s: (0, 0)),
            ],
            out_specs=[pl.BlockSpec((1, n_z, share, rows), lambda i, s: (i, 0, 0, 0))] * 2,
        ),
        out_shape=[jax.ShapeDtypeStruct((count, n_z, share, rows), jnp.float32)] * 2,
        cost_estimate=pl.CostEstimate(
            flops=6 * count * chunk * rows * depth,
            transcendentals=0,
            bytes_accessed=4 * (count * chunk + rows) * depth + 4 * count * chunk * rows,
        ),
        compiler_params=pltpu.CompilerParams(vmem_limit_bytes=24 << 20),
    )(place, users, factor)


def weights_body(diag, coupling, *outs):
    block = diag.shape[0]
    outs[0][...], outs[1][...] = halves(diag[...].T)
    for h in range(coupling.shape[1] // block):
        value = -three_pass(coupling[:, h * block : (h + 1) * block], diag[...], 0, 1)
        outs[2 + 2 * h][...], outs[3 + 2 * h][...] = halves(value)


def hop_weights(diag, coupling):
    block = diag.shape[0]
    count = 1 + coupling.shape[1] // block
    outs = pl.pallas_call(
        weights_body,
        out_shape=[jax.ShapeDtypeStruct((block, block), jnp.bfloat16)] * (2 * count),
        cost_estimate=pl.CostEstimate(
            flops=6 * (count - 1) * block**3, transcendentals=0, bytes_accessed=8 * count * block**2
        ),
        compiler_params=pltpu.CompilerParams(vmem_limit_bytes=24 << 20),
    )(diag, coupling)
    return [tuple(outs[2 * k : 2 * k + 2]) for k in range(count)]


def apply_body(group, count, place, *refs):
    values, weights, (base, out) = refs[:count], refs[count:-2], refs[-2:]
    total = base[...]
    for k, ref in enumerate(values):
        value = ref[...]
        if group is not None:
            value = jnp.where(place[0] == group, value, 0.0)
        high, low = halves(value)
        both = contract(jnp.concatenate([high, low]), weights[2 * k][...], 1, 0)
        change = both[: high.shape[0]] + both[high.shape[0] :]
        total = total + (change + contract(high, weights[2 * k + 1][...], 1, 0))
    out[...] = total


def applied(position, group, base, terms):
    def rows_at(at):
        return pl.BlockSpec(base.shape, lambda i, s: (at, 0))

    weights = [half for _, _, weight in terms for half in weight]
    return pl.pallas_call(
        functools.partial(apply_body, group, len(terms)),
        grid_spec=pltpu.PrefetchScalarGridSpec(
            num_scalar_prefetch=1,
            grid=(1,),
            in_specs=[rows_at(at) for _, at, _ in terms]
            + [pl.BlockSpec(half.shape, lambda i, s: (0, 0)) for half in weights]
            + [rows_at(0)],
            out_specs=rows_at(0),
        ),
        out_shape=jax.ShapeDtypeStruct(base.shape, jnp.float32),
        compiler_params=pltpu.CompilerParams(vmem_limit_bytes=8 << 20),
    )(position, *[value for value, _, _ in terms], *weights, base)


def chain(position, residue, weights):
    first = applied(position, None, jnp.zeros_like(residue), [(residue, 0, weights[0])])
    near = shifted(first, "grp", 1)
    back = shifted(first, "grp", -1)
    second = applied(position, 1, first, [(near, 0, weights[1])])
    both = shifted(jnp.concatenate([near, second]), "grp", 1)
    second = applied(position, 3, second, [(back, 0, weights[1])])
    third = applied(position, 2, second, [(both, 0, weights[1]), (both, 1, weights[2])])
    last = shifted(jnp.concatenate([both[residue.shape[0] :], third]), "grp", 1)
    return applied(position, 3, third, [(last, 0, weights[2]), (last, 1, weights[3])])


def after(place, value):
    mark = shifted(value[0, :8, :128], "core", 1)[0, 0]
    return jnp.where(mark != mark, jnp.zeros_like(place), place)


def reduced_over_z(blocks):
    share = blocks.shape[1]
    half = share // 2
    rows = blocks.reshape(-1, blocks.shape[2])
    middle = 4 * share + half
    up = shifted(rows[3 * share : middle], "z", 2)
    down = shifted(rows[middle : 6 * share], "z", -2)
    far_up = jnp.concatenate([blocks[2, :half] + up[share:], blocks[2, half:]])
    far_down = jnp.concatenate([blocks[6, :half], blocks[6, half:] + down[:half]])
    arrived = [
        shifted(far_up, "z", 2),
        shifted(far_down, "z", -2),
        shifted(blocks[1] + up[:share], "z", 1),
        shifted(blocks[7] + down[half:], "z", -1),
    ]
    return functools.reduce(lambda a, b: a + b, arrived, blocks[0])


def on_device(right_side, solved_factor, solved_users, diag_inverse, coupling):
    sizes = tuple(lax.axis_size(a) for a in COL)
    x, z, core = (lax.axis_index(a) for a in COL)
    place = [core, z] + [(x + o) % sizes[0] for o in ring_order(sizes[0])]
    place = jnp.stack(place).astype(jnp.int32)
    position = lax.axis_index("grp").reshape(1).astype(jnp.int32)
    users, factor = in_hbm(solved_users), in_hbm(solved_factor)

    own, sent = product(place, 0, 3, users, factor, sizes)
    other = shifted(sent[0], "core", 1)
    sent, other = lax.optimization_barrier((sent, other))
    far = own[0] + other
    near = own[1:] + shifted(sent[1:], "core", 1)
    cut = far.shape[0] // 2
    up = shifted(far[:cut], "x", 1)
    down = shifted(far[cut:], "x", -1)
    own, sent = product(after(place, far), 3, 1, users, factor, sizes)
    mine = own[0]
    near, sent = lax.optimization_barrier((near, sent))
    home = mine + shifted(sent[0], "core", 1)
    up = shifted(jnp.concatenate([near[0, :cut] + up, near[0, cut:]]), "x", 1)
    down = shifted(jnp.concatenate([near[1, :cut], near[1, cut:] + down]), "x", -1)
    weights = hop_weights(diag_inverse, coupling)
    home, weights = lax.optimization_barrier((home, weights))
    along_z = home + up + down
    residue = right_side.T - reduced_over_z(along_z)
    return chain(position, residue, weights).T


def solution(mesh):
    torus = Mesh(mesh.devices.reshape(mesh.shape["grp"], 4, 8, 2), ("grp",) + COL)
    placed = (P("grp", COL), P("grp", COL), P(COL, None), P("grp", None), P("grp", None))
    return jax.shard_map(
        on_device, mesh=torus, in_specs=placed, out_specs=P("grp", COL), check_vma=False
    )
```

time: 79.8 us -> 84.3 us (1.056)
  the two profiles are of different devices: /device:TPU:32 before, /device:TPU:6 now
where the time goes in v5:
time: 84.3 us; the launch traced here: 84.2 us
  waiting for transfers between devices  39.9 us (47%)
  starting transfers between devices  22.6 us (27%)
  Pallas kernels  16.2 us (19%)
  other arithmetic  2.9 us (3%)
  between operations  1.61 us (2%)
  local copies, waits for them, and re-layouts  0.88 us (1%)
    ppermute x18, waiting for transfers between devices, shifted(): lax.ppermute(value, axis, [(i, (i + by) % peers) for i in range(peers)])  39.9 us
    ppermute x18, starting transfers between devices, shifted(): lax.ppermute(value, axis, [(i, (i + by) % peers) for i in range(peers)])  22.6 us
    pallas_call x2, Pallas kernels, product(): pl.pallas_call(functools.partial(product_body, n_z, n_core), grid_spec=pl...  11 us
    pallas_call x1, Pallas kernels, hop_weights(): pl.pallas_call(weights_body, out_shape=[jax.ShapeDtypeStruct((block, bloc...  2.9 us
    pallas_call x5, Pallas kernels, applied(): pl.pallas_call(functools.partial(apply_body, group, len(terms)), grid_spe...  2.38 us
  transfers between devices with their start and end apart: 18, of which 12 were waited for; matrix products, arithmetic and copies ran while one was open for 3% of the time, Pallas kernels for 8%

profile of v5, /device:TPU:6, one launch (start us, length us, event | category | flops | bytes accessed | tf_op | source)
XLA Modules:
  0.0 84.2 jit_solution(1021922779071189227)
XLA Ops:
  0.0 0.1 stack.27.place
  0.1 7.0 %shard_map.55 = (f32[3,8,32,512]{3,2,1,0:T(8,128)S(1)}, f32[3,8,32,512]{3,2,1,0:T(8,128)S(1)}) custom-call(s32[6]{0:T(128)S(1)} %stack.27.place, f32[768,2048]{1,0:T(8,128)} %users.3, f32[512,768]{1,0:T(8,128)} %factor.3), custom_call_target="tpu_custom_call" | custom-call | flops 3623878656 | bytes 9437184 | tf_op jit(solution)/shard_map/pallas_call | solution.py:66
  7.2 0.1 collective-permute-start
  7.3 1.9 %collective-permute-done = f32[8,32,512]{2,1,0:T(8,128)S(1)} collective-permute-done((f32[8,32,512]{2,1,0:T(8,128)S(1)}, f32[8,32,512]{2,1,0:T(8,128)S(1)}, u32[]{:S(2)}, u32[]{:S(2)}) %collective-permute-start) | collective-permute-done | bytes 524320 | tf_op jit(solution)/shard_map/ppermute | solution.py:16
  9.2 0.1 slice.83
  9.3 0.2 collective-permute-start.2
  9.5 0.1 bitcast_add_fusion.1
  9.6 0.5 collective-permute-start.1
  10.1 2.3 %collective-permute-start.4 = (f32[4,32,512]{2,1,0:T(8,128)S(1)}, f32[4,32,512]{2,1,0:T(8,128)S(1)}, u32[]{:S(2)}, u32[]{:S(2)}) collective-permute-start(f32[4,32,512]{2,1,0:T(8,128)S(1)} %get-tuple-element.67), channel_id=1, source_target_pairs={{0,16},{16,32},{32,48},{48,0},{1,17},{17,33},{33,49},{49,1},{2,18}... | collective-permute-start | bytes 786440 | tf_op jit(solution)/shard_map/ppermute | solution.py:16
  12.4 0.0 collective-permute-start.6
  12.4 0.0 collective-permute-done.1
  12.4 0.5 slice.81
  14.2 3.9 %shard_map.56 = (f32[1,8,32,512]{3,2,1,0:T(8,128)S(1)}, f32[1,8,32,512]{3,2,1,0:T(8,128)S(1)}) custom-call(s32[6]{0:T(128)S(1)} %broadcast_select_fusion.place, f32[768,2048]{1,0:T(8,128)} %users.3, f32[512,768]{1,0:T(8,128)} %factor.3), custom_call_target="tpu_custom_call" | custom-call | flops 1207959552 | bytes 4194304 | tf_op jit(solution)/shard_map/pallas_call | solution.py:66
  18.2 0.0 collective-permute-done.2
  18.2 0.2 slice_add_fusion
  18.4 0.1 collective-permute-start.3
  18.5 0.0 collective-permute-done.4
  18.5 3.1 %collective-permute-done.6 = f32[4,32,512]{2,1,0:T(8,128)S(1)} collective-permute-done((f32[4,32,512]{2,1,0:T(8,128)S(1)}, f32[4,32,512]{2,1,0:T(8,128)S(1)}, u32[]{:S(2)}, u32[]{:S(2)}) %collective-permute-start.6) | collective-permute-done | bytes 262176 | tf_op jit(solution)/shard_map/ppermute | solution.py:16
  21.7 0.1 bitcast_add_fusion.3
  21.7 0.0 copy-start.4
  21.9 0.4 collective-permute-start.5
  22.3 1.8 %collective-permute-start.7 = (f32[8,32,512]{2,1,0:T(8,128)S(1)}, f32[8,32,512]{2,1,0:T(8,128)S(1)}, u32[]{:S(2)}, u32[]{:S(2)}) collective-permute-start(f32[8,32,512]{2,1,0:T(8,128)S(1)} %pad_maximum_fusion.1), channel_id=1, source_target_pairs={{0,48},{16,0},{32,16},{48,32},{1,49},{17,1},{33,17},{49,33},{2,50}... | collective-permute-start | bytes 1572872 | tf_op jit(solution)/shard_map/ppermute | solution.py:16
  24.1 0.0 copy-done.5
  24.1 0.0 copy-done.4
  24.1 2.9 %shard_map.57 = (bf16[512,512]{1,0:T(8,128)(2,1)S(1)}, bf16[512,512]{1,0:T(8,128)(2,1)S(1)}, bf16[512,512]{1,0:T(8,128)(2,1)S(1)}, bf16[512,512]{1,0:T(8,128)(2,...) custom-call(f32[512,512]{1,0:T(8,128)S(1)} %copy-done.5, ...), custom_call_target="tpu_custom_call" | custom-call | flops 2415919104 | bytes 8388608 | tf_op jit(solution)/shard_map/pallas_call | solution.py:98
  27.0 0.0 copy-start
  27.0 0.0 copy-start.2
  27.0 0.0 collective-permute-done.3
  27.0 0.1 bitcast_add_fusion
  27.1 0.0 copy-start.7
  27.1 7.6 %collective-permute-done.5 = f32[8,32,512]{2,1,0:T(8,128)S(1)} collective-permute-done((f32[8,32,512]{2,1,0:T(8,128)S(1)}, f32[8,32,512]{2,1,0:T(8,128)S(1)}, u32[]{:S(2)}, u32[]{:S(2)}) %collective-permute-start.5) | collective-permute-done | bytes 524320 | tf_op jit(solution)/shard_map/ppermute | solution.py:16
  34.8 2.6 %collective-permute-done.7 = f32[8,32,512]{2,1,0:T(8,128)S(1)} collective-permute-done((f32[8,32,512]{2,1,0:T(8,128)S(1)}, f32[8,32,512]{2,1,0:T(8,128)S(1)}, u32[]{:S(2)}, u32[]{:S(2)}) %collective-permute-start.7) | collective-permute-done | bytes 524320 | tf_op jit(solution)/shard_map/ppermute | solution.py:16
  37.4 0.1 add_add_fusion
  37.5 0.0 copy-done
  37.6 4.8 %collective-permute-start.10 = (f32[48,512]{1,0:T(8,128)S(1)}, f32[48,512]{1,0:T(8,128)S(1)}, u32[]{:S(2)}, u32[]{:S(2)}) collective-permute-start(f32[48,512]{1,0:T(8,128)S(1)} %get-tuple-element.66), channel_id=1, source_target_pairs={{0,12},{2,14},{4,0},{6,2},{8,4},{10,6},{12,8},{14,10},{1,13},{3,15... | collective-permute-start | bytes 294920 | tf_op jit(solution)/shard_map/ppermute | solution.py:16
  42.4 0.0 collective-permute-start.8
  42.4 4.0 %collective-permute-done.10 = f32[48,512]{1,0:T(8,128)S(1)} collective-permute-done((f32[48,512]{1,0:T(8,128)S(1)}, f32[48,512]{1,0:T(8,128)S(1)}, u32[]{:S(2)}, u32[]{:S(2)}) %collective-permute-start.10) | collective-permute-done | bytes 98336 | tf_op jit(solution)/shard_map/ppermute | solution.py:16
  46.4 3.2 %collective-permute-done.8 = f32[48,512]{1,0:T(8,128)S(1)} collective-permute-done((f32[48,512]{1,0:T(8,128)S(1)}, f32[48,512]{1,0:T(8,128)S(1)}, u32[]{:S(2)}, u32[]{:S(2)}) %collective-permute-start.8) | collective-permute-done | bytes 98336 | tf_op jit(solution)/shard_map/ppermute | solution.py:16
  49.7 0.1 collective-permute-start.9
  49.8 0.6 pad_maximum_fusion.5
  50.4 4.1 %collective-permute-start.11 = (f32[32,512]{1,0:T(8,128)}, f32[32,512]{1,0:T(8,128)S(1)}, u32[]{:S(2)}, u32[]{:S(2)}) collective-permute-start(f32[32,512]{1,0:T(8,128)} %pad_maximum_fusion.5), channel_id=1, source_target_pairs={{0,12},{2,14},{4,0},{6,2},{8,4},{10,6},{12,8},{14,10},{1,13},{3,15... | collective-permute-start | bytes 196616 | tf_op jit(solution)/shard_map/ppermute | solution.py:16
  54.5 0.0 copy-done.6
  54.5 0.7 slice_add_fusion.2
  55.2 1.9 %collective-permute-start.12 = (f32[32,512]{1,0:T(8,128)}, f32[32,512]{1,0:T(8,128)S(1)}, u32[]{:S(2)}, u32[]{:S(2)}) collective-permute-start(f32[32,512]{1,0:T(8,128)} %get-tuple-element.63), channel_id=1, source_target_pairs={{0,2},{2,4},{4,6},{6,8},{8,10},{10,12},{12,14},{14,0},{1,3},{3,5},... | collective-permute-start | bytes 196616 | tf_op jit(solution)/shard_map/ppermute | solution.py:16
  57.0 1.4 %collective-permute-start.13 = (f32[32,512]{1,0:T(8,128)}, f32[32,512]{1,0:T(8,128)S(1)}, u32[]{:S(2)}, u32[]{:S(2)}) collective-permute-start(f32[32,512]{1,0:T(8,128)} %get-tuple-element.64), channel_id=1, source_target_pairs={{0,14},{2,0},{4,2},{6,4},{8,6},{10,8},{12,10},{14,12},{1,15},{3,1}... | collective-permute-start | bytes 196616 | tf_op jit(solution)/shard_map/ppermute | solution.py:16
  58.4 0.0 collective-permute-done.9
  58.4 0.0 collective-permute-done.11
  58.4 2.4 %collective-permute-done.12 = f32[32,512]{1,0:T(8,128)S(1)} collective-permute-done((f32[32,512]{1,0:T(8,128)}, f32[32,512]{1,0:T(8,128)S(1)}, u32[]{:S(2)}, u32[]{:S(2)}) %collective-permute-start.12) | collective-permute-done | bytes 65568 | tf_op jit(solution)/shard_map/ppermute | solution.py:16
  60.8 0.7 collective-permute-done.13
  61.5 0.9 %fusion.4.refs_0_ = f32[32,512]{1,0:T(8,128)S(1)} fusion(f32[32,512]{1,0:T(8,128)S(1)} %collective-permute-done.13, f32[32,512]{1,0:T(8,128)S(1)} %collective-permute-done.12, f32[32,512]{1,0:T(8,128)S(1)} %collective-permute-done.11, f32[32,512]{1,0:T(8,128)S(1)} %collective-permute-done.9, f32[8,32,512]{2,1,0:T(8,128)} %copy-done.6, f32[512,32]{0,1:T(8,128)S(1)} %copy-done.7), kind=kLoop, calls=%fused_computation.22 | loop fusion | flops 81920 | bytes 458752 | tf_op jit(solution)/shard_map/sub | solution.py:203
  62.4 0.3 shard_map.58.refs_3_
  62.7 1.6 %collective-permute-start.14 = (f32[32,512]{1,0:T(8,128)S(1)}, f32[32,512]{1,0:T(8,128)S(1)}, u32[]{:S(2)}, u32[]{:S(2)}) collective-permute-start(f32[32,512]{1,0:T(8,128)S(1)} %shard_map.58.refs_3_), channel_id=1, source_target_pairs={{0,64},{64,128},{128,192},{192,0},{1,65},{65,129},{129,193},{193,1... | collective-permute-start | bytes 196616 | tf_op jit(solution)/shard_map/ppermute | solution.py:16
  64.3 4.6 %collective-permute-done.14.refs_0_ = f32[32,512]{1,0:T(8,128)S(1)} collective-permute-done((f32[32,512]{1,0:T(8,128)S(1)}, f32[32,512]{1,0:T(8,128)S(1)}, u32[]{:S(2)}, u32[]{:S(2)}) %collective-permute-start.14) | collective-permute-done | bytes 65568 | tf_op jit(solution)/shard_map/ppermute | solution.py:16
  68.9 0.3 shard_map.59.refs_3_
  69.2 0.1 collective-permute-start.15
  69.3 3.2 %collective-permute-start.16 = (f32[32,512]{1,0:T(8,128)S(1)}, f32[32,512]{1,0:T(8,128)S(1)}, u32[]{:S(2)}, u32[]{:S(2)}) collective-permute-start(f32[32,512]{1,0:T(8,128)S(1)} %shard_map.58.refs_3_), channel_id=1, source_target_pairs={{0,192},{64,0},{128,64},{192,128},{1,193},{65,1},{129,65},{193,129... | collective-permute-start | bytes 196616 | tf_op jit(solution)/shard_map/ppermute | solution.py:16
  72.5 1.9 %collective-permute-done.16.refs_0_ = f32[32,512]{1,0:T(8,128)S(1)} collective-permute-done((f32[32,512]{1,0:T(8,128)S(1)}, f32[32,512]{1,0:T(8,128)S(1)}, u32[]{:S(2)}, u32[]{:S(2)}) %collective-permute-start.16) | collective-permute-done | bytes 65568 | tf_op jit(solution)/shard_map/ppermute | solution.py:16
  74.4 0.3 shard_map.60.refs_6_
  74.7 0.0 copy-start.3
  74.7 1.6 %collective-permute-done.15.refs_0_.refs_1_ = f32[64,512]{1,0:T(8,128)S(1)} collective-permute-done((f32[64,512]{1,0:T(8,128)S(1)}, f32[64,512]{1,0:T(8,128)S(1)}, u32[]{:S(2)}, u32[]{:S(2)}) %collective-permute-start.15) | collective-permute-done | bytes 131104 | tf_op jit(solution)/shard_map/ppermute | solution.py:16
  76.3 0.5 shard_map.61.refs_6_
  76.8 0.1 collective-permute-start.17
  76.9 6.2 %collective-permute-done.17.refs_0_.refs_1_ = f32[64,512]{1,0:T(8,128)S(1)} collective-permute-done((f32[64,512]{1,0:T(8,128)S(1)}, f32[64,512]{1,0:T(8,128)S(1)}, u32[]{:S(2)}, u32[]{:S(2)}) %collective-permute-start.17) | collective-permute-done | bytes 131104 | tf_op jit(solution)/shard_map/ppermute | solution.py:16
  83.1 1.1 %shard_map.62 = f32[32,512]{1,0:T(8,128)} custom-call(s32[1]{0:T(128)} %bitcast.place, f32[64,512]{1,0:T(8,128)S(1)} %collective-permute-done.17.refs_0_.refs_1_, f32[64,512]{1,0:T(8,128)S(1)} %collective-permute-done.17.refs_0_.refs_1_, bf16[512,512]{1,0:T(8,128)(2,1)S(1)} %get-tuple-element.51.refs_4_.refs_2_, ...), custom_call_target="tpu_custom_call" | custom-call | tf_op jit(solution)/shard_map/pallas_call | solution.py:128
  (22 shorter events, 0.3 us)
Async XLA Ops:
  7.2 2.0 %collective-permute-start = (f32[8,32,512]{2,1,0:T(8,128)S(1)}, f32[8,32,512]{2,1,0:T(8,128)S(1)}, u32[]{:S(2)}, u32[]{:S(2)}) collective-permute-start(f32[8,32,512]{2,1,0:T(8,128)S(1)} %slice_bitcast_fusion), channel_id=1, source_target_pairs={{0,1},{1,0},{2,3},{3,2},{4,5},{5,4},{6,7},{7,6},{8,9},{9,8},{10,11... | collective-permute-start | bytes 1572872 | tf_op jit(solution)/shard_map/ppermute | solution.py:16
  9.3 8.9 %collective-permute-start.2 = (f32[2,8,32,512]{3,2,1,0:T(8,128)S(1)}, f32[2,8,32,512]{3,2,1,0:T(8,128)S(1)}, u32[]{:S(2)}, u32[]{:S(2)}) collective-permute-start(f32[2,8,32,512]{3,2,1,0:T(8,128)S(1)} %slice.83), channel_id=1, source_target_pairs={{0,1},{1,0},{2,3},{3,2},{4,5},{5,4},{6,7},{7,6},{8,9},{9,8},{10,11... | collective-permute-start | bytes 3145736 | tf_op jit(solution)/shard_map/ppermute | solution.py:16
  9.6 2.8 %collective-permute-start.1 = (f32[8,128]{1,0:T(8,128)S(1)}, f32[8,128]{1,0:T(8,128)S(1)}, u32[]{:S(2)}, u32[]{:S(2)}) collective-permute-start(f32[8,128]{1,0:T(8,128)S(1)} %slice_bitcast_fusion.10), channel_id=1, source_target_pairs={{0,1},{1,0},{2,3},{3,2},{4,5},{5,4},{6,7},{7,6},{8,9},{9,8},{10,11... | collective-permute-start | bytes 12296 | tf_op jit(solution)/shard_map/ppermute | solution.py:16
  10.1 8.4 %collective-permute-start.4 = (f32[4,32,512]{2,1,0:T(8,128)S(1)}, f32[4,32,512]{2,1,0:T(8,128)S(1)}, u32[]{:S(2)}, u32[]{:S(2)}) collective-permute-start(f32[4,32,512]{2,1,0:T(8,128)S(1)} %get-tuple-element.67), channel_id=1, source_target_pairs={{0,16},{16,32},{32,48},{48,0},{1,17},{17,33},{33,49},{49,1},{2,18}... | collective-permute-start | bytes 786440 | tf_op jit(solution)/shard_map/ppermute | solution.py:16
  12.4 9.3 %collective-permute-start.6 = (f32[4,32,512]{2,1,0:T(8,128)S(1)}, f32[4,32,512]{2,1,0:T(8,128)S(1)}, u32[]{:S(2)}, u32[]{:S(2)}) collective-permute-start(f32[4,32,512]{2,1,0:T(8,128)S(1)} %get-tuple-element.68), channel_id=1, source_target_pairs={{0,48},{16,0},{32,16},{48,32},{1,49},{17,1},{33,17},{49,33},{2,50}... | collective-permute-start | bytes 786440 | tf_op jit(solution)/shard_map/ppermute | solution.py:16
  18.4 8.7 %collective-permute-start.3 = (f32[8,32,512]{2,1,0:T(8,128)S(1)}, f32[8,32,512]{2,1,0:T(8,128)S(1)}, u32[]{:S(2)}, u32[]{:S(2)}) collective-permute-start(f32[8,32,512]{2,1,0:T(8,128)S(1)} %bitcast.61), channel_id=1, source_target_pairs={{0,1},{1,0},{2,3},{3,2},{4,5},{5,4},{6,7},{7,6},{8,9},{9,8},{10,11... | collective-permute-start | bytes 1572872 | tf_op jit(solution)/shard_map/ppermute | solution.py:16
  21.7 2.4 %copy-start.5 = (f32[512,512]{1,0:T(8,128)S(1)}, f32[512,512]{1,0:T(8,128)}, u32[]{:S(2)}) copy-start(f32[512,512]{1,0:T(8,128)} %diag.1) | copy-start | bytes 3145732
  21.7 2.3 %copy-start.4 = (f32[512,1536]{1,0:T(8,128)S(1)}, f32[512,1536]{1,0:T(8,128)}, u32[]{:S(2)}) copy-start(f32[512,1536]{1,0:T(8,128)} %coupling.1) | copy-start | bytes 9437188
  21.9 12.9 %collective-permute-start.5 = (f32[8,32,512]{2,1,0:T(8,128)S(1)}, f32[8,32,512]{2,1,0:T(8,128)S(1)}, u32[]{:S(2)}, u32[]{:S(2)}) collective-permute-start(f32[8,32,512]{2,1,0:T(8,128)S(1)} %pad_maximum_fusion), channel_id=1, source_target_pairs={{0,16},{16,32},{32,48},{48,0},{1,17},{17,33},{33,49},{49,1},{2,18}... | collective-permute-start | bytes 1572872 | tf_op jit(solution)/shard_map/ppermute | solution.py:16
  22.3 15.1 %collective-permute-start.7 = (f32[8,32,512]{2,1,0:T(8,128)S(1)}, f32[8,32,512]{2,1,0:T(8,128)S(1)}, u32[]{:S(2)}, u32[]{:S(2)}) collective-permute-start(f32[8,32,512]{2,1,0:T(8,128)S(1)} %pad_maximum_fusion.1), channel_id=1, source_target_pairs={{0,48},{16,0},{32,16},{48,32},{1,49},{17,1},{33,17},{49,33},{2,50}... | collective-permute-start | bytes 1572872 | tf_op jit(solution)/shard_map/ppermute | solution.py:16
  27.0 10.5 %copy-start = (bf16[512,512]{1,0:T(8,128)(2,1)}, bf16[512,512]{1,0:T(8,128)(2,1)S(1)}, u32[]{:S(2)}) copy-start(bf16[512,512]{1,0:T(8,128)(2,1)S(1)} %get-tuple-element.53.refs_4_) | copy-start | bytes 1572868
  27.0 10.5 %copy-start.2 = (bf16[512,512]{1,0:T(8,128)(2,1)}, bf16[512,512]{1,0:T(8,128)(2,1)S(1)}, u32[]{:S(2)}) copy-start(bf16[512,512]{1,0:T(8,128)(2,1)S(1)} %get-tuple-element.54.refs_5_) | copy-start | bytes 1572868
  27.1 34.4 %copy-start.7 = (f32[512,32]{0,1:T(8,128)S(1)}, f32[512,32]{0,1:T(8,128)}, u32[]{:S(2)}) copy-start(f32[512,32]{0,1:T(8,128)} %param.5) | copy-start | bytes 196612
  37.5 17.0 %copy-start.6 = (f32[8,32,512]{2,1,0:T(8,128)}, f32[8,32,512]{2,1,0:T(8,128)S(1)}, u32[]{:S(2)}) copy-start(f32[8,32,512]{2,1,0:T(8,128)S(1)} %add_add_fusion) | copy-start | bytes 1572868
  37.6 8.8 %collective-permute-start.10 = (f32[48,512]{1,0:T(8,128)S(1)}, f32[48,512]{1,0:T(8,128)S(1)}, u32[]{:S(2)}, u32[]{:S(2)}) collective-permute-start(f32[48,512]{1,0:T(8,128)S(1)} %get-tuple-element.66), channel_id=1, source_target_pairs={{0,12},{2,14},{4,0},{6,2},{8,4},{10,6},{12,8},{14,10},{1,13},{3,15... | collective-permute-start | bytes 294920 | tf_op jit(solution)/shard_map/ppermute | solution.py:16
  42.4 7.2 %collective-permute-start.8 = (f32[48,512]{1,0:T(8,128)S(1)}, f32[48,512]{1,0:T(8,128)S(1)}, u32[]{:S(2)}, u32[]{:S(2)}) collective-permute-start(f32[48,512]{1,0:T(8,128)S(1)} %get-tuple-element.65), channel_id=1, source_target_pairs={{0,4},{2,6},{4,8},{6,10},{8,12},{10,14},{12,0},{14,2},{1,5},{3,7},... | collective-permute-start | bytes 294920 | tf_op jit(solution)/shard_map/ppermute | solution.py:16
  49.7 8.7 %collective-permute-start.9 = (f32[32,512]{1,0:T(8,128)S(1)}, f32[32,512]{1,0:T(8,128)S(1)}, u32[]{:S(2)}, u32[]{:S(2)}) collective-permute-start(f32[32,512]{1,0:T(8,128)S(1)} %pad_maximum_fusion.4), channel_id=1, source_target_pairs={{0,4},{2,6},{4,8},{6,10},{8,12},{10,14},{12,0},{14,2},{1,5},{3,7},... | collective-permute-start | bytes 196616 | tf_op jit(solution)/shard_map/ppermute | solution.py:16
  50.4 8.0 %collective-permute-start.11 = (f32[32,512]{1,0:T(8,128)}, f32[32,512]{1,0:T(8,128)S(1)}, u32[]{:S(2)}, u32[]{:S(2)}) collective-permute-start(f32[32,512]{1,0:T(8,128)} %pad_maximum_fusion.5), channel_id=1, source_target_pairs={{0,12},{2,14},{4,0},{6,2},{8,4},{10,6},{12,8},{14,10},{1,13},{3,15... | collective-permute-start | bytes 196616 | tf_op jit(solution)/shard_map/ppermute | solution.py:16
  55.2 5.7 %collective-permute-start.12 = (f32[32,512]{1,0:T(8,128)}, f32[32,512]{1,0:T(8,128)S(1)}, u32[]{:S(2)}, u32[]{:S(2)}) collective-permute-start(f32[32,512]{1,0:T(8,128)} %get-tuple-element.63), channel_id=1, source_target_pairs={{0,2},{2,4},{4,6},{6,8},{8,10},{10,12},{12,14},{14,0},{1,3},{3,5},... | collective-permute-start | bytes 196616 | tf_op jit(solution)/shard_map/ppermute | solution.py:16
  57.0 4.5 %collective-permute-start.13 = (f32[32,512]{1,0:T(8,128)}, f32[32,512]{1,0:T(8,128)S(1)}, u32[]{:S(2)}, u32[]{:S(2)}) collective-permute-start(f32[32,512]{1,0:T(8,128)} %get-tuple-element.64), channel_id=1, source_target_pairs={{0,14},{2,0},{4,2},{6,4},{8,6},{10,8},{12,10},{14,12},{1,15},{3,1}... | collective-permute-start | bytes 196616 | tf_op jit(solution)/shard_map/ppermute | solution.py:16
  62.7 6.2 %collective-permute-start.14 = (f32[32,512]{1,0:T(8,128)S(1)}, f32[32,512]{1,0:T(8,128)S(1)}, u32[]{:S(2)}, u32[]{:S(2)}) collective-permute-start(f32[32,512]{1,0:T(8,128)S(1)} %shard_map.58.refs_3_), channel_id=1, source_target_pairs={{0,64},{64,128},{128,192},{192,0},{1,65},{65,129},{129,193},{193,1... | collective-permute-start | bytes 196616 | tf_op jit(solution)/shard_map/ppermute | solution.py:16
  69.2 7.2 %collective-permute-start.15 = (f32[64,512]{1,0:T(8,128)S(1)}, f32[64,512]{1,0:T(8,128)S(1)}, u32[]{:S(2)}, u32[]{:S(2)}) collective-permute-start(f32[64,512]{1,0:T(8,128)S(1)} %pad_maximum_fusion.2), channel_id=1, source_target_pairs={{0,64},{64,128},{128,192},{192,0},{1,65},{65,129},{129,193},{193,1... | collective-permute-start | bytes 393224 | tf_op jit(solution)/shard_map/ppermute | solution.py:16
  69.3 5.1 %collective-permute-start.16 = (f32[32,512]{1,0:T(8,128)S(1)}, f32[32,512]{1,0:T(8,128)S(1)}, u32[]{:S(2)}, u32[]{:S(2)}) collective-permute-start(f32[32,512]{1,0:T(8,128)S(1)} %shard_map.58.refs_3_), channel_id=1, source_target_pairs={{0,192},{64,0},{128,64},{192,128},{1,193},{65,1},{129,65},{193,129... | collective-permute-start | bytes 196616 | tf_op jit(solution)/shard_map/ppermute | solution.py:16
  74.7 8.4 %copy-start.1 = (bf16[512,512]{1,0:T(8,128)(2,1)S(1)}, bf16[512,512]{1,0:T(8,128)(2,1)}, u32[]{:S(2)}) copy-start(bf16[512,512]{1,0:T(8,128)(2,1)} %copy-done) | copy-start | bytes 1572868
  74.7 8.4 %copy-start.3 = (bf16[512,512]{1,0:T(8,128)(2,1)S(1)}, bf16[512,512]{1,0:T(8,128)(2,1)}, u32[]{:S(2)}) copy-start(bf16[512,512]{1,0:T(8,128)(2,1)} %copy-done.2) | copy-start | bytes 1572868
  76.8 6.3 %collective-permute-start.17 = (f32[64,512]{1,0:T(8,128)S(1)}, f32[64,512]{1,0:T(8,128)S(1)}, u32[]{:S(2)}, u32[]{:S(2)}) collective-permute-start(f32[64,512]{1,0:T(8,128)S(1)} %pad_maximum_fusion.3), channel_id=1, source_target_pairs={{0,64},{64,128},{128,192},{192,0},{1,65},{65,129},{129,193},{193,1... | collective-permute-start | bytes 393224 | tf_op jit(solution)/shard_map/ppermute | solution.py:16

commit v6 on v4

--- a/solution.py
+++ b/solution.py
@@ -14,6 +14,10 @@
 def shifted(value, axis, by):
     peers = lax.axis_size(axis)
     return lax.ppermute(value, axis, [(i, (i + by) % peers) for i in range(peers)])
+
+
+def in_pieces(value, axis, by):
+    return [shifted(part, axis, by) for part in jnp.split(value, 2)]
 
 
 def in_hbm(value):
@@ -95,34 +99,26 @@
     )(place, users, factor)
 
 
-def weights_body(diag, coupling, high, low):
-    step = pl.program_id(0)
-
-    def keep(value):
-        high[0], low[0] = halves(value)
-
-    pl.when(step == 0)(lambda: keep(diag[...].T))
-    pl.when(step > 0)(lambda: keep(-three_pass(coupling[...], diag[...], 0, 1)))
+def weights_body(diag, coupling, *outs):
+    block = diag.shape[0]
+    outs[0][...], outs[1][...] = halves(diag[...].T)
+    for h in range(coupling.shape[1] // block):
+        value = -three_pass(coupling[:, h * block : (h + 1) * block], diag[...], 0, 1)
+        outs[2 + 2 * h][...], outs[3 + 2 * h][...] = halves(value)
 
 
 def hop_weights(diag, coupling):
     block = diag.shape[0]
     count = 1 + coupling.shape[1] // block
-    shape = jax.ShapeDtypeStruct((count, block, block), jnp.bfloat16)
-    return pl.pallas_call(
+    outs = pl.pallas_call(
         weights_body,
-        grid=(count,),
-        in_specs=[
-            pl.BlockSpec((block, block), lambda i: (0, 0)),
-            pl.BlockSpec((block, block), lambda i: (0, lax.max(i - 1, 0))),
-        ],
-        out_specs=[pl.BlockSpec((1, block, block), lambda i: (i, 0, 0))] * 2,
-        out_shape=[shape] * 2,
+        out_shape=[jax.ShapeDtypeStruct((block, block), jnp.bfloat16)] * (2 * count),
         cost_estimate=pl.CostEstimate(
             flops=6 * (count - 1) * block**3, transcendentals=0, bytes_accessed=8 * count * block**2
         ),
         compiler_params=pltpu.CompilerParams(vmem_limit_bytes=24 << 20),
     )(diag, coupling)
+    return [tuple(outs[2 * k : 2 * k + 2]) for k in range(count)]
 
 
 def apply_body(wanted, place, *refs):
@@ -132,37 +128,37 @@
         total = total + (value[...] if group is None else jnp.where(place[0] == group, value[...], 0.0))
     value_high, value_low = halves(total)
     count = value_high.shape[0]
-    both = contract(jnp.concatenate([value_high, value_low]), high[0], 1, 0)
-    out[...] = base[...] + (both[:count] + both[count:] + contract(value_high, low[0], 1, 0))
-
-
-def applied(position, base, values, weights, index):
-    whole = pl.BlockSpec(base.shape, lambda i, s: (0, 0))
-    block = weights[0].shape[1]
-    weight = pl.BlockSpec((1, block, block), lambda i, s: (index, 0, 0))
+    both = contract(jnp.concatenate([value_high, value_low]), high[...], 1, 0)
+    out[...] = base[...] + (both[:count] + both[count:] + contract(value_high, low[...], 1, 0))
+
+
+def applied(position, base, values, weight):
+    def whole(shape):
+        return pl.BlockSpec(shape, lambda i, s: (0, 0))
+
     return pl.pallas_call(
         functools.partial(apply_body, [group for group, _ in values]),
         grid_spec=pltpu.PrefetchScalarGridSpec(
             num_scalar_prefetch=1,
             grid=(1,),
-            in_specs=[whole] * (len(values) + 1) + [weight] * 2,
-            out_specs=whole,
+            in_specs=[whole(base.shape)] * (len(values) + 1) + [whole(half.shape) for half in weight],
+            out_specs=whole(base.shape),
         ),
         out_shape=jax.ShapeDtypeStruct(base.shape, jnp.float32),
         compiler_params=pltpu.CompilerParams(vmem_limit_bytes=8 << 20),
-    )(position, *[value for _, value in values], base, *weights)
+    )(position, *[value for _, value in values], base, *weight)
 
 
 def chain(position, residue, weights):
     groups = lax.axis_size("grp")
-    result = applied(position, jnp.zeros_like(residue), [(None, residue)], weights, 0)
+    result = applied(position, jnp.zeros_like(residue), [(None, residue)], weights[0])
     later = []
     for step in range(groups - 1):
         near = shifted(result, "grp", 1)
         far = [(step + by, shifted(result, "grp", by)) for by in range(2, groups - step)]
         if later:
-            result = applied(position, result, later, weights, step)
-        result = applied(position, result, [(step + 1, near)], weights, step + 1)
+            result = applied(position, result, later, weights[step])
+        result = applied(position, result, [(step + 1, near)], weights[step + 1])
         later = far
     return result
 
@@ -194,18 +190,15 @@
     users, factor = in_hbm(solved_users), in_hbm(solved_factor)
 
     far_own, own, far_sent, sent = product(place, users, factor, sizes)
-    far_other = shifted(far_sent, "core", 1)
-    sent, far_other = lax.optimization_barrier((sent, far_other))
-    far = far_own + far_other
+    other = shifted(far_sent, "core", 1)
+    sent, other = lax.optimization_barrier((sent, other))
+    far = in_pieces(far_own + other, "x", 2)
     near = own + shifted(sent, "core", 1)
-    cut = far.shape[0] // 2
-    up = shifted(far[:cut], "x", 1)
-    down = shifted(far[cut:], "x", -1)
-    up = shifted(jnp.concatenate([near[0, :cut] + up, near[0, cut:]]), "x", 1)
-    down = shifted(jnp.concatenate([near[1, :cut], near[1, cut:] + down]), "x", -1)
+    up = in_pieces(near[0], "x", 1)
+    down = in_pieces(near[1], "x", -1)
     weights = hop_weights(diag_inverse, coupling)
     home, weights = lax.optimization_barrier((near[2], weights))
-    along_z = home + up + down
+    along_z = jnp.concatenate([part + f + u + d for part, f, u, d in zip(jnp.split(home, 2), far, up, down)])
     residue = right_side.T - reduced_over_z(along_z)
     return chain(position, residue, weights).T
 

time: 79.8 us -> 88.2 us (1.11); the launches traced: 79.3 us -> 86.5 us
  other arithmetic: 0.82 us -> 4.16 us
  starting transfers between devices: 27.7 us -> 30.1 us
  waiting for transfers between devices: 34.1 us -> 35.9 us
  Pallas kernels: 14.7 us -> 13.8 us
    ppermute x18 -> x20, starting transfers between devices: 27.7 us -> 30.1 us  [shifted(): lax.ppermute(value, axis, [(i, (i + by) % peers) for i in range(peers)])]
    ppermute x18 -> x20, waiting for transfers between devices: 34.1 us -> 35.9 us  [shifted(): lax.ppermute(value, axis, [(i, (i + by) % peers) for i in range(peers)])]
    pallas_call x1, Pallas kernels: 3.81 us -> 2.9 us  [hop_weights(): pl.pallas_call(weights_body, out_shape=[jax.ShapeDtypeStruct((block, bloc...]
    sub x1, other arithmetic: 0.03 us -> 0.93 us  [on_device(): residue = right_side.T - reduced_over_z(along_z)]
    unnamed x10 -> x14, local copies, waits for them, and re-layouts: 1.61 us -> 2.1 us
  transfers between devices with their start and end apart: 18 -> 20, of which waited for: 10 -> 13; matrix products, arithmetic and copies ran while one was open for 1% -> 4% of each run, Pallas kernels for 6% -> 5%
where the time goes in v6:
time: 88.2 us; the launch traced here: 86.5 us
  waiting for transfers between devices  35.9 us (41%)
  starting transfers between devices  30.1 us (34%)
  Pallas kernels  13.8 us (16%)
  other arithmetic  4.16 us (5%)
  local copies, waits for them, and re-layouts  2.38 us (3%)
    ppermute x20, waiting for transfers between devices, shifted(): lax.ppermute(value, axis, [(i, (i + by) % peers) for i in range(peers)])  35.9 us
    ppermute x20, starting transfers between devices, shifted(): lax.ppermute(value, axis, [(i, (i + by) % peers) for i in range(peers)])  30.1 us
    pallas_call x1, Pallas kernels, product(): pl.pallas_call(functools.partial(product_body, n_z, n_core), grid_spec=pl...  8.62 us
    pallas_call x1, Pallas kernels, hop_weights(): pl.pallas_call(weights_body, out_shape=[jax.ShapeDtypeStruct((block, bloc...  2.9 us
    pallas_call x6, Pallas kernels, applied(): pl.pallas_call(functools.partial(apply_body, [group for group, _ in value...  2.29 us
    unnamed x14, local copies, waits for them, and re-layouts  2.1 us
  transfers between devices with their start and end apart: 20, of which 13 were waited for; matrix products, arithmetic and copies ran while one was open for 4% of the time, Pallas kernels for 5%

profile of v6, /device:TPU:32, one launch (start us, length us, event | category | flops | bytes accessed | tf_op | source)
XLA Modules:
  0.0 86.5 jit_solution(2235133720339888865)
XLA Ops:
  0.0 0.1 stack.27.place
  0.1 8.6 %shard_map.55 = (f32[8,32,512]{2,1,0:T(8,128)S(1)}, f32[3,8,32,512]{3,2,1,0:T(8,128)S(1)}, f32[8,32,512]{2,1,0:T(8,128)S(1)}, f32[3,8,32,512]{3,2,1,0:T(8,128)S(1)}) custom-call(s32[6]{0:T(128)S(1)} %stack.27.place, f32[768,2048]{1,0:T(8,128)} %users.1, f32[512,768]{1,0:T(8,128)} %factor.1), custom_call_target="tpu_custom_call" | custom-call | flops 4831838208 | bytes 12058624 | tf_op jit(solution)/shard_map/pallas_call | solution.py:81
  8.7 0.1 collective-permute-start
  8.8 1.9 %collective-permute-done = f32[8,32,512]{2,1,0:T(8,128)S(1)} collective-permute-done((f32[8,32,512]{2,1,0:T(8,128)S(1)}, f32[8,32,512]{2,1,0:T(8,128)S(1)}, u32[]{:S(2)}, u32[]{:S(2)}) %collective-permute-start) | collective-permute-done | bytes 524320 | tf_op jit(solution)/shard_map/ppermute | solution.py:16
  10.7 0.1 collective-permute-start.1
  10.8 0.1 add.78
  11.0 3.1 %collective-permute-start.2 = (f32[4,32,512]{2,1,0:T(8,128)S(1)}, f32[4,32,512]{2,1,0:T(8,128)S(1)}, u32[]{:S(2)}, u32[]{:S(2)}) collective-permute-start(f32[4,32,512]{2,1,0:T(8,128)S(1)} %get-tuple-element.59), channel_id=1, source_target_pairs={{0,32},{16,48},{32,0},{48,16},{1,33},{17,49},{33,1},{49,17},{2,34}... | collective-permute-start | bytes 786440 | tf_op jit(solution)/shard_map/ppermute | solution.py:16
  14.1 0.5 collective-permute-start.5
  14.6 0.0 collective-permute-done.1
  14.6 0.3 add.77
  15.0 0.0 copy-start.5
  15.0 0.1 slice_bitcast_fusion.4
  15.1 2.8 %collective-permute-start.4 = (f32[4,32,512]{2,1,0:T(8,128)S(1)}, f32[4,32,512]{2,1,0:T(8,128)S(1)}, u32[]{:S(2)}, u32[]{:S(2)}) collective-permute-start(f32[4,32,512]{2,1,0:T(8,128)S(1)} %get-tuple-element.54), channel_id=1, source_target_pairs={{0,48},{16,0},{32,16},{48,32},{1,49},{17,1},{33,17},{49,33},{2,50}... | collective-permute-start | bytes 786440 | tf_op jit(solution)/shard_map/ppermute | solution.py:16
  17.9 0.0 collective-permute-start.3
  17.9 3.2 %collective-permute-start.7 = (f32[4,32,512]{2,1,0:T(8,128)S(1)}, f32[4,32,512]{2,1,0:T(8,128)S(1)}, u32[]{:S(2)}, u32[]{:S(2)}) collective-permute-start(f32[4,32,512]{2,1,0:T(8,128)S(1)} %get-tuple-element.52), channel_id=1, source_target_pairs={{0,48},{16,0},{32,16},{48,32},{1,49},{17,1},{33,17},{49,33},{2,50}... | collective-permute-start | bytes 786440 | tf_op jit(solution)/shard_map/ppermute | solution.py:16
  21.1 0.6 collective-permute-done.2
  21.8 1.5 %collective-permute-start.6 = (f32[4,32,512]{2,1,0:T(8,128)S(1)}, f32[4,32,512]{2,1,0:T(8,128)S(1)}, u32[]{:S(2)}, u32[]{:S(2)}) collective-permute-start(f32[4,32,512]{2,1,0:T(8,128)S(1)} %get-tuple-element.53), channel_id=1, source_target_pairs={{0,16},{16,32},{32,48},{48,0},{1,17},{17,33},{33,49},{49,1},{2,18}... | collective-permute-start | bytes 786440 | tf_op jit(solution)/shard_map/ppermute | solution.py:16
  23.3 0.0 copy-done.5
  23.3 2.9 %shard_map.56 = (bf16[512,512]{1,0:T(8,128)(2,1)S(1)}, bf16[512,512]{1,0:T(8,128)(2,1)S(1)}, bf16[512,512]{1,0:T(8,128)(2,1)S(1)}, bf16[512,512]{1,0:T(8,128)(2,...) custom-call(f32[512,512]{1,0:T(8,128)S(1)} %copy-done.5, ...), custom_call_target="tpu_custom_call" | custom-call | flops 2415919104 | bytes 8388608 | tf_op jit(solution)/shard_map/pallas_call | solution.py:113
  26.3 1.1 %collective-permute-done.5 = f32[4,32,512]{2,1,0:T(8,128)S(1)} collective-permute-done((f32[4,32,512]{2,1,0:T(8,128)S(1)}, f32[4,32,512]{2,1,0:T(8,128)S(1)}, u32[]{:S(2)}, u32[]{:S(2)}) %collective-permute-start.5) | collective-permute-done | bytes 262176 | tf_op jit(solution)/shard_map/ppermute | solution.py:16
  27.4 5.7 %collective-permute-done.4 = f32[4,32,512]{2,1,0:T(8,128)S(1)} collective-permute-done((f32[4,32,512]{2,1,0:T(8,128)S(1)}, f32[4,32,512]{2,1,0:T(8,128)S(1)}, u32[]{:S(2)}, u32[]{:S(2)}) %collective-permute-start.4) | collective-permute-done | bytes 262176 | tf_op jit(solution)/shard_map/ppermute | solution.py:16
  33.1 0.0 collective-permute-done.3
  33.1 5.1 %collective-permute-done.7 = f32[4,32,512]{2,1,0:T(8,128)S(1)} collective-permute-done((f32[4,32,512]{2,1,0:T(8,128)S(1)}, f32[4,32,512]{2,1,0:T(8,128)S(1)}, u32[]{:S(2)}, u32[]{:S(2)}) %collective-permute-start.7) | collective-permute-done | bytes 262176 | tf_op jit(solution)/shard_map/ppermute | solution.py:16
  38.1 0.0 collective-permute-done.6
  38.1 0.2 add_add_fusion.1
  38.4 0.0 copy-done
  38.4 0.0 copy-start.6
  38.5 5.5 %collective-permute-start.10 = (f32[48,512]{1,0:T(8,128)S(1)}, f32[48,512]{1,0:T(8,128)S(1)}, u32[]{:S(2)}, u32[]{:S(2)}) collective-permute-start(f32[48,512]{1,0:T(8,128)S(1)} %get-tuple-element.56), channel_id=1, source_target_pairs={{0,12},{2,14},{4,0},{6,2},{8,4},{10,6},{12,8},{14,10},{1,13},{3,15... | collective-permute-start | bytes 294920 | tf_op jit(solution)/shard_map/ppermute | solution.py:16
  44.0 0.0 collective-permute-start.8
  44.0 3.7 %collective-permute-done.10 = f32[48,512]{1,0:T(8,128)S(1)} collective-permute-done((f32[48,512]{1,0:T(8,128)S(1)}, f32[48,512]{1,0:T(8,128)S(1)}, u32[]{:S(2)}, u32[]{:S(2)}) %collective-permute-start.10) | collective-permute-done | bytes 98336 | tf_op jit(solution)/shard_map/ppermute | solution.py:16
  47.7 0.6 slice_add_fusion
  48.3 0.4 collective-permute-start.13
  48.7 3.8 %collective-permute-done.8 = f32[48,512]{1,0:T(8,128)S(1)} collective-permute-done((f32[48,512]{1,0:T(8,128)S(1)}, f32[48,512]{1,0:T(8,128)S(1)}, u32[]{:S(2)}, u32[]{:S(2)}) %collective-permute-start.8) | collective-permute-done | bytes 98336 | tf_op jit(solution)/shard_map/ppermute | solution.py:16
  52.5 0.6 slice_add_fusion.1
  53.1 0.0 collective-permute-start.12
  53.1 0.6 pad_maximum_fusion.2
  53.7 3.7 %collective-permute-start.11 = (f32[32,512]{1,0:T(8,128)}, f32[32,512]{1,0:T(8,128)}, u32[]{:S(2)}, u32[]{:S(2)}) collective-permute-start(f32[32,512]{1,0:T(8,128)} %pad_maximum_fusion.2), channel_id=1, source_target_pairs={{0,12},{2,14},{4,0},{6,2},{8,4},{10,6},{12,8},{14,10},{1,13},{3,15... | collective-permute-start | bytes 196616 | tf_op jit(solution)/shard_map/ppermute | solution.py:16
  57.5 0.6 pad_maximum_fusion.1
  58.1 0.0 collective-permute-start.9
  58.1 0.0 collective-permute-done.13
  58.1 0.0 collective-permute-done.12
  58.1 1.6 %collective-permute-done.11 = f32[32,512]{1,0:T(8,128)} collective-permute-done((f32[32,512]{1,0:T(8,128)}, f32[32,512]{1,0:T(8,128)}, u32[]{:S(2)}, u32[]{:S(2)}) %collective-permute-start.11) | collective-permute-done | bytes 65568 | tf_op jit(solution)/shard_map/ppermute | solution.py:16
  59.7 5.1 %collective-permute-done.9 = f32[32,512]{1,0:T(8,128)} collective-permute-done((f32[32,512]{1,0:T(8,128)}, f32[32,512]{1,0:T(8,128)}, u32[]{:S(2)}, u32[]{:S(2)}) %collective-permute-start.9) | collective-permute-done | bytes 65568 | tf_op jit(solution)/shard_map/ppermute | solution.py:16
  64.8 0.9 %fusion.4.refs_0_ = f32[32,512]{1,0:T(8,128)S(1)} fusion(f32[32,512]{1,0:T(8,128)S(1)} %collective-permute-done.13, f32[32,512]{1,0:T(8,128)} %collective-permute-done.12, f32[32,512]{1,0:T(8,128)} %collective-permute-done.11, f32[32,512]{1,0:T(8,128)} %collective-permute-done.9, f32[4,32,512]{2,1,0:T(8,128)S(1)} %get-tuple-element.57, ...), kind=kLoop, calls=%fused_computation.17 | loop fusion | flops 81920 | bytes 458752 | tf_op jit(solution)/shard_map/sub | solution.py:202
  65.7 1.0 %copy-done.1 = bf16[512,512]{1,0:T(8,128)(2,1)S(1)} copy-done((bf16[512,512]{1,0:T(8,128)(2,1)S(1)}, bf16[512,512]{1,0:T(8,128)(2,1)}, u32[]{:S(2)}) %copy-start.1) | copy-done | bytes 524312
  66.8 1.0 %copy-done.3 = bf16[512,512]{1,0:T(8,128)(2,1)S(1)} copy-done((bf16[512,512]{1,0:T(8,128)(2,1)S(1)}, bf16[512,512]{1,0:T(8,128)(2,1)}, u32[]{:S(2)}) %copy-start.3) | copy-done | bytes 524312
  67.8 0.3 shard_map.57.refs_1_
  68.1 1.7 %collective-permute-start.14 = (f32[32,512]{1,0:T(8,128)S(1)}, f32[32,512]{1,0:T(8,128)S(1)}, u32[]{:S(2)}, u32[]{:S(2)}) collective-permute-start(f32[32,512]{1,0:T(8,128)S(1)} %shard_map.57.refs_1_), channel_id=1, source_target_pairs={{0,64},{64,128},{128,192},{192,0},{1,65},{65,129},{129,193},{193,1... | collective-permute-start | bytes 196616 | tf_op jit(solution)/shard_map/ppermute | solution.py:16
  69.8 2.9 %collective-permute-start.16 = (f32[32,512]{1,0:T(8,128)S(1)}, f32[32,512]{1,0:T(8,128)S(1)}, u32[]{:S(2)}, u32[]{:S(2)}) collective-permute-start(f32[32,512]{1,0:T(8,128)S(1)} %shard_map.57.refs_1_), channel_id=1, source_target_pairs={{0,128},{64,192},{128,0},{192,64},{1,129},{65,193},{129,1},{193,65... | collective-permute-start | bytes 196616 | tf_op jit(solution)/shard_map/ppermute | solution.py:16
  72.7 1.3 %collective-permute-start.17 = (f32[32,512]{1,0:T(8,128)S(1)}, f32[32,512]{1,0:T(8,128)S(1)}, u32[]{:S(2)}, u32[]{:S(2)}) collective-permute-start(f32[32,512]{1,0:T(8,128)S(1)} %shard_map.57.refs_1_), channel_id=1, source_target_pairs={{0,192},{64,0},{128,64},{192,128},{1,193},{65,1},{129,65},{193,129... | collective-permute-start | bytes 196616 | tf_op jit(solution)/shard_map/ppermute | solution.py:16
  74.1 0.0 collective-permute-done.14.refs_0_
  74.1 0.3 shard_map.58.refs_2_
  74.4 0.7 collective-permute-start.15
  75.0 2.3 %collective-permute-start.19 = (f32[32,512]{1,0:T(8,128)S(1)}, f32[32,512]{1,0:T(8,128)S(1)}, u32[]{:S(2)}, u32[]{:S(2)}) collective-permute-start(f32[32,512]{1,0:T(8,128)S(1)} %shard_map.58.refs_2_), channel_id=1, source_target_pairs={{0,128},{64,192},{128,0},{192,64},{1,129},{65,193},{129,1},{193,65... | collective-permute-start | bytes 196616 | tf_op jit(solution)/shard_map/ppermute | solution.py:16
  77.3 0.0 collective-permute-done.16.refs_0_
  77.3 0.3 collective-permute-done.17.refs_1_
  77.6 0.3 shard_map.59.refs_1_
  77.9 1.9 %collective-permute-done.15.refs_0_ = f32[32,512]{1,0:T(8,128)S(1)} collective-permute-done((f32[32,512]{1,0:T(8,128)S(1)}, f32[32,512]{1,0:T(8,128)S(1)}, u32[]{:S(2)}, u32[]{:S(2)}) %collective-permute-start.15) | collective-permute-done | bytes 65568 | tf_op jit(solution)/shard_map/ppermute | solution.py:16
  79.8 0.3 shard_map.60.refs_1_
  80.1 0.0 collective-permute-start.18
  80.1 0.8 collective-permute-done.19.refs_0_
  81.0 0.3 shard_map.61.refs_1_
  81.3 4.4 %collective-permute-done.18.refs_0_ = f32[32,512]{1,0:T(8,128)S(1)} collective-permute-done((f32[32,512]{1,0:T(8,128)S(1)}, f32[32,512]{1,0:T(8,128)S(1)}, u32[]{:S(2)}, u32[]{:S(2)}) %collective-permute-start.18) | collective-permute-done | bytes 65568 | tf_op jit(solution)/shard_map/ppermute | solution.py:16
  85.6 0.9 %shard_map.62 = f32[32,512]{1,0:T(8,128)} custom-call(s32[1]{0:T(128)} %bitcast.place, f32[32,512]{1,0:T(8,128)S(1)} %collective-permute-done.18.refs_0_, f32[32,512]{1,0:T(8,128)S(1)} %shard_map.61.refs_1_, bf16[512,512]{1,0:T(8,128)(2,1)S(1)} %get-tuple-element.49.refs_2_, bf16[512,512]{1,0:T(8,128)(2,1)S(1)} %get-tuple-element.50.refs_3_), custom_call_target="tpu_custom_call" | custom-call | tf_op jit(solution)/shard_map/pallas_call | solution.py:139
  (17 shorter events, 0.2 us)
Async XLA Ops:
  8.7 2.0 %collective-permute-start = (f32[8,32,512]{2,1,0:T(8,128)S(1)}, f32[8,32,512]{2,1,0:T(8,128)S(1)}, u32[]{:S(2)}, u32[]{:S(2)}) collective-permute-start(f32[8,32,512]{2,1,0:T(8,128)S(1)} %get-tuple-element.30), channel_id=1, source_target_pairs={{0,1},{1,0},{2,3},{3,2},{4,5},{5,4},{6,7},{7,6},{8,9},{9,8},{10,11... | collective-permute-start | bytes 1572872 | tf_op jit(solution)/shard_map/ppermute | solution.py:16
  10.7 3.9 %collective-permute-start.1 = (f32[3,8,32,512]{3,2,1,0:T(8,128)S(1)}, f32[3,8,32,512]{3,2,1,0:T(8,128)S(1)}, u32[]{:S(2)}, u32[]{:S(2)}) collective-permute-start(f32[3,8,32,512]{3,2,1,0:T(8,128)S(1)} %get-tuple-element.31), channel_id=1, source_target_pairs={{0,1},{1,0},{2,3},{3,2},{4,5},{5,4},{6,7},{7,6},{8,9},{9,8},{10,11... | collective-permute-start | bytes 4718600 | tf_op jit(solution)/shard_map/ppermute | solution.py:16
  11.0 10.8 %collective-permute-start.2 = (f32[4,32,512]{2,1,0:T(8,128)S(1)}, f32[4,32,512]{2,1,0:T(8,128)S(1)}, u32[]{:S(2)}, u32[]{:S(2)}) collective-permute-start(f32[4,32,512]{2,1,0:T(8,128)S(1)} %get-tuple-element.59), channel_id=1, source_target_pairs={{0,32},{16,48},{32,0},{48,16},{1,33},{17,49},{33,1},{49,17},{2,34}... | collective-permute-start | bytes 786440 | tf_op jit(solution)/shard_map/ppermute | solution.py:16
  14.1 13.3 %collective-permute-start.5 = (f32[4,32,512]{2,1,0:T(8,128)S(1)}, f32[4,32,512]{2,1,0:T(8,128)S(1)}, u32[]{:S(2)}, u32[]{:S(2)}) collective-permute-start(f32[4,32,512]{2,1,0:T(8,128)S(1)} %get-tuple-element.60), channel_id=1, source_target_pairs={{0,32},{16,48},{32,0},{48,16},{1,33},{17,49},{33,1},{49,17},{2,34}... | collective-permute-start | bytes 786440 | tf_op jit(solution)/shard_map/ppermute | solution.py:16
  14.6 8.7 %copy-start.4 = (f32[512,1536]{1,0:T(8,128)S(1)}, f32[512,1536]{1,0:T(8,128)}, u32[]{:S(2)}) copy-start(f32[512,1536]{1,0:T(8,128)} %coupling.1) | copy-start | bytes 9437188
  15.0 8.3 %copy-start.5 = (f32[512,512]{1,0:T(8,128)S(1)}, f32[512,512]{1,0:T(8,128)}, u32[]{:S(2)}) copy-start(f32[512,512]{1,0:T(8,128)} %diag.1) | copy-start | bytes 3145732
  15.1 18.0 %collective-permute-start.4 = (f32[4,32,512]{2,1,0:T(8,128)S(1)}, f32[4,32,512]{2,1,0:T(8,128)S(1)}, u32[]{:S(2)}, u32[]{:S(2)}) collective-permute-start(f32[4,32,512]{2,1,0:T(8,128)S(1)} %get-tuple-element.54), channel_id=1, source_target_pairs={{0,48},{16,0},{32,16},{48,32},{1,49},{17,1},{33,17},{49,33},{2,50}... | collective-permute-start | bytes 786440 | tf_op jit(solution)/shard_map/ppermute | solution.py:16
  17.9 15.2 %collective-permute-start.3 = (f32[4,32,512]{2,1,0:T(8,128)S(1)}, f32[4,32,512]{2,1,0:T(8,128)S(1)}, u32[]{:S(2)}, u32[]{:S(2)}) collective-permute-start(f32[4,32,512]{2,1,0:T(8,128)S(1)} %get-tuple-element.51), channel_id=1, source_target_pairs={{0,16},{16,32},{32,48},{48,0},{1,17},{17,33},{33,49},{49,1},{2,18}... | collective-permute-start | bytes 786440 | tf_op jit(solution)/shard_map/ppermute | solution.py:16
  17.9 20.2 %collective-permute-start.7 = (f32[4,32,512]{2,1,0:T(8,128)S(1)}, f32[4,32,512]{2,1,0:T(8,128)S(1)}, u32[]{:S(2)}, u32[]{:S(2)}) collective-permute-start(f32[4,32,512]{2,1,0:T(8,128)S(1)} %get-tuple-element.52), channel_id=1, source_target_pairs={{0,48},{16,0},{32,16},{48,32},{1,49},{17,1},{33,17},{49,33},{2,50}... | collective-permute-start | bytes 786440 | tf_op jit(solution)/shard_map/ppermute | solution.py:16
  21.8 16.4 %collective-permute-start.6 = (f32[4,32,512]{2,1,0:T(8,128)S(1)}, f32[4,32,512]{2,1,0:T(8,128)S(1)}, u32[]{:S(2)}, u32[]{:S(2)}) collective-permute-start(f32[4,32,512]{2,1,0:T(8,128)S(1)} %get-tuple-element.53), channel_id=1, source_target_pairs={{0,16},{16,32},{32,48},{48,0},{1,17},{17,33},{33,49},{49,1},{2,18}... | collective-permute-start | bytes 786440 | tf_op jit(solution)/shard_map/ppermute | solution.py:16
  26.2 12.2 %copy-start = (bf16[512,512]{1,0:T(8,128)(2,1)}, bf16[512,512]{1,0:T(8,128)(2,1)S(1)}, u32[]{:S(2)}) copy-start(bf16[512,512]{1,0:T(8,128)(2,1)S(1)} %get-tuple-element.43.refs_2_) | copy-start | bytes 1572868
  26.2 12.2 %copy-start.2 = (bf16[512,512]{1,0:T(8,128)(2,1)}, bf16[512,512]{1,0:T(8,128)(2,1)S(1)}, u32[]{:S(2)}) copy-start(bf16[512,512]{1,0:T(8,128)(2,1)S(1)} %get-tuple-element.44.refs_3_) | copy-start | bytes 1572868
  38.4 26.4 %copy-start.6 = (f32[512,32]{0,1:T(8,128)S(1)}, f32[512,32]{0,1:T(8,128)}, u32[]{:S(2)}) copy-start(f32[512,32]{0,1:T(8,128)} %param.5) | copy-start | bytes 196612
  38.5 9.2 %collective-permute-start.10 = (f32[48,512]{1,0:T(8,128)S(1)}, f32[48,512]{1,0:T(8,128)S(1)}, u32[]{:S(2)}, u32[]{:S(2)}) collective-permute-start(f32[48,512]{1,0:T(8,128)S(1)} %get-tuple-element.56), channel_id=1, source_target_pairs={{0,12},{2,14},{4,0},{6,2},{8,4},{10,6},{12,8},{14,10},{1,13},{3,15... | collective-permute-start | bytes 294920 | tf_op jit(solution)/shard_map/ppermute | solution.py:16
  44.0 8.5 %collective-permute-start.8 = (f32[48,512]{1,0:T(8,128)S(1)}, f32[48,512]{1,0:T(8,128)S(1)}, u32[]{:S(2)}, u32[]{:S(2)}) collective-permute-start(f32[48,512]{1,0:T(8,128)S(1)} %get-tuple-element.55), channel_id=1, source_target_pairs={{0,4},{2,6},{4,8},{6,10},{8,12},{10,14},{12,0},{14,2},{1,5},{3,7},... | collective-permute-start | bytes 294920 | tf_op jit(solution)/shard_map/ppermute | solution.py:16
  48.3 9.8 %collective-permute-start.13 = (f32[32,512]{1,0:T(8,128)}, f32[32,512]{1,0:T(8,128)S(1)}, u32[]{:S(2)}, u32[]{:S(2)}) collective-permute-start(f32[32,512]{1,0:T(8,128)} %slice_add_fusion), channel_id=1, source_target_pairs={{0,14},{2,0},{4,2},{6,4},{8,6},{10,8},{12,10},{14,12},{1,15},{3,1}... | collective-permute-start | bytes 196616 | tf_op jit(solution)/shard_map/ppermute | solution.py:16
  53.1 5.0 %collective-permute-start.12 = (f32[32,512]{1,0:T(8,128)}, f32[32,512]{1,0:T(8,128)}, u32[]{:S(2)}, u32[]{:S(2)}) collective-permute-start(f32[32,512]{1,0:T(8,128)} %slice_add_fusion.1), channel_id=1, source_target_pairs={{0,2},{2,4},{4,6},{6,8},{8,10},{10,12},{12,14},{14,0},{1,3},{3,5},... | collective-permute-start | bytes 196616 | tf_op jit(solution)/shard_map/ppermute | solution.py:16
  53.7 5.9 %collective-permute-start.11 = (f32[32,512]{1,0:T(8,128)}, f32[32,512]{1,0:T(8,128)}, u32[]{:S(2)}, u32[]{:S(2)}) collective-permute-start(f32[32,512]{1,0:T(8,128)} %pad_maximum_fusion.2), channel_id=1, source_target_pairs={{0,12},{2,14},{4,0},{6,2},{8,4},{10,6},{12,8},{14,10},{1,13},{3,15... | collective-permute-start | bytes 196616 | tf_op jit(solution)/shard_map/ppermute | solution.py:16
  58.1 6.7 %collective-permute-start.9 = (f32[32,512]{1,0:T(8,128)}, f32[32,512]{1,0:T(8,128)}, u32[]{:S(2)}, u32[]{:S(2)}) collective-permute-start(f32[32,512]{1,0:T(8,128)} %pad_maximum_fusion.1), channel_id=1, source_target_pairs={{0,4},{2,6},{4,8},{6,10},{8,12},{10,14},{12,0},{14,2},{1,5},{3,7},... | collective-permute-start | bytes 196616 | tf_op jit(solution)/shard_map/ppermute | solution.py:16
  65.7 1.0 %copy-start.1 = (bf16[512,512]{1,0:T(8,128)(2,1)S(1)}, bf16[512,512]{1,0:T(8,128)(2,1)}, u32[]{:S(2)}) copy-start(bf16[512,512]{1,0:T(8,128)(2,1)} %copy-done) | copy-start | bytes 1572868
  66.8 1.0 %copy-start.3 = (bf16[512,512]{1,0:T(8,128)(2,1)S(1)}, bf16[512,512]{1,0:T(8,128)(2,1)}, u32[]{:S(2)}) copy-start(bf16[512,512]{1,0:T(8,128)(2,1)} %copy-done.2) | copy-start | bytes 1572868
  68.1 6.0 %collective-permute-start.14 = (f32[32,512]{1,0:T(8,128)S(1)}, f32[32,512]{1,0:T(8,128)S(1)}, u32[]{:S(2)}, u32[]{:S(2)}) collective-permute-start(f32[32,512]{1,0:T(8,128)S(1)} %shard_map.57.refs_1_), channel_id=1, source_target_pairs={{0,64},{64,128},{128,192},{192,0},{1,65},{65,129},{129,193},{193,1... | collective-permute-start | bytes 196616 | tf_op jit(solution)/shard_map/ppermute | solution.py:16
  69.8 7.5 %collective-permute-start.16 = (f32[32,512]{1,0:T(8,128)S(1)}, f32[32,512]{1,0:T(8,128)S(1)}, u32[]{:S(2)}, u32[]{:S(2)}) collective-permute-start(f32[32,512]{1,0:T(8,128)S(1)} %shard_map.57.refs_1_), channel_id=1, source_target_pairs={{0,128},{64,192},{128,0},{192,64},{1,129},{65,193},{129,1},{193,65... | collective-permute-start | bytes 196616 | tf_op jit(solution)/shard_map/ppermute | solution.py:16
  72.7 4.9 %collective-permute-start.17 = (f32[32,512]{1,0:T(8,128)S(1)}, f32[32,512]{1,0:T(8,128)S(1)}, u32[]{:S(2)}, u32[]{:S(2)}) collective-permute-start(f32[32,512]{1,0:T(8,128)S(1)} %shard_map.57.refs_1_), channel_id=1, source_target_pairs={{0,192},{64,0},{128,64},{192,128},{1,193},{65,1},{129,65},{193,129... | collective-permute-start | bytes 196616 | tf_op jit(solution)/shard_map/ppermute | solution.py:16
  74.4 5.5 %collective-permute-start.15 = (f32[32,512]{1,0:T(8,128)S(1)}, f32[32,512]{1,0:T(8,128)S(1)}, u32[]{:S(2)}, u32[]{:S(2)}) collective-permute-start(f32[32,512]{1,0:T(8,128)S(1)} %shard_map.58.refs_2_), channel_id=1, source_target_pairs={{0,64},{64,128},{128,192},{192,0},{1,65},{65,129},{129,193},{193,1... | collective-permute-start | bytes 196616 | tf_op jit(solution)/shard_map/ppermute | solution.py:16
  75.0 5.9 %collective-permute-start.19 = (f32[32,512]{1,0:T(8,128)S(1)}, f32[32,512]{1,0:T(8,128)S(1)}, u32[]{:S(2)}, u32[]{:S(2)}) collective-permute-start(f32[32,512]{1,0:T(8,128)S(1)} %shard_map.58.refs_2_), channel_id=1, source_target_pairs={{0,128},{64,192},{128,0},{192,64},{1,129},{65,193},{129,1},{193,65... | collective-permute-start | bytes 196616 | tf_op jit(solution)/shard_map/ppermute | solution.py:16
  80.1 5.5 %collective-permute-start.18 = (f32[32,512]{1,0:T(8,128)S(1)}, f32[32,512]{1,0:T(8,128)S(1)}, u32[]{:S(2)}, u32[]{:S(2)}) collective-permute-start(f32[32,512]{1,0:T(8,128)S(1)} %shard_map.60.refs_1_), channel_id=1, source_target_pairs={{0,64},{64,128},{128,192},{192,0},{1,65},{65,129},{129,193},{193,1... | collective-permute-start | bytes 196616 | tf_op jit(solution)/shard_map/ppermute | solution.py:16

commit v7 on v4

--- a/solution.py
+++ b/solution.py
@@ -201,11 +201,12 @@
     cut = far.shape[0] // 2
     up = shifted(far[:cut], "x", 1)
     down = shifted(far[cut:], "x", -1)
-    up = shifted(jnp.concatenate([near[0, :cut] + up, near[0, cut:]]), "x", 1)
-    down = shifted(jnp.concatenate([near[1, :cut], near[1, cut:] + down]), "x", -1)
+    ups = [shifted(half, "x", 1) for half in (near[0, :cut] + up, near[0, cut:])]
+    downs = [shifted(half, "x", -1) for half in (near[1, :cut], near[1, cut:] + down)]
     weights = hop_weights(diag_inverse, coupling)
     home, weights = lax.optimization_barrier((near[2], weights))
-    along_z = home + up + down
+    sums = [home[:cut] + ups[0] + downs[0], home[cut:] + ups[1] + downs[1]]
+    along_z = jnp.concatenate(sums)
     residue = right_side.T - reduced_over_z(along_z)
     return chain(position, residue, weights).T
 

time: 79.8 us -> 80.8 us (1.013)
    ppermute x18 -> x20, waiting for transfers between devices: 34.1 us -> 34.9 us  [shifted(): lax.ppermute(value, axis, [(i, (i + by) % peers) for i in range(peers)])]
    ppermute x18 -> x20, starting transfers between devices: 27.7 us -> 28.2 us  [shifted(): lax.ppermute(value, axis, [(i, (i + by) % peers) for i in range(peers)])]
  transfers between devices with their start and end apart: 18 -> 20, of which waited for: 10 -> 13; matrix products, arithmetic and copies ran while one was open for 1% -> 1% of each run, Pallas kernels for 6% -> 6%
where the time goes in v7:
time: 80.8 us; the launch traced here: 80.7 us
  waiting for transfers between devices  34.9 us (43%)
  starting transfers between devices  28.2 us (35%)
  Pallas kernels  14.7 us (18%)
  local copies, waits for them, and re-layouts  1.83 us (2%)
  other arithmetic  0.86 us (1%)
    ppermute x20, waiting for transfers between devices, shifted(): lax.ppermute(value, axis, [(i, (i + by) % peers) for i in range(peers)])  34.9 us
    ppermute x20, starting transfers between devices, shifted(): lax.ppermute(value, axis, [(i, (i + by) % peers) for i in range(peers)])  28.2 us
    pallas_call x1, Pallas kernels, product(): pl.pallas_call(functools.partial(product_body, n_z, n_core), grid_spec=pl...  8.62 us
    pallas_call x1, Pallas kernels, hop_weights(): pl.pallas_call(weights_body, grid=(count,), in_specs=[pl.BlockSpec((block...  3.81 us
    pallas_call x6, Pallas kernels, applied(): pl.pallas_call(functools.partial(apply_body, [group for group, _ in value...  2.29 us
  transfers between devices with their start and end apart: 20, of which 13 were waited for; matrix products, arithmetic and copies ran while one was open for 1% of the time, Pallas kernels for 6%

profile of v7, /device:TPU:32, one launch (start us, length us, event | category | flops | bytes accessed | tf_op | source)
XLA Modules:
  0.0 80.7 jit_solution(1008866233599520096)
XLA Ops:
  0.0 0.1 stack.27.place
  0.1 8.6 %shard_map.55 = (f32[8,32,512]{2,1,0:T(8,128)S(1)}, f32[3,8,32,512]{3,2,1,0:T(8,128)S(1)}, f32[8,32,512]{2,1,0:T(8,128)S(1)}, f32[3,8,32,512]{3,2,1,0:T(8,128)S(1)}) custom-call(s32[6]{0:T(128)S(1)} %stack.27.place, f32[768,2048]{1,0:T(8,128)} %users.1, f32[512,768]{1,0:T(8,128)} %factor.1), custom_call_target="tpu_custom_call" | custom-call | flops 4831838208 | bytes 12058624 | tf_op jit(solution)/shard_map/pallas_call | solution.py:77
  8.7 0.1 collective-permute-start
  8.8 1.9 %collective-permute-done = f32[8,32,512]{2,1,0:T(8,128)S(1)} collective-permute-done((f32[8,32,512]{2,1,0:T(8,128)S(1)}, f32[8,32,512]{2,1,0:T(8,128)S(1)}, u32[]{:S(2)}, u32[]{:S(2)}) %collective-permute-start) | collective-permute-done | bytes 524320 | tf_op jit(solution)/shard_map/ppermute | solution.py:16
  10.7 0.1 collective-permute-start.1
  10.8 0.1 add.78
  11.0 1.6 %collective-permute-start.2 = (f32[4,32,512]{2,1,0:T(8,128)S(1)}, f32[4,32,512]{2,1,0:T(8,128)S(1)}, u32[]{:S(2)}, u32[]{:S(2)}) collective-permute-start(f32[4,32,512]{2,1,0:T(8,128)S(1)} %get-tuple-element.35), channel_id=1, source_target_pairs={{0,16},{16,32},{32,48},{48,0},{1,17},{17,33},{33,49},{49,1},{2,18}... | collective-permute-start | bytes 786440 | tf_op jit(solution)/shard_map/ppermute | solution.py:16
  12.6 1.7 %collective-permute-start.6 = (f32[4,32,512]{2,1,0:T(8,128)S(1)}, f32[4,32,512]{2,1,0:T(8,128)S(1)}, u32[]{:S(2)}, u32[]{:S(2)}) collective-permute-start(f32[4,32,512]{2,1,0:T(8,128)S(1)} %get-tuple-element.36), channel_id=1, source_target_pairs={{0,48},{16,0},{32,16},{48,32},{1,49},{17,1},{33,17},{49,33},{2,50}... | collective-permute-start | bytes 786440 | tf_op jit(solution)/shard_map/ppermute | solution.py:16
  14.3 0.0 collective-permute-done.1
  14.3 0.0 copy-start.2
  14.3 0.4 add.77
  14.7 0.0 copy-start.3
  14.8 2.7 %collective-permute-start.4 = (f32[4,32,512]{2,1,0:T(8,128)S(1)}, f32[4,32,512]{2,1,0:T(8,128)S(1)}, u32[]{:S(2)}, u32[]{:S(2)}) collective-permute-start(f32[4,32,512]{2,1,0:T(8,128)S(1)} %get-tuple-element.29), channel_id=1, source_target_pairs={{0,48},{16,0},{32,16},{48,32},{1,49},{17,1},{33,17},{49,33},{2,50}... | collective-permute-start | bytes 786440 | tf_op jit(solution)/shard_map/ppermute | solution.py:16
  17.4 3.4 %collective-permute-done.2 = f32[4,32,512]{2,1,0:T(8,128)S(1)} collective-permute-done((f32[4,32,512]{2,1,0:T(8,128)S(1)}, f32[4,32,512]{2,1,0:T(8,128)S(1)}, u32[]{:S(2)}, u32[]{:S(2)}) %collective-permute-start.2) | collective-permute-done | bytes 262176 | tf_op jit(solution)/shard_map/ppermute | solution.py:16
  20.8 0.9 %collective-permute-done.6 = f32[4,32,512]{2,1,0:T(8,128)S(1)} collective-permute-done((f32[4,32,512]{2,1,0:T(8,128)S(1)}, f32[4,32,512]{2,1,0:T(8,128)S(1)}, u32[]{:S(2)}, u32[]{:S(2)}) %collective-permute-start.6) | collective-permute-done | bytes 262176 | tf_op jit(solution)/shard_map/ppermute | solution.py:16
  21.7 0.1 fusion.1
  21.8 1.6 %collective-permute-start.3 = (f32[4,32,512]{2,1,0:T(8,128)S(1)}, f32[4,32,512]{2,1,0:T(8,128)S(1)}, u32[]{:S(2)}, u32[]{:S(2)}) collective-permute-start(f32[4,32,512]{2,1,0:T(8,128)S(1)} %get-tuple-element.27), channel_id=1, source_target_pairs={{0,16},{16,32},{32,48},{48,0},{1,17},{17,33},{33,49},{49,1},{2,18}... | collective-permute-start | bytes 786440 | tf_op jit(solution)/shard_map/ppermute | solution.py:16
  23.4 1.7 %collective-permute-start.7 = (f32[4,32,512]{2,1,0:T(8,128)S(1)}, f32[4,32,512]{2,1,0:T(8,128)S(1)}, u32[]{:S(2)}, u32[]{:S(2)}) collective-permute-start(f32[4,32,512]{2,1,0:T(8,128)S(1)} %get-tuple-element.28), channel_id=1, source_target_pairs={{0,48},{16,0},{32,16},{48,32},{1,49},{17,1},{33,17},{49,33},{2,50}... | collective-permute-start | bytes 786440 | tf_op jit(solution)/shard_map/ppermute | solution.py:16
  25.1 0.3 collective-permute-start.5
  25.4 0.0 copy-done.2
  25.4 0.0 copy-done.3
  25.4 3.8 %shard_map.56 = (bf16[4,512,512]{2,1,0:T(8,128)(2,1)S(1)}, bf16[4,512,512]{2,1,0:T(8,128)(2,1)S(1)}) custom-call(f32[512,512]{1,0:T(8,128)S(1)} %copy-done.3, f32[512,1536]{1,0:T(8,128)S(1)} %copy-done.2), custom_call_target="tpu_custom_call" | custom-call | flops 2415919104 | bytes 8388608 | tf_op jit(solution)/shard_map/pallas_call | solution.py:112
  29.2 0.0 copy-start
  29.3 0.0 collective-permute-done.4
  29.3 3.0 %collective-permute-done.3 = f32[4,32,512]{2,1,0:T(8,128)S(1)} collective-permute-done((f32[4,32,512]{2,1,0:T(8,128)S(1)}, f32[4,32,512]{2,1,0:T(8,128)S(1)}, u32[]{:S(2)}, u32[]{:S(2)}) %collective-permute-start.3) | collective-permute-done | bytes 262176 | tf_op jit(solution)/shard_map/ppermute | solution.py:16
  32.3 0.0 collective-permute-done.7
  32.3 3.3 %collective-permute-done.5 = f32[4,32,512]{2,1,0:T(8,128)S(1)} collective-permute-done((f32[4,32,512]{2,1,0:T(8,128)S(1)}, f32[4,32,512]{2,1,0:T(8,128)S(1)}, u32[]{:S(2)}, u32[]{:S(2)}) %collective-permute-start.5) | collective-permute-done | bytes 262176 | tf_op jit(solution)/shard_map/ppermute | solution.py:16
  35.6 0.2 add_add_fusion.1
  35.8 0.0 copy-done
  35.8 0.0 copy-start.4
  35.9 5.5 %collective-permute-start.10 = (f32[48,512]{1,0:T(8,128)S(1)}, f32[48,512]{1,0:T(8,128)S(1)}, u32[]{:S(2)}, u32[]{:S(2)}) collective-permute-start(f32[48,512]{1,0:T(8,128)S(1)} %get-tuple-element.32), channel_id=1, source_target_pairs={{0,12},{2,14},{4,0},{6,2},{8,4},{10,6},{12,8},{14,10},{1,13},{3,15... | collective-permute-start | bytes 294920 | tf_op jit(solution)/shard_map/ppermute | solution.py:16
  41.4 0.0 collective-permute-start.8
  41.4 2.6 %collective-permute-done.10 = f32[48,512]{1,0:T(8,128)S(1)} collective-permute-done((f32[48,512]{1,0:T(8,128)S(1)}, f32[48,512]{1,0:T(8,128)S(1)}, u32[]{:S(2)}, u32[]{:S(2)}) %collective-permute-start.10) | collective-permute-done | bytes 98336 | tf_op jit(solution)/shard_map/ppermute | solution.py:16
  44.0 1.0 %collective-permute-start.13 = (f32[32,512]{1,0:T(8,128)S(1)}, f32[32,512]{1,0:T(8,128)S(1)}, u32[]{:S(2)}, u32[]{:S(2)}) collective-permute-start(f32[32,512]{1,0:T(8,128)S(1)} %slice_add_fusion), channel_id=1, source_target_pairs={{0,14},{2,0},{4,2},{6,4},{8,6},{10,8},{12,10},{14,12},{1,15},{3,1}... | collective-permute-start | bytes 196616 | tf_op jit(solution)/shard_map/ppermute | solution.py:16
  45.0 4.1 %collective-permute-done.8 = f32[48,512]{1,0:T(8,128)S(1)} collective-permute-done((f32[48,512]{1,0:T(8,128)S(1)}, f32[48,512]{1,0:T(8,128)S(1)}, u32[]{:S(2)}, u32[]{:S(2)}) %collective-permute-start.8) | collective-permute-done | bytes 98336 | tf_op jit(solution)/shard_map/ppermute | solution.py:16
  49.2 0.3 collective-permute-start.12
  49.5 3.2 %collective-permute-start.11 = (f32[32,512]{1,0:T(8,128)S(1)}, f32[32,512]{1,0:T(8,128)S(1)}, u32[]{:S(2)}, u32[]{:S(2)}) collective-permute-start(f32[32,512]{1,0:T(8,128)S(1)} %pad_maximum_fusion.2), channel_id=1, source_target_pairs={{0,12},{2,14},{4,0},{6,2},{8,4},{10,6},{12,8},{14,10},{1,13},{3,15... | collective-permute-start | bytes 196616 | tf_op jit(solution)/shard_map/ppermute | solution.py:16
  52.7 0.1 collective-permute-start.9
  52.8 0.0 collective-permute-done.13
  52.8 1.5 %collective-permute-done.12 = f32[32,512]{1,0:T(8,128)S(1)} collective-permute-done((f32[32,512]{1,0:T(8,128)S(1)}, f32[32,512]{1,0:T(8,128)S(1)}, u32[]{:S(2)}, u32[]{:S(2)}) %collective-permute-start.12) | collective-permute-done | bytes 65568 | tf_op jit(solution)/shard_map/ppermute | solution.py:16
  54.3 1.1 %collective-permute-done.11 = f32[32,512]{1,0:T(8,128)S(1)} collective-permute-done((f32[32,512]{1,0:T(8,128)S(1)}, f32[32,512]{1,0:T(8,128)S(1)}, u32[]{:S(2)}, u32[]{:S(2)}) %collective-permute-start.11) | collective-permute-done | bytes 65568 | tf_op jit(solution)/shard_map/ppermute | solution.py:16
  55.5 3.7 %collective-permute-done.9 = f32[32,512]{1,0:T(8,128)S(1)} collective-permute-done((f32[32,512]{1,0:T(8,128)S(1)}, f32[32,512]{1,0:T(8,128)S(1)}, u32[]{:S(2)}, u32[]{:S(2)}) %collective-permute-start.9) | collective-permute-done | bytes 65568 | tf_op jit(solution)/shard_map/ppermute | solution.py:16
  59.2 0.0 copy-done.4
  59.2 0.0 copy-start.1
  59.2 1.6 %copy-done.1 = bf16[4,512,512]{2,1,0:T(8,128)(2,1)S(1)} copy-done((bf16[4,512,512]{2,1,0:T(8,128)(2,1)S(1)}, bf16[4,512,512]{2,1,0:T(8,128)(2,1)}, u32[]{:S(2)}) %copy-start.1) | copy-done | bytes 2097176
  60.8 0.3 shard_map.57.refs_1_
  61.1 1.6 %collective-permute-start.14 = (f32[32,512]{1,0:T(8,128)S(1)}, f32[32,512]{1,0:T(8,128)S(1)}, u32[]{:S(2)}, u32[]{:S(2)}) collective-permute-start(f32[32,512]{1,0:T(8,128)S(1)} %shard_map.57.refs_1_), channel_id=1, source_target_pairs={{0,64},{64,128},{128,192},{192,0},{1,65},{65,129},{129,193},{193,1... | collective-permute-start | bytes 196616 | tf_op jit(solution)/shard_map/ppermute | solution.py:16
  62.7 2.9 %collective-permute-start.16 = (f32[32,512]{1,0:T(8,128)S(1)}, f32[32,512]{1,0:T(8,128)S(1)}, u32[]{:S(2)}, u32[]{:S(2)}) collective-permute-start(f32[32,512]{1,0:T(8,128)S(1)} %shard_map.57.refs_1_), channel_id=1, source_target_pairs={{0,128},{64,192},{128,0},{192,64},{1,129},{65,193},{129,1},{193,65... | collective-permute-start | bytes 196616 | tf_op jit(solution)/shard_map/ppermute | solution.py:16
  65.6 1.3 %collective-permute-start.17 = (f32[32,512]{1,0:T(8,128)S(1)}, f32[32,512]{1,0:T(8,128)S(1)}, u32[]{:S(2)}, u32[]{:S(2)}) collective-permute-start(f32[32,512]{1,0:T(8,128)S(1)} %shard_map.57.refs_1_), channel_id=1, source_target_pairs={{0,192},{64,0},{128,64},{192,128},{1,193},{65,1},{129,65},{193,129... | collective-permute-start | bytes 196616 | tf_op jit(solution)/shard_map/ppermute | solution.py:16
  67.0 0.6 collective-permute-done.14.refs_0_
  67.6 0.3 shard_map.58.refs_2_
  67.8 0.1 collective-permute-start.15
  68.0 2.2 %collective-permute-start.19 = (f32[32,512]{1,0:T(8,128)S(1)}, f32[32,512]{1,0:T(8,128)S(1)}, u32[]{:S(2)}, u32[]{:S(2)}) collective-permute-start(f32[32,512]{1,0:T(8,128)S(1)} %shard_map.58.refs_2_), channel_id=1, source_target_pairs={{0,128},{64,192},{128,0},{192,64},{1,129},{65,193},{129,1},{193,65... | collective-permute-start | bytes 196616 | tf_op jit(solution)/shard_map/ppermute | solution.py:16
  70.2 0.0 collective-permute-done.16.refs_0_
  70.2 0.0 collective-permute-done.17.refs_1_
  70.2 0.3 shard_map.59.refs_1_
  70.5 3.5 %collective-permute-done.15.refs_0_ = f32[32,512]{1,0:T(8,128)S(1)} collective-permute-done((f32[32,512]{1,0:T(8,128)S(1)}, f32[32,512]{1,0:T(8,128)S(1)}, u32[]{:S(2)}, u32[]{:S(2)}) %collective-permute-start.15) | collective-permute-done | bytes 65568 | tf_op jit(solution)/shard_map/ppermute | solution.py:16
  74.0 0.3 shard_map.60.refs_1_
  74.3 0.0 collective-permute-start.18
  74.3 0.0 collective-permute-done.19.refs_0_
  74.3 0.3 shard_map.61.refs_1_
  74.6 5.2 %collective-permute-done.18.refs_0_ = f32[32,512]{1,0:T(8,128)S(1)} collective-permute-done((f32[32,512]{1,0:T(8,128)S(1)}, f32[32,512]{1,0:T(8,128)S(1)}, u32[]{:S(2)}, u32[]{:S(2)}) %collective-permute-start.18) | collective-permute-done | bytes 65568 | tf_op jit(solution)/shard_map/ppermute | solution.py:16
  79.8 0.9 %shard_map.62 = f32[32,512]{1,0:T(8,128)} custom-call(s32[1]{0:T(128)} %bitcast.place, f32[32,512]{1,0:T(8,128)S(1)} %collective-permute-done.18.refs_0_, f32[32,512]{1,0:T(8,128)S(1)} %shard_map.61.refs_1_, bf16[4,512,512]{2,1,0:T(8,128)(2,1)S(1)} %get-tuple-element.25.refs_2_.refs_3_, bf16[4,512,512]{2,1,0:T(8,128)(2,1)S(1)} %copy-done.1), custom_call_target="tpu_custom_call" | custom-call | tf_op jit(solution)/shard_map/pallas_call | solution.py:143
  (15 shorter events, 0.3 us)
Async XLA Ops:
  8.7 2.0 %collective-permute-start = (f32[8,32,512]{2,1,0:T(8,128)S(1)}, f32[8,32,512]{2,1,0:T(8,128)S(1)}, u32[]{:S(2)}, u32[]{:S(2)}) collective-permute-start(f32[8,32,512]{2,1,0:T(8,128)S(1)} %get-tuple-element.18), channel_id=1, source_target_pairs={{0,1},{1,0},{2,3},{3,2},{4,5},{5,4},{6,7},{7,6},{8,9},{9,8},{10,11... | collective-permute-start | bytes 1572872 | tf_op jit(solution)/shard_map/ppermute | solution.py:16
  10.7 3.6 %collective-permute-start.1 = (f32[3,8,32,512]{3,2,1,0:T(8,128)S(1)}, f32[3,8,32,512]{3,2,1,0:T(8,128)S(1)}, u32[]{:S(2)}, u32[]{:S(2)}) collective-permute-start(f32[3,8,32,512]{3,2,1,0:T(8,128)S(1)} %get-tuple-element.19), channel_id=1, source_target_pairs={{0,1},{1,0},{2,3},{3,2},{4,5},{5,4},{6,7},{7,6},{8,9},{9,8},{10,11... | collective-permute-start | bytes 4718600 | tf_op jit(solution)/shard_map/ppermute | solution.py:16
  11.0 9.9 %collective-permute-start.2 = (f32[4,32,512]{2,1,0:T(8,128)S(1)}, f32[4,32,512]{2,1,0:T(8,128)S(1)}, u32[]{:S(2)}, u32[]{:S(2)}) collective-permute-start(f32[4,32,512]{2,1,0:T(8,128)S(1)} %get-tuple-element.35), channel_id=1, source_target_pairs={{0,16},{16,32},{32,48},{48,0},{1,17},{17,33},{33,49},{49,1},{2,18}... | collective-permute-start | bytes 786440 | tf_op jit(solution)/shard_map/ppermute | solution.py:16
  12.6 9.2 %collective-permute-start.6 = (f32[4,32,512]{2,1,0:T(8,128)S(1)}, f32[4,32,512]{2,1,0:T(8,128)S(1)}, u32[]{:S(2)}, u32[]{:S(2)}) collective-permute-start(f32[4,32,512]{2,1,0:T(8,128)S(1)} %get-tuple-element.36), channel_id=1, source_target_pairs={{0,48},{16,0},{32,16},{48,32},{1,49},{17,1},{33,17},{49,33},{2,50}... | collective-permute-start | bytes 786440 | tf_op jit(solution)/shard_map/ppermute | solution.py:16
  14.3 11.1 %copy-start.2 = (f32[512,1536]{1,0:T(8,128)S(1)}, f32[512,1536]{1,0:T(8,128)}, u32[]{:S(2)}) copy-start(f32[512,1536]{1,0:T(8,128)} %coupling.1) | copy-start | bytes 9437188
  14.7 10.7 %copy-start.3 = (f32[512,512]{1,0:T(8,128)S(1)}, f32[512,512]{1,0:T(8,128)}, u32[]{:S(2)}) copy-start(f32[512,512]{1,0:T(8,128)} %diag.1) | copy-start | bytes 3145732
  14.8 14.5 %collective-permute-start.4 = (f32[4,32,512]{2,1,0:T(8,128)S(1)}, f32[4,32,512]{2,1,0:T(8,128)S(1)}, u32[]{:S(2)}, u32[]{:S(2)}) collective-permute-start(f32[4,32,512]{2,1,0:T(8,128)S(1)} %get-tuple-element.29), channel_id=1, source_target_pairs={{0,48},{16,0},{32,16},{48,32},{1,49},{17,1},{33,17},{49,33},{2,50}... | collective-permute-start | bytes 786440 | tf_op jit(solution)/shard_map/ppermute | solution.py:16
  21.8 10.5 %collective-permute-start.3 = (f32[4,32,512]{2,1,0:T(8,128)S(1)}, f32[4,32,512]{2,1,0:T(8,128)S(1)}, u32[]{:S(2)}, u32[]{:S(2)}) collective-permute-start(f32[4,32,512]{2,1,0:T(8,128)S(1)} %get-tuple-element.27), channel_id=1, source_target_pairs={{0,16},{16,32},{32,48},{48,0},{1,17},{17,33},{33,49},{49,1},{2,18}... | collective-permute-start | bytes 786440 | tf_op jit(solution)/shard_map/ppermute | solution.py:16
  23.4 9.0 %collective-permute-start.7 = (f32[4,32,512]{2,1,0:T(8,128)S(1)}, f32[4,32,512]{2,1,0:T(8,128)S(1)}, u32[]{:S(2)}, u32[]{:S(2)}) collective-permute-start(f32[4,32,512]{2,1,0:T(8,128)S(1)} %get-tuple-element.28), channel_id=1, source_target_pairs={{0,48},{16,0},{32,16},{48,32},{1,49},{17,1},{33,17},{49,33},{2,50}... | collective-permute-start | bytes 786440 | tf_op jit(solution)/shard_map/ppermute | solution.py:16
  25.1 10.5 %collective-permute-start.5 = (f32[4,32,512]{2,1,0:T(8,128)S(1)}, f32[4,32,512]{2,1,0:T(8,128)S(1)}, u32[]{:S(2)}, u32[]{:S(2)}) collective-permute-start(f32[4,32,512]{2,1,0:T(8,128)S(1)} %get-tuple-element.30), channel_id=1, source_target_pairs={{0,16},{16,32},{32,48},{48,0},{1,17},{17,33},{33,49},{49,1},{2,18}... | collective-permute-start | bytes 786440 | tf_op jit(solution)/shard_map/ppermute | solution.py:16
  29.2 6.6 %copy-start = (bf16[4,512,512]{2,1,0:T(8,128)(2,1)}, bf16[4,512,512]{2,1,0:T(8,128)(2,1)S(1)}, u32[]{:S(2)}) copy-start(bf16[4,512,512]{2,1,0:T(8,128)(2,1)S(1)} %get-tuple-element.26.refs_3_.refs_4_) | copy-start | bytes 6291460
  35.8 23.4 %copy-start.4 = (f32[512,32]{0,1:T(8,128)S(1)}, f32[512,32]{0,1:T(8,128)}, u32[]{:S(2)}) copy-start(f32[512,32]{0,1:T(8,128)} %param.5) | copy-start | bytes 196612
  35.9 8.1 %collective-permute-start.10 = (f32[48,512]{1,0:T(8,128)S(1)}, f32[48,512]{1,0:T(8,128)S(1)}, u32[]{:S(2)}, u32[]{:S(2)}) collective-permute-start(f32[48,512]{1,0:T(8,128)S(1)} %get-tuple-element.32), channel_id=1, source_target_pairs={{0,12},{2,14},{4,0},{6,2},{8,4},{10,6},{12,8},{14,10},{1,13},{3,15... | collective-permute-start | bytes 294920 | tf_op jit(solution)/shard_map/ppermute | solution.py:16
  41.4 7.8 %collective-permute-start.8 = (f32[48,512]{1,0:T(8,128)S(1)}, f32[48,512]{1,0:T(8,128)S(1)}, u32[]{:S(2)}, u32[]{:S(2)}) collective-permute-start(f32[48,512]{1,0:T(8,128)S(1)} %get-tuple-element.31), channel_id=1, source_target_pairs={{0,4},{2,6},{4,8},{6,10},{8,12},{10,14},{12,0},{14,2},{1,5},{3,7},... | collective-permute-start | bytes 294920 | tf_op jit(solution)/shard_map/ppermute | solution.py:16
  44.0 8.8 %collective-permute-start.13 = (f32[32,512]{1,0:T(8,128)S(1)}, f32[32,512]{1,0:T(8,128)S(1)}, u32[]{:S(2)}, u32[]{:S(2)}) collective-permute-start(f32[32,512]{1,0:T(8,128)S(1)} %slice_add_fusion), channel_id=1, source_target_pairs={{0,14},{2,0},{4,2},{6,4},{8,6},{10,8},{12,10},{14,12},{1,15},{3,1}... | collective-permute-start | bytes 196616 | tf_op jit(solution)/shard_map/ppermute | solution.py:16
  49.2 5.2 %collective-permute-start.12 = (f32[32,512]{1,0:T(8,128)S(1)}, f32[32,512]{1,0:T(8,128)S(1)}, u32[]{:S(2)}, u32[]{:S(2)}) collective-permute-start(f32[32,512]{1,0:T(8,128)S(1)} %slice_add_fusion.1), channel_id=1, source_target_pairs={{0,2},{2,4},{4,6},{6,8},{8,10},{10,12},{12,14},{14,0},{1,3},{3,5},... | collective-permute-start | bytes 196616 | tf_op jit(solution)/shard_map/ppermute | solution.py:16
  49.5 6.0 %collective-permute-start.11 = (f32[32,512]{1,0:T(8,128)S(1)}, f32[32,512]{1,0:T(8,128)S(1)}, u32[]{:S(2)}, u32[]{:S(2)}) collective-permute-start(f32[32,512]{1,0:T(8,128)S(1)} %pad_maximum_fusion.2), channel_id=1, source_target_pairs={{0,12},{2,14},{4,0},{6,2},{8,4},{10,6},{12,8},{14,10},{1,13},{3,15... | collective-permute-start | bytes 196616 | tf_op jit(solution)/shard_map/ppermute | solution.py:16
  52.7 6.5 %collective-permute-start.9 = (f32[32,512]{1,0:T(8,128)S(1)}, f32[32,512]{1,0:T(8,128)S(1)}, u32[]{:S(2)}, u32[]{:S(2)}) collective-permute-start(f32[32,512]{1,0:T(8,128)S(1)} %pad_maximum_fusion.1), channel_id=1, source_target_pairs={{0,4},{2,6},{4,8},{6,10},{8,12},{10,14},{12,0},{14,2},{1,5},{3,7},... | collective-permute-start | bytes 196616 | tf_op jit(solution)/shard_map/ppermute | solution.py:16
  59.2 1.6 %copy-start.1 = (bf16[4,512,512]{2,1,0:T(8,128)(2,1)S(1)}, bf16[4,512,512]{2,1,0:T(8,128)(2,1)}, u32[]{:S(2)}) copy-start(bf16[4,512,512]{2,1,0:T(8,128)(2,1)} %copy-done) | copy-start | bytes 6291460
  61.1 6.5 %collective-permute-start.14 = (f32[32,512]{1,0:T(8,128)S(1)}, f32[32,512]{1,0:T(8,128)S(1)}, u32[]{:S(2)}, u32[]{:S(2)}) collective-permute-start(f32[32,512]{1,0:T(8,128)S(1)} %shard_map.57.refs_1_), channel_id=1, source_target_pairs={{0,64},{64,128},{128,192},{192,0},{1,65},{65,129},{129,193},{193,1... | collective-permute-start | bytes 196616 | tf_op jit(solution)/shard_map/ppermute | solution.py:16
  62.7 7.5 %collective-permute-start.16 = (f32[32,512]{1,0:T(8,128)S(1)}, f32[32,512]{1,0:T(8,128)S(1)}, u32[]{:S(2)}, u32[]{:S(2)}) collective-permute-start(f32[32,512]{1,0:T(8,128)S(1)} %shard_map.57.refs_1_), channel_id=1, source_target_pairs={{0,128},{64,192},{128,0},{192,64},{1,129},{65,193},{129,1},{193,65... | collective-permute-start | bytes 196616 | tf_op jit(solution)/shard_map/ppermute | solution.py:16
  65.6 4.6 %collective-permute-start.17 = (f32[32,512]{1,0:T(8,128)S(1)}, f32[32,512]{1,0:T(8,128)S(1)}, u32[]{:S(2)}, u32[]{:S(2)}) collective-permute-start(f32[32,512]{1,0:T(8,128)S(1)} %shard_map.57.refs_1_), channel_id=1, source_target_pairs={{0,192},{64,0},{128,64},{192,128},{1,193},{65,1},{129,65},{193,129... | collective-permute-start | bytes 196616 | tf_op jit(solution)/shard_map/ppermute | solution.py:16
  67.8 6.2 %collective-permute-start.15 = (f32[32,512]{1,0:T(8,128)S(1)}, f32[32,512]{1,0:T(8,128)S(1)}, u32[]{:S(2)}, u32[]{:S(2)}) collective-permute-start(f32[32,512]{1,0:T(8,128)S(1)} %shard_map.58.refs_2_), channel_id=1, source_target_pairs={{0,64},{64,128},{128,192},{192,0},{1,65},{65,129},{129,193},{193,1... | collective-permute-start | bytes 196616 | tf_op jit(solution)/shard_map/ppermute | solution.py:16
  68.0 6.4 %collective-permute-start.19 = (f32[32,512]{1,0:T(8,128)S(1)}, f32[32,512]{1,0:T(8,128)S(1)}, u32[]{:S(2)}, u32[]{:S(2)}) collective-permute-start(f32[32,512]{1,0:T(8,128)S(1)} %shard_map.58.refs_2_), channel_id=1, source_target_pairs={{0,128},{64,192},{128,0},{192,64},{1,129},{65,193},{129,1},{193,65... | collective-permute-start | bytes 196616 | tf_op jit(solution)/shard_map/ppermute | solution.py:16
  74.3 5.5 %collective-permute-start.18 = (f32[32,512]{1,0:T(8,128)S(1)}, f32[32,512]{1,0:T(8,128)S(1)}, u32[]{:S(2)}, u32[]{:S(2)}) collective-permute-start(f32[32,512]{1,0:T(8,128)S(1)} %shard_map.60.refs_1_), channel_id=1, source_target_pairs={{0,64},{64,128},{128,192},{192,0},{1,65},{65,129},{129,193},{193,1... | collective-permute-start | bytes 196616 | tf_op jit(solution)/shard_map/ppermute | solution.py:16

commit v8 on v7

--- a/solution.py
+++ b/solution.py
@@ -14,6 +14,10 @@
 def shifted(value, axis, by):
     peers = lax.axis_size(axis)
     return lax.ppermute(value, axis, [(i, (i + by) % peers) for i in range(peers)])
+
+
+def in_pieces(value, axis, by):
+    return jnp.concatenate([shifted(part, axis, by) for part in jnp.split(value, 2)])
 
 
 def in_hbm(value):
@@ -199,8 +203,8 @@
     far = far_own + far_other
     near = own + shifted(sent, "core", 1)
     cut = far.shape[0] // 2
-    up = shifted(far[:cut], "x", 1)
-    down = shifted(far[cut:], "x", -1)
+    up = in_pieces(far[:cut], "x", 1)
+    down = in_pieces(far[cut:], "x", -1)
     ups = [shifted(half, "x", 1) for half in (near[0, :cut] + up, near[0, cut:])]
     downs = [shifted(half, "x", -1) for half in (near[1, :cut], near[1, cut:] + down)]
     weights = hop_weights(diag_inverse, coupling)

time: 80.8 us -> 80.4 us (level)
  waiting for transfers between devices: 34.9 us -> 31.3 us
  starting transfers between devices: 28.2 us -> 31.4 us
    ppermute x20 -> x22, waiting for transfers between devices: 34.9 us -> 31.3 us  [shifted(): lax.ppermute(value, axis, [(i, (i + by) % peers) for i in range(peers)])]
    ppermute x20 -> x22, starting transfers between devices: 28.2 us -> 31.4 us  [shifted(): lax.ppermute(value, axis, [(i, (i + by) % peers) for i in range(peers)])]
  transfers between devices with their start and end apart: 20 -> 22, of which waited for: 13 -> 14; matrix products, arithmetic and copies ran while one was open for 1% -> 1% of each run, Pallas kernels for 6% -> 6%
where the time goes in v8:
time: 80.4 us; the launch traced here: 80.3 us
  starting transfers between devices  31.4 us (39%)
  waiting for transfers between devices  31.3 us (39%)
  Pallas kernels  14.7 us (18%)
  local copies, waits for them, and re-layouts  1.83 us (2%)
  other arithmetic  0.86 us (1%)
    ppermute x22, starting transfers between devices, shifted(): lax.ppermute(value, axis, [(i, (i + by) % peers) for i in range(peers)])  31.4 us
    ppermute x22, waiting for transfers between devices, shifted(): lax.ppermute(value, axis, [(i, (i + by) % peers) for i in range(peers)])  31.3 us
    pallas_call x1, Pallas kernels, product(): pl.pallas_call(functools.partial(product_body, n_z, n_core), grid_spec=pl...  8.62 us
    pallas_call x1, Pallas kernels, hop_weights(): pl.pallas_call(weights_body, grid=(count,), in_specs=[pl.BlockSpec((block...  3.83 us
    pallas_call x6, Pallas kernels, applied(): pl.pallas_call(functools.partial(apply_body, [group for group, _ in value...  2.29 us
  transfers between devices with their start and end apart: 22, of which 14 were waited for; matrix products, arithmetic and copies ran while one was open for 1% of the time, Pallas kernels for 6%

profile of v8, /device:TPU:32, one launch (start us, length us, event | category | flops | bytes accessed | tf_op | source)
XLA Modules:
  0.0 80.3 jit_solution(2450494664554056001)
XLA Ops:
  0.0 0.1 stack.27.place
  0.1 8.6 %shard_map.55 = (f32[8,32,512]{2,1,0:T(8,128)S(1)}, f32[3,8,32,512]{3,2,1,0:T(8,128)S(1)}, f32[8,32,512]{2,1,0:T(8,128)S(1)}, f32[3,8,32,512]{3,2,1,0:T(8,128)S(1)}) custom-call(s32[6]{0:T(128)S(1)} %stack.27.place, f32[768,2048]{1,0:T(8,128)} %users.1, f32[512,768]{1,0:T(8,128)} %factor.1), custom_call_target="tpu_custom_call" | custom-call | flops 4831838208 | bytes 12058624 | tf_op jit(solution)/shard_map/pallas_call | solution.py:81
  8.7 0.1 collective-permute-start
  8.8 1.9 %collective-permute-done = f32[8,32,512]{2,1,0:T(8,128)S(1)} collective-permute-done((f32[8,32,512]{2,1,0:T(8,128)S(1)}, f32[8,32,512]{2,1,0:T(8,128)S(1)}, u32[]{:S(2)}, u32[]{:S(2)}) %collective-permute-start) | collective-permute-done | bytes 524320 | tf_op jit(solution)/shard_map/ppermute | solution.py:16
  10.7 0.1 collective-permute-start.1
  10.8 0.1 add.78
  11.0 1.6 %collective-permute-start.3 = (f32[2,32,512]{2,1,0:T(8,128)S(1)}, f32[2,32,512]{2,1,0:T(8,128)S(1)}, u32[]{:S(2)}, u32[]{:S(2)}) collective-permute-start(f32[2,32,512]{2,1,0:T(8,128)S(1)} %get-tuple-element.38), channel_id=1, source_target_pairs={{0,16},{16,32},{32,48},{48,0},{1,17},{17,33},{33,49},{49,1},{2,18}... | collective-permute-start | bytes 393224 | tf_op jit(solution)/shard_map/ppermute | solution.py:16
  12.6 1.5 %collective-permute-start.2 = (f32[2,32,512]{2,1,0:T(8,128)S(1)}, f32[2,32,512]{2,1,0:T(8,128)S(1)}, u32[]{:S(2)}, u32[]{:S(2)}) collective-permute-start(f32[2,32,512]{2,1,0:T(8,128)S(1)} %get-tuple-element.35), channel_id=1, source_target_pairs={{0,16},{16,32},{32,48},{48,0},{1,17},{17,33},{33,49},{49,1},{2,18}... | collective-permute-start | bytes 393224 | tf_op jit(solution)/shard_map/ppermute | solution.py:16
  14.0 1.7 %collective-permute-start.8 = (f32[2,32,512]{2,1,0:T(8,128)S(1)}, f32[2,32,512]{2,1,0:T(8,128)S(1)}, u32[]{:S(2)}, u32[]{:S(2)}) collective-permute-start(f32[2,32,512]{2,1,0:T(8,128)S(1)} %get-tuple-element.36), channel_id=1, source_target_pairs={{0,48},{16,0},{32,16},{48,32},{1,49},{17,1},{33,17},{49,33},{2,50}... | collective-permute-start | bytes 393224 | tf_op jit(solution)/shard_map/ppermute | solution.py:16
  15.8 0.5 collective-permute-start.7
  16.3 0.0 collective-permute-done.1
  16.3 0.4 add.77
  16.8 0.0 copy-start.3
  16.8 1.6 %collective-permute-start.5 = (f32[4,32,512]{2,1,0:T(8,128)S(1)}, f32[4,32,512]{2,1,0:T(8,128)S(1)}, u32[]{:S(2)}, u32[]{:S(2)}) collective-permute-start(f32[4,32,512]{2,1,0:T(8,128)S(1)} %get-tuple-element.29), channel_id=1, source_target_pairs={{0,48},{16,0},{32,16},{48,32},{1,49},{17,1},{33,17},{49,33},{2,50}... | collective-permute-start | bytes 786440 | tf_op jit(solution)/shard_map/ppermute | solution.py:16
  18.4 0.1 collective-permute-done.3
  18.6 2.3 %collective-permute-done.2 = f32[2,32,512]{2,1,0:T(8,128)S(1)} collective-permute-done((f32[2,32,512]{2,1,0:T(8,128)S(1)}, f32[2,32,512]{2,1,0:T(8,128)S(1)}, u32[]{:S(2)}, u32[]{:S(2)}) %collective-permute-start.2) | collective-permute-done | bytes 131104 | tf_op jit(solution)/shard_map/ppermute | solution.py:16
  20.8 0.0 collective-permute-done.8
  20.8 2.4 %collective-permute-done.7 = f32[2,32,512]{2,1,0:T(8,128)S(1)} collective-permute-done((f32[2,32,512]{2,1,0:T(8,128)S(1)}, f32[2,32,512]{2,1,0:T(8,128)S(1)}, u32[]{:S(2)}, u32[]{:S(2)}) %collective-permute-start.7) | collective-permute-done | bytes 131104 | tf_op jit(solution)/shard_map/ppermute | solution.py:16
  23.2 0.1 fusion.1
  23.3 1.3 %collective-permute-start.4 = (f32[4,32,512]{2,1,0:T(8,128)S(1)}, f32[4,32,512]{2,1,0:T(8,128)S(1)}, u32[]{:S(2)}, u32[]{:S(2)}) collective-permute-start(f32[4,32,512]{2,1,0:T(8,128)S(1)} %get-tuple-element.27), channel_id=1, source_target_pairs={{0,16},{16,32},{32,48},{48,0},{1,17},{17,33},{33,49},{49,1},{2,18}... | collective-permute-start | bytes 786440 | tf_op jit(solution)/shard_map/ppermute | solution.py:16
  24.6 2.0 %collective-permute-start.9 = (f32[4,32,512]{2,1,0:T(8,128)S(1)}, f32[4,32,512]{2,1,0:T(8,128)S(1)}, u32[]{:S(2)}, u32[]{:S(2)}) collective-permute-start(f32[4,32,512]{2,1,0:T(8,128)S(1)} %get-tuple-element.28), channel_id=1, source_target_pairs={{0,48},{16,0},{32,16},{48,32},{1,49},{17,1},{33,17},{49,33},{2,50}... | collective-permute-start | bytes 786440 | tf_op jit(solution)/shard_map/ppermute | solution.py:16
  26.6 0.0 collective-permute-start.6
  26.6 0.0 copy-done.2
  26.7 0.0 copy-done.3
  26.7 3.8 %shard_map.56 = (bf16[4,512,512]{2,1,0:T(8,128)(2,1)S(1)}, bf16[4,512,512]{2,1,0:T(8,128)(2,1)S(1)}) custom-call(f32[512,512]{1,0:T(8,128)S(1)} %copy-done.3, f32[512,1536]{1,0:T(8,128)S(1)} %copy-done.2), custom_call_target="tpu_custom_call" | custom-call | flops 2415919104 | bytes 8388608 | tf_op jit(solution)/shard_map/pallas_call | solution.py:116
  30.5 0.0 copy-start
  30.5 0.0 collective-permute-done.5
  30.6 2.8 %collective-permute-done.4 = f32[4,32,512]{2,1,0:T(8,128)S(1)} collective-permute-done((f32[4,32,512]{2,1,0:T(8,128)S(1)}, f32[4,32,512]{2,1,0:T(8,128)S(1)}, u32[]{:S(2)}, u32[]{:S(2)}) %collective-permute-start.4) | collective-permute-done | bytes 262176 | tf_op jit(solution)/shard_map/ppermute | solution.py:16
  33.4 0.0 collective-permute-done.9
  33.4 2.8 %collective-permute-done.6 = f32[4,32,512]{2,1,0:T(8,128)S(1)} collective-permute-done((f32[4,32,512]{2,1,0:T(8,128)S(1)}, f32[4,32,512]{2,1,0:T(8,128)S(1)}, u32[]{:S(2)}, u32[]{:S(2)}) %collective-permute-start.6) | collective-permute-done | bytes 262176 | tf_op jit(solution)/shard_map/ppermute | solution.py:16
  36.2 0.2 add_add_fusion.1
  36.3 0.0 copy-done
  36.4 0.0 copy-start.4
  36.5 5.5 %collective-permute-start.12 = (f32[48,512]{1,0:T(8,128)S(1)}, f32[48,512]{1,0:T(8,128)S(1)}, u32[]{:S(2)}, u32[]{:S(2)}) collective-permute-start(f32[48,512]{1,0:T(8,128)S(1)} %get-tuple-element.32), channel_id=1, source_target_pairs={{0,12},{2,14},{4,0},{6,2},{8,4},{10,6},{12,8},{14,10},{1,13},{3,15... | collective-permute-start | bytes 294920 | tf_op jit(solution)/shard_map/ppermute | solution.py:16
  41.9 0.0 collective-permute-start.10
  41.9 2.2 %collective-permute-done.12 = f32[48,512]{1,0:T(8,128)S(1)} collective-permute-done((f32[48,512]{1,0:T(8,128)S(1)}, f32[48,512]{1,0:T(8,128)S(1)}, u32[]{:S(2)}, u32[]{:S(2)}) %collective-permute-start.12) | collective-permute-done | bytes 98336 | tf_op jit(solution)/shard_map/ppermute | solution.py:16
  44.2 2.2 %collective-permute-start.15 = (f32[32,512]{1,0:T(8,128)S(1)}, f32[32,512]{1,0:T(8,128)S(1)}, u32[]{:S(2)}, u32[]{:S(2)}) collective-permute-start(f32[32,512]{1,0:T(8,128)S(1)} %slice_add_fusion), channel_id=1, source_target_pairs={{0,14},{2,0},{4,2},{6,4},{8,6},{10,8},{12,10},{14,12},{1,15},{3,1}... | collective-permute-start | bytes 196616 | tf_op jit(solution)/shard_map/ppermute | solution.py:16
  46.4 3.2 %collective-permute-done.10 = f32[48,512]{1,0:T(8,128)S(1)} collective-permute-done((f32[48,512]{1,0:T(8,128)S(1)}, f32[48,512]{1,0:T(8,128)S(1)}, u32[]{:S(2)}, u32[]{:S(2)}) %collective-permute-start.10) | collective-permute-done | bytes 98336 | tf_op jit(solution)/shard_map/ppermute | solution.py:16
  49.6 0.1 collective-permute-start.14
  49.7 4.0 %collective-permute-start.13 = (f32[32,512]{1,0:T(8,128)S(1)}, f32[32,512]{1,0:T(8,128)S(1)}, u32[]{:S(2)}, u32[]{:S(2)}) collective-permute-start(f32[32,512]{1,0:T(8,128)S(1)} %pad_maximum_fusion.2), channel_id=1, source_target_pairs={{0,12},{2,14},{4,0},{6,2},{8,4},{10,6},{12,8},{14,10},{1,13},{3,15... | collective-permute-start | bytes 196616 | tf_op jit(solution)/shard_map/ppermute | solution.py:16
  53.8 0.1 collective-permute-start.11
  53.9 0.0 collective-permute-done.15
  53.9 0.7 collective-permute-done.14
  54.6 1.2 %collective-permute-done.13 = f32[32,512]{1,0:T(8,128)S(1)} collective-permute-done((f32[32,512]{1,0:T(8,128)S(1)}, f32[32,512]{1,0:T(8,128)S(1)}, u32[]{:S(2)}, u32[]{:S(2)}) %collective-permute-start.13) | collective-permute-done | bytes 65568 | tf_op jit(solution)/shard_map/ppermute | solution.py:16
  55.8 4.4 %collective-permute-done.11 = f32[32,512]{1,0:T(8,128)S(1)} collective-permute-done((f32[32,512]{1,0:T(8,128)S(1)}, f32[32,512]{1,0:T(8,128)S(1)}, u32[]{:S(2)}, u32[]{:S(2)}) %collective-permute-start.11) | collective-permute-done | bytes 65568 | tf_op jit(solution)/shard_map/ppermute | solution.py:16
  60.3 1.6 %copy-done.1 = bf16[4,512,512]{2,1,0:T(8,128)(2,1)S(1)} copy-done((bf16[4,512,512]{2,1,0:T(8,128)(2,1)S(1)}, bf16[4,512,512]{2,1,0:T(8,128)(2,1)}, u32[]{:S(2)}) %copy-start.1) | copy-done | bytes 2097176
  61.9 0.3 shard_map.57.refs_1_
  62.1 1.5 %collective-permute-start.16 = (f32[32,512]{1,0:T(8,128)S(1)}, f32[32,512]{1,0:T(8,128)S(1)}, u32[]{:S(2)}, u32[]{:S(2)}) collective-permute-start(f32[32,512]{1,0:T(8,128)S(1)} %shard_map.57.refs_1_), channel_id=1, source_target_pairs={{0,64},{64,128},{128,192},{192,0},{1,65},{65,129},{129,193},{193,1... | collective-permute-start | bytes 196616 | tf_op jit(solution)/shard_map/ppermute | solution.py:16
  63.6 2.9 %collective-permute-start.18 = (f32[32,512]{1,0:T(8,128)S(1)}, f32[32,512]{1,0:T(8,128)S(1)}, u32[]{:S(2)}, u32[]{:S(2)}) collective-permute-start(f32[32,512]{1,0:T(8,128)S(1)} %shard_map.57.refs_1_), channel_id=1, source_target_pairs={{0,128},{64,192},{128,0},{192,64},{1,129},{65,193},{129,1},{193,65... | collective-permute-start | bytes 196616 | tf_op jit(solution)/shard_map/ppermute | solution.py:16
  66.5 1.3 %collective-permute-start.19 = (f32[32,512]{1,0:T(8,128)S(1)}, f32[32,512]{1,0:T(8,128)S(1)}, u32[]{:S(2)}, u32[]{:S(2)}) collective-permute-start(f32[32,512]{1,0:T(8,128)S(1)} %shard_map.57.refs_1_), channel_id=1, source_target_pairs={{0,192},{64,0},{128,64},{192,128},{1,193},{65,1},{129,65},{193,129... | collective-permute-start | bytes 196616 | tf_op jit(solution)/shard_map/ppermute | solution.py:16
  67.8 0.0 collective-permute-done.16.refs_0_
  67.8 0.3 shard_map.58.refs_2_
  68.1 0.7 collective-permute-start.17
  68.8 2.5 %collective-permute-start.21 = (f32[32,512]{1,0:T(8,128)S(1)}, f32[32,512]{1,0:T(8,128)S(1)}, u32[]{:S(2)}, u32[]{:S(2)}) collective-permute-start(f32[32,512]{1,0:T(8,128)S(1)} %shard_map.58.refs_2_), channel_id=1, source_target_pairs={{0,128},{64,192},{128,0},{192,64},{1,129},{65,193},{129,1},{193,65... | collective-permute-start | bytes 196616 | tf_op jit(solution)/shard_map/ppermute | solution.py:16
  71.3 0.0 collective-permute-done.18.refs_0_
  71.3 0.0 collective-permute-done.19.refs_1_
  71.3 0.3 shard_map.59.refs_1_
  71.6 2.0 %collective-permute-done.17.refs_0_ = f32[32,512]{1,0:T(8,128)S(1)} collective-permute-done((f32[32,512]{1,0:T(8,128)S(1)}, f32[32,512]{1,0:T(8,128)S(1)}, u32[]{:S(2)}, u32[]{:S(2)}) %collective-permute-start.17) | collective-permute-done | bytes 65568 | tf_op jit(solution)/shard_map/ppermute | solution.py:16
  73.6 0.3 shard_map.60.refs_1_
  73.9 0.0 collective-permute-start.20
  73.9 0.7 collective-permute-done.21.refs_0_
  74.6 0.3 shard_map.61.refs_1_
  74.9 4.5 %collective-permute-done.20.refs_0_ = f32[32,512]{1,0:T(8,128)S(1)} collective-permute-done((f32[32,512]{1,0:T(8,128)S(1)}, f32[32,512]{1,0:T(8,128)S(1)}, u32[]{:S(2)}, u32[]{:S(2)}) %collective-permute-start.20) | collective-permute-done | bytes 65568 | tf_op jit(solution)/shard_map/ppermute | solution.py:16
  79.4 0.9 %shard_map.62 = f32[32,512]{1,0:T(8,128)} custom-call(s32[1]{0:T(128)} %bitcast.place, f32[32,512]{1,0:T(8,128)S(1)} %collective-permute-done.20.refs_0_, f32[32,512]{1,0:T(8,128)S(1)} %shard_map.61.refs_1_, bf16[4,512,512]{2,1,0:T(8,128)(2,1)S(1)} %get-tuple-element.25.refs_2_.refs_3_, bf16[4,512,512]{2,1,0:T(8,128)(2,1)S(1)} %copy-done.1), custom_call_target="tpu_custom_call" | custom-call | tf_op jit(solution)/shard_map/pallas_call | solution.py:147
  (18 shorter events, 0.3 us)
Async XLA Ops:
  8.7 2.0 %collective-permute-start = (f32[8,32,512]{2,1,0:T(8,128)S(1)}, f32[8,32,512]{2,1,0:T(8,128)S(1)}, u32[]{:S(2)}, u32[]{:S(2)}) collective-permute-start(f32[8,32,512]{2,1,0:T(8,128)S(1)} %get-tuple-element.18), channel_id=1, source_target_pairs={{0,1},{1,0},{2,3},{3,2},{4,5},{5,4},{6,7},{7,6},{8,9},{9,8},{10,11... | collective-permute-start | bytes 1572872 | tf_op jit(solution)/shard_map/ppermute | solution.py:16
  10.7 5.6 %collective-permute-start.1 = (f32[3,8,32,512]{3,2,1,0:T(8,128)S(1)}, f32[3,8,32,512]{3,2,1,0:T(8,128)S(1)}, u32[]{:S(2)}, u32[]{:S(2)}) collective-permute-start(f32[3,8,32,512]{3,2,1,0:T(8,128)S(1)} %get-tuple-element.19), channel_id=1, source_target_pairs={{0,1},{1,0},{2,3},{3,2},{4,5},{5,4},{6,7},{7,6},{8,9},{9,8},{10,11... | collective-permute-start | bytes 4718600 | tf_op jit(solution)/shard_map/ppermute | solution.py:16
  11.0 7.6 %collective-permute-start.3 = (f32[2,32,512]{2,1,0:T(8,128)S(1)}, f32[2,32,512]{2,1,0:T(8,128)S(1)}, u32[]{:S(2)}, u32[]{:S(2)}) collective-permute-start(f32[2,32,512]{2,1,0:T(8,128)S(1)} %get-tuple-element.38), channel_id=1, source_target_pairs={{0,16},{16,32},{32,48},{48,0},{1,17},{17,33},{33,49},{49,1},{2,18}... | collective-permute-start | bytes 393224 | tf_op jit(solution)/shard_map/ppermute | solution.py:16
  12.6 8.3 %collective-permute-start.2 = (f32[2,32,512]{2,1,0:T(8,128)S(1)}, f32[2,32,512]{2,1,0:T(8,128)S(1)}, u32[]{:S(2)}, u32[]{:S(2)}) collective-permute-start(f32[2,32,512]{2,1,0:T(8,128)S(1)} %get-tuple-element.35), channel_id=1, source_target_pairs={{0,16},{16,32},{32,48},{48,0},{1,17},{17,33},{33,49},{49,1},{2,18}... | collective-permute-start | bytes 393224 | tf_op jit(solution)/shard_map/ppermute | solution.py:16
  14.0 6.8 %collective-permute-start.8 = (f32[2,32,512]{2,1,0:T(8,128)S(1)}, f32[2,32,512]{2,1,0:T(8,128)S(1)}, u32[]{:S(2)}, u32[]{:S(2)}) collective-permute-start(f32[2,32,512]{2,1,0:T(8,128)S(1)} %get-tuple-element.36), channel_id=1, source_target_pairs={{0,48},{16,0},{32,16},{48,32},{1,49},{17,1},{33,17},{49,33},{2,50}... | collective-permute-start | bytes 393224 | tf_op jit(solution)/shard_map/ppermute | solution.py:16
  15.8 7.5 %collective-permute-start.7 = (f32[2,32,512]{2,1,0:T(8,128)S(1)}, f32[2,32,512]{2,1,0:T(8,128)S(1)}, u32[]{:S(2)}, u32[]{:S(2)}) collective-permute-start(f32[2,32,512]{2,1,0:T(8,128)S(1)} %get-tuple-element.37), channel_id=1, source_target_pairs={{0,48},{16,0},{32,16},{48,32},{1,49},{17,1},{33,17},{49,33},{2,50}... | collective-permute-start | bytes 393224 | tf_op jit(solution)/shard_map/ppermute | solution.py:16
  16.3 10.3 %copy-start.2 = (f32[512,1536]{1,0:T(8,128)S(1)}, f32[512,1536]{1,0:T(8,128)}, u32[]{:S(2)}) copy-start(f32[512,1536]{1,0:T(8,128)} %coupling.1) | copy-start | bytes 9437188
  16.8 9.9 %copy-start.3 = (f32[512,512]{1,0:T(8,128)S(1)}, f32[512,512]{1,0:T(8,128)}, u32[]{:S(2)}) copy-start(f32[512,512]{1,0:T(8,128)} %diag.1) | copy-start | bytes 3145732
  16.8 13.7 %collective-permute-start.5 = (f32[4,32,512]{2,1,0:T(8,128)S(1)}, f32[4,32,512]{2,1,0:T(8,128)S(1)}, u32[]{:S(2)}, u32[]{:S(2)}) collective-permute-start(f32[4,32,512]{2,1,0:T(8,128)S(1)} %get-tuple-element.29), channel_id=1, source_target_pairs={{0,48},{16,0},{32,16},{48,32},{1,49},{17,1},{33,17},{49,33},{2,50}... | collective-permute-start | bytes 786440 | tf_op jit(solution)/shard_map/ppermute | solution.py:16
  23.3 10.0 %collective-permute-start.4 = (f32[4,32,512]{2,1,0:T(8,128)S(1)}, f32[4,32,512]{2,1,0:T(8,128)S(1)}, u32[]{:S(2)}, u32[]{:S(2)}) collective-permute-start(f32[4,32,512]{2,1,0:T(8,128)S(1)} %get-tuple-element.27), channel_id=1, source_target_pairs={{0,16},{16,32},{32,48},{48,0},{1,17},{17,33},{33,49},{49,1},{2,18}... | collective-permute-start | bytes 786440 | tf_op jit(solution)/shard_map/ppermute | solution.py:16
  24.6 8.8 %collective-permute-start.9 = (f32[4,32,512]{2,1,0:T(8,128)S(1)}, f32[4,32,512]{2,1,0:T(8,128)S(1)}, u32[]{:S(2)}, u32[]{:S(2)}) collective-permute-start(f32[4,32,512]{2,1,0:T(8,128)S(1)} %get-tuple-element.28), channel_id=1, source_target_pairs={{0,48},{16,0},{32,16},{48,32},{1,49},{17,1},{33,17},{49,33},{2,50}... | collective-permute-start | bytes 786440 | tf_op jit(solution)/shard_map/ppermute | solution.py:16
  26.6 9.5 %collective-permute-start.6 = (f32[4,32,512]{2,1,0:T(8,128)S(1)}, f32[4,32,512]{2,1,0:T(8,128)S(1)}, u32[]{:S(2)}, u32[]{:S(2)}) collective-permute-start(f32[4,32,512]{2,1,0:T(8,128)S(1)} %get-tuple-element.30), channel_id=1, source_target_pairs={{0,16},{16,32},{32,48},{48,0},{1,17},{17,33},{33,49},{49,1},{2,18}... | collective-permute-start | bytes 786440 | tf_op jit(solution)/shard_map/ppermute | solution.py:16
  30.5 5.9 %copy-start = (bf16[4,512,512]{2,1,0:T(8,128)(2,1)}, bf16[4,512,512]{2,1,0:T(8,128)(2,1)S(1)}, u32[]{:S(2)}) copy-start(bf16[4,512,512]{2,1,0:T(8,128)(2,1)S(1)} %get-tuple-element.26.refs_3_.refs_4_) | copy-start | bytes 6291460
  36.4 23.9 %copy-start.4 = (f32[512,32]{0,1:T(8,128)S(1)}, f32[512,32]{0,1:T(8,128)}, u32[]{:S(2)}) copy-start(f32[512,32]{0,1:T(8,128)} %param.5) | copy-start | bytes 196612
  36.5 7.7 %collective-permute-start.12 = (f32[48,512]{1,0:T(8,128)S(1)}, f32[48,512]{1,0:T(8,128)S(1)}, u32[]{:S(2)}, u32[]{:S(2)}) collective-permute-start(f32[48,512]{1,0:T(8,128)S(1)} %get-tuple-element.32), channel_id=1, source_target_pairs={{0,12},{2,14},{4,0},{6,2},{8,4},{10,6},{12,8},{14,10},{1,13},{3,15... | collective-permute-start | bytes 294920 | tf_op jit(solution)/shard_map/ppermute | solution.py:16
  41.9 7.7 %collective-permute-start.10 = (f32[48,512]{1,0:T(8,128)S(1)}, f32[48,512]{1,0:T(8,128)S(1)}, u32[]{:S(2)}, u32[]{:S(2)}) collective-permute-start(f32[48,512]{1,0:T(8,128)S(1)} %get-tuple-element.31), channel_id=1, source_target_pairs={{0,4},{2,6},{4,8},{6,10},{8,12},{10,14},{12,0},{14,2},{1,5},{3,7},... | collective-permute-start | bytes 294920 | tf_op jit(solution)/shard_map/ppermute | solution.py:16
  44.2 9.7 %collective-permute-start.15 = (f32[32,512]{1,0:T(8,128)S(1)}, f32[32,512]{1,0:T(8,128)S(1)}, u32[]{:S(2)}, u32[]{:S(2)}) collective-permute-start(f32[32,512]{1,0:T(8,128)S(1)} %slice_add_fusion), channel_id=1, source_target_pairs={{0,14},{2,0},{4,2},{6,4},{8,6},{10,8},{12,10},{14,12},{1,15},{3,1}... | collective-permute-start | bytes 196616 | tf_op jit(solution)/shard_map/ppermute | solution.py:16
  49.6 5.0 %collective-permute-start.14 = (f32[32,512]{1,0:T(8,128)S(1)}, f32[32,512]{1,0:T(8,128)S(1)}, u32[]{:S(2)}, u32[]{:S(2)}) collective-permute-start(f32[32,512]{1,0:T(8,128)S(1)} %slice_add_fusion.1), channel_id=1, source_target_pairs={{0,2},{2,4},{4,6},{6,8},{8,10},{10,12},{12,14},{14,0},{1,3},{3,5},... | collective-permute-start | bytes 196616 | tf_op jit(solution)/shard_map/ppermute | solution.py:16
  49.7 6.0 %collective-permute-start.13 = (f32[32,512]{1,0:T(8,128)S(1)}, f32[32,512]{1,0:T(8,128)S(1)}, u32[]{:S(2)}, u32[]{:S(2)}) collective-permute-start(f32[32,512]{1,0:T(8,128)S(1)} %pad_maximum_fusion.2), channel_id=1, source_target_pairs={{0,12},{2,14},{4,0},{6,2},{8,4},{10,6},{12,8},{14,10},{1,13},{3,15... | collective-permute-start | bytes 196616 | tf_op jit(solution)/shard_map/ppermute | solution.py:16
  53.8 6.5 %collective-permute-start.11 = (f32[32,512]{1,0:T(8,128)S(1)}, f32[32,512]{1,0:T(8,128)S(1)}, u32[]{:S(2)}, u32[]{:S(2)}) collective-permute-start(f32[32,512]{1,0:T(8,128)S(1)} %pad_maximum_fusion.1), channel_id=1, source_target_pairs={{0,4},{2,6},{4,8},{6,10},{8,12},{10,14},{12,0},{14,2},{1,5},{3,7},... | collective-permute-start | bytes 196616 | tf_op jit(solution)/shard_map/ppermute | solution.py:16
  60.3 1.6 %copy-start.1 = (bf16[4,512,512]{2,1,0:T(8,128)(2,1)S(1)}, bf16[4,512,512]{2,1,0:T(8,128)(2,1)}, u32[]{:S(2)}) copy-start(bf16[4,512,512]{2,1,0:T(8,128)(2,1)} %copy-done) | copy-start | bytes 6291460
  62.1 5.7 %collective-permute-start.16 = (f32[32,512]{1,0:T(8,128)S(1)}, f32[32,512]{1,0:T(8,128)S(1)}, u32[]{:S(2)}, u32[]{:S(2)}) collective-permute-start(f32[32,512]{1,0:T(8,128)S(1)} %shard_map.57.refs_1_), channel_id=1, source_target_pairs={{0,64},{64,128},{128,192},{192,0},{1,65},{65,129},{129,193},{193,1... | collective-permute-start | bytes 196616 | tf_op jit(solution)/shard_map/ppermute | solution.py:16
  63.6 7.7 %collective-permute-start.18 = (f32[32,512]{1,0:T(8,128)S(1)}, f32[32,512]{1,0:T(8,128)S(1)}, u32[]{:S(2)}, u32[]{:S(2)}) collective-permute-start(f32[32,512]{1,0:T(8,128)S(1)} %shard_map.57.refs_1_), channel_id=1, source_target_pairs={{0,128},{64,192},{128,0},{192,64},{1,129},{65,193},{129,1},{193,65... | collective-permute-start | bytes 196616 | tf_op jit(solution)/shard_map/ppermute | solution.py:16
  66.5 4.8 %collective-permute-start.19 = (f32[32,512]{1,0:T(8,128)S(1)}, f32[32,512]{1,0:T(8,128)S(1)}, u32[]{:S(2)}, u32[]{:S(2)}) collective-permute-start(f32[32,512]{1,0:T(8,128)S(1)} %shard_map.57.refs_1_), channel_id=1, source_target_pairs={{0,192},{64,0},{128,64},{192,128},{1,193},{65,1},{129,65},{193,129... | collective-permute-start | bytes 196616 | tf_op jit(solution)/shard_map/ppermute | solution.py:16
  68.1 5.5 %collective-permute-start.17 = (f32[32,512]{1,0:T(8,128)S(1)}, f32[32,512]{1,0:T(8,128)S(1)}, u32[]{:S(2)}, u32[]{:S(2)}) collective-permute-start(f32[32,512]{1,0:T(8,128)S(1)} %shard_map.58.refs_2_), channel_id=1, source_target_pairs={{0,64},{64,128},{128,192},{192,0},{1,65},{65,129},{129,193},{193,1... | collective-permute-start | bytes 196616 | tf_op jit(solution)/shard_map/ppermute | solution.py:16
  68.8 5.8 %collective-permute-start.21 = (f32[32,512]{1,0:T(8,128)S(1)}, f32[32,512]{1,0:T(8,128)S(1)}, u32[]{:S(2)}, u32[]{:S(2)}) collective-permute-start(f32[32,512]{1,0:T(8,128)S(1)} %shard_map.58.refs_2_), channel_id=1, source_target_pairs={{0,128},{64,192},{128,0},{192,64},{1,129},{65,193},{129,1},{193,65... | collective-permute-start | bytes 196616 | tf_op jit(solution)/shard_map/ppermute | solution.py:16
  73.9 5.5 %collective-permute-start.20 = (f32[32,512]{1,0:T(8,128)S(1)}, f32[32,512]{1,0:T(8,128)S(1)}, u32[]{:S(2)}, u32[]{:S(2)}) collective-permute-start(f32[32,512]{1,0:T(8,128)S(1)} %shard_map.60.refs_1_), channel_id=1, source_target_pairs={{0,64},{64,128},{128,192},{192,0},{1,65},{65,129},{129,193},{193,1... | collective-permute-start | bytes 196616 | tf_op jit(solution)/shard_map/ppermute | solution.py:16

commit v9 on v7

--- a/solution.py
+++ b/solution.py
@@ -96,33 +96,39 @@
 
 
 def weights_body(diag, coupling, high, low):
-    step = pl.program_id(0)
-
-    def keep(value):
-        high[0], low[0] = halves(value)
-
-    pl.when(step == 0)(lambda: keep(diag[...].T))
-    pl.when(step > 0)(lambda: keep(-three_pass(coupling[...], diag[...], 0, 1)))
+    high[0], low[0] = halves(-three_pass(coupling[...], diag[...], 0, 1))
 
 
 def hop_weights(diag, coupling):
     block = diag.shape[0]
-    count = 1 + coupling.shape[1] // block
+    count = coupling.shape[1] // block
     shape = jax.ShapeDtypeStruct((count, block, block), jnp.bfloat16)
     return pl.pallas_call(
         weights_body,
         grid=(count,),
         in_specs=[
             pl.BlockSpec((block, block), lambda i: (0, 0)),
-            pl.BlockSpec((block, block), lambda i: (0, lax.max(i - 1, 0))),
+            pl.BlockSpec((block, block), lambda i: (0, i)),
         ],
         out_specs=[pl.BlockSpec((1, block, block), lambda i: (i, 0, 0))] * 2,
         out_shape=[shape] * 2,
         cost_estimate=pl.CostEstimate(
-            flops=6 * (count - 1) * block**3, transcendentals=0, bytes_accessed=8 * count * block**2
+            flops=6 * count * block**3, transcendentals=0, bytes_accessed=8 * (count + 1) * block**2
         ),
         compiler_params=pltpu.CompilerParams(vmem_limit_bytes=24 << 20),
     )(diag, coupling)
+
+
+def solved_alone_body(residue, diag, out):
+    out[...] = three_pass(residue[...], diag[...], 1, 1)
+
+
+def solved_alone(residue, diag):
+    return pl.pallas_call(
+        solved_alone_body,
+        out_shape=jax.ShapeDtypeStruct(residue.shape, jnp.float32),
+        compiler_params=pltpu.CompilerParams(vmem_limit_bytes=8 << 20),
+    )(residue, diag)
 
 
 def apply_body(wanted, place, *refs):
@@ -153,16 +159,16 @@
     )(position, *[value for _, value in values], base, *weights)
 
 
-def chain(position, residue, weights):
+def chain(position, residue, diag, weights):
     groups = lax.axis_size("grp")
-    result = applied(position, jnp.zeros_like(residue), [(None, residue)], weights, 0)
+    result = solved_alone(residue, diag)
     later = []
     for step in range(groups - 1):
         near = shifted(result, "grp", 1)
         far = [(step + by, shifted(result, "grp", by)) for by in range(2, groups - step)]
         if later:
-            result = applied(position, result, later, weights, step)
-        result = applied(position, result, [(step + 1, near)], weights, step + 1)
+            result = applied(position, result, later, weights, step - 1)
+        result = applied(position, result, [(step + 1, near)], weights, step)
         later = far
     return result
 
@@ -208,7 +214,7 @@
     sums = [home[:cut] + ups[0] + downs[0], home[cut:] + ups[1] + downs[1]]
     along_z = jnp.concatenate(sums)
     residue = right_side.T - reduced_over_z(along_z)
-    return chain(position, residue, weights).T
+    return chain(position, residue, diag_inverse, weights).T
 
 
 def solution(mesh):

time: 80.8 us -> 79.5 us (0.984)
  local copies, waits for them, and re-layouts: 1.83 us -> 0.23 us
    unnamed x10 -> x6, local copies, waits for them, and re-layouts: 1.6 us -> 0.02 us
    pallas_call x6 -> x5, Pallas kernels: 2.29 us -> 2.02 us  [applied(): pl.pallas_call(functools.partial(apply_body, [group for group, _ in value...]
where the time goes in v9:
time: 79.5 us; the launch traced here: 79.4 us
  waiting for transfers between devices  35.4 us (45%)
  starting transfers between devices  28.2 us (35%)
  Pallas kernels  14.6 us (18%)
  other arithmetic  0.8 us (1%)
    ppermute x20, waiting for transfers between devices, shifted(): lax.ppermute(value, axis, [(i, (i + by) % peers) for i in range(peers)])  35.4 us
    ppermute x20, starting transfers between devices, shifted(): lax.ppermute(value, axis, [(i, (i + by) % peers) for i in range(peers)])  28.2 us
    pallas_call x1, Pallas kernels, product(): pl.pallas_call(functools.partial(product_body, n_z, n_core), grid_spec=pl...  8.62 us
    pallas_call x1, Pallas kernels, hop_weights(): pl.pallas_call(weights_body, grid=(count,), in_specs=[pl.BlockSpec((block...  3.42 us
    pallas_call x5, Pallas kernels, applied(): pl.pallas_call(functools.partial(apply_body, [group for group, _ in value...  2.02 us
  transfers between devices with their start and end apart: 20, of which 13 were waited for; matrix products, arithmetic and copies ran while one was open for 1% of the time, Pallas kernels for 6%

profile of v9, /device:TPU:32, one launch (start us, length us, event | category | flops | bytes accessed | tf_op | source)
XLA Modules:
  0.0 79.4 jit_solution(9864545226511210844)
XLA Ops:
  0.0 0.1 stack.27.place
  0.1 8.6 %shard_map.55 = (f32[8,32,512]{2,1,0:T(8,128)S(1)}, f32[3,8,32,512]{3,2,1,0:T(8,128)S(1)}, f32[8,32,512]{2,1,0:T(8,128)S(1)}, f32[3,8,32,512]{3,2,1,0:T(8,128)S(1)}) custom-call(s32[6]{0:T(128)S(1)} %stack.27.place, f32[768,2048]{1,0:T(8,128)} %users.1, f32[512,768]{1,0:T(8,128)} %factor.1), custom_call_target="tpu_custom_call" | custom-call | flops 4831838208 | bytes 12058624 | tf_op jit(solution)/shard_map/pallas_call | solution.py:77
  8.7 0.1 collective-permute-start
  8.8 1.9 %collective-permute-done = f32[8,32,512]{2,1,0:T(8,128)S(1)} collective-permute-done((f32[8,32,512]{2,1,0:T(8,128)S(1)}, f32[8,32,512]{2,1,0:T(8,128)S(1)}, u32[]{:S(2)}, u32[]{:S(2)}) %collective-permute-start) | collective-permute-done | bytes 524320 | tf_op jit(solution)/shard_map/ppermute | solution.py:16
  10.7 0.1 collective-permute-start.1
  10.8 0.1 add.78
  11.0 1.6 %collective-permute-start.2 = (f32[4,32,512]{2,1,0:T(8,128)S(1)}, f32[4,32,512]{2,1,0:T(8,128)S(1)}, u32[]{:S(2)}, u32[]{:S(2)}) collective-permute-start(f32[4,32,512]{2,1,0:T(8,128)S(1)} %get-tuple-element.35), channel_id=1, source_target_pairs={{0,16},{16,32},{32,48},{48,0},{1,17},{17,33},{33,49},{49,1},{2,18}... | collective-permute-start | bytes 786440 | tf_op jit(solution)/shard_map/ppermute | solution.py:16
  12.6 1.7 %collective-permute-start.6 = (f32[4,32,512]{2,1,0:T(8,128)S(1)}, f32[4,32,512]{2,1,0:T(8,128)S(1)}, u32[]{:S(2)}, u32[]{:S(2)}) collective-permute-start(f32[4,32,512]{2,1,0:T(8,128)S(1)} %get-tuple-element.36), channel_id=1, source_target_pairs={{0,48},{16,0},{32,16},{48,32},{1,49},{17,1},{33,17},{49,33},{2,50}... | collective-permute-start | bytes 786440 | tf_op jit(solution)/shard_map/ppermute | solution.py:16
  14.3 0.0 collective-permute-done.1
  14.3 0.0 copy-start.1
  14.3 0.3 add.77
  14.7 0.0 copy-start
  14.7 2.6 %collective-permute-start.4 = (f32[4,32,512]{2,1,0:T(8,128)S(1)}, f32[4,32,512]{2,1,0:T(8,128)S(1)}, u32[]{:S(2)}, u32[]{:S(2)}) collective-permute-start(f32[4,32,512]{2,1,0:T(8,128)S(1)} %get-tuple-element.29), channel_id=1, source_target_pairs={{0,48},{16,0},{32,16},{48,32},{1,49},{17,1},{33,17},{49,33},{2,50}... | collective-permute-start | bytes 786440 | tf_op jit(solution)/shard_map/ppermute | solution.py:16
  17.4 3.5 %collective-permute-done.2 = f32[4,32,512]{2,1,0:T(8,128)S(1)} collective-permute-done((f32[4,32,512]{2,1,0:T(8,128)S(1)}, f32[4,32,512]{2,1,0:T(8,128)S(1)}, u32[]{:S(2)}, u32[]{:S(2)}) %collective-permute-start.2) | collective-permute-done | bytes 262176 | tf_op jit(solution)/shard_map/ppermute | solution.py:16
  20.8 0.9 %collective-permute-done.6 = f32[4,32,512]{2,1,0:T(8,128)S(1)} collective-permute-done((f32[4,32,512]{2,1,0:T(8,128)S(1)}, f32[4,32,512]{2,1,0:T(8,128)S(1)}, u32[]{:S(2)}, u32[]{:S(2)}) %collective-permute-start.6) | collective-permute-done | bytes 262176 | tf_op jit(solution)/shard_map/ppermute | solution.py:16
  21.7 0.1 fusion.1
  21.8 1.6 %collective-permute-start.3 = (f32[4,32,512]{2,1,0:T(8,128)S(1)}, f32[4,32,512]{2,1,0:T(8,128)S(1)}, u32[]{:S(2)}, u32[]{:S(2)}) collective-permute-start(f32[4,32,512]{2,1,0:T(8,128)S(1)} %get-tuple-element.27), channel_id=1, source_target_pairs={{0,16},{16,32},{32,48},{48,0},{1,17},{17,33},{33,49},{49,1},{2,18}... | collective-permute-start | bytes 786440 | tf_op jit(solution)/shard_map/ppermute | solution.py:16
  23.4 1.7 %collective-permute-start.7 = (f32[4,32,512]{2,1,0:T(8,128)S(1)}, f32[4,32,512]{2,1,0:T(8,128)S(1)}, u32[]{:S(2)}, u32[]{:S(2)}) collective-permute-start(f32[4,32,512]{2,1,0:T(8,128)S(1)} %get-tuple-element.28), channel_id=1, source_target_pairs={{0,48},{16,0},{32,16},{48,32},{1,49},{17,1},{33,17},{49,33},{2,50}... | collective-permute-start | bytes 786440 | tf_op jit(solution)/shard_map/ppermute | solution.py:16
  25.1 0.3 collective-permute-start.5
  25.4 0.0 copy-done.1
  25.4 0.0 copy-done
  25.4 3.4 %shard_map.56 = (bf16[3,512,512]{2,1,0:T(8,128)(2,1)S(1)}, bf16[3,512,512]{2,1,0:T(8,128)(2,1)S(1)}) custom-call(f32[512,512]{1,0:T(8,128)S(1)} %copy-done, f32[512,1536]{1,0:T(8,128)S(1)} %copy-done.1), custom_call_target="tpu_custom_call" | custom-call | flops 2415919104 | bytes 8388608 | tf_op jit(solution)/shard_map/pallas_call | solution.py:106
  28.9 0.0 collective-permute-done.4
  28.9 3.4 %collective-permute-done.3 = f32[4,32,512]{2,1,0:T(8,128)S(1)} collective-permute-done((f32[4,32,512]{2,1,0:T(8,128)S(1)}, f32[4,32,512]{2,1,0:T(8,128)S(1)}, u32[]{:S(2)}, u32[]{:S(2)}) %collective-permute-start.3) | collective-permute-done | bytes 262176 | tf_op jit(solution)/shard_map/ppermute | solution.py:16
  32.3 0.0 collective-permute-done.7
  32.3 3.3 %collective-permute-done.5 = f32[4,32,512]{2,1,0:T(8,128)S(1)} collective-permute-done((f32[4,32,512]{2,1,0:T(8,128)S(1)}, f32[4,32,512]{2,1,0:T(8,128)S(1)}, u32[]{:S(2)}, u32[]{:S(2)}) %collective-permute-start.5) | collective-permute-done | bytes 262176 | tf_op jit(solution)/shard_map/ppermute | solution.py:16
  35.6 0.2 add_add_fusion.1
  35.8 0.0 copy-start.2
  35.9 5.5 %collective-permute-start.10 = (f32[48,512]{1,0:T(8,128)S(1)}, f32[48,512]{1,0:T(8,128)S(1)}, u32[]{:S(2)}, u32[]{:S(2)}) collective-permute-start(f32[48,512]{1,0:T(8,128)S(1)} %get-tuple-element.32), channel_id=1, source_target_pairs={{0,12},{2,14},{4,0},{6,2},{8,4},{10,6},{12,8},{14,10},{1,13},{3,15... | collective-permute-start | bytes 294920 | tf_op jit(solution)/shard_map/ppermute | solution.py:16
  41.4 0.0 collective-permute-start.8
  41.4 2.6 %collective-permute-done.10 = f32[48,512]{1,0:T(8,128)S(1)} collective-permute-done((f32[48,512]{1,0:T(8,128)S(1)}, f32[48,512]{1,0:T(8,128)S(1)}, u32[]{:S(2)}, u32[]{:S(2)}) %collective-permute-start.10) | collective-permute-done | bytes 98336 | tf_op jit(solution)/shard_map/ppermute | solution.py:16
  44.0 1.0 %collective-permute-start.13 = (f32[32,512]{1,0:T(8,128)S(1)}, f32[32,512]{1,0:T(8,128)S(1)}, u32[]{:S(2)}, u32[]{:S(2)}) collective-permute-start(f32[32,512]{1,0:T(8,128)S(1)} %slice_add_fusion), channel_id=1, source_target_pairs={{0,14},{2,0},{4,2},{6,4},{8,6},{10,8},{12,10},{14,12},{1,15},{3,1}... | collective-permute-start | bytes 196616 | tf_op jit(solution)/shard_map/ppermute | solution.py:16
  45.0 4.1 %collective-permute-done.8 = f32[48,512]{1,0:T(8,128)S(1)} collective-permute-done((f32[48,512]{1,0:T(8,128)S(1)}, f32[48,512]{1,0:T(8,128)S(1)}, u32[]{:S(2)}, u32[]{:S(2)}) %collective-permute-start.8) | collective-permute-done | bytes 98336 | tf_op jit(solution)/shard_map/ppermute | solution.py:16
  49.2 0.3 collective-permute-start.12
  49.5 3.2 %collective-permute-start.11 = (f32[32,512]{1,0:T(8,128)S(1)}, f32[32,512]{1,0:T(8,128)S(1)}, u32[]{:S(2)}, u32[]{:S(2)}) collective-permute-start(f32[32,512]{1,0:T(8,128)S(1)} %pad_maximum_fusion.2), channel_id=1, source_target_pairs={{0,12},{2,14},{4,0},{6,2},{8,4},{10,6},{12,8},{14,10},{1,13},{3,15... | collective-permute-start | bytes 196616 | tf_op jit(solution)/shard_map/ppermute | solution.py:16
  52.7 0.1 collective-permute-start.9
  52.8 0.0 collective-permute-done.13
  52.8 1.5 %collective-permute-done.12 = f32[32,512]{1,0:T(8,128)S(1)} collective-permute-done((f32[32,512]{1,0:T(8,128)S(1)}, f32[32,512]{1,0:T(8,128)S(1)}, u32[]{:S(2)}, u32[]{:S(2)}) %collective-permute-start.12) | collective-permute-done | bytes 65568 | tf_op jit(solution)/shard_map/ppermute | solution.py:16
  54.3 1.1 %collective-permute-done.11 = f32[32,512]{1,0:T(8,128)S(1)} collective-permute-done((f32[32,512]{1,0:T(8,128)S(1)}, f32[32,512]{1,0:T(8,128)S(1)}, u32[]{:S(2)}, u32[]{:S(2)}) %collective-permute-start.11) | collective-permute-done | bytes 65568 | tf_op jit(solution)/shard_map/ppermute | solution.py:16
  55.5 3.7 %collective-permute-done.9 = f32[32,512]{1,0:T(8,128)S(1)} collective-permute-done((f32[32,512]{1,0:T(8,128)S(1)}, f32[32,512]{1,0:T(8,128)S(1)}, u32[]{:S(2)}, u32[]{:S(2)}) %collective-permute-start.9) | collective-permute-done | bytes 65568 | tf_op jit(solution)/shard_map/ppermute | solution.py:16
  59.2 0.0 copy-done.2
  59.2 0.6 shard_map.57.refs_1_
  59.8 1.7 %collective-permute-start.14 = (f32[32,512]{1,0:T(8,128)S(1)}, f32[32,512]{1,0:T(8,128)S(1)}, u32[]{:S(2)}, u32[]{:S(2)}) collective-permute-start(f32[32,512]{1,0:T(8,128)S(1)} %shard_map.57.refs_1_), channel_id=1, source_target_pairs={{0,64},{64,128},{128,192},{192,0},{1,65},{65,129},{129,193},{193,1... | collective-permute-start | bytes 196616 | tf_op jit(solution)/shard_map/ppermute | solution.py:16
  61.4 2.9 %collective-permute-start.16 = (f32[32,512]{1,0:T(8,128)S(1)}, f32[32,512]{1,0:T(8,128)S(1)}, u32[]{:S(2)}, u32[]{:S(2)}) collective-permute-start(f32[32,512]{1,0:T(8,128)S(1)} %shard_map.57.refs_1_), channel_id=1, source_target_pairs={{0,128},{64,192},{128,0},{192,64},{1,129},{65,193},{129,1},{193,65... | collective-permute-start | bytes 196616 | tf_op jit(solution)/shard_map/ppermute | solution.py:16
  64.3 1.3 %collective-permute-start.17 = (f32[32,512]{1,0:T(8,128)S(1)}, f32[32,512]{1,0:T(8,128)S(1)}, u32[]{:S(2)}, u32[]{:S(2)}) collective-permute-start(f32[32,512]{1,0:T(8,128)S(1)} %shard_map.57.refs_1_), channel_id=1, source_target_pairs={{0,192},{64,0},{128,64},{192,128},{1,193},{65,1},{129,65},{193,129... | collective-permute-start | bytes 196616 | tf_op jit(solution)/shard_map/ppermute | solution.py:16
  65.7 0.6 collective-permute-done.14.refs_0_
  66.2 0.3 shard_map.58.refs_2_
  66.5 0.1 collective-permute-start.15
  66.7 2.2 %collective-permute-start.19 = (f32[32,512]{1,0:T(8,128)S(1)}, f32[32,512]{1,0:T(8,128)S(1)}, u32[]{:S(2)}, u32[]{:S(2)}) collective-permute-start(f32[32,512]{1,0:T(8,128)S(1)} %shard_map.58.refs_2_), channel_id=1, source_target_pairs={{0,128},{64,192},{128,0},{192,64},{1,129},{65,193},{129,1},{193,65... | collective-permute-start | bytes 196616 | tf_op jit(solution)/shard_map/ppermute | solution.py:16
  68.9 0.0 collective-permute-done.16.refs_0_
  68.9 0.0 collective-permute-done.17.refs_1_
  68.9 0.3 shard_map.59.refs_1_
  69.2 3.5 %collective-permute-done.15.refs_0_ = f32[32,512]{1,0:T(8,128)S(1)} collective-permute-done((f32[32,512]{1,0:T(8,128)S(1)}, f32[32,512]{1,0:T(8,128)S(1)}, u32[]{:S(2)}, u32[]{:S(2)}) %collective-permute-start.15) | collective-permute-done | bytes 65568 | tf_op jit(solution)/shard_map/ppermute | solution.py:16
  72.7 0.3 shard_map.60.refs_1_
  73.0 0.0 collective-permute-start.18
  73.0 0.0 collective-permute-done.19.refs_0_
  73.0 0.3 shard_map.61.refs_1_
  73.3 5.2 %collective-permute-done.18.refs_0_ = f32[32,512]{1,0:T(8,128)S(1)} collective-permute-done((f32[32,512]{1,0:T(8,128)S(1)}, f32[32,512]{1,0:T(8,128)S(1)}, u32[]{:S(2)}, u32[]{:S(2)}) %collective-permute-start.18) | collective-permute-done | bytes 65568 | tf_op jit(solution)/shard_map/ppermute | solution.py:16
  78.5 0.9 %shard_map.62 = f32[32,512]{1,0:T(8,128)} custom-call(s32[1]{0:T(128)} %bitcast.place, f32[32,512]{1,0:T(8,128)S(1)} %collective-permute-done.18.refs_0_, f32[32,512]{1,0:T(8,128)S(1)} %shard_map.61.refs_1_, bf16[3,512,512]{2,1,0:T(8,128)(2,1)S(1)} %get-tuple-element.25.refs_2_.refs_3_, bf16[3,512,512]{2,1,0:T(8,128)(2,1)S(1)} %get-tuple-element.26.refs_3_.refs_4_), custom_call_target="tpu_custom_call" | custom-call | tf_op jit(solution)/shard_map/pallas_call | solution.py:149
  (14 shorter events, 0.3 us)
Async XLA Ops:
  8.7 2.0 %collective-permute-start = (f32[8,32,512]{2,1,0:T(8,128)S(1)}, f32[8,32,512]{2,1,0:T(8,128)S(1)}, u32[]{:S(2)}, u32[]{:S(2)}) collective-permute-start(f32[8,32,512]{2,1,0:T(8,128)S(1)} %get-tuple-element.18), channel_id=1, source_target_pairs={{0,1},{1,0},{2,3},{3,2},{4,5},{5,4},{6,7},{7,6},{8,9},{9,8},{10,11... | collective-permute-start | bytes 1572872 | tf_op jit(solution)/shard_map/ppermute | solution.py:16
  10.7 3.6 %collective-permute-start.1 = (f32[3,8,32,512]{3,2,1,0:T(8,128)S(1)}, f32[3,8,32,512]{3,2,1,0:T(8,128)S(1)}, u32[]{:S(2)}, u32[]{:S(2)}) collective-permute-start(f32[3,8,32,512]{3,2,1,0:T(8,128)S(1)} %get-tuple-element.19), channel_id=1, source_target_pairs={{0,1},{1,0},{2,3},{3,2},{4,5},{5,4},{6,7},{7,6},{8,9},{9,8},{10,11... | collective-permute-start | bytes 4718600 | tf_op jit(solution)/shard_map/ppermute | solution.py:16
  11.0 9.9 %collective-permute-start.2 = (f32[4,32,512]{2,1,0:T(8,128)S(1)}, f32[4,32,512]{2,1,0:T(8,128)S(1)}, u32[]{:S(2)}, u32[]{:S(2)}) collective-permute-start(f32[4,32,512]{2,1,0:T(8,128)S(1)} %get-tuple-element.35), channel_id=1, source_target_pairs={{0,16},{16,32},{32,48},{48,0},{1,17},{17,33},{33,49},{49,1},{2,18}... | collective-permute-start | bytes 786440 | tf_op jit(solution)/shard_map/ppermute | solution.py:16
  12.6 9.2 %collective-permute-start.6 = (f32[4,32,512]{2,1,0:T(8,128)S(1)}, f32[4,32,512]{2,1,0:T(8,128)S(1)}, u32[]{:S(2)}, u32[]{:S(2)}) collective-permute-start(f32[4,32,512]{2,1,0:T(8,128)S(1)} %get-tuple-element.36), channel_id=1, source_target_pairs={{0,48},{16,0},{32,16},{48,32},{1,49},{17,1},{33,17},{49,33},{2,50}... | collective-permute-start | bytes 786440 | tf_op jit(solution)/shard_map/ppermute | solution.py:16
  14.3 11.1 %copy-start.1 = (f32[512,1536]{1,0:T(8,128)S(1)}, f32[512,1536]{1,0:T(8,128)}, u32[]{:S(2)}) copy-start(f32[512,1536]{1,0:T(8,128)} %coupling.1) | copy-start | bytes 9437188
  14.7 10.7 %copy-start = (f32[512,512]{1,0:T(8,128)S(1)}, f32[512,512]{1,0:T(8,128)}, u32[]{:S(2)}) copy-start(f32[512,512]{1,0:T(8,128)} %diag.3) | copy-start | bytes 3145732
  14.7 14.2 %collective-permute-start.4 = (f32[4,32,512]{2,1,0:T(8,128)S(1)}, f32[4,32,512]{2,1,0:T(8,128)S(1)}, u32[]{:S(2)}, u32[]{:S(2)}) collective-permute-start(f32[4,32,512]{2,1,0:T(8,128)S(1)} %get-tuple-element.29), channel_id=1, source_target_pairs={{0,48},{16,0},{32,16},{48,32},{1,49},{17,1},{33,17},{49,33},{2,50}... | collective-permute-start | bytes 786440 | tf_op jit(solution)/shard_map/ppermute | solution.py:16
  21.8 10.5 %collective-permute-start.3 = (f32[4,32,512]{2,1,0:T(8,128)S(1)}, f32[4,32,512]{2,1,0:T(8,128)S(1)}, u32[]{:S(2)}, u32[]{:S(2)}) collective-permute-start(f32[4,32,512]{2,1,0:T(8,128)S(1)} %get-tuple-element.27), channel_id=1, source_target_pairs={{0,16},{16,32},{32,48},{48,0},{1,17},{17,33},{33,49},{49,1},{2,18}... | collective-permute-start | bytes 786440 | tf_op jit(solution)/shard_map/ppermute | solution.py:16
  23.4 9.0 %collective-permute-start.7 = (f32[4,32,512]{2,1,0:T(8,128)S(1)}, f32[4,32,512]{2,1,0:T(8,128)S(1)}, u32[]{:S(2)}, u32[]{:S(2)}) collective-permute-start(f32[4,32,512]{2,1,0:T(8,128)S(1)} %get-tuple-element.28), channel_id=1, source_target_pairs={{0,48},{16,0},{32,16},{48,32},{1,49},{17,1},{33,17},{49,33},{2,50}... | collective-permute-start | bytes 786440 | tf_op jit(solution)/shard_map/ppermute | solution.py:16
  25.1 10.5 %collective-permute-start.5 = (f32[4,32,512]{2,1,0:T(8,128)S(1)}, f32[4,32,512]{2,1,0:T(8,128)S(1)}, u32[]{:S(2)}, u32[]{:S(2)}) collective-permute-start(f32[4,32,512]{2,1,0:T(8,128)S(1)} %get-tuple-element.30), channel_id=1, source_target_pairs={{0,16},{16,32},{32,48},{48,0},{1,17},{17,33},{33,49},{49,1},{2,18}... | collective-permute-start | bytes 786440 | tf_op jit(solution)/shard_map/ppermute | solution.py:16
  35.8 23.4 %copy-start.2 = (f32[512,32]{0,1:T(8,128)S(1)}, f32[512,32]{0,1:T(8,128)}, u32[]{:S(2)}) copy-start(f32[512,32]{0,1:T(8,128)} %param.5) | copy-start | bytes 196612
  35.9 8.1 %collective-permute-start.10 = (f32[48,512]{1,0:T(8,128)S(1)}, f32[48,512]{1,0:T(8,128)S(1)}, u32[]{:S(2)}, u32[]{:S(2)}) collective-permute-start(f32[48,512]{1,0:T(8,128)S(1)} %get-tuple-element.32), channel_id=1, source_target_pairs={{0,12},{2,14},{4,0},{6,2},{8,4},{10,6},{12,8},{14,10},{1,13},{3,15... | collective-permute-start | bytes 294920 | tf_op jit(solution)/shard_map/ppermute | solution.py:16
  41.4 7.8 %collective-permute-start.8 = (f32[48,512]{1,0:T(8,128)S(1)}, f32[48,512]{1,0:T(8,128)S(1)}, u32[]{:S(2)}, u32[]{:S(2)}) collective-permute-start(f32[48,512]{1,0:T(8,128)S(1)} %get-tuple-element.31), channel_id=1, source_target_pairs={{0,4},{2,6},{4,8},{6,10},{8,12},{10,14},{12,0},{14,2},{1,5},{3,7},... | collective-permute-start | bytes 294920 | tf_op jit(solution)/shard_map/ppermute | solution.py:16
  44.0 8.8 %collective-permute-start.13 = (f32[32,512]{1,0:T(8,128)S(1)}, f32[32,512]{1,0:T(8,128)S(1)}, u32[]{:S(2)}, u32[]{:S(2)}) collective-permute-start(f32[32,512]{1,0:T(8,128)S(1)} %slice_add_fusion), channel_id=1, source_target_pairs={{0,14},{2,0},{4,2},{6,4},{8,6},{10,8},{12,10},{14,12},{1,15},{3,1}... | collective-permute-start | bytes 196616 | tf_op jit(solution)/shard_map/ppermute | solution.py:16
  49.2 5.2 %collective-permute-start.12 = (f32[32,512]{1,0:T(8,128)S(1)}, f32[32,512]{1,0:T(8,128)S(1)}, u32[]{:S(2)}, u32[]{:S(2)}) collective-permute-start(f32[32,512]{1,0:T(8,128)S(1)} %slice_add_fusion.1), channel_id=1, source_target_pairs={{0,2},{2,4},{4,6},{6,8},{8,10},{10,12},{12,14},{14,0},{1,3},{3,5},... | collective-permute-start | bytes 196616 | tf_op jit(solution)/shard_map/ppermute | solution.py:16
  49.5 6.0 %collective-permute-start.11 = (f32[32,512]{1,0:T(8,128)S(1)}, f32[32,512]{1,0:T(8,128)S(1)}, u32[]{:S(2)}, u32[]{:S(2)}) collective-permute-start(f32[32,512]{1,0:T(8,128)S(1)} %pad_maximum_fusion.2), channel_id=1, source_target_pairs={{0,12},{2,14},{4,0},{6,2},{8,4},{10,6},{12,8},{14,10},{1,13},{3,15... | collective-permute-start | bytes 196616 | tf_op jit(solution)/shard_map/ppermute | solution.py:16
  52.7 6.5 %collective-permute-start.9 = (f32[32,512]{1,0:T(8,128)S(1)}, f32[32,512]{1,0:T(8,128)S(1)}, u32[]{:S(2)}, u32[]{:S(2)}) collective-permute-start(f32[32,512]{1,0:T(8,128)S(1)} %pad_maximum_fusion.1), channel_id=1, source_target_pairs={{0,4},{2,6},{4,8},{6,10},{8,12},{10,14},{12,0},{14,2},{1,5},{3,7},... | collective-permute-start | bytes 196616 | tf_op jit(solution)/shard_map/ppermute | solution.py:16
  59.8 6.5 %collective-permute-start.14 = (f32[32,512]{1,0:T(8,128)S(1)}, f32[32,512]{1,0:T(8,128)S(1)}, u32[]{:S(2)}, u32[]{:S(2)}) collective-permute-start(f32[32,512]{1,0:T(8,128)S(1)} %shard_map.57.refs_1_), channel_id=1, source_target_pairs={{0,64},{64,128},{128,192},{192,0},{1,65},{65,129},{129,193},{193,1... | collective-permute-start | bytes 196616 | tf_op jit(solution)/shard_map/ppermute | solution.py:16
  61.4 7.5 %collective-permute-start.16 = (f32[32,512]{1,0:T(8,128)S(1)}, f32[32,512]{1,0:T(8,128)S(1)}, u32[]{:S(2)}, u32[]{:S(2)}) collective-permute-start(f32[32,512]{1,0:T(8,128)S(1)} %shard_map.57.refs_1_), channel_id=1, source_target_pairs={{0,128},{64,192},{128,0},{192,64},{1,129},{65,193},{129,1},{193,65... | collective-permute-start | bytes 196616 | tf_op jit(solution)/shard_map/ppermute | solution.py:16
  64.3 4.6 %collective-permute-start.17 = (f32[32,512]{1,0:T(8,128)S(1)}, f32[32,512]{1,0:T(8,128)S(1)}, u32[]{:S(2)}, u32[]{:S(2)}) collective-permute-start(f32[32,512]{1,0:T(8,128)S(1)} %shard_map.57.refs_1_), channel_id=1, source_target_pairs={{0,192},{64,0},{128,64},{192,128},{1,193},{65,1},{129,65},{193,129... | collective-permute-start | bytes 196616 | tf_op jit(solution)/shard_map/ppermute | solution.py:16
  66.5 6.2 %collective-permute-start.15 = (f32[32,512]{1,0:T(8,128)S(1)}, f32[32,512]{1,0:T(8,128)S(1)}, u32[]{:S(2)}, u32[]{:S(2)}) collective-permute-start(f32[32,512]{1,0:T(8,128)S(1)} %shard_map.58.refs_2_), channel_id=1, source_target_pairs={{0,64},{64,128},{128,192},{192,0},{1,65},{65,129},{129,193},{193,1... | collective-permute-start | bytes 196616 | tf_op jit(solution)/shard_map/ppermute | solution.py:16
  66.7 6.4 %collective-permute-start.19 = (f32[32,512]{1,0:T(8,128)S(1)}, f32[32,512]{1,0:T(8,128)S(1)}, u32[]{:S(2)}, u32[]{:S(2)}) collective-permute-start(f32[32,512]{1,0:T(8,128)S(1)} %shard_map.58.refs_2_), channel_id=1, source_target_pairs={{0,128},{64,192},{128,0},{192,64},{1,129},{65,193},{129,1},{193,65... | collective-permute-start | bytes 196616 | tf_op jit(solution)/shard_map/ppermute | solution.py:16
  73.0 5.5 %collective-permute-start.18 = (f32[32,512]{1,0:T(8,128)S(1)}, f32[32,512]{1,0:T(8,128)S(1)}, u32[]{:S(2)}, u32[]{:S(2)}) collective-permute-start(f32[32,512]{1,0:T(8,128)S(1)} %shard_map.60.refs_1_), channel_id=1, source_target_pairs={{0,64},{64,128},{128,192},{192,0},{1,65},{65,129},{129,193},{193,1... | collective-permute-start | bytes 196616 | tf_op jit(solution)/shard_map/ppermute | solution.py:16

commit v10 on v9

--- a/solution.py
+++ b/solution.py
@@ -50,7 +50,7 @@
 
     def keep(mine, kept, given):
         for k in range(n_z):
-            ahead = lax.rem(k - place[1] + n_z, n_z)
+            ahead = lax.rem(k - place[1] + 2 * n_z - 2, n_z)
             kept[ahead] = total[k, mine]
             given[ahead] = total[k, 1 - mine]
 
@@ -173,22 +173,21 @@
     return result
 
 
-def reduced_over_z(blocks):
-    share = blocks.shape[1]
+def reduced_over_z(early, late):
+    share, rows = early.shape[1:]
     half = share // 2
-    rows = blocks.reshape(-1, blocks.shape[2])
-    middle = 4 * share + half
-    up = shifted(rows[3 * share : middle], "z", 2)
-    down = shifted(rows[middle : 6 * share], "z", -2)
-    far_up = jnp.concatenate([blocks[2, :half] + up[share:], blocks[2, half:]])
-    far_down = jnp.concatenate([blocks[6, :half], blocks[6, half:] + down[:half]])
+    far = early[1:].reshape(-1, rows)
+    up = shifted(far[: share + half], "z", 2)
+    down = shifted(far[share + half :], "z", -2)
+    far_up = jnp.concatenate([early[0, :half] + up[share:], early[0, half:]])
+    far_down = jnp.concatenate([late[0, :half], late[0, half:] + down[:half]])
     arrived = [
         shifted(far_up, "z", 2),
         shifted(far_down, "z", -2),
-        shifted(blocks[1] + up[:share], "z", 1),
-        shifted(blocks[7] + down[half:], "z", -1),
+        shifted(late[3] + up[:share], "z", 1),
+        shifted(late[1] + down[half:], "z", -1),
     ]
-    return functools.reduce(lambda a, b: a + b, arrived, blocks[0])
+    return functools.reduce(lambda a, b: a + b, arrived, late[2])
 
 
 def on_device(right_side, solved_factor, solved_users, diag_inverse, coupling):
@@ -211,9 +210,10 @@
     downs = [shifted(half, "x", -1) for half in (near[1, :cut], near[1, cut:] + down)]
     weights = hop_weights(diag_inverse, coupling)
     home, weights = lax.optimization_barrier((near[2], weights))
-    sums = [home[:cut] + ups[0] + downs[0], home[cut:] + ups[1] + downs[1]]
-    along_z = jnp.concatenate(sums)
-    residue = right_side.T - reduced_over_z(along_z)
+    early = home[:cut] + ups[0] + downs[0]
+    early, home = lax.optimization_barrier((early, home))
+    late = home[cut:] + ups[1] + downs[1]
+    residue = right_side.T - reduced_over_z(early, late)
     return chain(position, residue, diag_inverse, weights).T
 
 

time: 79.5 us -> 76.4 us (0.961)
  waiting for transfers between devices: 35.4 us -> 29.6 us
  starting transfers between devices: 28.2 us -> 30.9 us
    ppermute x20, waiting for transfers between devices: 35.4 us -> 29.6 us  [shifted(): lax.ppermute(value, axis, [(i, (i + by) % peers) for i in range(peers)])]
    ppermute x20, starting transfers between devices: 28.2 us -> 30.9 us  [shifted(): lax.ppermute(value, axis, [(i, (i + by) % peers) for i in range(peers)])]
where the time goes in v10:
time: 76.4 us; the launch traced here: 76.3 us
  starting transfers between devices  30.9 us (40%)
  waiting for transfers between devices  29.6 us (39%)
  Pallas kernels  14.6 us (19%)
    ppermute x20, starting transfers between devices, shifted(): lax.ppermute(value, axis, [(i, (i + by) % peers) for i in range(peers)])  30.9 us
    ppermute x20, waiting for transfers between devices, shifted(): lax.ppermute(value, axis, [(i, (i + by) % peers) for i in range(peers)])  29.6 us
    pallas_call x1, Pallas kernels, product(): pl.pallas_call(functools.partial(product_body, n_z, n_core), grid_spec=pl...  8.62 us
    pallas_call x1, Pallas kernels, hop_weights(): pl.pallas_call(weights_body, grid=(count,), in_specs=[pl.BlockSpec((block...  3.43 us
    pallas_call x5, Pallas kernels, applied(): pl.pallas_call(functools.partial(apply_body, [group for group, _ in value...  2.02 us
  transfers between devices with their start and end apart: 20, of which 13 were waited for; matrix products, arithmetic and copies ran while one was open for 1% of the time, Pallas kernels for 6%

profile of v10, /device:TPU:32, one launch (start us, length us, event | category | flops | bytes accessed | tf_op | source)
XLA Modules:
  0.0 76.3 jit_solution(16879662077489791873)
XLA Ops:
  0.0 0.1 stack.27.place
  0.1 8.6 %shard_map.55 = (f32[8,32,512]{2,1,0:T(8,128)S(1)}, f32[3,8,32,512]{3,2,1,0:T(8,128)S(1)}, f32[8,32,512]{2,1,0:T(8,128)S(1)}, f32[3,8,32,512]{3,2,1,0:T(8,128)S(1)}) custom-call(s32[6]{0:T(128)S(1)} %stack.27.place, f32[768,2048]{1,0:T(8,128)} %users.1, f32[512,768]{1,0:T(8,128)} %factor.1), custom_call_target="tpu_custom_call" | custom-call | flops 4831838208 | bytes 12058624 | tf_op jit(solution)/shard_map/pallas_call | solution.py:77
  8.7 0.1 collective-permute-start
  8.8 1.9 %collective-permute-done = f32[8,32,512]{2,1,0:T(8,128)S(1)} collective-permute-done((f32[8,32,512]{2,1,0:T(8,128)S(1)}, f32[8,32,512]{2,1,0:T(8,128)S(1)}, u32[]{:S(2)}, u32[]{:S(2)}) %collective-permute-start) | collective-permute-done | bytes 524320 | tf_op jit(solution)/shard_map/ppermute | solution.py:16
  10.7 0.1 collective-permute-start.1
  10.8 0.1 add.78
  11.0 2.9 %collective-permute-start.6 = (f32[4,32,512]{2,1,0:T(8,128)S(1)}, f32[4,32,512]{2,1,0:T(8,128)S(1)}, u32[]{:S(2)}, u32[]{:S(2)}) collective-permute-start(f32[4,32,512]{2,1,0:T(8,128)S(1)} %get-tuple-element.35), channel_id=1, source_target_pairs={{0,48},{16,0},{32,16},{48,32},{1,49},{17,1},{33,17},{49,33},{2,50}... | collective-permute-start | bytes 786440 | tf_op jit(solution)/shard_map/ppermute | solution.py:16
  13.8 0.0 collective-permute-start.2
  13.8 0.3 collective-permute-done.1
  14.1 0.0 copy-start.1
  14.1 0.3 add.77
  14.5 0.0 copy-start
  14.5 3.0 %collective-permute-start.4 = (f32[4,32,512]{2,1,0:T(8,128)S(1)}, f32[4,32,512]{2,1,0:T(8,128)S(1)}, u32[]{:S(2)}, u32[]{:S(2)}) collective-permute-start(f32[4,32,512]{2,1,0:T(8,128)S(1)} %get-tuple-element.32), channel_id=1, source_target_pairs={{0,48},{16,0},{32,16},{48,32},{1,49},{17,1},{33,17},{49,33},{2,50}... | collective-permute-start | bytes 786440 | tf_op jit(solution)/shard_map/ppermute | solution.py:16
  17.6 2.9 %collective-permute-done.6 = f32[4,32,512]{2,1,0:T(8,128)S(1)} collective-permute-done((f32[4,32,512]{2,1,0:T(8,128)S(1)}, f32[4,32,512]{2,1,0:T(8,128)S(1)}, u32[]{:S(2)}, u32[]{:S(2)}) %collective-permute-start.6) | collective-permute-done | bytes 262176 | tf_op jit(solution)/shard_map/ppermute | solution.py:16
  20.5 2.9 %collective-permute-done.2 = f32[4,32,512]{2,1,0:T(8,128)S(1)} collective-permute-done((f32[4,32,512]{2,1,0:T(8,128)S(1)}, f32[4,32,512]{2,1,0:T(8,128)S(1)}, u32[]{:S(2)}, u32[]{:S(2)}) %collective-permute-start.2) | collective-permute-done | bytes 262176 | tf_op jit(solution)/shard_map/ppermute | solution.py:16
  23.3 0.1 fusion
  23.4 0.1 collective-permute-start.3
  23.5 0.0 copy-done.1
  23.5 0.0 copy-done
  23.5 3.4 %shard_map.56 = (bf16[3,512,512]{2,1,0:T(8,128)(2,1)S(1)}, bf16[3,512,512]{2,1,0:T(8,128)(2,1)S(1)}) custom-call(f32[512,512]{1,0:T(8,128)S(1)} %copy-done, f32[512,1536]{1,0:T(8,128)S(1)} %copy-done.1), custom_call_target="tpu_custom_call" | custom-call | flops 2415919104 | bytes 8388608 | tf_op jit(solution)/shard_map/pallas_call | solution.py:106
  27.0 3.3 %collective-permute-start.7 = (f32[4,32,512]{2,1,0:T(8,128)S(1)}, f32[4,32,512]{2,1,0:T(8,128)S(1)}, u32[]{:S(2)}, u32[]{:S(2)}) collective-permute-start(f32[4,32,512]{2,1,0:T(8,128)S(1)} %get-tuple-element.33), channel_id=1, source_target_pairs={{0,48},{16,0},{32,16},{48,32},{1,49},{17,1},{33,17},{49,33},{2,50}... | collective-permute-start | bytes 786440 | tf_op jit(solution)/shard_map/ppermute | solution.py:16
  30.3 0.0 collective-permute-start.5
  30.3 0.0 collective-permute-done.4
  30.3 1.9 %collective-permute-done.3 = f32[4,32,512]{2,1,0:T(8,128)S(1)} collective-permute-done((f32[4,32,512]{2,1,0:T(8,128)S(1)}, f32[4,32,512]{2,1,0:T(8,128)S(1)}, u32[]{:S(2)}, u32[]{:S(2)}) %collective-permute-start.3) | collective-permute-done | bytes 262176 | tf_op jit(solution)/shard_map/ppermute | solution.py:16
  32.2 0.1 add_add_fusion.1
  32.2 0.0 copy-start.2
  32.3 3.3 %collective-permute-start.8 = (f32[48,512]{1,0:T(8,128)S(1)}, f32[48,512]{1,0:T(8,128)S(1)}, u32[]{:S(2)}, u32[]{:S(2)}) collective-permute-start(f32[48,512]{1,0:T(8,128)S(1)} %get-tuple-element.39), channel_id=1, source_target_pairs={{0,4},{2,6},{4,8},{6,10},{8,12},{10,14},{12,0},{14,2},{1,5},{3,7},... | collective-permute-start | bytes 294920 | tf_op jit(solution)/shard_map/ppermute | solution.py:16
  35.6 2.2 %collective-permute-start.10 = (f32[48,512]{1,0:T(8,128)S(1)}, f32[48,512]{1,0:T(8,128)S(1)}, u32[]{:S(2)}, u32[]{:S(2)}) collective-permute-start(f32[48,512]{1,0:T(8,128)S(1)} %get-tuple-element.40), channel_id=1, source_target_pairs={{0,12},{2,14},{4,0},{6,2},{8,4},{10,6},{12,8},{14,10},{1,13},{3,15... | collective-permute-start | bytes 294920 | tf_op jit(solution)/shard_map/ppermute | solution.py:16
  37.8 0.0 collective-permute-done.7
  37.8 0.5 collective-permute-done.5
  38.4 0.1 add_add_fusion
  38.5 2.9 %collective-permute-done.8 = f32[48,512]{1,0:T(8,128)S(1)} collective-permute-done((f32[48,512]{1,0:T(8,128)S(1)}, f32[48,512]{1,0:T(8,128)S(1)}, u32[]{:S(2)}, u32[]{:S(2)}) %collective-permute-start.8) | collective-permute-done | bytes 98336 | tf_op jit(solution)/shard_map/ppermute | solution.py:16
  41.4 1.4 %collective-permute-done.10 = f32[48,512]{1,0:T(8,128)S(1)} collective-permute-done((f32[48,512]{1,0:T(8,128)S(1)}, f32[48,512]{1,0:T(8,128)S(1)}, u32[]{:S(2)}, u32[]{:S(2)}) %collective-permute-start.10) | collective-permute-done | bytes 98336 | tf_op jit(solution)/shard_map/ppermute | solution.py:16
  42.8 0.4 collective-permute-start.13
  43.2 2.9 %collective-permute-start.12 = (f32[32,512]{1,0:T(8,128)S(1)}, f32[32,512]{1,0:T(8,128)S(1)}, u32[]{:S(2)}, u32[]{:S(2)}) collective-permute-start(f32[32,512]{1,0:T(8,128)S(1)} %get-tuple-element.37), channel_id=1, source_target_pairs={{0,2},{2,4},{4,6},{6,8},{8,10},{10,12},{12,14},{14,0},{1,3},{3,5},... | collective-permute-start | bytes 196616 | tf_op jit(solution)/shard_map/ppermute | solution.py:16
  46.1 3.1 %collective-permute-start.11 = (f32[32,512]{1,0:T(8,128)S(1)}, f32[32,512]{1,0:T(8,128)S(1)}, u32[]{:S(2)}, u32[]{:S(2)}) collective-permute-start(f32[32,512]{1,0:T(8,128)S(1)} %pad_maximum_fusion.1), channel_id=1, source_target_pairs={{0,12},{2,14},{4,0},{6,2},{8,4},{10,6},{12,8},{14,10},{1,13},{3,15... | collective-permute-start | bytes 196616 | tf_op jit(solution)/shard_map/ppermute | solution.py:16
  49.2 1.6 %collective-permute-start.9 = (f32[32,512]{1,0:T(8,128)S(1)}, f32[32,512]{1,0:T(8,128)S(1)}, u32[]{:S(2)}, u32[]{:S(2)}) collective-permute-start(f32[32,512]{1,0:T(8,128)S(1)} %pad_maximum_fusion), channel_id=1, source_target_pairs={{0,4},{2,6},{4,8},{6,10},{8,12},{10,14},{12,0},{14,2},{1,5},{3,7},... | collective-permute-start | bytes 196616 | tf_op jit(solution)/shard_map/ppermute | solution.py:16
  50.9 0.0 collective-permute-done.13
  50.9 0.0 collective-permute-done.12
  50.9 2.1 %collective-permute-done.11 = f32[32,512]{1,0:T(8,128)S(1)} collective-permute-done((f32[32,512]{1,0:T(8,128)S(1)}, f32[32,512]{1,0:T(8,128)S(1)}, u32[]{:S(2)}, u32[]{:S(2)}) %collective-permute-start.11) | collective-permute-done | bytes 65568 | tf_op jit(solution)/shard_map/ppermute | solution.py:16
  53.0 2.7 %collective-permute-done.9 = f32[32,512]{1,0:T(8,128)S(1)} collective-permute-done((f32[32,512]{1,0:T(8,128)S(1)}, f32[32,512]{1,0:T(8,128)S(1)}, u32[]{:S(2)}, u32[]{:S(2)}) %collective-permute-start.9) | collective-permute-done | bytes 65568 | tf_op jit(solution)/shard_map/ppermute | solution.py:16
  55.7 0.0 copy-done.2
  55.7 0.6 shard_map.57.refs_1_
  56.3 1.6 %collective-permute-start.14 = (f32[32,512]{1,0:T(8,128)S(1)}, f32[32,512]{1,0:T(8,128)S(1)}, u32[]{:S(2)}, u32[]{:S(2)}) collective-permute-start(f32[32,512]{1,0:T(8,128)S(1)} %shard_map.57.refs_1_), channel_id=1, source_target_pairs={{0,64},{64,128},{128,192},{192,0},{1,65},{65,129},{129,193},{193,1... | collective-permute-start | bytes 196616 | tf_op jit(solution)/shard_map/ppermute | solution.py:16
  57.9 2.9 %collective-permute-start.16 = (f32[32,512]{1,0:T(8,128)S(1)}, f32[32,512]{1,0:T(8,128)S(1)}, u32[]{:S(2)}, u32[]{:S(2)}) collective-permute-start(f32[32,512]{1,0:T(8,128)S(1)} %shard_map.57.refs_1_), channel_id=1, source_target_pairs={{0,128},{64,192},{128,0},{192,64},{1,129},{65,193},{129,1},{193,65... | collective-permute-start | bytes 196616 | tf_op jit(solution)/shard_map/ppermute | solution.py:16
  60.8 1.3 %collective-permute-start.17 = (f32[32,512]{1,0:T(8,128)S(1)}, f32[32,512]{1,0:T(8,128)S(1)}, u32[]{:S(2)}, u32[]{:S(2)}) collective-permute-start(f32[32,512]{1,0:T(8,128)S(1)} %shard_map.57.refs_1_), channel_id=1, source_target_pairs={{0,192},{64,0},{128,64},{192,128},{1,193},{65,1},{129,65},{193,129... | collective-permute-start | bytes 196616 | tf_op jit(solution)/shard_map/ppermute | solution.py:16
  62.1 1.0 %collective-permute-done.14.refs_0_ = f32[32,512]{1,0:T(8,128)S(1)} collective-permute-done((f32[32,512]{1,0:T(8,128)S(1)}, f32[32,512]{1,0:T(8,128)S(1)}, u32[]{:S(2)}, u32[]{:S(2)}) %collective-permute-start.14) | collective-permute-done | bytes 65568 | tf_op jit(solution)/shard_map/ppermute | solution.py:16
  63.2 0.3 shard_map.58.refs_2_
  63.4 0.0 collective-permute-start.15
  63.5 2.0 %collective-permute-start.19 = (f32[32,512]{1,0:T(8,128)S(1)}, f32[32,512]{1,0:T(8,128)S(1)}, u32[]{:S(2)}, u32[]{:S(2)}) collective-permute-start(f32[32,512]{1,0:T(8,128)S(1)} %shard_map.58.refs_2_), channel_id=1, source_target_pairs={{0,128},{64,192},{128,0},{192,64},{1,129},{65,193},{129,1},{193,65... | collective-permute-start | bytes 196616 | tf_op jit(solution)/shard_map/ppermute | solution.py:16
  65.4 0.0 collective-permute-done.16.refs_0_
  65.4 0.0 collective-permute-done.17.refs_1_
  65.4 0.3 shard_map.59.refs_1_
  65.7 3.9 %collective-permute-done.15.refs_0_ = f32[32,512]{1,0:T(8,128)S(1)} collective-permute-done((f32[32,512]{1,0:T(8,128)S(1)}, f32[32,512]{1,0:T(8,128)S(1)}, u32[]{:S(2)}, u32[]{:S(2)}) %collective-permute-start.15) | collective-permute-done | bytes 65568 | tf_op jit(solution)/shard_map/ppermute | solution.py:16
  69.6 0.3 shard_map.60.refs_1_
  69.9 0.0 collective-permute-start.18
  69.9 0.0 collective-permute-done.19.refs_0_
  69.9 0.3 shard_map.61.refs_1_
  70.2 5.2 %collective-permute-done.18.refs_0_ = f32[32,512]{1,0:T(8,128)S(1)} collective-permute-done((f32[32,512]{1,0:T(8,128)S(1)}, f32[32,512]{1,0:T(8,128)S(1)}, u32[]{:S(2)}, u32[]{:S(2)}) %collective-permute-start.18) | collective-permute-done | bytes 65568 | tf_op jit(solution)/shard_map/ppermute | solution.py:16
  75.4 0.9 %shard_map.62 = f32[32,512]{1,0:T(8,128)} custom-call(s32[1]{0:T(128)} %bitcast.place, f32[32,512]{1,0:T(8,128)S(1)} %collective-permute-done.18.refs_0_, f32[32,512]{1,0:T(8,128)S(1)} %shard_map.61.refs_1_, bf16[3,512,512]{2,1,0:T(8,128)(2,1)S(1)} %get-tuple-element.29.refs_2_.refs_3_, bf16[3,512,512]{2,1,0:T(8,128)(2,1)S(1)} %get-tuple-element.30.refs_3_.refs_4_), custom_call_target="tpu_custom_call" | custom-call | tf_op jit(solution)/shard_map/pallas_call | solution.py:149
  (13 shorter events, 0.2 us)
Async XLA Ops:
  8.7 2.0 %collective-permute-start = (f32[8,32,512]{2,1,0:T(8,128)S(1)}, f32[8,32,512]{2,1,0:T(8,128)S(1)}, u32[]{:S(2)}, u32[]{:S(2)}) collective-permute-start(f32[8,32,512]{2,1,0:T(8,128)S(1)} %get-tuple-element.20), channel_id=1, source_target_pairs={{0,1},{1,0},{2,3},{3,2},{4,5},{5,4},{6,7},{7,6},{8,9},{9,8},{10,11... | collective-permute-start | bytes 1572872 | tf_op jit(solution)/shard_map/ppermute | solution.py:16
  10.7 3.4 %collective-permute-start.1 = (f32[3,8,32,512]{3,2,1,0:T(8,128)S(1)}, f32[3,8,32,512]{3,2,1,0:T(8,128)S(1)}, u32[]{:S(2)}, u32[]{:S(2)}) collective-permute-start(f32[3,8,32,512]{3,2,1,0:T(8,128)S(1)} %get-tuple-element.21), channel_id=1, source_target_pairs={{0,1},{1,0},{2,3},{3,2},{4,5},{5,4},{6,7},{7,6},{8,9},{9,8},{10,11... | collective-permute-start | bytes 4718600 | tf_op jit(solution)/shard_map/ppermute | solution.py:16
  11.0 9.5 %collective-permute-start.6 = (f32[4,32,512]{2,1,0:T(8,128)S(1)}, f32[4,32,512]{2,1,0:T(8,128)S(1)}, u32[]{:S(2)}, u32[]{:S(2)}) collective-permute-start(f32[4,32,512]{2,1,0:T(8,128)S(1)} %get-tuple-element.35), channel_id=1, source_target_pairs={{0,48},{16,0},{32,16},{48,32},{1,49},{17,1},{33,17},{49,33},{2,50}... | collective-permute-start | bytes 786440 | tf_op jit(solution)/shard_map/ppermute | solution.py:16
  13.8 9.5 %collective-permute-start.2 = (f32[4,32,512]{2,1,0:T(8,128)S(1)}, f32[4,32,512]{2,1,0:T(8,128)S(1)}, u32[]{:S(2)}, u32[]{:S(2)}) collective-permute-start(f32[4,32,512]{2,1,0:T(8,128)S(1)} %get-tuple-element.36), channel_id=1, source_target_pairs={{0,16},{16,32},{32,48},{48,0},{1,17},{17,33},{33,49},{49,1},{2,18}... | collective-permute-start | bytes 786440 | tf_op jit(solution)/shard_map/ppermute | solution.py:16
  14.1 9.4 %copy-start.1 = (f32[512,1536]{1,0:T(8,128)S(1)}, f32[512,1536]{1,0:T(8,128)}, u32[]{:S(2)}) copy-start(f32[512,1536]{1,0:T(8,128)} %coupling.1) | copy-start | bytes 9437188
  14.5 9.1 %copy-start = (f32[512,512]{1,0:T(8,128)S(1)}, f32[512,512]{1,0:T(8,128)}, u32[]{:S(2)}) copy-start(f32[512,512]{1,0:T(8,128)} %diag.3) | copy-start | bytes 3145732
  14.5 15.8 %collective-permute-start.4 = (f32[4,32,512]{2,1,0:T(8,128)S(1)}, f32[4,32,512]{2,1,0:T(8,128)S(1)}, u32[]{:S(2)}, u32[]{:S(2)}) collective-permute-start(f32[4,32,512]{2,1,0:T(8,128)S(1)} %get-tuple-element.32), channel_id=1, source_target_pairs={{0,48},{16,0},{32,16},{48,32},{1,49},{17,1},{33,17},{49,33},{2,50}... | collective-permute-start | bytes 786440 | tf_op jit(solution)/shard_map/ppermute | solution.py:16
  23.4 8.7 %collective-permute-start.3 = (f32[4,32,512]{2,1,0:T(8,128)S(1)}, f32[4,32,512]{2,1,0:T(8,128)S(1)}, u32[]{:S(2)}, u32[]{:S(2)}) collective-permute-start(f32[4,32,512]{2,1,0:T(8,128)S(1)} %get-tuple-element.34), channel_id=1, source_target_pairs={{0,16},{16,32},{32,48},{48,0},{1,17},{17,33},{33,49},{49,1},{2,18}... | collective-permute-start | bytes 786440 | tf_op jit(solution)/shard_map/ppermute | solution.py:16
  27.0 10.8 %collective-permute-start.7 = (f32[4,32,512]{2,1,0:T(8,128)S(1)}, f32[4,32,512]{2,1,0:T(8,128)S(1)}, u32[]{:S(2)}, u32[]{:S(2)}) collective-permute-start(f32[4,32,512]{2,1,0:T(8,128)S(1)} %get-tuple-element.33), channel_id=1, source_target_pairs={{0,48},{16,0},{32,16},{48,32},{1,49},{17,1},{33,17},{49,33},{2,50}... | collective-permute-start | bytes 786440 | tf_op jit(solution)/shard_map/ppermute | solution.py:16
  30.3 8.1 %collective-permute-start.5 = (f32[4,32,512]{2,1,0:T(8,128)S(1)}, f32[4,32,512]{2,1,0:T(8,128)S(1)}, u32[]{:S(2)}, u32[]{:S(2)}) collective-permute-start(f32[4,32,512]{2,1,0:T(8,128)S(1)} %get-tuple-element.31), channel_id=1, source_target_pairs={{0,16},{16,32},{32,48},{48,0},{1,17},{17,33},{33,49},{49,1},{2,18}... | collective-permute-start | bytes 786440 | tf_op jit(solution)/shard_map/ppermute | solution.py:16
  32.2 23.5 %copy-start.2 = (f32[512,32]{0,1:T(8,128)S(1)}, f32[512,32]{0,1:T(8,128)}, u32[]{:S(2)}) copy-start(f32[512,32]{0,1:T(8,128)} %param.5) | copy-start | bytes 196612
  32.3 9.1 %collective-permute-start.8 = (f32[48,512]{1,0:T(8,128)S(1)}, f32[48,512]{1,0:T(8,128)S(1)}, u32[]{:S(2)}, u32[]{:S(2)}) collective-permute-start(f32[48,512]{1,0:T(8,128)S(1)} %get-tuple-element.39), channel_id=1, source_target_pairs={{0,4},{2,6},{4,8},{6,10},{8,12},{10,14},{12,0},{14,2},{1,5},{3,7},... | collective-permute-start | bytes 294920 | tf_op jit(solution)/shard_map/ppermute | solution.py:16
  35.6 7.1 %collective-permute-start.10 = (f32[48,512]{1,0:T(8,128)S(1)}, f32[48,512]{1,0:T(8,128)S(1)}, u32[]{:S(2)}, u32[]{:S(2)}) collective-permute-start(f32[48,512]{1,0:T(8,128)S(1)} %get-tuple-element.40), channel_id=1, source_target_pairs={{0,12},{2,14},{4,0},{6,2},{8,4},{10,6},{12,8},{14,10},{1,13},{3,15... | collective-permute-start | bytes 294920 | tf_op jit(solution)/shard_map/ppermute | solution.py:16
  42.8 8.1 %collective-permute-start.13 = (f32[32,512]{1,0:T(8,128)S(1)}, f32[32,512]{1,0:T(8,128)S(1)}, u32[]{:S(2)}, u32[]{:S(2)}) collective-permute-start(f32[32,512]{1,0:T(8,128)S(1)} %get-tuple-element.38), channel_id=1, source_target_pairs={{0,14},{2,0},{4,2},{6,4},{8,6},{10,8},{12,10},{14,12},{1,15},{3,1}... | collective-permute-start | bytes 196616 | tf_op jit(solution)/shard_map/ppermute | solution.py:16
  43.2 7.7 %collective-permute-start.12 = (f32[32,512]{1,0:T(8,128)S(1)}, f32[32,512]{1,0:T(8,128)S(1)}, u32[]{:S(2)}, u32[]{:S(2)}) collective-permute-start(f32[32,512]{1,0:T(8,128)S(1)} %get-tuple-element.37), channel_id=1, source_target_pairs={{0,2},{2,4},{4,6},{6,8},{8,10},{10,12},{12,14},{14,0},{1,3},{3,5},... | collective-permute-start | bytes 196616 | tf_op jit(solution)/shard_map/ppermute | solution.py:16
  46.1 6.9 %collective-permute-start.11 = (f32[32,512]{1,0:T(8,128)S(1)}, f32[32,512]{1,0:T(8,128)S(1)}, u32[]{:S(2)}, u32[]{:S(2)}) collective-permute-start(f32[32,512]{1,0:T(8,128)S(1)} %pad_maximum_fusion.1), channel_id=1, source_target_pairs={{0,12},{2,14},{4,0},{6,2},{8,4},{10,6},{12,8},{14,10},{1,13},{3,15... | collective-permute-start | bytes 196616 | tf_op jit(solution)/shard_map/ppermute | solution.py:16
  49.2 6.5 %collective-permute-start.9 = (f32[32,512]{1,0:T(8,128)S(1)}, f32[32,512]{1,0:T(8,128)S(1)}, u32[]{:S(2)}, u32[]{:S(2)}) collective-permute-start(f32[32,512]{1,0:T(8,128)S(1)} %pad_maximum_fusion), channel_id=1, source_target_pairs={{0,4},{2,6},{4,8},{6,10},{8,12},{10,14},{12,0},{14,2},{1,5},{3,7},... | collective-permute-start | bytes 196616 | tf_op jit(solution)/shard_map/ppermute | solution.py:16
  56.3 6.9 %collective-permute-start.14 = (f32[32,512]{1,0:T(8,128)S(1)}, f32[32,512]{1,0:T(8,128)S(1)}, u32[]{:S(2)}, u32[]{:S(2)}) collective-permute-start(f32[32,512]{1,0:T(8,128)S(1)} %shard_map.57.refs_1_), channel_id=1, source_target_pairs={{0,64},{64,128},{128,192},{192,0},{1,65},{65,129},{129,193},{193,1... | collective-permute-start | bytes 196616 | tf_op jit(solution)/shard_map/ppermute | solution.py:16
  57.9 7.5 %collective-permute-start.16 = (f32[32,512]{1,0:T(8,128)S(1)}, f32[32,512]{1,0:T(8,128)S(1)}, u32[]{:S(2)}, u32[]{:S(2)}) collective-permute-start(f32[32,512]{1,0:T(8,128)S(1)} %shard_map.57.refs_1_), channel_id=1, source_target_pairs={{0,128},{64,192},{128,0},{192,64},{1,129},{65,193},{129,1},{193,65... | collective-permute-start | bytes 196616 | tf_op jit(solution)/shard_map/ppermute | solution.py:16
  60.8 4.6 %collective-permute-start.17 = (f32[32,512]{1,0:T(8,128)S(1)}, f32[32,512]{1,0:T(8,128)S(1)}, u32[]{:S(2)}, u32[]{:S(2)}) collective-permute-start(f32[32,512]{1,0:T(8,128)S(1)} %shard_map.57.refs_1_), channel_id=1, source_target_pairs={{0,192},{64,0},{128,64},{192,128},{1,193},{65,1},{129,65},{193,129... | collective-permute-start | bytes 196616 | tf_op jit(solution)/shard_map/ppermute | solution.py:16
  63.4 6.2 %collective-permute-start.15 = (f32[32,512]{1,0:T(8,128)S(1)}, f32[32,512]{1,0:T(8,128)S(1)}, u32[]{:S(2)}, u32[]{:S(2)}) collective-permute-start(f32[32,512]{1,0:T(8,128)S(1)} %shard_map.58.refs_2_), channel_id=1, source_target_pairs={{0,64},{64,128},{128,192},{192,0},{1,65},{65,129},{129,193},{193,1... | collective-permute-start | bytes 196616 | tf_op jit(solution)/shard_map/ppermute | solution.py:16
  63.5 6.5 %collective-permute-start.19 = (f32[32,512]{1,0:T(8,128)S(1)}, f32[32,512]{1,0:T(8,128)S(1)}, u32[]{:S(2)}, u32[]{:S(2)}) collective-permute-start(f32[32,512]{1,0:T(8,128)S(1)} %shard_map.58.refs_2_), channel_id=1, source_target_pairs={{0,128},{64,192},{128,0},{192,64},{1,129},{65,193},{129,1},{193,65... | collective-permute-start | bytes 196616 | tf_op jit(solution)/shard_map/ppermute | solution.py:16
  69.9 5.5 %collective-permute-start.18 = (f32[32,512]{1,0:T(8,128)S(1)}, f32[32,512]{1,0:T(8,128)S(1)}, u32[]{:S(2)}, u32[]{:S(2)}) collective-permute-start(f32[32,512]{1,0:T(8,128)S(1)} %shard_map.60.refs_1_), channel_id=1, source_target_pairs={{0,64},{64,128},{128,192},{192,0},{1,65},{65,129},{129,193},{193,1... | collective-permute-start | bytes 196616 | tf_op jit(solution)/shard_map/ppermute | solution.py:16

commit v11 on v10

--- a/solution.py
+++ b/solution.py
@@ -206,10 +206,11 @@
     cut = far.shape[0] // 2
     up = shifted(far[:cut], "x", 1)
     down = shifted(far[cut:], "x", -1)
-    ups = [shifted(half, "x", 1) for half in (near[0, :cut] + up, near[0, cut:])]
+    weights = hop_weights(diag_inverse, coupling)
+    ahead, weights = lax.optimization_barrier((near[0], weights))
+    ups = [shifted(half, "x", 1) for half in (ahead[:cut] + up, ahead[cut:])]
     downs = [shifted(half, "x", -1) for half in (near[1, :cut], near[1, cut:] + down)]
-    weights = hop_weights(diag_inverse, coupling)
-    home, weights = lax.optimization_barrier((near[2], weights))
+    home = near[2]
     early = home[:cut] + ups[0] + downs[0]
     early, home = lax.optimization_barrier((early, home))
     late = home[cut:] + ups[1] + downs[1]

time: 76.4 us -> 79.8 us (1.045)
  the two profiles are of different devices: /device:TPU:32 before, /device:TPU:64 now
where the time goes in v11:
time: 79.8 us; the launch traced here: 79.7 us
  waiting for transfers between devices  36.6 us (46%)
  starting transfers between devices  26.9 us (34%)
  Pallas kernels  15 us (19%)
    ppermute x20, waiting for transfers between devices, shifted(): lax.ppermute(value, axis, [(i, (i + by) % peers) for i in range(peers)])  36.6 us
    ppermute x20, starting transfers between devices, shifted(): lax.ppermute(value, axis, [(i, (i + by) % peers) for i in range(peers)])  26.9 us
    pallas_call x1, Pallas kernels, product(): pl.pallas_call(functools.partial(product_body, n_z, n_core), grid_spec=pl...  8.89 us
    pallas_call x1, Pallas kernels, hop_weights(): pl.pallas_call(weights_body, grid=(count,), in_specs=[pl.BlockSpec((block...  3.54 us
    pallas_call x5, Pallas kernels, applied(): pl.pallas_call(functools.partial(apply_body, [group for group, _ in value...  2.01 us
  transfers between devices with their start and end apart: 20, of which 11 were waited for; matrix products, arithmetic and copies ran while one was open for 1% of the time, Pallas kernels for 6%

profile of v11, /device:TPU:64, one launch (start us, length us, event | category | flops | bytes accessed | tf_op | source)
XLA Modules:
  0.0 79.7 jit_solution(14801592305339122824)
XLA Ops:
  0.0 0.1 stack.27.place
  0.1 0.0 copy-start
  0.1 0.0 copy-start.1
  0.1 8.9 %shard_map.55 = (f32[8,32,512]{2,1,0:T(8,128)S(1)}, f32[3,8,32,512]{3,2,1,0:T(8,128)S(1)}, f32[8,32,512]{2,1,0:T(8,128)S(1)}, f32[3,8,32,512]{3,2,1,0:T(8,128)S(1)}) custom-call(s32[6]{0:T(128)S(1)} %stack.27.place, f32[768,2048]{1,0:T(8,128)} %users.1, f32[512,768]{1,0:T(8,128)} %factor.1), custom_call_target="tpu_custom_call" | custom-call | flops 4831838208 | bytes 12058624 | tf_op jit(solution)/shard_map/pallas_call | solution.py:77
  9.0 0.1 collective-permute-start
  9.1 1.9 %collective-permute-done = f32[8,32,512]{2,1,0:T(8,128)S(1)} collective-permute-done((f32[8,32,512]{2,1,0:T(8,128)S(1)}, f32[8,32,512]{2,1,0:T(8,128)S(1)}, u32[]{:S(2)}, u32[]{:S(2)}) %collective-permute-start) | collective-permute-done | bytes 524320 | tf_op jit(solution)/shard_map/ppermute | solution.py:16
  11.0 0.1 collective-permute-start.1
  11.1 0.0 copy-done
  11.1 0.0 copy-done.1
  11.1 3.5 %shard_map.56 = (bf16[3,512,512]{2,1,0:T(8,128)(2,1)S(1)}, bf16[3,512,512]{2,1,0:T(8,128)(2,1)S(1)}) custom-call(f32[512,512]{1,0:T(8,128)S(1)} %copy-done, f32[512,1536]{1,0:T(8,128)S(1)} %copy-done.1), custom_call_target="tpu_custom_call" | custom-call | flops 2415919104 | bytes 8388608 | tf_op jit(solution)/shard_map/pallas_call | solution.py:106
  14.7 0.1 add.78
  14.8 2.9 %collective-permute-start.6 = (f32[4,32,512]{2,1,0:T(8,128)S(1)}, f32[4,32,512]{2,1,0:T(8,128)S(1)}, u32[]{:S(2)}, u32[]{:S(2)}) collective-permute-start(f32[4,32,512]{2,1,0:T(8,128)S(1)} %get-tuple-element.37), channel_id=1, source_target_pairs={{0,48},{16,0},{32,16},{48,32},{1,49},{17,1},{33,17},{49,33},{2,50}... | collective-permute-start | bytes 786440 | tf_op jit(solution)/shard_map/ppermute | solution.py:16
  17.7 0.0 collective-permute-start.2
  17.7 0.0 collective-permute-done.1
  17.7 0.3 add.77
  18.0 3.3 %collective-permute-start.4 = (f32[4,32,512]{2,1,0:T(8,128)S(1)}, f32[4,32,512]{2,1,0:T(8,128)S(1)}, u32[]{:S(2)}, u32[]{:S(2)}) collective-permute-start(f32[4,32,512]{2,1,0:T(8,128)S(1)} %slice_bitcast_fusion.3), channel_id=1, source_target_pairs={{0,48},{16,0},{32,16},{48,32},{1,49},{17,1},{33,17},{49,33},{2,50}... | collective-permute-start | bytes 786440 | tf_op jit(solution)/shard_map/ppermute | solution.py:16
  21.3 0.1 slice_bitcast_fusion
  21.4 5.7 %collective-permute-done.2 = f32[4,32,512]{2,1,0:T(8,128)S(1)} collective-permute-done((f32[4,32,512]{2,1,0:T(8,128)S(1)}, f32[4,32,512]{2,1,0:T(8,128)S(1)}, u32[]{:S(2)}, u32[]{:S(2)}) %collective-permute-start.2) | collective-permute-done | bytes 262176 | tf_op jit(solution)/shard_map/ppermute | solution.py:16
  27.2 0.1 fusion.8
  27.2 0.1 collective-permute-start.3
  27.3 0.1 collective-permute-start.5
  27.4 0.0 collective-permute-done.6
  27.4 1.9 %collective-permute-done.4 = f32[4,32,512]{2,1,0:T(8,128)S(1)} collective-permute-done((f32[4,32,512]{2,1,0:T(8,128)S(1)}, f32[4,32,512]{2,1,0:T(8,128)S(1)}, u32[]{:S(2)}, u32[]{:S(2)}) %collective-permute-start.4) | collective-permute-done | bytes 262176 | tf_op jit(solution)/shard_map/ppermute | solution.py:16
  29.4 8.4 %collective-permute-done.3 = f32[4,32,512]{2,1,0:T(8,128)S(1)} collective-permute-done((f32[4,32,512]{2,1,0:T(8,128)S(1)}, f32[4,32,512]{2,1,0:T(8,128)S(1)}, u32[]{:S(2)}, u32[]{:S(2)}) %collective-permute-start.3) | collective-permute-done | bytes 262176 | tf_op jit(solution)/shard_map/ppermute | solution.py:16
  37.8 0.1 fusion
  37.9 0.0 copy-start.2
  37.9 4.6 %collective-permute-start.8 = (f32[48,512]{1,0:T(8,128)S(1)}, f32[48,512]{1,0:T(8,128)S(1)}, u32[]{:S(2)}, u32[]{:S(2)}) collective-permute-start(f32[48,512]{1,0:T(8,128)S(1)} %get-tuple-element.41), channel_id=1, source_target_pairs={{0,4},{2,6},{4,8},{6,10},{8,12},{10,14},{12,0},{14,2},{1,5},{3,7},... | collective-permute-start | bytes 294920 | tf_op jit(solution)/shard_map/ppermute | solution.py:16
  42.5 0.0 collective-permute-start.7
  42.5 0.0 collective-permute-start.10
  42.5 4.1 %collective-permute-done.8 = f32[48,512]{1,0:T(8,128)S(1)} collective-permute-done((f32[48,512]{1,0:T(8,128)S(1)}, f32[48,512]{1,0:T(8,128)S(1)}, u32[]{:S(2)}, u32[]{:S(2)}) %collective-permute-start.8) | collective-permute-done | bytes 98336 | tf_op jit(solution)/shard_map/ppermute | solution.py:16
  46.6 4.8 %collective-permute-start.9 = (f32[32,512]{1,0:T(8,128)S(1)}, f32[32,512]{1,0:T(8,128)S(1)}, u32[]{:S(2)}, u32[]{:S(2)}) collective-permute-start(f32[32,512]{1,0:T(8,128)S(1)} %pad_maximum_fusion), channel_id=1, source_target_pairs={{0,4},{2,6},{4,8},{6,10},{8,12},{10,14},{12,0},{14,2},{1,5},{3,7},... | collective-permute-start | bytes 196616 | tf_op jit(solution)/shard_map/ppermute | solution.py:16
  51.4 0.0 collective-permute-done.5
  51.4 0.0 collective-permute-done.7
  51.4 0.1 add_add_fusion
  51.5 0.0 collective-permute-done.10
  51.5 0.1 collective-permute-start.13
  51.6 2.0 %collective-permute-start.12 = (f32[32,512]{1,0:T(8,128)S(1)}, f32[32,512]{1,0:T(8,128)S(1)}, u32[]{:S(2)}, u32[]{:S(2)}) collective-permute-start(f32[32,512]{1,0:T(8,128)S(1)} %get-tuple-element.39), channel_id=1, source_target_pairs={{0,2},{2,4},{4,6},{6,8},{8,10},{10,12},{12,14},{14,0},{1,3},{3,5},... | collective-permute-start | bytes 196616 | tf_op jit(solution)/shard_map/ppermute | solution.py:16
  53.7 0.1 collective-permute-start.11
  53.7 0.0 collective-permute-done.9
  53.8 2.1 %collective-permute-done.13 = f32[32,512]{1,0:T(8,128)S(1)} collective-permute-done((f32[32,512]{1,0:T(8,128)S(1)}, f32[32,512]{1,0:T(8,128)S(1)}, u32[]{:S(2)}, u32[]{:S(2)}) %collective-permute-start.13) | collective-permute-done | bytes 65568 | tf_op jit(solution)/shard_map/ppermute | solution.py:16
  55.9 0.3 collective-permute-done.12
  56.1 4.7 %collective-permute-done.11 = f32[32,512]{1,0:T(8,128)S(1)} collective-permute-done((f32[32,512]{1,0:T(8,128)S(1)}, f32[32,512]{1,0:T(8,128)S(1)}, u32[]{:S(2)}, u32[]{:S(2)}) %collective-permute-start.11) | collective-permute-done | bytes 65568 | tf_op jit(solution)/shard_map/ppermute | solution.py:16
  60.8 0.0 copy-done.2
  60.8 0.6 shard_map.57.refs_1_
  61.4 1.6 %collective-permute-start.14 = (f32[32,512]{1,0:T(8,128)S(1)}, f32[32,512]{1,0:T(8,128)S(1)}, u32[]{:S(2)}, u32[]{:S(2)}) collective-permute-start(f32[32,512]{1,0:T(8,128)S(1)} %shard_map.57.refs_1_), channel_id=1, source_target_pairs={{0,64},{64,128},{128,192},{192,0},{1,65},{65,129},{129,193},{193,1... | collective-permute-start | bytes 196616 | tf_op jit(solution)/shard_map/ppermute | solution.py:16
  63.0 2.9 %collective-permute-start.16 = (f32[32,512]{1,0:T(8,128)S(1)}, f32[32,512]{1,0:T(8,128)S(1)}, u32[]{:S(2)}, u32[]{:S(2)}) collective-permute-start(f32[32,512]{1,0:T(8,128)S(1)} %shard_map.57.refs_1_), channel_id=1, source_target_pairs={{0,128},{64,192},{128,0},{192,64},{1,129},{65,193},{129,1},{193,65... | collective-permute-start | bytes 196616 | tf_op jit(solution)/shard_map/ppermute | solution.py:16
  65.9 1.3 %collective-permute-start.17 = (f32[32,512]{1,0:T(8,128)S(1)}, f32[32,512]{1,0:T(8,128)S(1)}, u32[]{:S(2)}, u32[]{:S(2)}) collective-permute-start(f32[32,512]{1,0:T(8,128)S(1)} %shard_map.57.refs_1_), channel_id=1, source_target_pairs={{0,192},{64,0},{128,64},{192,128},{1,193},{65,1},{129,65},{193,129... | collective-permute-start | bytes 196616 | tf_op jit(solution)/shard_map/ppermute | solution.py:16
  67.3 0.0 collective-permute-done.14.refs_0_
  67.3 0.3 shard_map.58.refs_2_
  67.5 0.7 collective-permute-start.15
  68.2 2.2 %collective-permute-start.19 = (f32[32,512]{1,0:T(8,128)S(1)}, f32[32,512]{1,0:T(8,128)S(1)}, u32[]{:S(2)}, u32[]{:S(2)}) collective-permute-start(f32[32,512]{1,0:T(8,128)S(1)} %shard_map.58.refs_2_), channel_id=1, source_target_pairs={{0,128},{64,192},{128,0},{192,64},{1,129},{65,193},{129,1},{193,65... | collective-permute-start | bytes 196616 | tf_op jit(solution)/shard_map/ppermute | solution.py:16
  70.5 0.0 collective-permute-done.16.refs_0_
  70.5 0.0 collective-permute-done.17.refs_1_
  70.5 0.3 shard_map.59.refs_1_
  70.7 2.3 %collective-permute-done.15.refs_0_ = f32[32,512]{1,0:T(8,128)S(1)} collective-permute-done((f32[32,512]{1,0:T(8,128)S(1)}, f32[32,512]{1,0:T(8,128)S(1)}, u32[]{:S(2)}, u32[]{:S(2)}) %collective-permute-start.15) | collective-permute-done | bytes 65568 | tf_op jit(solution)/shard_map/ppermute | solution.py:16
  73.0 0.3 shard_map.60.refs_1_
  73.3 0.0 collective-permute-start.18
  73.3 0.7 collective-permute-done.19.refs_0_
  74.0 0.3 shard_map.61.refs_1_
  74.3 4.5 %collective-permute-done.18.refs_0_ = f32[32,512]{1,0:T(8,128)S(1)} collective-permute-done((f32[32,512]{1,0:T(8,128)S(1)}, f32[32,512]{1,0:T(8,128)S(1)}, u32[]{:S(2)}, u32[]{:S(2)}) %collective-permute-start.18) | collective-permute-done | bytes 65568 | tf_op jit(solution)/shard_map/ppermute | solution.py:16
  78.8 0.9 %shard_map.62 = f32[32,512]{1,0:T(8,128)} custom-call(s32[1]{0:T(128)} %bitcast.place, f32[32,512]{1,0:T(8,128)S(1)} %collective-permute-done.18.refs_0_, f32[32,512]{1,0:T(8,128)S(1)} %shard_map.61.refs_1_, bf16[3,512,512]{2,1,0:T(8,128)(2,1)S(1)} %get-tuple-element.29.refs_2_.refs_3_, bf16[3,512,512]{2,1,0:T(8,128)(2,1)S(1)} %get-tuple-element.30.refs_3_.refs_4_), custom_call_target="tpu_custom_call" | custom-call | tf_op jit(solution)/shard_map/pallas_call | solution.py:149
  (12 shorter events, 0.2 us)
Async XLA Ops:
  0.1 11.0 %copy-start = (f32[512,512]{1,0:T(8,128)S(1)}, f32[512,512]{1,0:T(8,128)}, u32[]{:S(2)}) copy-start(f32[512,512]{1,0:T(8,128)} %diag.3) | copy-start | bytes 3145732
  0.1 11.0 %copy-start.1 = (f32[512,1536]{1,0:T(8,128)S(1)}, f32[512,1536]{1,0:T(8,128)}, u32[]{:S(2)}) copy-start(f32[512,1536]{1,0:T(8,128)} %coupling.1) | copy-start | bytes 9437188
  9.0 2.0 %collective-permute-start = (f32[8,32,512]{2,1,0:T(8,128)S(1)}, f32[8,32,512]{2,1,0:T(8,128)S(1)}, u32[]{:S(2)}, u32[]{:S(2)}) collective-permute-start(f32[8,32,512]{2,1,0:T(8,128)S(1)} %get-tuple-element.20), channel_id=1, source_target_pairs={{0,1},{1,0},{2,3},{3,2},{4,5},{5,4},{6,7},{7,6},{8,9},{9,8},{10,11... | collective-permute-start | bytes 1572872 | tf_op jit(solution)/shard_map/ppermute | solution.py:16
  11.0 6.7 %collective-permute-start.1 = (f32[3,8,32,512]{3,2,1,0:T(8,128)S(1)}, f32[3,8,32,512]{3,2,1,0:T(8,128)S(1)}, u32[]{:S(2)}, u32[]{:S(2)}) collective-permute-start(f32[3,8,32,512]{3,2,1,0:T(8,128)S(1)} %get-tuple-element.21), channel_id=1, source_target_pairs={{0,1},{1,0},{2,3},{3,2},{4,5},{5,4},{6,7},{7,6},{8,9},{9,8},{10,11... | collective-permute-start | bytes 4718600 | tf_op jit(solution)/shard_map/ppermute | solution.py:16
  14.8 12.6 %collective-permute-start.6 = (f32[4,32,512]{2,1,0:T(8,128)S(1)}, f32[4,32,512]{2,1,0:T(8,128)S(1)}, u32[]{:S(2)}, u32[]{:S(2)}) collective-permute-start(f32[4,32,512]{2,1,0:T(8,128)S(1)} %get-tuple-element.37), channel_id=1, source_target_pairs={{0,48},{16,0},{32,16},{48,32},{1,49},{17,1},{33,17},{49,33},{2,50}... | collective-permute-start | bytes 786440 | tf_op jit(solution)/shard_map/ppermute | solution.py:16
  17.7 9.5 %collective-permute-start.2 = (f32[4,32,512]{2,1,0:T(8,128)S(1)}, f32[4,32,512]{2,1,0:T(8,128)S(1)}, u32[]{:S(2)}, u32[]{:S(2)}) collective-permute-start(f32[4,32,512]{2,1,0:T(8,128)S(1)} %get-tuple-element.38), channel_id=1, source_target_pairs={{0,16},{16,32},{32,48},{48,0},{1,17},{17,33},{33,49},{49,1},{2,18}... | collective-permute-start | bytes 786440 | tf_op jit(solution)/shard_map/ppermute | solution.py:16
  18.0 11.3 %collective-permute-start.4 = (f32[4,32,512]{2,1,0:T(8,128)S(1)}, f32[4,32,512]{2,1,0:T(8,128)S(1)}, u32[]{:S(2)}, u32[]{:S(2)}) collective-permute-start(f32[4,32,512]{2,1,0:T(8,128)S(1)} %slice_bitcast_fusion.3), channel_id=1, source_target_pairs={{0,48},{16,0},{32,16},{48,32},{1,49},{17,1},{33,17},{49,33},{2,50}... | collective-permute-start | bytes 786440 | tf_op jit(solution)/shard_map/ppermute | solution.py:16
  27.2 10.5 %collective-permute-start.3 = (f32[4,32,512]{2,1,0:T(8,128)S(1)}, f32[4,32,512]{2,1,0:T(8,128)S(1)}, u32[]{:S(2)}, u32[]{:S(2)}) collective-permute-start(f32[4,32,512]{2,1,0:T(8,128)S(1)} %get-tuple-element.36), channel_id=1, source_target_pairs={{0,16},{16,32},{32,48},{48,0},{1,17},{17,33},{33,49},{49,1},{2,18}... | collective-permute-start | bytes 786440 | tf_op jit(solution)/shard_map/ppermute | solution.py:16
  27.3 24.1 %collective-permute-start.5 = (f32[4,32,512]{2,1,0:T(8,128)S(1)}, f32[4,32,512]{2,1,0:T(8,128)S(1)}, u32[]{:S(2)}, u32[]{:S(2)}) collective-permute-start(f32[4,32,512]{2,1,0:T(8,128)S(1)} %get-tuple-element.35), channel_id=1, source_target_pairs={{0,16},{16,32},{32,48},{48,0},{1,17},{17,33},{33,49},{49,1},{2,18}... | collective-permute-start | bytes 786440 | tf_op jit(solution)/shard_map/ppermute | solution.py:16
  37.9 22.9 %copy-start.2 = (f32[512,32]{0,1:T(8,128)S(1)}, f32[512,32]{0,1:T(8,128)}, u32[]{:S(2)}) copy-start(f32[512,32]{0,1:T(8,128)} %param.5) | copy-start | bytes 196612
  37.9 8.7 %collective-permute-start.8 = (f32[48,512]{1,0:T(8,128)S(1)}, f32[48,512]{1,0:T(8,128)S(1)}, u32[]{:S(2)}, u32[]{:S(2)}) collective-permute-start(f32[48,512]{1,0:T(8,128)S(1)} %get-tuple-element.41), channel_id=1, source_target_pairs={{0,4},{2,6},{4,8},{6,10},{8,12},{10,14},{12,0},{14,2},{1,5},{3,7},... | collective-permute-start | bytes 294920 | tf_op jit(solution)/shard_map/ppermute | solution.py:16
  42.5 8.9 %collective-permute-start.7 = (f32[4,32,512]{2,1,0:T(8,128)S(1)}, f32[4,32,512]{2,1,0:T(8,128)S(1)}, u32[]{:S(2)}, u32[]{:S(2)}) collective-permute-start(f32[4,32,512]{2,1,0:T(8,128)S(1)} %get-tuple-element.31), channel_id=1, source_target_pairs={{0,48},{16,0},{32,16},{48,32},{1,49},{17,1},{33,17},{49,33},{2,50}... | collective-permute-start | bytes 786440 | tf_op jit(solution)/shard_map/ppermute | solution.py:16
  42.5 9.0 %collective-permute-start.10 = (f32[48,512]{1,0:T(8,128)S(1)}, f32[48,512]{1,0:T(8,128)S(1)}, u32[]{:S(2)}, u32[]{:S(2)}) collective-permute-start(f32[48,512]{1,0:T(8,128)S(1)} %get-tuple-element.42), channel_id=1, source_target_pairs={{0,12},{2,14},{4,0},{6,2},{8,4},{10,6},{12,8},{14,10},{1,13},{3,15... | collective-permute-start | bytes 294920 | tf_op jit(solution)/shard_map/ppermute | solution.py:16
  46.6 7.1 %collective-permute-start.9 = (f32[32,512]{1,0:T(8,128)S(1)}, f32[32,512]{1,0:T(8,128)S(1)}, u32[]{:S(2)}, u32[]{:S(2)}) collective-permute-start(f32[32,512]{1,0:T(8,128)S(1)} %pad_maximum_fusion), channel_id=1, source_target_pairs={{0,4},{2,6},{4,8},{6,10},{8,12},{10,14},{12,0},{14,2},{1,5},{3,7},... | collective-permute-start | bytes 196616 | tf_op jit(solution)/shard_map/ppermute | solution.py:16
  51.5 4.3 %collective-permute-start.13 = (f32[32,512]{1,0:T(8,128)S(1)}, f32[32,512]{1,0:T(8,128)S(1)}, u32[]{:S(2)}, u32[]{:S(2)}) collective-permute-start(f32[32,512]{1,0:T(8,128)S(1)} %get-tuple-element.40), channel_id=1, source_target_pairs={{0,14},{2,0},{4,2},{6,4},{8,6},{10,8},{12,10},{14,12},{1,15},{3,1}... | collective-permute-start | bytes 196616 | tf_op jit(solution)/shard_map/ppermute | solution.py:16
  51.6 4.5 %collective-permute-start.12 = (f32[32,512]{1,0:T(8,128)S(1)}, f32[32,512]{1,0:T(8,128)S(1)}, u32[]{:S(2)}, u32[]{:S(2)}) collective-permute-start(f32[32,512]{1,0:T(8,128)S(1)} %get-tuple-element.39), channel_id=1, source_target_pairs={{0,2},{2,4},{4,6},{6,8},{8,10},{10,12},{12,14},{14,0},{1,3},{3,5},... | collective-permute-start | bytes 196616 | tf_op jit(solution)/shard_map/ppermute | solution.py:16
  53.7 7.2 %collective-permute-start.11 = (f32[32,512]{1,0:T(8,128)S(1)}, f32[32,512]{1,0:T(8,128)S(1)}, u32[]{:S(2)}, u32[]{:S(2)}) collective-permute-start(f32[32,512]{1,0:T(8,128)S(1)} %pad_maximum_fusion.1), channel_id=1, source_target_pairs={{0,12},{2,14},{4,0},{6,2},{8,4},{10,6},{12,8},{14,10},{1,13},{3,15... | collective-permute-start | bytes 196616 | tf_op jit(solution)/shard_map/ppermute | solution.py:16
  61.4 5.8 %collective-permute-start.14 = (f32[32,512]{1,0:T(8,128)S(1)}, f32[32,512]{1,0:T(8,128)S(1)}, u32[]{:S(2)}, u32[]{:S(2)}) collective-permute-start(f32[32,512]{1,0:T(8,128)S(1)} %shard_map.57.refs_1_), channel_id=1, source_target_pairs={{0,64},{64,128},{128,192},{192,0},{1,65},{65,129},{129,193},{193,1... | collective-permute-start | bytes 196616 | tf_op jit(solution)/shard_map/ppermute | solution.py:16
  63.0 7.5 %collective-permute-start.16 = (f32[32,512]{1,0:T(8,128)S(1)}, f32[32,512]{1,0:T(8,128)S(1)}, u32[]{:S(2)}, u32[]{:S(2)}) collective-permute-start(f32[32,512]{1,0:T(8,128)S(1)} %shard_map.57.refs_1_), channel_id=1, source_target_pairs={{0,128},{64,192},{128,0},{192,64},{1,129},{65,193},{129,1},{193,65... | collective-permute-start | bytes 196616 | tf_op jit(solution)/shard_map/ppermute | solution.py:16
  65.9 4.6 %collective-permute-start.17 = (f32[32,512]{1,0:T(8,128)S(1)}, f32[32,512]{1,0:T(8,128)S(1)}, u32[]{:S(2)}, u32[]{:S(2)}) collective-permute-start(f32[32,512]{1,0:T(8,128)S(1)} %shard_map.57.refs_1_), channel_id=1, source_target_pairs={{0,192},{64,0},{128,64},{192,128},{1,193},{65,1},{129,65},{193,129... | collective-permute-start | bytes 196616 | tf_op jit(solution)/shard_map/ppermute | solution.py:16
  67.5 5.5 %collective-permute-start.15 = (f32[32,512]{1,0:T(8,128)S(1)}, f32[32,512]{1,0:T(8,128)S(1)}, u32[]{:S(2)}, u32[]{:S(2)}) collective-permute-start(f32[32,512]{1,0:T(8,128)S(1)} %shard_map.58.refs_2_), channel_id=1, source_target_pairs={{0,64},{64,128},{128,192},{192,0},{1,65},{65,129},{129,193},{193,1... | collective-permute-start | bytes 196616 | tf_op jit(solution)/shard_map/ppermute | solution.py:16
  68.2 5.8 %collective-permute-start.19 = (f32[32,512]{1,0:T(8,128)S(1)}, f32[32,512]{1,0:T(8,128)S(1)}, u32[]{:S(2)}, u32[]{:S(2)}) collective-permute-start(f32[32,512]{1,0:T(8,128)S(1)} %shard_map.58.refs_2_), channel_id=1, source_target_pairs={{0,128},{64,192},{128,0},{192,64},{1,129},{65,193},{129,1},{193,65... | collective-permute-start | bytes 196616 | tf_op jit(solution)/shard_map/ppermute | solution.py:16
  73.3 5.5 %collective-permute-start.18 = (f32[32,512]{1,0:T(8,128)S(1)}, f32[32,512]{1,0:T(8,128)S(1)}, u32[]{:S(2)}, u32[]{:S(2)}) collective-permute-start(f32[32,512]{1,0:T(8,128)S(1)} %shard_map.60.refs_1_), channel_id=1, source_target_pairs={{0,64},{64,128},{128,192},{192,0},{1,65},{65,129},{129,193},{193,1... | collective-permute-start | bytes 196616 | tf_op jit(solution)/shard_map/ppermute | solution.py:16
